TPU v7x, 256 devices: a whole 4x4x8 slice. The times are simulated.
256 devices in a mesh: slab: 64 (over z_hi, x, y, core), rep: 4 (over z_lo).
Axes of the slice: x: 4, y: 4, z: 8 (z_hi: 2, z_lo: 4; z = z_hi * 4 + z_lo), core: 2. Of those that a mesh axis runs over, the one named last changes fastest.
Arguments:
- embeddings: bfloat16 [262144, 512], P(('slab', 'rep')), may hold values from -6 to 6
- indicators: bfloat16 [262144, 256], P(('slab', 'rep')), may hold values from -6 to 6
- neighbours: int32 [256, 4], P(('slab', 'rep')), may hold values from 0 to 257, as said below
- hub_ids: int32 [2], replicated, may hold values from 0 to 255, as said below
- columns: int32 [262144, 4, 16], P(('slab', 'rep')), may hold values from 0 to 1023
Outputs:
- propagated: bfloat16 [262144, 256], P(('slab', 'rep'))
Inputs may be any that keep to these rules, and one draw needn't show every extreme that they name: `neighbours`: slot 0 of block b is b; slot 1 names a block c with c // 4 == b // 4; slots 2 to 3 hold 256 + h for each hub number h once, in some order. `hub_ids`: distinct block ids; the last block, 255, is always one of the hubs.
All inputs are finite; a program needn't handle non-finite values.
Results may differ from a plain program's by a relative error of at most 0.0048.
Values may be sent and summed in bfloat16 or wider, within the bound.
No kernel may reach another device: no remote copies, remote signals or barrier semaphores. Data moves between devices by JAX's collectives and lax.ppermute only.
A program may use at most 64 MiB of HBM per device.

v0:
```python
import jax
import jax.numpy as jnp
from jax import lax
from jax.sharding import PartitionSpec as P

K = 4
HUBS = 2
ITERS = 2


EPS = 1e-06
TAU = 0.04
ALPHA = 0.8


def from_root(block, axis, source):
    block = jnp.where(lax.axis_index(axis) == source, block, jnp.zeros_like(block))
    return lax.psum(block, axis)


def normalize(rows):
    values = rows.astype(jnp.float32)
    return (values * lax.rsqrt(jnp.sum(values * values, axis=1, keepdims=True) + EPS)).astype(
        jnp.bfloat16
    )


def edge_weight(cosine, kept):
    col_ids = lax.broadcasted_iota(jnp.int32, cosine.shape, 1)
    hit = kept[:, 0:1] == col_ids
    for which in range(1, kept.shape[1]):
        hit = hit | (kept[:, which : which + 1] == col_ids)
    return jnp.where(hit, jnp.exp((cosine - 1.0) / TAU), 0.0)


def pick_block(pool, pool_ids, target):
    position = jnp.argmax((pool_ids == target).astype(jnp.int32))
    return lax.dynamic_index_in_dim(pool, position, 0, keepdims=False)


def spread_hubs(joined, hub_ids, first):
    received = []
    for which in range(HUBS):
        root = hub_ids[which]
        if first:
            got = from_root(joined, ("slab", "rep"), root)
        else:
            got = from_root(joined, ("slab", "rep"), root)
        received.append(got)
    return jnp.stack(received, axis=0)


def body(embeddings, indicators, neighbours, hub_ids, columns):
    group_size = lax.axis_size("rep")
    total_blocks = lax.axis_size("slab") * group_size
    own_block = lax.axis_index(("slab", "rep"))
    group_ids = own_block - own_block % group_size + jnp.arange(group_size, dtype=jnp.int32)
    pool_ids = jnp.concatenate(
        [group_ids, total_blocks + jnp.arange(HUBS, dtype=jnp.int32)], axis=0
    )
    width = embeddings.shape[1]
    normed = normalize(embeddings)
    joined = jnp.concatenate([normed, indicators], axis=1)
    group_joined = lax.all_gather(joined[None], "rep", axis=0, tiled=True)
    hub_joined = spread_hubs(joined, hub_ids, True)
    pool = jnp.concatenate([group_joined, hub_joined], axis=0)
    pool_x = pool[:, :, :width]
    pool_y = pool[:, :, width:]
    degree = jnp.zeros((embeddings.shape[0],), jnp.float32)
    tiles = []
    for slot in range(K):
        other = pick_block(pool_x, pool_ids, neighbours[0, slot])
        cosine = jnp.dot(normed, other.T, preferred_element_type=jnp.float32)
        raw = edge_weight(cosine, columns[:, slot, :])
        degree = degree + jnp.sum(raw, axis=1)
        tiles.append(raw.astype(jnp.bfloat16))
    anchor = indicators.astype(jnp.float32)
    current = indicators
    for step in range(ITERS):
        if step > 0:
            group_y = lax.all_gather(current[None], "rep", axis=0, tiled=True)
            hub_y = spread_hubs(current, hub_ids, False)
            pool_y = jnp.concatenate([group_y, hub_y], axis=0)
        gathered = jnp.zeros((indicators.shape[0], indicators.shape[1]), jnp.float32)
        for slot in range(K):
            other_y = pick_block(pool_y, pool_ids, neighbours[0, slot])
            gathered = gathered + jnp.dot(tiles[slot], other_y, preferred_element_type=jnp.float32)
        current = (ALPHA * gathered / degree[:, None] + (1.0 - ALPHA) * anchor).astype(jnp.bfloat16)
    return current


def solution(mesh):
    return jax.shard_map(
        body,
        mesh=mesh,
        in_specs=(
            P(("slab", "rep"), None),
            P(("slab", "rep"), None),
            P(("slab", "rep"), None),
            P(),
            P(("slab", "rep"), None, None),
        ),
        out_specs=P(("slab", "rep"), None),
        check_vma=False,
    )
```

profile of v0, /device:TPU:161, one launch (start us, length us, event | category | flops | bytes accessed | tf_op | source)
XLA Modules:
  0.0 720.0 jit_solution(13616563797122136400)
XLA Ops:
  7.4 1.4 fusion.125
  10.1 1.5 fusion.60
  11.6 1.5 fusion.61
  13.2 4.0 pad_maximum_fusion.3
  17.9 0.6 fusion.124
  18.6 1.3 fusion.119
  21.0 1.3 fusion.117
  23.6 1.3 fusion.116
  26.2 1.3 fusion.118
  31.5 340.7 %all-reduce.7.cloned.1.call-done = (bf16[1,1024,768]{2,1,0:T(8,128)(2,1)}, bf16[1,1024,768]{2,1,0:T(8,128)(2,1)}) async-done(((bf16[1,1024,768]{2,1,0:T(8,128)(2,1)}, bf16[1,1024,768]{2,1,0:T(8,128)(2,1)}), (bf16[1,1024,768]{2,1,0:T(8,128)(2,1)}, bf16[1,1024,768]{2,1,0:T(8,128)(2,1)})) %all-reduce.7.cloned.1.call-update) | async-done | bytes 3145744 | tf_op jit(solution)/shard_map/psum | solution.py:18
  372.1 4.0 pad_maximum_fusion.1
  376.1 1.0 slice-done.1
  378.0 1.2 pad_maximum_fusion
  379.7 9.4 %fusion.128 = (f32[1024]{0:T(1024)S(1)}, bf16[1024,1024]{0,1:T(8,128)(2,1)S(1)}) fusion(bf16[1024,512]{1,0:T(8,128)(2,1)S(1)} %fusion.61, bf16[6,1024,512]{2,1,0:T(8,128)(2,1)S(1)} %slice.330, s32[]{:T(128)S(6)} %select_n.85, s32[1024]{0:T(1024)S(1)} %bitcast.198, s32[1024]{0:T(1024)S(1)} %bitcast.199, s32[1024]{0:T(1024)S(1)} %bitcast.200, ...), kind=kOutput, calls=%fused_computation.226 | convolution fusion | flops 1111489536 | bytes 4263940 | tf_op jit(solution)/shard_map/dot_general | solution.py:73
  389.1 0.8 fusion.85
  389.9 0.6 copy-done.11
  390.4 9.3 %fusion.129 = (f32[1024]{0:T(1024)S(1)}, bf16[1024,1024]{0,1:T(8,128)(2,1)S(1)}) fusion(bf16[1024,512]{1,0:T(8,128)(2,1)S(1)} %fusion.61, bf16[6,1024,512]{2,1,0:T(8,128)(2,1)S(1)} %slice.330, s32[]{:T(128)S(6)} %select_n.87, s32[1024]{0:T(1024)S(1)} %bitcast.166, s32[1024]{0:T(1024)S(1)} %bitcast.167, s32[1024]{0:T(1024)S(1)} %bitcast.168, ...), kind=kOutput, calls=%fused_computation.227 | convolution fusion | flops 1111489536 | bytes 4263940 | tf_op jit(solution)/shard_map/dot_general | solution.py:73
  399.8 0.8 convolution_add_fusion.5
  400.6 9.4 %fusion.127 = (f32[1024]{0:T(1024)S(1)}, bf16[1024,1024]{0,1:T(8,128)(2,1)S(1)}) fusion(bf16[1024,512]{1,0:T(8,128)(2,1)S(1)} %fusion.61, bf16[6,1024,512]{2,1,0:T(8,128)(2,1)S(1)} %slice.330, s32[]{:T(128)S(6)} %select_n.89, s32[1024]{0:T(1024)S(1)} %bitcast.182, s32[1024]{0:T(1024)S(1)} %bitcast.183, s32[1024]{0:T(1024)S(1)} %bitcast.184, ...), kind=kOutput, calls=%fused_computation.225 | convolution fusion | flops 1111489536 | bytes 4263940 | tf_op jit(solution)/shard_map/dot_general | solution.py:73
  410.0 0.8 convolution_add_fusion.4
  410.8 9.6 %fusion.126 = (f32[1024]{0:T(1024)S(1)}, bf16[1024,1024]{0,1:T(8,128)(2,1)S(1)}) fusion(bf16[1024,512]{1,0:T(8,128)(2,1)S(1)} %fusion.61, bf16[6,1024,512]{2,1,0:T(8,128)(2,1)S(1)} %slice.330, s32[]{:T(128)S(6)} %select_n.91, s32[1024]{0:T(1024)S(1)} %bitcast.150, s32[1024]{0:T(1024)S(1)} %bitcast.151, s32[1024]{0:T(1024)S(1)} %bitcast.152, ...), kind=kOutput, calls=%fused_computation.224 | convolution fusion | flops 1111489536 | bytes 4263940 | tf_op jit(solution)/shard_map/dot_general | solution.py:73
  420.4 1.3 copy-done.12
  421.7 0.9 fusion.68
  422.6 1.2 select_bitcast_fusion.3
  424.4 278.6 %all-reduce.5.cloned.1.call-done = (bf16[1,1024,256]{2,1,0:T(8,128)(2,1)}, bf16[1,1024,256]{2,1,0:T(8,128)(2,1)}) async-done(((bf16[1,1024,256]{2,1,0:T(8,128)(2,1)}, bf16[1,1024,256]{2,1,0:T(8,128)(2,1)}), (bf16[1,1024,256]{2,1,0:T(8,128)(2,1)}, bf16[1,1024,256]{2,1,0:T(8,128)(2,1)})) %all-reduce.5.cloned.1.call-update) | async-done | bytes 1048592 | tf_op jit(solution)/shard_map/psum | solution.py:18
  702.9 2.3 pad_maximum_fusion.2
  705.3 2.5 fusion.83
  707.8 0.8 convolution_add_fusion.2
  708.5 0.8 copy-done.10
  709.3 0.7 convolution_add_fusion.1
  710.1 0.8 copy-done.13
  710.9 1.7 fusion.69
  (49 shorter events, 3.0 us)
Async XLA Ops:
  7.4 364.7 %all-reduce.7.cloned.1.call-start = ((), (), s32[]{:S(2)}) async-start(), calls=%async_computation.3 | async-start | bytes 6291456 | tf_op jit(solution)/shard_map/psum | solution.py:18
  13.1 4.8 copy-start.6
  13.2 18.0 %copy-start.5 = (s32[1024,4,16]{0,2,1:T(8,128)S(1)}, s32[1024,4,16]{0,2,1:T(8,128)}, u32[]{:S(2)}) copy-start(s32[1024,4,16]{0,2,1:T(8,128)} %param.9) | copy-start | bytes 786436
  17.2 354.9 %all-gather.5.cloned.1.call-start = ((), (), s32[]{:S(2)}) async-start(), calls=%async_computation | async-start | bytes 7864320 | tf_op jit(solution)/shard_map/all_gather | solution.py:64
  17.8 685.2 %all-reduce.5.cloned.1.call-start = ((), (), s32[]{:S(2)}) async-start(), calls=%async_computation.2 | async-start | bytes 2097152 | tf_op jit(solution)/shard_map/psum | solution.py:18
  372.1 4.0 slice-start
  372.1 5.0 slice-start.1
  372.1 5.4 copy-start
  372.1 5.8 copy-start.1
  379.7 9.4 %copy-start.2 = (bf16[6,1024,256]{2,1,0:T(8,128)(2,1)S(1)}, bf16[6,1024,256]{2,1,0:T(8,128)(2,1)}, u32[]{:S(2)}) copy-start(bf16[6,1024,256]{2,1,0:T(8,128)(2,1)} %pad_maximum_fusion.1) | copy-start | bytes 9437188
  389.1 1.4 copy-start.11
  399.8 10.2 %copy-start.7 = (bf16[1024,1024]{0,1:T(8,128)(2,1)}, bf16[1024,1024]{0,1:T(8,128)(2,1)S(1)}, u32[]{:S(2)}) copy-start(bf16[1024,1024]{0,1:T(8,128)(2,1)S(1)} %get-tuple-element.103) | copy-start | bytes 6291460
  410.0 10.4 %copy-start.9 = (bf16[1024,1024]{0,1:T(8,128)(2,1)}, bf16[1024,1024]{0,1:T(8,128)(2,1)S(1)}, u32[]{:S(2)}) copy-start(bf16[1024,1024]{0,1:T(8,128)(2,1)S(1)} %get-tuple-element.99) | copy-start | bytes 6291460
  410.8 10.9 %copy-start.4 = (bf16[1024,256]{1,0:T(8,128)(2,1)S(1)}, bf16[1024,256]{1,0:T(8,128)(2,1)}, u32[]{:S(2)}) copy-start(bf16[1024,256]{1,0:T(8,128)(2,1)} %param.6) | copy-start | bytes 1572868
  420.4 1.3 copy-start.12
  422.6 1.2 copy-start.3
  423.8 279.2 %all-gather.7.cloned.1.call-start = ((), (), s32[]{:S(2)}) async-start(), calls=%async_computation.1 | async-start | bytes 2621440 | tf_op jit(solution)/shard_map/all_gather | solution.py:81
  705.2 2.5 copy-start.8
  707.7 1.6 copy-start.10
  709.3 1.6 copy-start.13
Sparse Core Ops, SparseCore 0:
  17.3 354.7 all-reduce.6
  423.9 278.9 all-reduce.4
Sparse Core Ops, SparseCore 1:
  19.6 118.1 all-gather.4
  426.1 50.9 all-gather.6
where the time goes:
time: 726 us; the launch traced here: 720 us
  waiting for transfers between devices  620 us (85%)
  matrix products  46.5 us (6%)
  between operations  23.9 us (3%)
  other arithmetic  21 us (3%)
  local copies, waits for them, and re-layouts  8.25 us (1%)
    psum x2, waiting for transfers between devices, from_root(): return lax.psum(block, axis)  619 us
    dot_general x4, matrix products, body(): cosine = jnp.dot(normed, other.T, preferred_element_type=jnp.float32)  37.7 us
  transfers between devices with their start and end apart: 4, of which 2 were waited for; matrix products, arithmetic and copies ran while one was open for 1% of the time, Pallas kernels for 0%

commit v1 on v0

v1 whole, which is shorter than its diff:
```python
import functools

import jax
import jax.numpy as jnp
from jax import lax
from jax.experimental import pallas as pl
from jax.experimental.pallas import tpu as pltpu
from jax.sharding import PartitionSpec as P

K = 4
HUBS = 2
TOPK = 16
LANES = 128
EPS = 1e-06
TAU = 0.04
ALPHA = 0.8
AXES = ("slab", "rep")
ROW_TILE = 256


def normalize(rows):
    values = rows.astype(jnp.float32)
    return (values * lax.rsqrt(jnp.sum(values * values, axis=1, keepdims=True) + EPS)).astype(
        jnp.bfloat16
    )


def words_kernel(cols_ref, out_ref):
    cols = cols_ref[...]
    low = cols & (LANES - 1)
    bit = jnp.left_shift(jnp.ones_like(cols), cols >> 7)
    lane = lax.broadcasted_iota(jnp.int32, (cols.shape[0], LANES), 1)
    for slot in range(K):
        word = jnp.zeros(lane.shape, jnp.int32)
        for t in range(slot * TOPK, (slot + 1) * TOPK):
            word = word | jnp.where(lane == low[:, t : t + 1], bit[:, t : t + 1], 0)
        out_ref[slot] = word


def keep_words(columns):
    rows = columns.shape[0]
    flat = columns.reshape(rows, K * TOPK)
    tile = 128
    return pl.pallas_call(
        words_kernel,
        out_shape=jax.ShapeDtypeStruct((K, rows, LANES), jnp.int32),
        grid=(rows // tile,),
        in_specs=[pl.BlockSpec((tile, K * TOPK), lambda r: (r, 0))],
        out_specs=pl.BlockSpec((K, tile, LANES), lambda r: (0, r, 0)),
        cost_estimate=pl.CostEstimate(
            flops=rows * LANES * K * TOPK * 3, bytes_accessed=rows * K * (TOPK + LANES) * 4, transcendentals=0
        ),
        name="keep_words",
    )(flat)


def mix(acc, degree, anchor):
    return (ALPHA * acc / degree + (1.0 - ALPHA) * anchor.astype(jnp.float32)).astype(jnp.bfloat16)


def tile_kernel(width, has_in, sel_ref, x_ref, pool_ref, w_ref, *refs):
    if has_in:
        acc_in, deg_in, tile_ref, acc_ref, deg_ref = refs
    else:
        tile_ref, acc_ref, deg_ref = refs
    slot, row = pl.program_id(0), pl.program_id(1)
    here = pl.ds(pl.multiple_of(row * ROW_TILE, ROW_TILE), ROW_TILE)
    rows = pool_ref.shape[0] * pool_ref.shape[2]
    other = pool_ref[:, 0].reshape(rows, pool_ref.shape[3])
    cosine = lax.dot_general(
        x_ref[...], other[:, :width], (((1,), (1,)), ((), ())), preferred_element_type=jnp.float32
    )
    word = w_ref[0]
    total = jnp.zeros(word.shape, jnp.float32)
    for j in range(rows // LANES):
        part = cosine[:, j * LANES : (j + 1) * LANES]
        raw = jnp.where((word & (1 << j)) != 0, jnp.exp((part - 1.0) * (1.0 / TAU)), 0.0)
        total = total + raw
        tile_ref[0, :, j * LANES : (j + 1) * LANES] = raw.astype(jnp.bfloat16)
    gathered = jnp.dot(tile_ref[0], other[:, width:], preferred_element_type=jnp.float32)

    @pl.when(slot == 0)
    def _():
        acc_ref[here, :] = acc_in[here, :] + gathered if has_in else gathered
        deg_ref[here, :] = deg_in[here, :] + total if has_in else total

    @pl.when(slot > 0)
    def _():
        acc_ref[here, :] += gathered
        deg_ref[here, :] += total


def tiles_of(slots, pick, joined, pool, words, carry, width):
    rows, full = joined.shape
    clust = full - width
    first = slots[0]
    n = len(slots)
    whole = lambda shape: pl.BlockSpec(shape, lambda s, r, pick_ref: (0,) * len(shape))
    has_in = carry is not None
    outs = [
        jax.ShapeDtypeStruct((n, rows, rows), jnp.bfloat16),
        jax.ShapeDtypeStruct((rows, clust), jnp.float32),
        jax.ShapeDtypeStruct((rows, LANES), jnp.float32),
    ]
    return pl.pallas_call(
        functools.partial(tile_kernel, width, has_in),
        out_shape=outs,
        grid_spec=pltpu.PrefetchScalarGridSpec(
            num_scalar_prefetch=1,
            grid=(n, rows // ROW_TILE),
            in_specs=[
                pl.BlockSpec((ROW_TILE, width), lambda s, r, pick_ref: (r, 0)),
                pl.BlockSpec(
                    (pool.shape[0], 1, pool.shape[2], full), lambda s, r, pick_ref: (0, pick_ref[s], 0, 0)
                ),
                pl.BlockSpec((1, ROW_TILE, LANES), lambda s, r, pick_ref: (first + s, r, 0)),
            ]
            + ([whole((rows, clust)), whole((rows, LANES))] if has_in else []),
            out_specs=[
                pl.BlockSpec((1, ROW_TILE, rows), lambda s, r, pick_ref: (s, r, 0)),
                whole((rows, clust)),
                whole((rows, LANES)),
            ],
        ),
        compiler_params=pltpu.CompilerParams(vmem_limit_bytes=40 << 20),
        cost_estimate=pl.CostEstimate(
            flops=2 * n * rows * rows * full,
            bytes_accessed=n * rows * (2 * rows + 2 * full + 4 * LANES),
            transcendentals=n * rows * rows,
        ),
        name="tiles",
    )(pick, joined, pool, words, *(carry or ()))


def gather_kernel(last, has_in, sel_ref, tile_ref, pool_ref, *refs):
    refs = list(refs)
    acc_in = refs.pop(0) if has_in else None
    deg_ref, anchor_ref = (refs.pop(0), refs.pop(0)) if last else (None, None)
    out_ref, acc_ref = refs if last else (None, refs[0])
    slot = pl.program_id(0)
    row = pl.program_id(1)
    here = pl.ds(pl.multiple_of(row * ROW_TILE, ROW_TILE), ROW_TILE)
    rows = pool_ref.shape[0] * pool_ref.shape[2]
    other = pool_ref[:, 0].reshape(rows, pool_ref.shape[3])
    gathered = jnp.dot(tile_ref[0], other, preferred_element_type=jnp.float32)

    @pl.when(slot == 0)
    def _():
        acc_ref[here, :] = acc_in[here, :] + gathered if has_in else gathered

    @pl.when(slot > 0)
    def _():
        acc_ref[here, :] += gathered

    if last:

        @pl.when(slot == pl.num_programs(0) - 1)
        def _():
            degree = jnp.sum(deg_ref[here, :], axis=1, keepdims=True)
            out_ref[here, :] = mix(acc_ref[here, :], degree, anchor_ref[here, :])


def gather_of(pick, tiles, pool, acc, finish=None):
    n, rows, _ = tiles.shape
    clust = pool.shape[3]
    whole = lambda shape: pl.BlockSpec(shape, lambda s, r, pick_ref: (0,) * len(shape))
    has_in, last = acc is not None, finish is not None
    args = ([acc] if has_in else []) + (list(finish) if last else [])
    specs = ([whole((rows, clust))] if has_in else []) + (
        [whole((rows, LANES)), whole((rows, clust))] if last else []
    )
    return pl.pallas_call(
        functools.partial(gather_kernel, last, has_in),
        out_shape=jax.ShapeDtypeStruct((rows, clust), jnp.bfloat16 if last else jnp.float32),
        grid_spec=pltpu.PrefetchScalarGridSpec(
            num_scalar_prefetch=1,
            grid=(n, rows // ROW_TILE),
            in_specs=[
                pl.BlockSpec((1, ROW_TILE, rows), lambda s, r, pick_ref: (s, r, 0)),
                pl.BlockSpec(
                    (pool.shape[0], 1, pool.shape[2], clust), lambda s, r, pick_ref: (0, pick_ref[s], 0, 0)
                ),
            ]
            + specs,
            out_specs=whole((rows, clust)),
            scratch_shapes=[pltpu.VMEM((rows, clust), jnp.float32)] if last else [],
        ),
        compiler_params=pltpu.CompilerParams(vmem_limit_bytes=40 << 20),
        cost_estimate=pl.CostEstimate(
            flops=2 * n * rows * rows * clust,
            bytes_accessed=n * rows * (2 * rows + 2 * clust) + 8 * rows * clust,
            transcendentals=0,
        ),
        name="gather",
    )(pick, tiles, pool, *args)


def spread_hubs(block, hub_ids):
    slabs, reps = lax.axis_size("slab"), lax.axis_size("rep")
    halves = 2
    members = slabs // halves
    planes = [[h * members + m for m in range(members)] for h in range(halves)]
    rows, width = block.shape
    piece = rows // members
    mine = lax.all_to_all(
        block.reshape(members, piece, width), "slab", 0, 0, axis_index_groups=planes, tiled=True
    )
    own_z = lax.axis_index("slab") // members * reps + lax.axis_index("rep")
    hub_slab, hub_rep = hub_ids // reps, hub_ids % reps
    hub_z = hub_slab // members * reps + hub_rep
    member = hub_slab % members
    held = jnp.stack(
        [lax.dynamic_index_in_dim(mine, member[h], 0, keepdims=False) for h in range(HUBS)], axis=0
    )
    away = own_z ^ hub_z
    total = slabs * reps
    for bit in range((halves * reps - 1).bit_length()):
        pairs = []
        for device in range(total):
            slab, rep = divmod(device, reps)
            z = (slab // members * reps + rep) ^ (1 << bit)
            pairs.append((device, (z // reps * members + slab % members) * reps + z % reps))
        received = lax.ppermute(held, AXES, pairs)
        held = jnp.where(((away >> bit) & 1 == 1)[:, None, None], received, held)
    repeated = jnp.broadcast_to(held[None], (members,) + held.shape)
    return lax.all_to_all(repeated, "slab", 0, 0, axis_index_groups=planes, tiled=True)


def body(embeddings, indicators, neighbours, hub_ids, columns):
    rows, width = embeddings.shape
    clust = indicators.shape[1]
    reps = lax.axis_size("rep")
    total = lax.axis_size("slab") * reps
    slots = neighbours[0].astype(jnp.int32)
    zero = jnp.zeros((1,), jnp.int32)
    group_pick = (slots[1] % reps)[None]
    hub_pick = slots[2:] - total
    joined = jnp.concatenate([normalize(embeddings), indicators], axis=1)
    group = lax.all_gather(joined[None], "rep", axis=0, tiled=True)
    hubs = spread_hubs(joined, hub_ids)
    words = keep_words(columns)
    own_tiles, *carry = tiles_of((0,), zero, joined, joined[None, None], words, None, width)
    hub_tiles, *carry = tiles_of((2, 3), hub_pick, joined, hubs, words, carry, width)
    group_tiles, acc, degree = tiles_of((1,), group_pick, joined, group[None], words, carry, width)
    current = mix(acc, jnp.sum(degree, axis=1, keepdims=True), indicators)
    group = lax.all_gather(current[None], "rep", axis=0, tiled=True)
    hubs = spread_hubs(current, hub_ids)
    acc = gather_of(zero, own_tiles, current[None, None], None)
    acc = gather_of(group_pick, group_tiles, group[None], acc)
    return gather_of(hub_pick, hub_tiles, hubs, acc, (degree, indicators))


def solution(mesh):
    return jax.shard_map(
        body,
        mesh=mesh,
        in_specs=(
            P(("slab", "rep"), None),
            P(("slab", "rep"), None),
            P(("slab", "rep"), None),
            P(),
            P(("slab", "rep"), None, None),
        ),
        out_specs=P(("slab", "rep"), None),
        check_vma=False,
    )
```

time: 726 us -> 234 us (0.32)
  waiting for transfers between devices: 620 us -> 80.3 us
  matrix products: 46.5 us -> 0 us
  Pallas kernels: 0 us -> 45.4 us
  starting transfers between devices: 0.13 us -> 28.5 us
  local copies, waits for them, and re-layouts: 8.25 us -> 30.9 us
  blocking collectives: 0 us -> 16.7 us
  other arithmetic: 21 us -> 8.17 us
    psum x2 -> x0, waiting for transfers between devices: 619 us -> none  [from_root(): return lax.psum(block, axis)]
    ppermute x0 -> x6, waiting for transfers between devices: none -> 47.9 us  [spread_hubs(): received = lax.ppermute(held, AXES, pairs)]
    dot_general x12 -> x0, matrix products: 46.5 us -> none  [the longest x4 37.7 us: body(): cosine = jnp.dot(normed, other.T, preferred_element_type=jnp.float32)]
    pallas_call x0 -> x7, Pallas kernels: none -> 45.4 us  [the longest x1 20.4 us: keep_words(): pl.pallas_call(words_kernel, out_shape=jax.ShapeDtypeStruct((K, rows, LAN...]
    all_to_all x0 -> x3, waiting for transfers between devices: none -> 29.5 us  [the longest x1 17.9 us: spread_hubs(): lax.all_to_all(block.reshape(members, piece, width), 'slab', 0, 0, axis_i...]
    all_to_all x0 -> x3, starting transfers between devices: none -> 21.3 us  [the longest x2 13.6 us: spread_hubs(): lax.all_to_all(repeated, 'slab', 0, 0, axis_index_groups=planes, tiled=True)]
    unnamed x32 -> x52, local copies, waits for them, and re-layouts: 5.46 us -> 25.5 us
    all_to_all x0 -> x1, blocking collectives: none -> 16.7 us  [spread_hubs(): lax.all_to_all(block.reshape(members, piece, width), 'slab', 0, 0, axis_i...]
  transfers between devices with their start and end apart: 4 -> 11, of which waited for: 2 -> 10; matrix products, arithmetic and copies ran while one was open for 1% -> 3% of each run, Pallas kernels for 0% -> 16%
where the time goes in v1:
time: 234 us; the launch traced here: 230 us
  waiting for transfers between devices  80.3 us (34%)
  Pallas kernels  45.4 us (19%)
  local copies, waits for them, and re-layouts  30.9 us (13%)
  starting transfers between devices  28.5 us (12%)
  between operations  19.6 us (8%)
  blocking collectives  16.7 us (7%)
  other arithmetic  8.17 us (3%)
    ppermute x6, waiting for transfers between devices, spread_hubs(): received = lax.ppermute(held, AXES, pairs)  47.9 us
    unnamed x52, local copies, waits for them, and re-layouts  25.5 us
    pallas_call x1, Pallas kernels, keep_words(): pl.pallas_call(words_kernel, out_shape=jax.ShapeDtypeStruct((K, rows, LAN...  20.4 us
    all_to_all x1, waiting for transfers between devices, spread_hubs(): lax.all_to_all(block.reshape(members, piece, width), 'slab', 0, 0, axis_i...  17.9 us
    pallas_call x3, Pallas kernels, tiles_of(): pl.pallas_call(functools.partial(tile_kernel, width, has_in), out_shape=o...  17.8 us
    all_to_all x1, blocking collectives, spread_hubs(): lax.all_to_all(block.reshape(members, piece, width), 'slab', 0, 0, axis_i...  16.7 us
    all_to_all x2, starting transfers between devices, spread_hubs(): lax.all_to_all(repeated, 'slab', 0, 0, axis_index_groups=planes, tiled=True)  13.6 us
    all_to_all x2, waiting for transfers between devices, spread_hubs(): lax.all_to_all(repeated, 'slab', 0, 0, axis_index_groups=planes, tiled=True)  11.6 us
  transfers between devices with their start and end apart: 11, of which 10 were waited for; matrix products, arithmetic and copies ran while one was open for 3% of the time, Pallas kernels for 16%

profile of v1, /device:TPU:161, one launch (start us, length us, event | category | flops | bytes accessed | tf_op | source)
XLA Modules:
  0.0 229.7 jit_solution(12211860794634184382)
XLA Ops:
  9.6 2.0 fusion.4
  11.6 7.8 %all-to-all-start = ((bf16[32,32,768]{2,1,0:T(8,128)(2,1)}), bf16[32,32,768]{2,1,0:T(8,128)(2,1)S(1)}, u32[]{:S(2)}, u32[]{:S(2)}) async-start(bf16[32,32,768]{2,1,0:T(8,128)(2,1)} %bitcast.14), calls=%async_computation | async-start | bytes 3145728 | tf_op jit(solution)/shard_map/all_to_all | solution.py:205
  24.2 17.9 %all-to-all-done = bf16[32,32,768]{2,1,0:T(8,128)(2,1)S(1)} async-done(((bf16[32,32,768]{2,1,0:T(8,128)(2,1)}), bf16[32,32,768]{2,1,0:T(8,128)(2,1)S(1)}, u32[]{:S(2)}, u32[]{:S(2)}) %all-to-all-start) | async-done | bytes 1572896 | tf_op jit(solution)/shard_map/all_to_all | solution.py:205
  43.0 6.5 %collective-permute-done = bf16[2,32,768]{2,1,0:T(8,128)(2,1)S(1)} collective-permute-done((bf16[2,32,768]{2,1,0:T(8,128)(2,1)S(1)}, bf16[2,32,768]{2,1,0:T(8,128)(2,1)S(1)}, u32[]{:S(2)}, u32[]{:S(2)}) %collective-permute-start) | collective-permute-done | bytes 98336 | tf_op jit(solution)/shard_map/ppermute | solution.py:223
  49.5 3.2 %collective-permute-start.1 = (bf16[2,32,768]{2,1,0:T(8,128)(2,1)S(1)}, bf16[2,32,768]{2,1,0:T(8,128)(2,1)S(1)}, u32[]{:S(2)}, u32[]{:S(2)}) collective-permute-start(bf16[2,32,768]{2,1,0:T(8,128)(2,1)S(1)} %broadcast_select_fusion), channel_id=1, source_target_pairs={{0,2},{1,3},{2,0},{3,1},{4,6},{5,7},{6,4},{7,5},{8,10},{9,11},{10,... | collective-permute-start | bytes 294920 | tf_op jit(solution)/shard_map/ppermute | solution.py:223
  52.8 9.2 %collective-permute-done.1 = bf16[2,32,768]{2,1,0:T(8,128)(2,1)S(1)} collective-permute-done((bf16[2,32,768]{2,1,0:T(8,128)(2,1)S(1)}, bf16[2,32,768]{2,1,0:T(8,128)(2,1)S(1)}, u32[]{:S(2)}, u32[]{:S(2)}) %collective-permute-start.1) | collective-permute-done | bytes 98336 | tf_op jit(solution)/shard_map/ppermute | solution.py:223
  62.2 17.0 %collective-permute-done.2 = bf16[2,32,768]{2,1,0:T(8,128)(2,1)S(1)} collective-permute-done((bf16[2,32,768]{2,1,0:T(8,128)(2,1)S(1)}, bf16[2,32,768]{2,1,0:T(8,128)(2,1)S(1)}, u32[]{:S(2)}, u32[]{:S(2)}) %collective-permute-start.2) | collective-permute-done | bytes 98336 | tf_op jit(solution)/shard_map/ppermute | solution.py:223
  79.2 2.1 broadcast_in_dim.80
  81.3 7.2 %all-to-all-start.1 = ((bf16[32,2,32,768]{3,2,1,0:T(8,128)(2,1)}), bf16[32,2,32,768]{3,2,1,0:T(8,128)(2,1)}, u32[]{:S(2)}, u32[]{:S(2)}) async-start(bf16[32,2,32,768]{3,2,1,0:T(8,128)(2,1)} %broadcast_in_dim.80), calls=%async_computation.1 | async-start | bytes 6291456 | tf_op jit(solution)/shard_map/all_to_all | solution.py:226
  92.2 20.4 %keep_words.1.w_ref = s32[4,1024,128]{2,1,0:T(8,128)} custom-call(s32[1024,64]{1,0:T(8,128)} %copy.7.cols_ref), custom_call_target="tpu_custom_call" | custom-call | flops 25165824 | bytes 2359296 | tf_op jit(solution)/shard_map/keep_words/pallas_call | solution.py:44
  112.6 1.6 copy-done.1
  115.6 3.4 %tiles.3 = (bf16[1,1024,1024]{2,1,0:T(8,128)(2,1)S(1)}, f32[1024,256]{1,0:T(8,128)S(1)}, f32[1024,128]{1,0:T(8,128)S(1)}) custom-call(s32[1]{0:T(128)} %constant.110.clone.1.sel_ref, bf16[1024,768]{1,0:T(8,128)(2,1)S(1)} %copy-done, bf16[1,1,1024,768]{3,2,1,0:T(8,128)(2,1)S(1)} %copy-done.17, s32[4,1024,128]{2,1,0:T(8,128)S(1)} %copy-done.1), custom_call_target="tpu_custom_call" | custom-call | flops 1610612736 | bytes 4194304 | tf_op jit(solution)/shard_map/tiles/pallas_call | solution.py:105
  121.3 7.1 %all-to-all-done.1.pool_ref = bf16[32,2,32,768]{3,2,1,0:T(8,128)(2,1)} async-done(((bf16[32,2,32,768]{3,2,1,0:T(8,128)(2,1)}), bf16[32,2,32,768]{3,2,1,0:T(8,128)(2,1)}, u32[]{:S(2)}, u32[]{:S(2)}) %all-to-all-start.1) | async-done | bytes 3145760 | tf_op jit(solution)/shard_map/all_to_all | solution.py:226
  128.4 1.6 copy-done.2
  131.2 9.6 %tiles.4 = (bf16[2,1024,1024]{2,1,0:T(8,128)(2,1)S(1)}, f32[1024,256]{1,0:T(8,128)S(1)}, f32[1024,128]{1,0:T(8,128)S(1)}) custom-call(s32[2]{0:T(128)S(1)} %add_bitcast_fusion.sel_ref, bf16[1024,768]{1,0:T(8,128)(2,1)S(1)} %copy-done, bf16[32,2,32,768]{3,2,1,0:T(8,128)(2,1)} %all-to-all-done.1.pool_ref, s32[4,1024,128]{2,1,0:T(8,128)S(1)} %copy-done.2, ...), custom_call_target="tpu_custom_call" | custom-call | flops 3221225472 | bytes 8388608 | tf_op jit(solution)/shard_map/tiles/pallas_call | solution.py:105
  140.9 2.0 copy-done.6
  143.9 1.6 copy-done.3
  146.7 4.8 %tiles.5 = (bf16[1,1024,1024]{2,1,0:T(8,128)(2,1)S(1)}, f32[1024,256]{1,0:T(8,128)S(1)}, f32[1024,128]{1,0:T(8,128)S(1)}) custom-call(s32[1]{0:T(128)} %bitcast.7.sel_ref, bf16[1024,768]{1,0:T(8,128)(2,1)S(1)} %copy-done, bf16[1,4,1024,768]{3,2,1,0:T(8,128)(2,1)} %bitcast.18, s32[4,1024,128]{2,1,0:T(8,128)S(1)} %copy-done.3, f32[1024,256]{1,0:T(8,128)S(1)} %copy-done.19, ...), custom_call_target="tpu_custom_call" | custom-call | flops 1610612736 | bytes 4194304 | tf_op jit(solution)/shard_map/tiles/pallas_call | solution.py:105
  154.1 2.3 %add_convert_fusion = bf16[1024,256]{1,0:T(8,128)(2,1)} fusion(bf16[1024,256]{1,0:T(8,128)(2,1)S(1)} %copy-done.5, f32[1024,256]{1,0:T(8,128)} %copy-done.20, f32[1024]{0:T(1024)S(1)} %reduce_sum.19), kind=kLoop, calls=%fused_computation.5 | loop fusion | flops 1572864 | bytes 2101248 | tf_op jit(solution)/shard_map/convert_element_type | solution.py:58
  156.5 16.7 %all_to_all.20 = bf16[32,32,256]{2,1,0:T(8,128)(2,1)S(1)} all-to-all(bf16[32,32,256]{2,1,0:T(8,128)(2,1)} %bitcast.15), channel_id=1, replica_groups={{0,4,8,12,16,20,24,28,32,36,40,44,48,52,56,60,64,68,72,76,80,84,88,92,9..., dimensions={0} | all-to-all | bytes 1048576 | tf_op jit(solution)/shard_map/all_to_all | solution.py:205
  173.3 4.1 %collective-permute-done.3 = bf16[2,32,256]{2,1,0:T(8,128)(2,1)S(1)} collective-permute-done((bf16[2,32,256]{2,1,0:T(8,128)(2,1)S(1)}, bf16[2,32,256]{2,1,0:T(8,128)(2,1)S(1)}, u32[]{:S(2)}, u32[]{:S(2)}) %collective-permute-start.3) | collective-permute-done | bytes 32800 | tf_op jit(solution)/shard_map/ppermute | solution.py:223
  177.5 1.9 collective-permute-start.4
  179.3 3.0 %collective-permute-done.4 = bf16[2,32,256]{2,1,0:T(8,128)(2,1)S(1)} collective-permute-done((bf16[2,32,256]{2,1,0:T(8,128)(2,1)S(1)}, bf16[2,32,256]{2,1,0:T(8,128)(2,1)S(1)}, u32[]{:S(2)}, u32[]{:S(2)}) %collective-permute-start.4) | collective-permute-done | bytes 32800 | tf_op jit(solution)/shard_map/ppermute | solution.py:223
  183.4 8.1 %collective-permute-done.5 = bf16[2,32,256]{2,1,0:T(8,128)(2,1)S(1)} collective-permute-done((bf16[2,32,256]{2,1,0:T(8,128)(2,1)S(1)}, bf16[2,32,256]{2,1,0:T(8,128)(2,1)S(1)}, u32[]{:S(2)}, u32[]{:S(2)}) %collective-permute-start.5) | collective-permute-done | bytes 32800 | tf_op jit(solution)/shard_map/ppermute | solution.py:223
  192.7 6.3 %all-to-all-start.3 = ((bf16[32,2,32,256]{3,2,1,0:T(8,128)(2,1)}), bf16[32,2,32,256]{3,2,1,0:T(8,128)(2,1)S(1)}, u32[]{:S(2)}, u32[]{:S(2)}) async-start(bf16[32,2,32,256]{3,2,1,0:T(8,128)(2,1)} %broadcast_in_dim.88), calls=%async_computation.3 | async-start | bytes 2097152 | tf_op jit(solution)/shard_map/all_to_all | solution.py:226
  199.1 1.6 copy-done.16
  203.0 2.9 %all-gather.7.cloned.1.call-done = bf16[4096,256]{1,0:T(8,128)(2,1)} async-done(((bf16[1024,256]{1,0:T(8,128)(2,1)}), bf16[4096,256]{1,0:T(8,128)(2,1)}) %all-gather.7.cloned.1.call-update) | async-done | bytes 2097168 | tf_op jit(solution)/shard_map/all_gather | solution.py:246
  207.0 1.6 copy-done.11
  208.6 1.6 copy-done.12
  211.5 4.5 %all-to-all-done.3.pool_ref = bf16[32,2,32,256]{3,2,1,0:T(8,128)(2,1)S(1)} async-done(((bf16[32,2,32,256]{3,2,1,0:T(8,128)(2,1)}), bf16[32,2,32,256]{3,2,1,0:T(8,128)(2,1)S(1)}, u32[]{:S(2)}, u32[]{:S(2)}) %all-to-all-start.3) | async-done | bytes 1048608 | tf_op jit(solution)/shard_map/all_to_all | solution.py:226
  216.0 2.2 copy-done.7
  218.2 4.7 %gather.5 = bf16[1024,256]{1,0:T(8,128)(2,1)} custom-call(s32[2]{0:T(128)S(1)} %add_bitcast_fusion.sel_ref, bf16[2,1024,1024]{2,1,0:T(8,128)(2,1)S(1)} %copy-done.7, bf16[32,2,32,256]{3,2,1,0:T(8,128)(2,1)S(1)} %all-to-all-done.3.pool_ref, f32[1024,256]{1,0:T(8,128)S(1)} %gather.4.refs_0_, f32[1024,128]{1,0:T(8,128)S(1)} %copy-done.14, ...), custom_call_target="tpu_custom_call" | custom-call | flops 1073741824 | bytes 7340032 | tf_op jit(solution)/shard_map/gather/pallas_call | solution.py:172
  (77 shorter events, 23.6 us)
Async XLA Ops:
  6.5 3.1 %copy-start.5 = (bf16[1024,256]{1,0:T(8,128)(2,1)S(1)}, bf16[1024,256]{1,0:T(8,128)(2,1)}, u32[]{:S(2)}) copy-start(bf16[1024,256]{1,0:T(8,128)(2,1)} %refs_2_.1) | copy-start | bytes 1572868
  6.5 137.4 %all-gather.5.cloned.1.call-start = ((), (), s32[]{:S(2)}) async-start(), calls=%async_computation.4 | async-start | bytes 7864320 | tf_op jit(solution)/shard_map/all_gather | solution.py:239
  11.6 7.8 %copy-start.24 = (s32[2]{0:T(128)S(1)}, s32[2]{0:T(128)}, u32[]{:S(2)}) copy-start(s32[2]{0:T(128)} %param.8) | copy-start | bytes 28
  11.6 30.5 %all-to-all-start = ((bf16[32,32,768]{2,1,0:T(8,128)(2,1)}), bf16[32,32,768]{2,1,0:T(8,128)(2,1)S(1)}, u32[]{:S(2)}, u32[]{:S(2)}) async-start(bf16[32,32,768]{2,1,0:T(8,128)(2,1)} %bitcast.14), calls=%async_computation | async-start | bytes 3145728 | tf_op jit(solution)/shard_map/all_to_all | solution.py:205
  42.1 7.3 %collective-permute-start = (bf16[2,32,768]{2,1,0:T(8,128)(2,1)S(1)}, bf16[2,32,768]{2,1,0:T(8,128)(2,1)S(1)}, u32[]{:S(2)}, u32[]{:S(2)}) collective-permute-start(bf16[2,32,768]{2,1,0:T(8,128)(2,1)S(1)} %pad_maximum_fusion.1), channel_id=1, source_target_pairs={{0,1},{1,0},{2,3},{3,2},{4,5},{5,4},{6,7},{7,6},{8,9},{9,8},{10,11... | collective-permute-start | bytes 294920 | tf_op jit(solution)/shard_map/ppermute | solution.py:223
  49.5 12.5 %collective-permute-start.1 = (bf16[2,32,768]{2,1,0:T(8,128)(2,1)S(1)}, bf16[2,32,768]{2,1,0:T(8,128)(2,1)S(1)}, u32[]{:S(2)}, u32[]{:S(2)}) collective-permute-start(bf16[2,32,768]{2,1,0:T(8,128)(2,1)S(1)} %broadcast_select_fusion), channel_id=1, source_target_pairs={{0,2},{1,3},{2,0},{3,1},{4,6},{5,7},{6,4},{7,5},{8,10},{9,11},{10,... | collective-permute-start | bytes 294920 | tf_op jit(solution)/shard_map/ppermute | solution.py:223
  62.1 17.1 %collective-permute-start.2 = (bf16[2,32,768]{2,1,0:T(8,128)(2,1)S(1)}, bf16[2,32,768]{2,1,0:T(8,128)(2,1)S(1)}, u32[]{:S(2)}, u32[]{:S(2)}) collective-permute-start(bf16[2,32,768]{2,1,0:T(8,128)(2,1)S(1)} %broadcast_select_fusion.1), channel_id=1, source_target_pairs={{0,128},{1,129},{2,130},{3,131},{4,132},{5,133},{6,134},{7,135},{8... | collective-permute-start | bytes 294920 | tf_op jit(solution)/shard_map/ppermute | solution.py:223
  81.3 7.3 %copy-start.25 = (s32[1,4]{1,0:T(1,128)S(1)}, s32[1,4]{1,0:T(1,128)}, u32[]{:S(2)}) copy-start(s32[1,4]{1,0:T(1,128)} %param.7) | copy-start | bytes 52
  81.3 9.9 %copy-start.23 = (s32[1024,4,16]{0,2,1:T(8,128)S(1)}, s32[1024,4,16]{0,2,1:T(8,128)}, u32[]{:S(2)}) copy-start(s32[1024,4,16]{0,2,1:T(8,128)} %param.9) | copy-start | bytes 786436
  81.3 47.1 %all-to-all-start.1 = ((bf16[32,2,32,768]{3,2,1,0:T(8,128)(2,1)}), bf16[32,2,32,768]{3,2,1,0:T(8,128)(2,1)}, u32[]{:S(2)}, u32[]{:S(2)}) async-start(bf16[32,2,32,768]{3,2,1,0:T(8,128)(2,1)} %broadcast_in_dim.80), calls=%async_computation.1 | async-start | bytes 6291456 | tf_op jit(solution)/shard_map/all_to_all | solution.py:226
  88.6 24.0 %copy-start = (bf16[1024,768]{1,0:T(8,128)(2,1)S(1)}, bf16[1024,768]{1,0:T(8,128)(2,1)}, u32[]{:S(2)}) copy-start(bf16[1024,768]{1,0:T(8,128)(2,1)} %get-tuple-element.27.x_ref) | copy-start | bytes 4718596
  88.6 117.2 %all-gather.7.cloned.1.call-start = ((), (), s32[]{:S(2)}) async-start(), calls=%async_computation.5 | async-start | bytes 2621440 | tf_op jit(solution)/shard_map/all_gather | solution.py:246
  112.6 1.6 copy-start.1
  114.2 1.4 copy-start.17
  119.0 1.3 copy-start.15
  128.4 1.6 copy-start.2
  130.0 1.2 copy-start.22
  140.9 2.1 copy-start.6
  143.9 1.6 copy-start.3
  145.5 1.2 copy-start.19
  151.5 1.4 copy-start.10
  153.9 19.3 %copy-start.13 = (f32[1024,128]{1,0:T(8,128)}, f32[1024,128]{1,0:T(8,128)S(1)}, u32[]{:S(2)}) copy-start(f32[1024,128]{1,0:T(8,128)S(1)} %get-tuple-element.20.refs_1_) | copy-start | bytes 1572868
  156.4 42.6 %copy-start.4 = (bf16[1024,256]{1,0:T(8,128)(2,1)S(1)}, bf16[1024,256]{1,0:T(8,128)(2,1)}, u32[]{:S(2)}) copy-start(bf16[1024,256]{1,0:T(8,128)(2,1)} %add_convert_fusion) | copy-start | bytes 1572868
  173.2 4.2 %collective-permute-start.3 = (bf16[2,32,256]{2,1,0:T(8,128)(2,1)S(1)}, bf16[2,32,256]{2,1,0:T(8,128)(2,1)S(1)}, u32[]{:S(2)}, u32[]{:S(2)}) collective-permute-start(bf16[2,32,256]{2,1,0:T(8,128)(2,1)S(1)} %pad_maximum_fusion.2), channel_id=1, source_target_pairs={{0,1},{1,0},{2,3},{3,2},{4,5},{5,4},{6,7},{7,6},{8,9},{9,8},{10,11... | collective-permute-start | bytes 98312 | tf_op jit(solution)/shard_map/ppermute | solution.py:223
  177.5 4.8 %collective-permute-start.4 = (bf16[2,32,256]{2,1,0:T(8,128)(2,1)S(1)}, bf16[2,32,256]{2,1,0:T(8,128)(2,1)S(1)}, u32[]{:S(2)}, u32[]{:S(2)}) collective-permute-start(bf16[2,32,256]{2,1,0:T(8,128)(2,1)S(1)} %broadcast_select_fusion.3), channel_id=1, source_target_pairs={{0,2},{1,3},{2,0},{3,1},{4,6},{5,7},{6,4},{7,5},{8,10},{9,11},{10,... | collective-permute-start | bytes 98312 | tf_op jit(solution)/shard_map/ppermute | solution.py:223
  182.4 9.2 %collective-permute-start.5 = (bf16[2,32,256]{2,1,0:T(8,128)(2,1)S(1)}, bf16[2,32,256]{2,1,0:T(8,128)(2,1)S(1)}, u32[]{:S(2)}, u32[]{:S(2)}) collective-permute-start(bf16[2,32,256]{2,1,0:T(8,128)(2,1)S(1)} %broadcast_select_fusion.4), channel_id=1, source_target_pairs={{0,128},{1,129},{2,130},{3,131},{4,132},{5,133},{6,134},{7,135},{8... | collective-permute-start | bytes 98312 | tf_op jit(solution)/shard_map/ppermute | solution.py:223
  192.7 23.3 %all-to-all-start.3 = ((bf16[32,2,32,256]{3,2,1,0:T(8,128)(2,1)}), bf16[32,2,32,256]{3,2,1,0:T(8,128)(2,1)S(1)}, u32[]{:S(2)}, u32[]{:S(2)}) async-start(bf16[32,2,32,256]{3,2,1,0:T(8,128)(2,1)} %broadcast_in_dim.88), calls=%async_computation.3 | async-start | bytes 2097152 | tf_op jit(solution)/shard_map/all_to_all | solution.py:226
  199.1 1.6 copy-start.16
  207.0 1.6 copy-start.11
  208.6 1.6 copy-start.12
  210.2 5.8 %copy-start.14 = (f32[1024,128]{1,0:T(8,128)S(1)}, f32[1024,128]{1,0:T(8,128)}, u32[]{:S(2)}) copy-start(f32[1024,128]{1,0:T(8,128)} %copy-done.13) | copy-start | bytes 1572868
  216.0 2.2 copy-start.7
  (5 other events, 5.1 us)
Sparse Core Ops, SparseCore 0:
  11.8 126.6 all-gather.4
  156.6 49.2 all-gather.6

commit v2 on v0

v2 whole, which is shorter than its diff:
```python
import functools

import jax
import jax.numpy as jnp
from jax import lax
from jax.experimental import pallas as pl
from jax.experimental.pallas import tpu as pltpu
from jax.sharding import PartitionSpec as P

K = 4
HUBS = 2
TOPK = 16
LANES = 128
EPS = 1e-06
TAU = 0.04
ALPHA = 0.8
AXES = ("slab", "rep")
ROW_TILE = 256
VMEM_LIMIT = 16 << 20
HALF = 32


def join_kernel(flag_ref, x_ref, y_ref, cols_ref, all_ref, rows_ref):
    width, clust = x_ref.shape[1], y_ref.shape[1]
    values = x_ref[...].astype(jnp.float32)
    scale = lax.rsqrt(jnp.sum(values * values, axis=1, keepdims=True) + EPS)
    normed = (values * scale).astype(jnp.bfloat16)
    cols = cols_ref[...].reshape(K * TOPK, cols_ref.shape[2])
    coded = jnp.concatenate([cols // HALF + HALF * flag_ref[0], cols % HALF], axis=0)
    coded = coded.astype(jnp.float32).T.astype(jnp.bfloat16)
    all_ref[:, :width] = normed
    all_ref[:, width : width + clust] = y_ref[...]
    all_ref[:, width + clust :] = coded
    rows_ref[:, :width] = normed
    rows_ref[:, width:] = coded


def join(flag, embeddings, indicators, columns):
    rows, width = embeddings.shape
    clust = indicators.shape[1]
    by_row = lambda cols: pl.BlockSpec((ROW_TILE, cols), lambda r, flag: (r, 0))
    wide = (width + clust + 2 * K * TOPK, width + 2 * K * TOPK)
    return pl.pallas_call(
        join_kernel,
        out_shape=[jax.ShapeDtypeStruct((rows, w), jnp.bfloat16) for w in wide],
        grid_spec=pltpu.PrefetchScalarGridSpec(
            num_scalar_prefetch=1,
            grid=(rows // ROW_TILE,),
            in_specs=[
                by_row(width),
                by_row(clust),
                pl.BlockSpec((K, TOPK, ROW_TILE), lambda r, flag: (0, 0, r)),
            ],
            out_specs=[by_row(w) for w in wide],
        ),
        compiler_params=pltpu.CompilerParams(vmem_limit_bytes=VMEM_LIMIT),
        name="join",
    )(flag, embeddings, indicators, jnp.transpose(columns, (1, 2, 0)))


def words_kernel(pick_ref, coded_ref, out_ref):
    half = K * TOPK
    lane = lax.broadcasted_iota(jnp.int32, (LANES, LANES), 0)

    @pl.loop(0, coded_ref.shape[0] // LANES)
    def _(block):
        here = pl.ds(pl.multiple_of(block * LANES, LANES), LANES)
        coded = coded_ref[here, :].astype(jnp.float32).T.astype(jnp.int32)
        high = coded[:half] & (HALF - 1)
        low = (high & 3) * HALF + coded[half:]
        bit = jnp.left_shift(jnp.ones_like(high), high >> 2)
        for slot in range(K):
            word = jnp.zeros((LANES, LANES), jnp.int32)
            for t in range(slot * TOPK, (slot + 1) * TOPK):
                word = word | jnp.where(lane == low[t : t + 1], bit[t : t + 1], 0)
            out_ref[slot, here, :] = word.T


def keep_words(pick, coded, place, rows):
    return pl.pallas_call(
        words_kernel,
        out_shape=jax.ShapeDtypeStruct((K, rows, LANES), jnp.int32),
        grid_spec=pltpu.PrefetchScalarGridSpec(
            num_scalar_prefetch=1,
            grid=(1,),
            in_specs=[pl.BlockSpec((rows, LANES), lambda i, pick: place(pick))],
            out_specs=pl.BlockSpec((K, rows, LANES), lambda i, pick: (0, 0, 0)),
        ),
        compiler_params=pltpu.CompilerParams(vmem_limit_bytes=VMEM_LIMIT),
        cost_estimate=pl.CostEstimate(flops=rows * LANES * K * TOPK, bytes_accessed=rows * 512, transcendentals=0),
        name="keep_words",
    )(pick, coded)


def mix(acc, degree, anchor):
    return (ALPHA * acc / degree + (1.0 - ALPHA) * anchor.astype(jnp.float32)).astype(jnp.bfloat16)


def weights(cosine, word, total, put):
    for j in range(cosine.shape[1] // LANES):
        part = cosine[:, j * LANES : (j + 1) * LANES]
        raw = jnp.where((word & (1 << j)) != 0, jnp.exp((part - 1.0) * (1.0 / TAU)), 0.0)
        total = total + raw
        put(slice(j * LANES, (j + 1) * LANES), raw.astype(jnp.bfloat16))
    return total


def cosines(rows, others):
    return lax.dot_general(rows, others, (((1,), (1,)), ((), ())), preferred_element_type=jnp.float32)


def flat(ref):
    value = ref[...]
    return value.reshape(-1, value.shape[-1])


def tile_kernel(has_deg, has_y, has_acc, keep, pick_ref, x_ref, other_ref, w_ref, *refs):
    refs = list(refs)
    y_ref = refs.pop(0) if has_y else None
    deg_in = refs.pop(0) if has_deg else None
    acc_in = refs.pop(0) if has_acc else None
    deg_ref = refs.pop(0)
    acc_ref = refs.pop(0) if has_y else None
    tile_ref = refs.pop(0)
    word = w_ref[0]
    total = deg_in[...] if has_deg else jnp.zeros(word.shape, jnp.float32)

    def put(lanes, value):
        tile_ref[:, lanes] = value

    deg_ref[...] = weights(cosines(x_ref[...], flat(other_ref)), word, total, put)
    if has_y:
        gathered = jnp.dot(tile_ref[...], flat(y_ref), preferred_element_type=jnp.float32)
        acc_ref[...] = acc_in[...] + gathered if has_acc else gathered


def tile_of(pick, x, other, words, slot, degree, y=None, acc=None, keep=True):
    rows = words.shape[1]
    by_row = lambda cols: pl.BlockSpec((ROW_TILE, cols), lambda r, pick: (r, 0))
    spec = lambda operand: pl.BlockSpec(operand[1], operand[2])
    clust = y[1][-1] if y else 0
    args = [x[0], other[0], words] + ([y[0]] if y else [])
    specs = [spec(x), spec(other), pl.BlockSpec((1, ROW_TILE, LANES), lambda r, pick: (slot(pick), r, 0))]
    specs += [spec(y)] if y else []
    for extra, cols in ((degree, LANES), (acc, clust)):
        if extra is not None:
            args.append(extra)
            specs.append(by_row(cols))
    outs = [(LANES, jnp.float32)] + ([(clust, jnp.float32)] if y else []) + ([(rows, jnp.bfloat16)] if keep else [])
    return pl.pallas_call(
        functools.partial(tile_kernel, degree is not None, y is not None, acc is not None, keep),
        out_shape=[jax.ShapeDtypeStruct((rows, cols), kind) for cols, kind in outs],
        grid_spec=pltpu.PrefetchScalarGridSpec(
            num_scalar_prefetch=1,
            grid=(rows // ROW_TILE,),
            in_specs=specs,
            out_specs=[by_row(cols) for cols, _ in outs],
            scratch_shapes=[] if keep else [pltpu.VMEM((ROW_TILE, rows), jnp.bfloat16)],
        ),
        compiler_params=pltpu.CompilerParams(vmem_limit_bytes=VMEM_LIMIT),
        cost_estimate=pl.CostEstimate(flops=2 * rows * rows * 768, bytes_accessed=4 * rows * rows, transcendentals=rows * rows),
        name="tile",
    )(pick, *args)


def gather_kernel(has_acc, last, pick_ref, tile_ref, y_ref, *refs):
    refs = list(refs)
    acc_in = refs.pop(0) if has_acc else None
    deg_ref, anchor_ref = (refs.pop(0), refs.pop(0)) if last else (None, None)
    gathered = jnp.dot(tile_ref[...], flat(y_ref), preferred_element_type=jnp.float32)
    if has_acc:
        gathered = acc_in[...] + gathered
    if last:
        gathered = mix(gathered, jnp.sum(deg_ref[...], axis=1, keepdims=True), anchor_ref[...])
    refs[0][...] = gathered


def gather_of(pick, tile, y, acc, degree=None, anchor=None):
    rows, clust = tile.shape[0], y[1][-1]
    by_row = lambda cols: pl.BlockSpec((ROW_TILE, cols), lambda r, pick: (r, 0))
    spec = lambda operand: pl.BlockSpec(operand[1], operand[2])
    last = degree is not None
    args = [tile, y[0]] + ([acc] if acc is not None else []) + ([degree, anchor[0]] if last else [])
    specs = [by_row(rows), spec(y)] + ([by_row(clust)] if acc is not None else [])
    specs += [by_row(LANES), spec(anchor)] if last else []
    return pl.pallas_call(
        functools.partial(gather_kernel, acc is not None, last),
        out_shape=jax.ShapeDtypeStruct((rows, clust), jnp.bfloat16 if last else jnp.float32),
        grid_spec=pltpu.PrefetchScalarGridSpec(
            num_scalar_prefetch=1, grid=(rows // ROW_TILE,), in_specs=specs, out_specs=by_row(clust)
        ),
        compiler_params=pltpu.CompilerParams(vmem_limit_bytes=VMEM_LIMIT),
        cost_estimate=pl.CostEstimate(flops=2 * rows * rows * clust, bytes_accessed=3 * rows * rows, transcendentals=0),
        name="gather",
    )(pick, *args)


def hub_rows_kernel(width, pick_ref, rows_ref, near_ref, far_ref, out_ref, word_ref, tile_ref):
    clust = out_ref.shape[1]
    half = K * TOPK
    coded = rows_ref[:, width + clust :].astype(jnp.float32).astype(jnp.int32)
    high = coded[:, :half] & (HALF - 1)
    low = (high & 3) * HALF + coded[:, half:]
    bit = jnp.left_shift(jnp.ones_like(high), high >> 2)
    lane = lax.broadcasted_iota(jnp.int32, (rows_ref.shape[0], LANES), 1)
    for slot in range(K):
        word = jnp.zeros(lane.shape, jnp.int32)
        for t in range(slot * TOPK, (slot + 1) * TOPK):
            word = word | jnp.where(lane == low[:, t : t + 1], bit[:, t : t + 1], 0)
        word_ref[slot] = word
    total = jnp.zeros(lane.shape, jnp.float32)
    acc = jnp.zeros(out_ref.shape, jnp.float32)

    def put(lanes, value):
        tile_ref[:, lanes] = value

    self_block = near_ref[:, 0].reshape(-1, width + clust)
    member_block = near_ref[:, 1].reshape(-1, width + clust)
    far_block = flat(far_ref)
    slots = (0, 1, pick_ref[0], 5 - pick_ref[0])
    for slot, block in zip(slots, (self_block, member_block, self_block, far_block)):
        total = weights(cosines(rows_ref[:, :width], block[:, :width]), word_ref[slot], total, put)
        acc = acc + jnp.dot(tile_ref[...], block[:, width:], preferred_element_type=jnp.float32)
    out_ref[...] = mix(acc, jnp.sum(total, axis=1, keepdims=True), rows_ref[:, width : width + clust])


def hub_rows(self_slot, mine, near, far, width):
    share = mine.shape[0]
    clust = near.shape[3] - width
    rows = near.shape[0] * near.shape[2]
    return pl.pallas_call(
        functools.partial(hub_rows_kernel, width),
        out_shape=jax.ShapeDtypeStruct((share, clust), jnp.bfloat16),
        grid_spec=pltpu.PrefetchScalarGridSpec(
            num_scalar_prefetch=1,
            grid=(1,),
            in_specs=[
                pl.BlockSpec(mine.shape, lambda i, pick: (0, 0)),
                pl.BlockSpec(near.shape, lambda i, pick: (0, 0, 0, 0)),
                pl.BlockSpec(far.shape, lambda i, pick: (0, 0, 0)),
            ],
            out_specs=pl.BlockSpec((share, clust), lambda i, pick: (0, 0)),
            scratch_shapes=[pltpu.VMEM((K, share, LANES), jnp.int32), pltpu.VMEM((share, rows), jnp.bfloat16)],
        ),
        compiler_params=pltpu.CompilerParams(vmem_limit_bytes=20 << 20),
        cost_estimate=pl.CostEstimate(flops=share * rows * 6144, bytes_accessed=6 << 20, transcendentals=share * rows * K),
        name="hub_rows",
    )(self_slot, mine, near, far)


def send(block, target):
    slabs, reps = lax.axis_size("slab"), lax.axis_size("rep")
    chips = slabs // 4
    pairs = []
    for device in range(slabs * reps):
        slab, rep = divmod(device, reps)
        to = target(slab // (2 * chips), slab // 2 % chips, slab % 2, rep)
        pairs.append((device, ((to[0] * chips + to[1]) * 2 + to[2]) * reps + to[3]))
    return lax.ppermute(block, AXES, pairs)


def swap_cores(block):
    return send(block, lambda half, chip, core, rep: (half, chip, 1 - core, rep))


def flags_of(code):
    flag = code.astype(jnp.float32).astype(jnp.int32) // HALF
    return flag & 3, (flag >> 2) & 1


def join_pieces(piece):
    slabs = lax.axis_size("slab")
    members, chips = slabs // 2, slabs // 4
    layers = [[h * members + c * 2 + core for c in range(chips)] for h in range(2) for core in range(2)]
    repeated = jnp.broadcast_to(piece[None], (chips,) + piece.shape)
    return lax.all_to_all(repeated, "slab", 0, 0, axis_index_groups=layers, tiled=True)


def hub_pieces(block, hub_ids, code_at):
    slabs, reps = lax.axis_size("slab"), lax.axis_size("rep")
    members = slabs // 2
    rows, width = block.shape
    piece = rows // members
    planes = [[h * members + m for m in range(members)] for h in range(2)]
    mine = lax.all_to_all(
        block.reshape(members, piece, width), "slab", 0, 0, axis_index_groups=planes, tiled=True
    )
    slab, rep = lax.axis_index("slab"), lax.axis_index("rep")
    hub_slab, hub_rep = lax.div(hub_ids, reps), lax.rem(hub_ids, reps)
    member = lax.rem(hub_slab, members)
    held = jnp.stack(
        [lax.dynamic_index_in_dim(mine, member[h], 0, keepdims=False) for h in range(HUBS)], axis=0
    )[None]
    for bit in range(2):
        got = send(held, lambda half, chip, core, rep: (half, chip, core, rep ^ (1 << bit)))
        upper = (rep >> bit) & 1 == 1
        held = jnp.concatenate([jnp.where(upper, got, held), jnp.where(upper, held, got)], axis=0)
    chosen = []
    for h in range(HUBS):
        hub = lax.dynamic_index_in_dim(held[:, h], hub_rep[h], 0, keepdims=False)
        want, _ = flags_of(hub[0, code_at])
        chosen.append(jnp.stack([hub, lax.dynamic_index_in_dim(held[:, h], want, 0, keepdims=False)], axis=0))
    held = jnp.stack(chosen, axis=0)
    got = send(held, lambda half, chip, core, rep: (1 - half, chip, core, rep))
    away = lax.div(hub_slab, members) != lax.div(slab, members)
    held = jnp.where(away[:, None, None, None], got, held)
    first_core = lax.rem(slab, 2) == 0
    keep = jnp.where(first_core, held[0], held[1])
    got = swap_cores(jnp.where(first_core, held[1], held[0]))
    return jnp.concatenate([jnp.where(first_core, keep, got), jnp.where(first_core, got, keep)], axis=1)


def body(embeddings, indicators, neighbours, hub_ids, columns):
    rows, width = embeddings.shape
    clust = indicators.shape[1]
    full = width + clust
    reps = lax.axis_size("rep")
    total = lax.axis_size("slab") * reps
    steps = rows // ROW_TILE
    slots = neighbours[0].astype(jnp.int32)
    want = slots[1] & 3
    order = slots[2] - total
    core = lax.rem(lax.axis_index("slab"), 2)

    joined, coded = join((want + 4 * order)[None], embeddings, indicators, columns)
    group_x = lax.all_gather(coded, "rep", axis=0, tiled=True)
    anchor_in, group_x = lax.optimization_barrier((indicators, group_x))
    group_y = lax.all_gather(anchor_in, "rep", axis=0, tiled=True)

    both = hub_pieces(joined, hub_ids, full)
    near = join_pieces(both[:, :, :full])
    far = swap_cores(near[:, 0])
    _, hub_order = flags_of(both[0, 0, full])
    share = hub_rows(jnp.where(hub_order == core, 2, 3)[None], both[0], near, far, width)
    near_y = join_pieces(share).reshape(rows, clust)
    far_y = swap_cores(near_y)

    member_want, member_order = flags_of(lax.dynamic_index_in_dim(group_x[:, width], want * rows, 0, keepdims=False))
    near_slot = jnp.where(order == core, 2, 3)
    member_near = jnp.where(member_order == core, 2, 3)
    pick = jnp.stack([want, member_want, near_slot, member_near]).astype(jnp.int32)
    words = keep_words(pick, joined, lambda pick: (0, full // LANES), rows)
    member_words = keep_words(pick, group_x, lambda pick: (pick[0], width // LANES), rows)
    own_rows = (joined, (ROW_TILE, width), lambda r, pick: (r, 0))
    member_rows = (group_x, (ROW_TILE, width), lambda r, pick: (pick[0] * steps + r, 0))
    own_x = (joined, (rows, width), lambda r, pick: (0, 0))
    own_y = (indicators, (rows, clust), lambda r, pick: (0, 0))
    at_member = lambda array, cols: (array, (rows, cols), lambda r, pick: (pick[0], 0))
    at_second = lambda array, cols: (array, (rows, cols), lambda r, pick: (pick[1], 0))
    chips, piece = near.shape[0], near.shape[2]
    near_x0 = (near, (chips, 1, piece, width), lambda r, pick: (0, 0, 0, 0))
    near_y0 = (near, (chips, 1, piece, clust), lambda r, pick: (0, 0, 0, width // clust))
    far_x0 = (far, (chips, piece, width), lambda r, pick: (0, 0, 0))
    far_y0 = (far, (chips, piece, clust), lambda r, pick: (0, 0, width // clust))
    whole = lambda array: (array, array.shape, lambda r, pick: (0, 0))

    degree, acc, own_tile = tile_of(pick, own_rows, own_x, words, lambda pick: 0, None, own_y)
    degree, member_tile = tile_of(pick, own_rows, at_member(group_x, width), words, lambda pick: 1, degree)
    degree_c, tile_c0 = tile_of(pick, member_rows, at_member(group_x, width), member_words, lambda pick: 0, None)
    degree_c, tile_c1 = tile_of(pick, member_rows, at_second(group_x, width), member_words, lambda pick: 1, degree_c)
    degree, acc, near_tile = tile_of(pick, own_rows, near_x0, words, lambda pick: pick[2], degree, near_y0, acc)
    degree_c, acc_c = tile_of(
        pick, member_rows, near_x0, member_words, lambda pick: pick[3], degree_c, near_y0, None, False
    )
    degree, acc, far_tile = tile_of(pick, own_rows, far_x0, words, lambda pick: 5 - pick[2], degree, far_y0, acc)
    degree_c, acc_c = tile_of(
        pick, member_rows, far_x0, member_words, lambda pick: 5 - pick[3], degree_c, far_y0, acc_c, False
    )
    by_row = (indicators, (ROW_TILE, clust), lambda r, pick: (r, 0))
    member_anchor = (group_y, (ROW_TILE, clust), lambda r, pick: (pick[0] * steps + r, 0))
    acc_c = gather_of(pick, tile_c0, at_member(group_y, clust), acc_c)
    member_new = gather_of(pick, tile_c1, at_second(group_y, clust), acc_c, degree_c, member_anchor)
    new = gather_of(pick, member_tile, at_member(group_y, clust), acc, degree, by_row)

    acc = gather_of(pick, near_tile, whole(near_y), None)
    acc = gather_of(pick, far_tile, whole(far_y), acc)
    acc = gather_of(pick, own_tile, whole(new), acc)
    return gather_of(pick, member_tile, whole(member_new), acc, degree, by_row)


def solution(mesh):
    return jax.shard_map(
        body,
        mesh=mesh,
        in_specs=(
            P(("slab", "rep"), None),
            P(("slab", "rep"), None),
            P(("slab", "rep"), None),
            P(),
            P(("slab", "rep"), None, None),
        ),
        out_specs=P(("slab", "rep"), None),
        check_vma=False,
    )
```

time: 726 us -> 275 us (0.38)
  waiting for transfers between devices: 620 us -> 79.1 us
  Pallas kernels: 0 us -> 70.2 us
  matrix products: 46.5 us -> 0 us
  blocking collectives: 0 us -> 41 us
  starting transfers between devices: 0.13 us -> 30.3 us
  other arithmetic: 21 us -> 1.1 us
  local copies, waits for them, and re-layouts: 8.25 us -> 22.1 us
    psum x2 -> x0, waiting for transfers between devices: 619 us -> none  [from_root(): return lax.psum(block, axis)]
    pallas_call x0 -> x19, Pallas kernels: none -> 70.2 us  [the longest x8 35.8 us: tile_of(): pl.pallas_call(functools.partial(tile_kernel, degree is not None, y is no...]
    ppermute x0 -> x6, waiting for transfers between devices: none -> 48 us  [send(): return lax.ppermute(block, AXES, pairs)]
    dot_general x12 -> x0, matrix products: 46.5 us -> none  [the longest x4 37.7 us: body(): cosine = jnp.dot(normed, other.T, preferred_element_type=jnp.float32)]
    all_to_all x0 -> x1, blocking collectives: none -> 41 us  [join_pieces(): lax.all_to_all(repeated, 'slab', 0, 0, axis_index_groups=layers, tiled=True)]
    all_to_all x0 -> x2, waiting for transfers between devices: none -> 30.4 us  [the longest x1 20.2 us: hub_pieces(): lax.all_to_all(block.reshape(members, piece, width), 'slab', 0, 0, axis_i...]
    ppermute x0 -> x6, starting transfers between devices: none -> 18.8 us  [send(): return lax.ppermute(block, AXES, pairs)]
    all_to_all x0 -> x2, starting transfers between devices: none -> 11.5 us  [the longest x1 7.89 us: hub_pieces(): lax.all_to_all(block.reshape(members, piece, width), 'slab', 0, 0, axis_i...]
  transfers between devices with their start and end apart: 4 -> 10, of which waited for: 2 -> 7; matrix products, arithmetic and copies ran while one was open for 1% -> 2% of each run, Pallas kernels for 0% -> 21%
where the time goes in v2:
time: 275 us; the launch traced here: 269 us
  waiting for transfers between devices  79.1 us (29%)
  Pallas kernels  70.2 us (26%)
  blocking collectives  41 us (15%)
  starting transfers between devices  30.3 us (11%)
  between operations  25.7 us (9%)
  local copies, waits for them, and re-layouts  22.1 us (8%)
    ppermute x6, waiting for transfers between devices, send(): return lax.ppermute(block, AXES, pairs)  48 us
    all_to_all x1, blocking collectives, join_pieces(): lax.all_to_all(repeated, 'slab', 0, 0, axis_index_groups=layers, tiled=True)  41 us
    pallas_call x8, Pallas kernels, tile_of(): pl.pallas_call(functools.partial(tile_kernel, degree is not None, y is no...  35.8 us
    all_to_all x1, waiting for transfers between devices, hub_pieces(): lax.all_to_all(block.reshape(members, piece, width), 'slab', 0, 0, axis_i...  20.2 us
    ppermute x6, starting transfers between devices, send(): return lax.ppermute(block, AXES, pairs)  18.8 us
    unnamed x60, local copies, waits for them, and re-layouts  15.4 us
    pallas_call x7, Pallas kernels, gather_of(): pl.pallas_call(functools.partial(gather_kernel, acc is not None, last), o...  15 us
    pallas_call x2, Pallas kernels, keep_words(): pl.pallas_call(words_kernel, out_shape=jax.ShapeDtypeStruct((K, rows, LAN...  13.3 us
  transfers between devices with their start and end apart: 10, of which 7 were waited for; matrix products, arithmetic and copies ran while one was open for 2% of the time, Pallas kernels for 21%

profile of v2, /device:TPU:161, one launch (start us, length us, event | category | flops | bytes accessed | tf_op | source)
XLA Modules:
  0.0 269.5 jit_solution(223516928651492999)
XLA Ops:
  12.5 2.4 join.1
  14.9 7.9 %all-to-all-start = ((bf16[32,32,896]{2,1,0:T(8,128)(2,1)}), bf16[32,32,896]{2,1,0:T(8,128)(2,1)S(1)}, u32[]{:S(2)}, u32[]{:S(2)}) async-start(bf16[32,32,896]{2,1,0:T(8,128)(2,1)} %bitcast.9), calls=%async_computation | async-start | bytes 3670016 | tf_op jit(solution)/shard_map/all_to_all | solution.py:285
  28.1 20.2 %all-to-all-done = bf16[32,32,896]{2,1,0:T(8,128)(2,1)S(1)} async-done(((bf16[32,32,896]{2,1,0:T(8,128)(2,1)}), bf16[32,32,896]{2,1,0:T(8,128)(2,1)S(1)}, u32[]{:S(2)}, u32[]{:S(2)}) %all-to-all-start) | async-done | bytes 1835040 | tf_op jit(solution)/shard_map/all_to_all | solution.py:285
  49.2 7.0 %collective-permute-done = bf16[1,2,32,896]{3,2,1,0:T(8,128)(2,1)S(1)} collective-permute-done((bf16[1,2,32,896]{3,2,1,0:T(8,128)(2,1)S(1)}, bf16[1,2,32,896]{3,2,1,0:T(8,128)(2,1)S(1)}, u32[]{:S(2)}, u32[]{:S(2)}) %collective-permute-start) | collective-permute-done | bytes 114720 | tf_op jit(solution)/shard_map/ppermute | solution.py:259
  62.2 16.8 %collective-permute-done.1 = bf16[2,2,32,896]{3,2,1,0:T(8,128)(2,1)S(1)} collective-permute-done((bf16[2,2,32,896]{3,2,1,0:T(8,128)(2,1)S(1)}, bf16[2,2,32,896]{3,2,1,0:T(8,128)(2,1)S(1)}, u32[]{:S(2)}, u32[]{:S(2)}) %collective-permute-start.1) | collective-permute-done | bytes 229408 | tf_op jit(solution)/shard_map/ppermute | solution.py:259
  81.7 7.2 %collective-permute-start.2 = (bf16[2,2,32,896]{3,2,1,0:T(8,128)(2,1)S(1)}, bf16[2,2,32,896]{3,2,1,0:T(8,128)(2,1)S(1)}, u32[]{:S(2)}, u32[]{:S(2)}) collective-permute-start(bf16[2,2,32,896]{3,2,1,0:T(8,128)(2,1)S(1)} %pad_maximum_fusion.1), channel_id=1, source_target_pairs={{0,128},{1,129},{2,130},{3,131},{4,132},{5,133},{6,134},{7,135},{8... | collective-permute-start | bytes 688136 | tf_op jit(solution)/shard_map/ppermute | solution.py:259
  88.8 21.1 %collective-permute-done.2 = bf16[2,2,32,896]{3,2,1,0:T(8,128)(2,1)S(1)} collective-permute-done((bf16[2,2,32,896]{3,2,1,0:T(8,128)(2,1)S(1)}, bf16[2,2,32,896]{3,2,1,0:T(8,128)(2,1)S(1)}, u32[]{:S(2)}, u32[]{:S(2)}) %collective-permute-start.2) | collective-permute-done | bytes 229408 | tf_op jit(solution)/shard_map/ppermute | solution.py:259
  110.1 4.9 %collective-permute-start.3 = (bf16[2,32,896]{2,1,0:T(8,128)(2,1)S(1)}, bf16[2,32,896]{2,1,0:T(8,128)(2,1)S(1)}, u32[]{:S(2)}, u32[]{:S(2)}) collective-permute-start(bf16[2,32,896]{2,1,0:T(8,128)(2,1)S(1)} %select_bitcast_fusion), channel_id=1, source_target_pairs={{0,4},{1,5},{2,6},{3,7},{4,0},{5,1},{6,2},{7,3},{8,12},{9,13},{10,... | collective-permute-start | bytes 344072 | tf_op jit(solution)/shard_map/ppermute | solution.py:259
  116.3 41.0 %all_to_all.15.other_ref.refs_0_.near_ref = bf16[16,2,64,768]{3,2,1,0:T(8,128)(2,1)S(1)} all-to-all(bf16[16,2,64,768]{3,2,1,0:T(8,128)(2,1)S(1)} %broadcast_in_dim.33), channel_id=1, replica_groups={{0,8,16,24,32,40,48,56,64,72,80,88,96,104,112,120},{4,12,20,28,36,44,52..., dimensions={0} | all-to-all | bytes 6291456 | tf_op jit(solution)/shard_map/all_to_all | solution.py:276
  158.7 2.2 collective-permute-start.4
  162.2 2.1 collective-permute-done.4.other_ref.refs_0_.far_ref
  164.3 3.6 %hub_rows.1 = bf16[64,256]{1,0:T(8,128)(2,1)S(1)} custom-call(s32[1]{0:T(128)} %bitcast.29.pick_ref, bf16[64,896]{1,0:T(8,128)(2,1)S(1)} %fusion.2.rows_ref, bf16[16,2,64,768]{3,2,1,0:T(8,128)(2,1)S(1)} %all_to_all.15.other_ref.refs_0_.near_ref, bf16[16,64,768]{2,1,0:T(8,128)(2,1)} %collective-permute-done.4.other_ref.refs_0_.far_ref), custom_call_target="tpu_custom_call" | custom-call | flops 402653184 | bytes 6291456 | tf_op jit(solution)/shard_map/hub_rows/pallas_call | solution.py:231
  168.8 3.6 %all-to-all-start.2 = ((bf16[16,64,256]{2,1,0:T(8,128)(2,1)}), bf16[16,64,256]{2,1,0:T(8,128)(2,1)S(1)}, u32[]{:S(2)}, u32[]{:S(2)}) async-start(bf16[16,64,256]{2,1,0:T(8,128)(2,1)} %broadcast_in_dim.35), calls=%async_computation.2 | async-start | bytes 1048576 | tf_op jit(solution)/shard_map/all_to_all | solution.py:276
  172.4 10.2 %all-to-all-done.2 = bf16[16,64,256]{2,1,0:T(8,128)(2,1)S(1)} async-done(((bf16[16,64,256]{2,1,0:T(8,128)(2,1)}), bf16[16,64,256]{2,1,0:T(8,128)(2,1)S(1)}, u32[]{:S(2)}, u32[]{:S(2)}) %all-to-all-start.2) | async-done | bytes 524320 | tf_op jit(solution)/shard_map/all_to_all | solution.py:276
  182.6 2.2 collective-permute-start.5
  186.0 7.1 %keep_words.2.w_ref = s32[4,1024,128]{2,1,0:T(8,128)S(1)} custom-call(s32[4]{0:T(128)S(1)} %pad_add_fusion.pick_ref, bf16[1024,896]{1,0:T(8,128)(2,1)} %get-tuple-element.30.coded_ref.x_ref.other_ref), custom_call_target="tpu_custom_call" | custom-call | flops 8388608 | bytes 524288 | tf_op jit(solution)/shard_map/keep_words/pallas_call | solution.py:80
  193.2 2.5 copy-done
  195.7 6.2 %keep_words.3.w_ref = s32[4,1024,128]{2,1,0:T(8,128)S(1)} custom-call(s32[4]{0:T(128)S(1)} %pad_add_fusion.pick_ref, bf16[4096,640]{1,0:T(8,128)(2,1)S(1)} %copy-done), custom_call_target="tpu_custom_call" | custom-call | flops 8388608 | bytes 524288 | tf_op jit(solution)/shard_map/keep_words/pallas_call | solution.py:80
  201.9 5.3 %tile.8 = (f32[1024,128]{1,0:T(8,128)S(1)}, f32[1024,256]{1,0:T(8,128)S(1)}, bf16[1024,1024]{1,0:T(8,128)(2,1)S(1)}) custom-call(s32[4]{0:T(128)S(1)} %pad_add_fusion.pick_ref, bf16[1024,896]{1,0:T(8,128)(2,1)} %get-tuple-element.30.coded_ref.x_ref.other_ref, bf16[1024,896]{1,0:T(8,128)(2,1)} %get-tuple-element.30.coded_ref.x_ref.other_ref, ...), custom_call_target="tpu_custom_call" | custom-call | flops 1610612736 | bytes 4194304 | tf_op jit(solution)/shard_map/tile/pallas_call | solution.py:150
  208.7 4.3 %tile.9 = (f32[1024,128]{1,0:T(8,128)S(1)}, bf16[1024,1024]{1,0:T(8,128)(2,1)S(1)}) custom-call(s32[4]{0:T(128)S(1)} %pad_add_fusion.pick_ref, bf16[1024,896]{1,0:T(8,128)(2,1)} %get-tuple-element.30.coded_ref.x_ref.other_ref, bf16[4096,640]{1,0:T(8,128)(2,1)S(1)} %bitcast.51, s32[4,1024,128]{2,1,0:T(8,128)S(1)} %keep_words.2.w_ref, ...), custom_call_target="tpu_custom_call" | custom-call | flops 1610612736 | bytes 4194304 | tf_op jit(solution)/shard_map/tile/pallas_call | solution.py:150
  212.9 3.1 %tile.10 = (f32[1024,128]{1,0:T(8,128)S(1)}, bf16[1024,1024]{1,0:T(8,128)(2,1)S(1)}) custom-call(s32[4]{0:T(128)S(1)} %pad_add_fusion.pick_ref, bf16[4096,640]{1,0:T(8,128)(2,1)S(1)} %bitcast.51, bf16[4096,640]{1,0:T(8,128)(2,1)S(1)} %bitcast.51, s32[4,1024,128]{2,1,0:T(8,128)S(1)} %keep_words.3.w_ref), custom_call_target="tpu_custom_call" | custom-call | flops 1610612736 | bytes 4194304 | tf_op jit(solution)/shard_map/tile/pallas_call | solution.py:150
  216.1 3.1 %tile.11 = (f32[1024,128]{1,0:T(8,128)S(1)}, bf16[1024,1024]{1,0:T(8,128)(2,1)S(1)}) custom-call(s32[4]{0:T(128)S(1)} %pad_add_fusion.pick_ref, bf16[4096,640]{1,0:T(8,128)(2,1)S(1)} %bitcast.51, bf16[4096,640]{1,0:T(8,128)(2,1)S(1)} %bitcast.51, s32[4,1024,128]{2,1,0:T(8,128)S(1)} %keep_words.3.w_ref, f32[1024,128]{1,0:T(8,128)S(1)} %get-tuple-element.33.refs_0_), custom_call_target="tpu_custom_call" | custom-call | flops 1610612736 | bytes 4194304 | tf_op jit(solution)/shard_map/tile/pallas_call | solution.py:150
  220.6 5.0 %tile.14 = (f32[1024,128]{1,0:T(8,128)S(1)}, f32[1024,256]{1,0:T(8,128)S(1)}, bf16[1024,1024]{1,0:T(8,128)(2,1)S(1)}) custom-call(s32[4]{0:T(128)S(1)} %pad_add_fusion.pick_ref, bf16[1024,896]{1,0:T(8,128)(2,1)} %get-tuple-element.30.coded_ref.x_ref.other_ref, bf16[16,2,64,768]{3,2,1,0:T(8,128)(2,1)S(1)} %copy-done.2, s32[4,1024,128]{2,1,0:T(8,128)S(1)} %keep_words.2.w_ref, ...), custom_call_target="tpu_custom_call" | custom-call | flops 1610612736 | bytes 4194304 | tf_op jit(solution)/shard_map/tile/pallas_call | solution.py:150
  227.4 4.1 %tile.12 = (f32[1024,128]{1,0:T(8,128)S(1)}, f32[1024,256]{1,0:T(8,128)S(1)}) custom-call(s32[4]{0:T(128)S(1)} %pad_add_fusion.pick_ref, bf16[4096,640]{1,0:T(8,128)(2,1)S(1)} %bitcast.51, bf16[16,2,64,768]{3,2,1,0:T(8,128)(2,1)S(1)} %copy-done.2, s32[4,1024,128]{2,1,0:T(8,128)S(1)} %keep_words.3.w_ref, bf16[16,2,64,768]{3,2,1,0:T(8,128)(2,1)S(1)} %copy-done.2, ...), custom_call_target="tpu_custom_call" | custom-call | flops 1610612736 | bytes 4194304 | tf_op jit(solution)/shard_map/tile/pallas_call | solution.py:150
  231.5 5.5 %tile.15 = (f32[1024,128]{1,0:T(8,128)S(1)}, f32[1024,256]{1,0:T(8,128)S(1)}, bf16[1024,1024]{1,0:T(8,128)(2,1)S(1)}) custom-call(s32[4]{0:T(128)S(1)} %pad_add_fusion.pick_ref, bf16[1024,896]{1,0:T(8,128)(2,1)} %get-tuple-element.30.coded_ref.x_ref.other_ref, bf16[16,64,768]{2,1,0:T(8,128)(2,1)} %collective-permute-done.4.other_ref.refs_0_.far_ref, ...), custom_call_target="tpu_custom_call" | custom-call | flops 1610612736 | bytes 4194304 | tf_op jit(solution)/shard_map/tile/pallas_call | solution.py:150
  237.8 5.3 %tile.13 = (f32[1024,128]{1,0:T(8,128)S(1)}, f32[1024,256]{1,0:T(8,128)S(1)}) custom-call(s32[4]{0:T(128)S(1)} %pad_add_fusion.pick_ref, bf16[4096,640]{1,0:T(8,128)(2,1)S(1)} %bitcast.51, bf16[16,64,768]{2,1,0:T(8,128)(2,1)} %collective-permute-done.4.other_ref.refs_0_.far_ref, s32[4,1024,128]{2,1,0:T(8,128)S(1)} %keep_words.3.w_ref, ...), custom_call_target="tpu_custom_call" | custom-call | flops 1610612736 | bytes 4194304 | tf_op jit(solution)/shard_map/tile/pallas_call | solution.py:150
  245.0 3.1 %gather.11.refs_0_ = f32[1024,256]{1,0:T(8,128)S(1)} custom-call(s32[4]{0:T(128)S(1)} %pad_add_fusion.pick_ref, bf16[1024,1024]{1,0:T(8,128)(2,1)S(1)} %get-tuple-element.49.tile_ref, bf16[1024,256]{1,0:T(8,128)(2,1)} %collective-permute-done.5.y_ref, f32[1024,256]{1,0:T(8,128)S(1)} %gather.10.refs_0_), custom_call_target="tpu_custom_call" | custom-call | flops 536870912 | bytes 3145728 | tf_op jit(solution)/shard_map/gather/pallas_call | solution.py:186
  251.9 1.9 gather.9.y_ref
  253.8 1.8 gather.12.refs_0_
  256.1 1.8 gather.7.refs_0_
  257.9 1.9 gather.8.y_ref
  259.8 2.8 %gather.13 = bf16[1024,256]{1,0:T(8,128)(2,1)} custom-call(s32[4]{0:T(128)S(1)} %pad_add_fusion.pick_ref, bf16[1024,1024]{1,0:T(8,128)(2,1)S(1)} %copy-done.8, bf16[1024,256]{1,0:T(8,128)(2,1)S(1)} %gather.8.y_ref, f32[1024,256]{1,0:T(8,128)S(1)} %gather.12.refs_0_, f32[1024,128]{1,0:T(8,128)S(1)} %copy-done.18, bf16[1024,256]{1,0:T(8,128)(2,1)S(1)} %copy-done.6), custom_call_target="tpu_custom_call" | custom-call | flops 536870912 | bytes 3145728 | tf_op jit(solution)/shard_map/gather/pallas_call | solution.py:186
  (104 shorter events, 26.6 us)
Async XLA Ops:
  14.9 8.7 %copy-start.27 = (s32[2]{0:T(128)S(1)}, s32[2]{0:T(128)}, u32[]{:S(2)}) copy-start(s32[2]{0:T(128)} %param.8) | copy-start | bytes 28
  14.9 33.4 %all-to-all-start = ((bf16[32,32,896]{2,1,0:T(8,128)(2,1)}), bf16[32,32,896]{2,1,0:T(8,128)(2,1)S(1)}, u32[]{:S(2)}, u32[]{:S(2)}) async-start(bf16[32,32,896]{2,1,0:T(8,128)(2,1)} %bitcast.9), calls=%async_computation | async-start | bytes 3670016 | tf_op jit(solution)/shard_map/all_to_all | solution.py:285
  22.8 138.1 %all-gather.3.cloned.1.call-start = ((), (), s32[]{:S(2)}) async-start(), calls=%async_computation.3 | async-start | bytes 6553600 | tf_op jit(solution)/shard_map/all_gather | solution.py:326
  23.5 225.5 %all-gather.5.cloned.1.call-start = ((), (), s32[]{:S(2)}) async-start(), calls=%async_computation.4 | async-start | bytes 2621440 | tf_op jit(solution)/shard_map/all_gather | solution.py:328
  48.3 7.8 %collective-permute-start = (bf16[1,2,32,896]{3,2,1,0:T(8,128)(2,1)S(1)}, bf16[1,2,32,896]{3,2,1,0:T(8,128)(2,1)S(1)}, u32[]{:S(2)}, u32[]{:S(2)}) collective-permute-start(bf16[1,2,32,896]{3,2,1,0:T(8,128)(2,1)S(1)} %maximum_bitcast_fusion), channel_id=1, source_target_pairs={{0,1},{1,0},{2,3},{3,2},{4,5},{5,4},{6,7},{7,6},{8,9},{9,8},{10,11... | collective-permute-start | bytes 344072 | tf_op jit(solution)/shard_map/ppermute | solution.py:259
  56.2 22.7 %collective-permute-start.1 = (bf16[2,2,32,896]{3,2,1,0:T(8,128)(2,1)S(1)}, bf16[2,2,32,896]{3,2,1,0:T(8,128)(2,1)S(1)}, u32[]{:S(2)}, u32[]{:S(2)}) collective-permute-start(bf16[2,2,32,896]{3,2,1,0:T(8,128)(2,1)S(1)} %pad_maximum_fusion), channel_id=1, source_target_pairs={{0,2},{1,3},{2,0},{3,1},{4,6},{5,7},{6,4},{7,5},{8,10},{9,11},{10,... | collective-permute-start | bytes 688136 | tf_op jit(solution)/shard_map/ppermute | solution.py:259
  81.7 28.3 %collective-permute-start.2 = (bf16[2,2,32,896]{3,2,1,0:T(8,128)(2,1)S(1)}, bf16[2,2,32,896]{3,2,1,0:T(8,128)(2,1)S(1)}, u32[]{:S(2)}, u32[]{:S(2)}) collective-permute-start(bf16[2,2,32,896]{3,2,1,0:T(8,128)(2,1)S(1)} %pad_maximum_fusion.1), channel_id=1, source_target_pairs={{0,128},{1,129},{2,130},{3,131},{4,132},{5,133},{6,134},{7,135},{8... | collective-permute-start | bytes 688136 | tf_op jit(solution)/shard_map/ppermute | solution.py:259
  110.1 5.9 %collective-permute-start.3 = (bf16[2,32,896]{2,1,0:T(8,128)(2,1)S(1)}, bf16[2,32,896]{2,1,0:T(8,128)(2,1)S(1)}, u32[]{:S(2)}, u32[]{:S(2)}) collective-permute-start(bf16[2,32,896]{2,1,0:T(8,128)(2,1)S(1)} %select_bitcast_fusion), channel_id=1, source_target_pairs={{0,4},{1,5},{2,6},{3,7},{4,0},{5,1},{6,2},{7,3},{8,12},{9,13},{10,... | collective-permute-start | bytes 344072 | tf_op jit(solution)/shard_map/ppermute | solution.py:259
  157.3 7.0 %copy-start.1 = (bf16[16,2,64,768]{3,2,1,0:T(8,128)(2,1)}, bf16[16,2,64,768]{3,2,1,0:T(8,128)(2,1)S(1)}, u32[]{:S(2)}) copy-start(bf16[16,2,64,768]{3,2,1,0:T(8,128)(2,1)S(1)} %all_to_all.15.other_ref.refs_0_.near_ref) | copy-start | bytes 9437188
  158.7 5.6 %collective-permute-start.4 = (bf16[16,64,768]{2,1,0:T(8,128)(2,1)}, bf16[16,64,768]{2,1,0:T(8,128)(2,1)}, u32[]{:S(2)}, u32[]{:S(2)}) collective-permute-start(bf16[16,64,768]{2,1,0:T(8,128)(2,1)} %slice_bitcast_fusion), channel_id=1, source_target_pairs={{0,4},{1,5},{2,6},{3,7},{4,0},{5,1},{6,2},{7,3},{8,12},{9,13},{10,... | collective-permute-start | bytes 4718600 | tf_op jit(solution)/shard_map/ppermute | solution.py:259
  167.9 16.9 %slice-start.2 = ((bf16[4096,640]{1,0:T(8,128)(2,1)}), bf16[4096,1]{1,0:T(8,128)(2,1)S(1)}, s32[]{:S(2)}) async-start(bf16[4096,640]{1,0:T(8,128)(2,1)} %all-gather.3.cloned.1.call-done.other_ref.coded_ref.x_ref), calls=%async_computation.7 | async-start | bytes 2097152 | tf_op jit(solution)/shard_map/slice | solution.py:338
  168.8 13.8 %all-to-all-start.2 = ((bf16[16,64,256]{2,1,0:T(8,128)(2,1)}), bf16[16,64,256]{2,1,0:T(8,128)(2,1)S(1)}, u32[]{:S(2)}, u32[]{:S(2)}) async-start(bf16[16,64,256]{2,1,0:T(8,128)(2,1)} %broadcast_in_dim.35), calls=%async_computation.2 | async-start | bytes 1048576 | tf_op jit(solution)/shard_map/all_to_all | solution.py:276
  182.6 62.4 %collective-permute-start.5 = (bf16[1024,256]{1,0:T(8,128)(2,1)S(1)}, bf16[1024,256]{1,0:T(8,128)(2,1)}, u32[]{:S(2)}, u32[]{:S(2)}) collective-permute-start(bf16[1024,256]{1,0:T(8,128)(2,1)S(1)} %bitcast.52), channel_id=1, source_target_pairs={{0,4},{1,5},{2,6},{3,7},{4,0},{5,1},{6,2},{7,3},{8,12},{9,13},{10,... | collective-permute-start | bytes 1572872 | tf_op jit(solution)/shard_map/ppermute | solution.py:259
  184.8 23.9 %slice-start = ((s8[5242880]{0:T(1024)(128)(4,1)}), s8[1048576]{0:T(1024)(128)(4,1)S(1)}, s32[]{:S(2)}) async-start(s8[5242880]{0:T(1024)(128)(4,1)} %bitcast.50), calls=%async_computation.5 | async-start | bytes 2097152
  193.2 2.5 copy-start
  195.7 6.2 %copy-start.6 = (bf16[1024,256]{1,0:T(8,128)(2,1)S(1)}, bf16[1024,256]{1,0:T(8,128)(2,1)}, u32[]{:S(2)}) copy-start(bf16[1024,256]{1,0:T(8,128)(2,1)} %refs_2_.3) | copy-start | bytes 1572868
  195.7 13.0 %slice-start.1 = ((s8[5242880]{0:T(1024)(128)(4,1)}), s8[4194304]{0:T(1024)(128)(4,1)S(1)}, s32[]{:S(2)}) async-start(s8[5242880]{0:T(1024)(128)(4,1)} %bitcast.50), calls=%async_computation.6 | async-start | bytes 8388608
  207.2 1.4 copy-start.13
  212.9 3.1 %copy-start.7 = (bf16[1024,1024]{1,0:T(8,128)(2,1)}, bf16[1024,1024]{1,0:T(8,128)(2,1)S(1)}, u32[]{:S(2)}) copy-start(bf16[1024,1024]{1,0:T(8,128)(2,1)S(1)} %get-tuple-element.32.tile_ref) | copy-start | bytes 6291460
  216.1 3.2 %copy-start.11 = (bf16[1024,1024]{1,0:T(8,128)(2,1)}, bf16[1024,1024]{1,0:T(8,128)(2,1)S(1)}, u32[]{:S(2)}) copy-start(bf16[1024,1024]{1,0:T(8,128)(2,1)S(1)} %get-tuple-element.36.tile_ref) | copy-start | bytes 6291460
  216.1 4.5 %copy-start.2 = (bf16[16,2,64,768]{3,2,1,0:T(8,128)(2,1)S(1)}, bf16[16,2,64,768]{3,2,1,0:T(8,128)(2,1)}, u32[]{:S(2)}) copy-start(bf16[16,2,64,768]{3,2,1,0:T(8,128)(2,1)} %copy-done.1) | copy-start | bytes 9437188
  237.8 5.4 %copy-start.22 = (f32[1024,256]{1,0:T(8,128)}, f32[1024,256]{1,0:T(8,128)S(1)}, u32[]{:S(2)}) copy-start(f32[1024,256]{1,0:T(8,128)S(1)} %get-tuple-element.47.refs_0_) | copy-start | bytes 3145732
  245.0 4.1 %copy-start.8 = (bf16[1024,1024]{1,0:T(8,128)(2,1)S(1)}, bf16[1024,1024]{1,0:T(8,128)(2,1)}, u32[]{:S(2)}) copy-start(bf16[1024,1024]{1,0:T(8,128)(2,1)} %copy-done.7) | copy-start | bytes 6291460
  245.0 4.1 %copy-start.18 = (f32[1024,128]{1,0:T(8,128)S(1)}, f32[1024,128]{1,0:T(8,128)}, u32[]{:S(2)}) copy-start(f32[1024,128]{1,0:T(8,128)} %copy-done.17) | copy-start | bytes 1572868
  249.1 1.6 copy-start.3
  251.9 1.9 copy-start.10
  251.9 1.9 copy-start.14
  251.9 3.7 %copy-start.20 = (f32[1024,256]{1,0:T(8,128)S(1)}, f32[1024,256]{1,0:T(8,128)}, u32[]{:S(2)}) copy-start(f32[1024,256]{1,0:T(8,128)} %copy-done.19) | copy-start | bytes 3145732
  253.8 1.8 copy-start.4
  253.8 2.3 copy-start.12
  256.1 1.8 copy-start.16
  256.1 1.8 copy-start.25
  (9 other events, 9.4 us)
Sparse Core Ops, SparseCore 0:
  25.5 120.3 all-gather.2
  161.1 45.0 all-gather.4

commit v3 on v2

--- a/solution.py
+++ b/solution.py
@@ -20,7 +20,7 @@
 HALF = 32
 
 
-def join_kernel(flag_ref, x_ref, y_ref, cols_ref, all_ref, rows_ref):
+def join_kernel(flag_ref, x_ref, y_ref, cols_ref, all_ref, normed_ref, rest_ref):
     width, clust = x_ref.shape[1], y_ref.shape[1]
     values = x_ref[...].astype(jnp.float32)
     scale = lax.rsqrt(jnp.sum(values * values, axis=1, keepdims=True) + EPS)
@@ -31,15 +31,16 @@
     all_ref[:, :width] = normed
     all_ref[:, width : width + clust] = y_ref[...]
     all_ref[:, width + clust :] = coded
-    rows_ref[:, :width] = normed
-    rows_ref[:, width:] = coded
+    normed_ref[...] = normed
+    rest_ref[:, :clust] = y_ref[...]
+    rest_ref[:, clust:] = coded
 
 
 def join(flag, embeddings, indicators, columns):
     rows, width = embeddings.shape
     clust = indicators.shape[1]
     by_row = lambda cols: pl.BlockSpec((ROW_TILE, cols), lambda r, flag: (r, 0))
-    wide = (width + clust + 2 * K * TOPK, width + 2 * K * TOPK)
+    wide = (width + clust + 2 * K * TOPK, width, clust + 2 * K * TOPK)
     return pl.pallas_call(
         join_kernel,
         out_shape=[jax.ShapeDtypeStruct((rows, w), jnp.bfloat16) for w in wide],
@@ -114,41 +115,38 @@
     return value.reshape(-1, value.shape[-1])
 
 
-def tile_kernel(has_deg, has_y, has_acc, keep, pick_ref, x_ref, other_ref, w_ref, *refs):
+def tile_kernel(has_carry, last, pick_ref, x_ref, other_ref, w_ref, y_ref, *refs):
     refs = list(refs)
-    y_ref = refs.pop(0) if has_y else None
-    deg_in = refs.pop(0) if has_deg else None
-    acc_in = refs.pop(0) if has_acc else None
-    deg_ref = refs.pop(0)
-    acc_ref = refs.pop(0) if has_y else None
-    tile_ref = refs.pop(0)
+    deg_in, acc_in = (refs.pop(0), refs.pop(0)) if has_carry else (None, None)
+    anchor_ref = refs.pop(0) if last else None
+    deg_ref, acc_ref, tile_ref = refs
     word = w_ref[0]
-    total = deg_in[...] if has_deg else jnp.zeros(word.shape, jnp.float32)
+    total = deg_in[...] if has_carry else jnp.zeros(word.shape, jnp.float32)
 
     def put(lanes, value):
         tile_ref[:, lanes] = value
 
-    deg_ref[...] = weights(cosines(x_ref[...], flat(other_ref)), word, total, put)
-    if has_y:
-        gathered = jnp.dot(tile_ref[...], flat(y_ref), preferred_element_type=jnp.float32)
-        acc_ref[...] = acc_in[...] + gathered if has_acc else gathered
-
-
-def tile_of(pick, x, other, words, slot, degree, y=None, acc=None, keep=True):
-    rows = words.shape[1]
+    total = weights(cosines(x_ref[...], flat(other_ref)), word, total, put)
+    deg_ref[...] = total
+    gathered = jnp.dot(tile_ref[...], flat(y_ref), preferred_element_type=jnp.float32)
+    if has_carry:
+        gathered = acc_in[...] + gathered
+    if last:
+        gathered = mix(gathered, jnp.sum(total, axis=1, keepdims=True), anchor_ref[...])
+    acc_ref[...] = gathered
+
+
+def tile_of(pick, x, other, y, words, slot, carry=None, anchor=None, keep=True):
+    rows, clust = words.shape[1], y[1][-1]
     by_row = lambda cols: pl.BlockSpec((ROW_TILE, cols), lambda r, pick: (r, 0))
     spec = lambda operand: pl.BlockSpec(operand[1], operand[2])
-    clust = y[1][-1] if y else 0
-    args = [x[0], other[0], words] + ([y[0]] if y else [])
-    specs = [spec(x), spec(other), pl.BlockSpec((1, ROW_TILE, LANES), lambda r, pick: (slot(pick), r, 0))]
-    specs += [spec(y)] if y else []
-    for extra, cols in ((degree, LANES), (acc, clust)):
-        if extra is not None:
-            args.append(extra)
-            specs.append(by_row(cols))
-    outs = [(LANES, jnp.float32)] + ([(clust, jnp.float32)] if y else []) + ([(rows, jnp.bfloat16)] if keep else [])
+    last = anchor is not None
+    args = [x[0], other[0], words, y[0], *(carry or ())] + ([anchor[0]] if last else [])
+    specs = [spec(x), spec(other), pl.BlockSpec((1, ROW_TILE, LANES), lambda r, pick: (slot(pick), r, 0)), spec(y)]
+    specs += ([by_row(LANES), by_row(clust)] if carry else []) + ([spec(anchor)] if last else [])
+    outs = [(LANES, jnp.float32), (clust, jnp.bfloat16 if last else jnp.float32)] + [(rows, jnp.bfloat16)] * keep
     return pl.pallas_call(
-        functools.partial(tile_kernel, degree is not None, y is not None, acc is not None, keep),
+        functools.partial(tile_kernel, carry is not None, last),
         out_shape=[jax.ShapeDtypeStruct((rows, cols), kind) for cols, kind in outs],
         grid_spec=pltpu.PrefetchScalarGridSpec(
             num_scalar_prefetch=1,
@@ -255,8 +253,15 @@
     for device in range(slabs * reps):
         slab, rep = divmod(device, reps)
         to = target(slab // (2 * chips), slab // 2 % chips, slab % 2, rep)
-        pairs.append((device, ((to[0] * chips + to[1]) * 2 + to[2]) * reps + to[3]))
+        if to is not None:
+            pairs.append((device, ((to[0] * chips + to[1]) * 2 + to[2]) * reps + to[3]))
     return lax.ppermute(block, AXES, pairs)
+
+
+def along_line(block, table):
+    return send(
+        block, lambda half, chip, core, rep: (half, chip, core, table[rep]) if rep in table else None
+    )
 
 
 def swap_cores(block):
@@ -276,25 +281,24 @@
     return lax.all_to_all(repeated, "slab", 0, 0, axis_index_groups=layers, tiled=True)
 
 
-def hub_pieces(block, hub_ids, code_at):
-    slabs, reps = lax.axis_size("slab"), lax.axis_size("rep")
-    members = slabs // 2
+def scatter(block):
+    members = lax.axis_size("slab") // 2
     rows, width = block.shape
-    piece = rows // members
     planes = [[h * members + m for m in range(members)] for h in range(2)]
-    mine = lax.all_to_all(
-        block.reshape(members, piece, width), "slab", 0, 0, axis_index_groups=planes, tiled=True
-    )
-    slab, rep = lax.axis_index("slab"), lax.axis_index("rep")
+    return lax.all_to_all(
+        block.reshape(members, rows // members, width), "slab", 0, 0, axis_index_groups=planes, tiled=True
+    )
+
+
+def hub_pieces(mine, hub_ids, code_at):
+    members, reps = lax.axis_size("slab") // 2, lax.axis_size("rep")
+    slab = lax.axis_index("slab")
     hub_slab, hub_rep = lax.div(hub_ids, reps), lax.rem(hub_ids, reps)
     member = lax.rem(hub_slab, members)
     held = jnp.stack(
         [lax.dynamic_index_in_dim(mine, member[h], 0, keepdims=False) for h in range(HUBS)], axis=0
-    )[None]
-    for bit in range(2):
-        got = send(held, lambda half, chip, core, rep: (half, chip, core, rep ^ (1 << bit)))
-        upper = (rep >> bit) & 1 == 1
-        held = jnp.concatenate([jnp.where(upper, got, held), jnp.where(upper, held, got)], axis=0)
+    )
+    held = lax.all_gather(held, "rep", axis=0, tiled=False)
     chosen = []
     for h in range(HUBS):
         hub = lax.dynamic_index_in_dim(held[:, h], hub_rep[h], 0, keepdims=False)
@@ -316,66 +320,84 @@
     full = width + clust
     reps = lax.axis_size("rep")
     total = lax.axis_size("slab") * reps
+    rep = lax.axis_index("rep")
     steps = rows // ROW_TILE
     slots = neighbours[0].astype(jnp.int32)
     want = slots[1] & 3
     order = slots[2] - total
     core = lax.rem(lax.axis_index("slab"), 2)
-
-    joined, coded = join((want + 4 * order)[None], embeddings, indicators, columns)
-    group_x = lax.all_gather(coded, "rep", axis=0, tiled=True)
-    anchor_in, group_x = lax.optimization_barrier((indicators, group_x))
-    group_y = lax.all_gather(anchor_in, "rep", axis=0, tiled=True)
-
-    both = hub_pieces(joined, hub_ids, full)
+    near_slot = jnp.where(order == core, 2, 3)
+    barrier = lax.optimization_barrier
+
+    joined, normed, rest = join((want + 4 * order)[None], embeddings, indicators, columns)
+    group_x = lax.all_gather(normed, "rep", axis=0, tiled=True)
+    across = along_line(rest, {0: 2, 2: 0, 1: 3, 3: 1})
+    beside = along_line(rest, {0: 1, 1: 0, 2: 3, 3: 2})
+    middle = along_line(rest, {1: 2, 2: 1})
+
+    pick = jnp.stack([near_slot]).astype(jnp.int32)
+    own_rows = (joined, (ROW_TILE, width), lambda r, pick: (r, 0))
+    own_x = (joined, (rows, width), lambda r, pick: (0, 0))
+    own_y = (joined, (rows, clust), lambda r, pick: (0, width // clust))
+    words = keep_words(pick, joined, lambda pick: (0, full // LANES), rows)
+    *carry, own_tile = tile_of(pick, own_rows, own_x, own_y, words, lambda pick: 0)
+    mine, words, carry, own_tile = barrier((scatter(joined), words, carry, own_tile))
+
+    both = hub_pieces(mine, hub_ids, full)
+    outer = along_line(across, {1: 0, 2: 3})
+    third = jnp.where((rep == 0) | (rep == 3), outer, middle)
+    group_rest = jnp.concatenate([rest, beside, across, third], axis=0)
+    at = want ^ rep
+    member_want, member_order = flags_of(
+        lax.dynamic_index_in_dim(group_rest[:, clust], at * rows, 0, keepdims=False)
+    )
+    pick = jnp.stack(
+        [near_slot, want, member_want, jnp.where(member_order == core, 2, 3), at, member_want ^ rep]
+    ).astype(jnp.int32)
+    member_words = keep_words(pick, group_rest, lambda pick: (pick[4], clust // LANES), rows)
+    both, group_rest, member_words = barrier((both, group_rest, member_words))
+
+    member_rows = (group_x, (ROW_TILE, width), lambda r, pick: (pick[1] * steps + r, 0))
+    member_x = (group_x, (rows, width), lambda r, pick: (pick[1], 0))
+    second_x = (group_x, (rows, width), lambda r, pick: (pick[2], 0))
+    member_y = (group_rest, (rows, clust), lambda r, pick: (pick[4], 0))
+    second_y = (group_rest, (rows, clust), lambda r, pick: (pick[5], 0))
     near = join_pieces(both[:, :, :full])
+    *carry, member_tile = tile_of(pick, own_rows, member_x, member_y, words, lambda pick: 1, carry)
+    carry_c = tile_of(pick, member_rows, member_x, member_y, member_words, lambda pick: 0, None, None, False)
+    carry_c = tile_of(pick, member_rows, second_x, second_y, member_words, lambda pick: 1, carry_c, None, False)
+    near, carry, carry_c = barrier((near, carry, carry_c))
+
+    chips, _, piece, _ = near.shape
+    near_x = (near, (chips, 1, piece, width), lambda r, pick: (0, 0, 0, 0))
+    near_y = (near, (chips, 1, piece, clust), lambda r, pick: (0, 0, 0, width // clust))
     far = swap_cores(near[:, 0])
+    far_x = (far, (chips, piece, width), lambda r, pick: (0, 0, 0))
+    far_y = (far, (chips, piece, clust), lambda r, pick: (0, 0, width // clust))
+    *carry, near_tile = tile_of(pick, own_rows, near_x, near_y, words, lambda pick: pick[0], carry)
+    far, carry = barrier((far, carry))
+    far_x, far_y = (far, *far_x[1:]), (far, *far_y[1:])
     _, hub_order = flags_of(both[0, 0, full])
     share = hub_rows(jnp.where(hub_order == core, 2, 3)[None], both[0], near, far, width)
-    near_y = join_pieces(share).reshape(rows, clust)
-    far_y = swap_cores(near_y)
-
-    member_want, member_order = flags_of(lax.dynamic_index_in_dim(group_x[:, width], want * rows, 0, keepdims=False))
-    near_slot = jnp.where(order == core, 2, 3)
-    member_near = jnp.where(member_order == core, 2, 3)
-    pick = jnp.stack([want, member_want, near_slot, member_near]).astype(jnp.int32)
-    words = keep_words(pick, joined, lambda pick: (0, full // LANES), rows)
-    member_words = keep_words(pick, group_x, lambda pick: (pick[0], width // LANES), rows)
-    own_rows = (joined, (ROW_TILE, width), lambda r, pick: (r, 0))
-    member_rows = (group_x, (ROW_TILE, width), lambda r, pick: (pick[0] * steps + r, 0))
-    own_x = (joined, (rows, width), lambda r, pick: (0, 0))
-    own_y = (indicators, (rows, clust), lambda r, pick: (0, 0))
-    at_member = lambda array, cols: (array, (rows, cols), lambda r, pick: (pick[0], 0))
-    at_second = lambda array, cols: (array, (rows, cols), lambda r, pick: (pick[1], 0))
-    chips, piece = near.shape[0], near.shape[2]
-    near_x0 = (near, (chips, 1, piece, width), lambda r, pick: (0, 0, 0, 0))
-    near_y0 = (near, (chips, 1, piece, clust), lambda r, pick: (0, 0, 0, width // clust))
-    far_x0 = (far, (chips, piece, width), lambda r, pick: (0, 0, 0))
-    far_y0 = (far, (chips, piece, clust), lambda r, pick: (0, 0, width // clust))
+
+    near_new = join_pieces(share).reshape(rows, clust)
+    by_row = (indicators, (ROW_TILE, clust), lambda r, pick: (r, 0))
+    member_anchor = (group_rest, (ROW_TILE, clust), lambda r, pick: (pick[4] * steps + r, 0))
+    carry_c = tile_of(
+        pick, member_rows, near_x, near_y, member_words, lambda pick: pick[3], carry_c, None, False
+    )
+    degree, new, far_tile = tile_of(pick, own_rows, far_x, far_y, words, lambda pick: 5 - pick[0], carry, by_row)
+    _, member_new = tile_of(
+        pick, member_rows, far_x, far_y, member_words, lambda pick: 5 - pick[3], carry_c, member_anchor, False
+    )
+    near_new, new, member_new = barrier((near_new, new, member_new))
+    far_new = swap_cores(near_new)
+
     whole = lambda array: (array, array.shape, lambda r, pick: (0, 0))
-
-    degree, acc, own_tile = tile_of(pick, own_rows, own_x, words, lambda pick: 0, None, own_y)
-    degree, member_tile = tile_of(pick, own_rows, at_member(group_x, width), words, lambda pick: 1, degree)
-    degree_c, tile_c0 = tile_of(pick, member_rows, at_member(group_x, width), member_words, lambda pick: 0, None)
-    degree_c, tile_c1 = tile_of(pick, member_rows, at_second(group_x, width), member_words, lambda pick: 1, degree_c)
-    degree, acc, near_tile = tile_of(pick, own_rows, near_x0, words, lambda pick: pick[2], degree, near_y0, acc)
-    degree_c, acc_c = tile_of(
-        pick, member_rows, near_x0, member_words, lambda pick: pick[3], degree_c, near_y0, None, False
-    )
-    degree, acc, far_tile = tile_of(pick, own_rows, far_x0, words, lambda pick: 5 - pick[2], degree, far_y0, acc)
-    degree_c, acc_c = tile_of(
-        pick, member_rows, far_x0, member_words, lambda pick: 5 - pick[3], degree_c, far_y0, acc_c, False
-    )
-    by_row = (indicators, (ROW_TILE, clust), lambda r, pick: (r, 0))
-    member_anchor = (group_y, (ROW_TILE, clust), lambda r, pick: (pick[0] * steps + r, 0))
-    acc_c = gather_of(pick, tile_c0, at_member(group_y, clust), acc_c)
-    member_new = gather_of(pick, tile_c1, at_second(group_y, clust), acc_c, degree_c, member_anchor)
-    new = gather_of(pick, member_tile, at_member(group_y, clust), acc, degree, by_row)
-
-    acc = gather_of(pick, near_tile, whole(near_y), None)
-    acc = gather_of(pick, far_tile, whole(far_y), acc)
-    acc = gather_of(pick, own_tile, whole(new), acc)
-    return gather_of(pick, member_tile, whole(member_new), acc, degree, by_row)
+    acc = gather_of(pick, own_tile, whole(new), None)
+    acc = gather_of(pick, member_tile, whole(member_new), acc)
+    acc = gather_of(pick, near_tile, whole(near_new), acc)
+    return gather_of(pick, far_tile, whole(far_new), acc, degree, by_row)
 
 
 def solution(mesh):

time: 275 us -> 330 us (1.20)
  waiting for transfers between devices: 79.1 us -> 113 us
  local copies, waits for them, and re-layouts: 22.1 us -> 44 us
  starting transfers between devices: 30.3 us -> 49.9 us
  blocking collectives: 41 us -> 22.3 us
  other arithmetic: 1.1 us -> 4.77 us
    ppermute x6 -> x8, waiting for transfers between devices: 48 us -> 94.5 us  [send(): return lax.ppermute(block, AXES, pairs)]
    all_to_all x1 -> x0, blocking collectives: 41 us -> none  [join_pieces(): lax.all_to_all(repeated, 'slab', 0, 0, axis_index_groups=layers, tiled=True)]
    all_gather x0 -> x1, blocking collectives: none -> 22.3 us  [hub_pieces(): held = lax.all_gather(held, 'rep', axis=0, tiled=False)]
    all_to_all x1, waiting for transfers between devices: 20.2 us -> 0.01 us  [scatter(): lax.all_to_all(block.reshape(members, rows // members, width), 'slab', 0,...]
    unnamed x60 -> x100, local copies, waits for them, and re-layouts: 15.4 us -> 35.2 us
    all_to_all x1 -> x2, starting transfers between devices: 3.57 us -> 20.3 us  [join_pieces(): lax.all_to_all(repeated, 'slab', 0, 0, axis_index_groups=layers, tiled=True)]
    all_to_all x1 -> x2, waiting for transfers between devices: 10.2 us -> 18.2 us  [join_pieces(): lax.all_to_all(repeated, 'slab', 0, 0, axis_index_groups=layers, tiled=True)]
    pallas_call x7 -> x4, Pallas kernels: 15 us -> 9.56 us  [gather_of(): pl.pallas_call(functools.partial(gather_kernel, acc is not None, last), o...]
  transfers between devices with their start and end apart: 10 -> 12, of which waited for: 7 -> 3; matrix products, arithmetic and copies ran while one was open for 2% -> 3% of each run, Pallas kernels for 21% -> 18%
where the time goes in v3:
time: 330 us; the launch traced here: 327 us
  waiting for transfers between devices  113 us (34%)
  Pallas kernels  67.4 us (20%)
  starting transfers between devices  49.9 us (15%)
  local copies, waits for them, and re-layouts  44 us (13%)
  between operations  26.1 us (8%)
  blocking collectives  22.3 us (7%)
  other arithmetic  4.77 us (1%)
    ppermute x8, waiting for transfers between devices, send(): return lax.ppermute(block, AXES, pairs)  94.5 us
    pallas_call x8, Pallas kernels, tile_of(): pl.pallas_call(functools.partial(tile_kernel, carry is not None, last), o...  39 us
    unnamed x100, local copies, waits for them, and re-layouts  35.2 us
    all_gather x1, blocking collectives, hub_pieces(): held = lax.all_gather(held, 'rep', axis=0, tiled=False)  22.3 us
    ppermute x8, starting transfers between devices, send(): return lax.ppermute(block, AXES, pairs)  21.8 us
    all_to_all x2, starting transfers between devices, join_pieces(): lax.all_to_all(repeated, 'slab', 0, 0, axis_index_groups=layers, tiled=True)  20.3 us
    all_to_all x2, waiting for transfers between devices, join_pieces(): lax.all_to_all(repeated, 'slab', 0, 0, axis_index_groups=layers, tiled=True)  18.2 us
    pallas_call x2, Pallas kernels, keep_words(): pl.pallas_call(words_kernel, out_shape=jax.ShapeDtypeStruct((K, rows, LAN...  12.8 us
  transfers between devices with their start and end apart: 12, of which 3 were waited for; matrix products, arithmetic and copies ran while one was open for 3% of the time, Pallas kernels for 18%

profile of v3, /device:TPU:161, one launch (start us, length us, event | category | flops | bytes accessed | tf_op | source)
XLA Modules:
  0.0 327.3 jit_solution(17267485524636120302)
XLA Ops:
  12.3 2.4 join.1
  14.7 7.8 %all-to-all-start = ((bf16[32,32,896]{2,1,0:T(8,128)(2,1)}), bf16[32,32,896]{2,1,0:T(8,128)(2,1)S(1)}, u32[]{:S(2)}, u32[]{:S(2)}) async-start(bf16[32,32,896]{2,1,0:T(8,128)(2,1)} %bitcast.11), calls=%async_computation | async-start | bytes 3670016 | tf_op jit(solution)/shard_map/all_to_all | solution.py:288
  22.5 2.6 collective-permute-start.3
  25.2 1.9 collective-permute-start
  36.4 6.6 %keep_words.2.w_ref = s32[4,1024,128]{2,1,0:T(8,128)S(1)} custom-call(s32[1]{0:T(128)} %bitcast.1.pick_ref, bf16[1024,896]{1,0:T(8,128)(2,1)} %get-tuple-element.47.coded_ref.x_ref.other_ref.y_ref), custom_call_target="tpu_custom_call" | custom-call | flops 8388608 | bytes 524288 | tf_op jit(solution)/shard_map/keep_words/pallas_call | solution.py:81
  43.0 5.7 %tile.8 = (f32[1024,128]{1,0:T(8,128)S(1)}, f32[1024,256]{1,0:T(8,128)S(1)}, bf16[1024,1024]{1,0:T(8,128)(2,1)S(1)}) custom-call(s32[1]{0:T(128)} %bitcast.1.pick_ref, bf16[1024,896]{1,0:T(8,128)(2,1)} %get-tuple-element.47.coded_ref.x_ref.other_ref.y_ref, bf16[1024,896]{1,0:T(8,128)(2,1)} %get-tuple-element.47.coded_ref.x_ref.other_ref.y_ref, ...), custom_call_target="tpu_custom_call" | custom-call | flops 1610612736 | bytes 4194304 | tf_op jit(solution)/shard_map/tile/pallas_call | solution.py:148
  52.0 88.4 %collective-permute-done.1 = bf16[1024,384]{1,0:T(8,128)(2,1)S(1)} collective-permute-done((bf16[1024,384]{1,0:T(8,128)(2,1)S(1)}, bf16[1024,384]{1,0:T(8,128)(2,1)S(1)}, u32[]{:S(2)}, u32[]{:S(2)}) %collective-permute-start.1) | collective-permute-done | bytes 786464 | tf_op jit(solution)/shard_map/ppermute | solution.py:258
  140.3 5.4 %collective-permute-start.2 = (bf16[1024,384]{1,0:T(8,128)(2,1)S(1)}, bf16[1024,384]{1,0:T(8,128)(2,1)}, u32[]{:S(2)}, u32[]{:S(2)}) collective-permute-start(bf16[1024,384]{1,0:T(8,128)(2,1)S(1)} %collective-permute-done.1), channel_id=1, source_target_pairs={{1,0},{2,3},{5,4},{6,7},{9,8},{10,11},{13,12},{14,15},{17,16},{18,... | collective-permute-start | bytes 2359304 | tf_op jit(solution)/shard_map/ppermute | solution.py:258
  145.8 22.3 %all-gather = bf16[8,32,896]{2,1,0:T(8,128)(2,1)S(1)} all-gather(bf16[2,32,896]{2,1,0:T(8,128)(2,1)S(1)} %pad_maximum_fusion.3), channel_id=2, replica_groups=mesh['slab'=64,'rep'=4] {'rep'}, dimensions={0}, use_global_device_ids=true | all-gather | bytes 573440 | tf_op jit(solution)/shard_map/all_gather | solution.py:301
  170.9 1.8 collective-permute-start.4
  174.0 6.1 %collective-permute-done.4 = bf16[2,2,32,896]{3,2,1,0:T(8,128)(2,1)S(1)} collective-permute-done((bf16[2,2,32,896]{3,2,1,0:T(8,128)(2,1)S(1)}, bf16[2,2,32,896]{3,2,1,0:T(8,128)(2,1)S(1)}, u32[]{:S(2)}, u32[]{:S(2)}) %collective-permute-start.4) | collective-permute-done | bytes 229408 | tf_op jit(solution)/shard_map/ppermute | solution.py:258
  180.8 7.8 %collective-permute-start.5 = (bf16[2,32,896]{2,1,0:T(8,128)(2,1)}, bf16[2,32,896]{2,1,0:T(8,128)(2,1)S(1)}, u32[]{:S(2)}, u32[]{:S(2)}) collective-permute-start(bf16[2,32,896]{2,1,0:T(8,128)(2,1)} %select_bitcast_fusion), channel_id=1, source_target_pairs={{0,4},{1,5},{2,6},{3,7},{4,0},{5,1},{6,2},{7,3},{8,12},{9,13},{10,... | collective-permute-start | bytes 344072 | tf_op jit(solution)/shard_map/ppermute | solution.py:258
  188.7 1.9 pad_maximum_fusion.coded_ref.y_ref.refs_2_
  192.2 6.2 %keep_words.3.w_ref = s32[4,1024,128]{2,1,0:T(8,128)S(1)} custom-call(s32[6]{0:T(128)S(1)} %stack.52.pick_ref, bf16[4096,384]{1,0:T(8,128)(2,1)S(1)} %pad_maximum_fusion.coded_ref.y_ref.refs_2_), custom_call_target="tpu_custom_call" | custom-call | flops 8388608 | bytes 524288 | tf_op jit(solution)/shard_map/keep_words/pallas_call | solution.py:81
  199.8 2.1 broadcast_in_dim.29
  201.9 9.6 %all-to-all-start.1 = ((bf16[16,2,64,768]{3,2,1,0:T(8,128)(2,1)}), bf16[16,2,64,768]{3,2,1,0:T(8,128)(2,1)S(1)}, u32[]{:S(2)}, u32[]{:S(2)}) async-start(bf16[16,2,64,768]{3,2,1,0:T(8,128)(2,1)} %broadcast_in_dim.29), calls=%async_computation.1 | async-start | bytes 6291456 | tf_op jit(solution)/shard_map/all_to_all | solution.py:281
  211.5 2.2 copy-done
  213.7 1.9 copy-done.5
  217.2 3.9 %tile.10 = (f32[1024,128]{1,0:T(8,128)S(1)}, f32[1024,256]{1,0:T(8,128)S(1)}) custom-call(s32[6]{0:T(128)S(1)} %stack.52.pick_ref, bf16[4096,512]{1,0:T(8,128)(2,1)S(1)} %copy-done, bf16[4096,512]{1,0:T(8,128)(2,1)S(1)} %copy-done, s32[4,1024,128]{2,1,0:T(8,128)S(1)} %copy-done.13, bf16[4096,384]{1,0:T(8,128)(2,1)S(1)} %copy-done.5), custom_call_target="tpu_custom_call" | custom-call | flops 1610612736 | bytes 4194304 | tf_op jit(solution)/shard_map/tile/pallas_call | solution.py:148
  221.1 3.9 %tile.11 = (f32[1024,128]{1,0:T(8,128)S(1)}, f32[1024,256]{1,0:T(8,128)S(1)}) custom-call(s32[6]{0:T(128)S(1)} %stack.52.pick_ref, bf16[4096,512]{1,0:T(8,128)(2,1)S(1)} %copy-done, bf16[4096,512]{1,0:T(8,128)(2,1)S(1)} %copy-done, s32[4,1024,128]{2,1,0:T(8,128)S(1)} %copy-done.13, bf16[4096,384]{1,0:T(8,128)(2,1)S(1)} %copy-done.5, ...), custom_call_target="tpu_custom_call" | custom-call | flops 1610612736 | bytes 4194304 | tf_op jit(solution)/shard_map/tile/pallas_call | solution.py:148
  226.9 4.9 %tile.9 = (f32[1024,128]{1,0:T(8,128)S(1)}, f32[1024,256]{1,0:T(8,128)S(1)}, bf16[1024,1024]{1,0:T(8,128)(2,1)S(1)}) custom-call(s32[6]{0:T(128)S(1)} %stack.52.pick_ref, bf16[1024,896]{1,0:T(8,128)(2,1)} %get-tuple-element.47.coded_ref.x_ref.other_ref.y_ref, bf16[4096,512]{1,0:T(8,128)(2,1)S(1)} %copy-done.1, s32[4,1024,128]{2,1,0:T(8,128)S(1)} %copy-done.9, ...), custom_call_target="tpu_custom_call" | custom-call | flops 1610612736 | bytes 4194304 | tf_op jit(solution)/shard_map/tile/pallas_call | solution.py:148
  234.9 18.2 %all-to-all-done.1.other_ref.y_ref.near_ref = bf16[16,2,64,768]{3,2,1,0:T(8,128)(2,1)S(1)} async-done(((bf16[16,2,64,768]{3,2,1,0:T(8,128)(2,1)}), bf16[16,2,64,768]{3,2,1,0:T(8,128)(2,1)S(1)}, u32[]{:S(2)}, u32[]{:S(2)}) %all-to-all-start.1) | async-done | bytes 3145760 | tf_op jit(solution)/shard_map/all_to_all | solution.py:281
  254.4 1.9 collective-permute-start.6
  261.5 4.9 %tile.12 = (f32[1024,128]{1,0:T(8,128)S(1)}, f32[1024,256]{1,0:T(8,128)S(1)}, bf16[1024,1024]{1,0:T(8,128)(2,1)S(1)}) custom-call(s32[6]{0:T(128)S(1)} %stack.52.pick_ref, bf16[1024,896]{1,0:T(8,128)(2,1)} %get-tuple-element.47.coded_ref.x_ref.other_ref.y_ref, bf16[16,2,64,768]{3,2,1,0:T(8,128)(2,1)S(1)} %all-to-all-done.1.other_ref.y_ref.near_ref, ...), custom_call_target="tpu_custom_call" | custom-call | flops 1610612736 | bytes 4194304 | tf_op jit(solution)/shard_map/tile/pallas_call | solution.py:148
  269.6 3.6 %hub_rows.1 = bf16[64,256]{1,0:T(8,128)(2,1)S(1)} custom-call(s32[1]{0:T(128)} %bitcast.31.pick_ref, bf16[64,896]{1,0:T(8,128)(2,1)S(1)} %slice_bitcast_fusion.1.rows_ref, bf16[16,2,64,768]{3,2,1,0:T(8,128)(2,1)S(1)} %all-to-all-done.1.other_ref.y_ref.near_ref, bf16[16,64,768]{2,1,0:T(8,128)(2,1)} %collective-permute-done.6.other_ref.y_ref.far_ref), custom_call_target="tpu_custom_call" | custom-call | flops 402653184 | bytes 6291456 | tf_op jit(solution)/shard_map/hub_rows/pallas_call | solution.py:229
  274.0 10.7 %all-to-all-start.2 = ((bf16[16,64,256]{2,1,0:T(8,128)(2,1)}), bf16[16,64,256]{2,1,0:T(8,128)(2,1)}, u32[]{:S(2)}, u32[]{:S(2)}) async-start(bf16[16,64,256]{2,1,0:T(8,128)(2,1)} %broadcast_in_dim.31), calls=%async_computation.2 | async-start | bytes 1048576 | tf_op jit(solution)/shard_map/all_to_all | solution.py:281
  284.8 2.2 copy-done.2
  290.8 3.9 %tile.14 = (f32[1024,128]{1,0:T(8,128)S(1)}, f32[1024,256]{1,0:T(8,128)S(1)}) custom-call(s32[6]{0:T(128)S(1)} %stack.52.pick_ref, bf16[4096,512]{1,0:T(8,128)(2,1)S(1)} %copy-done.2, bf16[16,2,64,768]{3,2,1,0:T(8,128)(2,1)S(1)} %all-to-all-done.1.other_ref.y_ref.near_ref, s32[4,1024,128]{2,1,0:T(8,128)S(1)} %copy-done.14, ...), custom_call_target="tpu_custom_call" | custom-call | flops 1610612736 | bytes 4194304 | tf_op jit(solution)/shard_map/tile/pallas_call | solution.py:148
  294.9 5.8 %tile.13 = (f32[1024,128]{1,0:T(8,128)S(1)}, bf16[1024,256]{1,0:T(8,128)(2,1)S(1)}, bf16[1024,1024]{1,0:T(8,128)(2,1)S(1)}) custom-call(s32[6]{0:T(128)S(1)} %stack.52.pick_ref, bf16[1024,896]{1,0:T(8,128)(2,1)} %get-tuple-element.47.coded_ref.x_ref.other_ref.y_ref, bf16[16,64,768]{2,1,0:T(8,128)(2,1)} %collective-permute-done.6.other_ref.y_ref.far_ref, ...), custom_call_target="tpu_custom_call" | custom-call | flops 1610612736 | bytes 4194304 | tf_op jit(solution)/shard_map/tile/pallas_call | solution.py:148
  302.8 5.9 %tile.15 = (f32[1024,128]{1,0:T(8,128)}, bf16[1024,256]{1,0:T(8,128)(2,1)S(1)}) custom-call(s32[6]{0:T(128)S(1)} %stack.52.pick_ref, bf16[4096,512]{1,0:T(8,128)(2,1)S(1)} %copy-done.3, bf16[16,64,768]{2,1,0:T(8,128)(2,1)} %collective-permute-done.6.other_ref.y_ref.far_ref, s32[4,1024,128]{2,1,0:T(8,128)S(1)} %copy-done.15, ...), custom_call_target="tpu_custom_call" | custom-call | flops 1610612736 | bytes 4194304 | tf_op jit(solution)/shard_map/tile/pallas_call | solution.py:148
  314.4 3.1 gather.6.refs_0_
  317.6 2.8 gather.7
  (142 shorter events, 42.6 us)
Async XLA Ops:
  12.3 14.9 %copy-start.49 = (s32[2]{0:T(128)S(1)}, s32[2]{0:T(128)}, u32[]{:S(2)}) copy-start(s32[2]{0:T(128)} %param.8) | copy-start | bytes 28
  14.7 28.4 %copy-start.36 = (bf16[1024,384]{1,0:T(8,128)(2,1)}, bf16[1024,384]{1,0:T(8,128)(2,1)S(1)}, u32[]{:S(2)}) copy-start(bf16[1024,384]{1,0:T(8,128)(2,1)S(1)} %get-tuple-element.46) | copy-start | bytes 2359300
  14.7 131.1 %all-to-all-start = ((bf16[32,32,896]{2,1,0:T(8,128)(2,1)}), bf16[32,32,896]{2,1,0:T(8,128)(2,1)S(1)}, u32[]{:S(2)}, u32[]{:S(2)}) async-start(bf16[32,32,896]{2,1,0:T(8,128)(2,1)} %bitcast.11), calls=%async_computation | async-start | bytes 3670016 | tf_op jit(solution)/shard_map/all_to_all | solution.py:288
  22.4 189.1 %all-gather.3.cloned.1.call-start = ((), (), s32[]{:S(2)}) async-start(), calls=%async_computation.3 | async-start | bytes 5242880 | tf_op jit(solution)/shard_map/all_gather | solution.py:333
  22.5 150.3 %collective-permute-start.3 = (bf16[1024,384]{1,0:T(8,128)(2,1)S(1)}, bf16[1024,384]{1,0:T(8,128)(2,1)}, u32[]{:S(2)}, u32[]{:S(2)}) collective-permute-start(bf16[1024,384]{1,0:T(8,128)(2,1)S(1)} %get-tuple-element.46), channel_id=1, source_target_pairs={{1,2},{2,1},{5,6},{6,5},{9,10},{10,9},{13,14},{14,13},{17,18},{18,... | collective-permute-start | bytes 2359304 | tf_op jit(solution)/shard_map/ppermute | solution.py:258
  25.1 115.2 %collective-permute-start.1 = (bf16[1024,384]{1,0:T(8,128)(2,1)S(1)}, bf16[1024,384]{1,0:T(8,128)(2,1)S(1)}, u32[]{:S(2)}, u32[]{:S(2)}) collective-permute-start(bf16[1024,384]{1,0:T(8,128)(2,1)S(1)} %get-tuple-element.46), channel_id=1, source_target_pairs={{0,2},{1,3},{2,0},{3,1},{4,6},{5,7},{6,4},{7,5},{8,10},{9,11},{10,... | collective-permute-start | bytes 2359304 | tf_op jit(solution)/shard_map/ppermute | solution.py:258
  25.2 163.4 %collective-permute-start = (bf16[1024,384]{1,0:T(8,128)(2,1)S(1)}, bf16[1024,384]{1,0:T(8,128)(2,1)}, u32[]{:S(2)}, u32[]{:S(2)}) collective-permute-start(bf16[1024,384]{1,0:T(8,128)(2,1)S(1)} %get-tuple-element.46), channel_id=1, source_target_pairs={{0,1},{1,0},{2,3},{3,2},{4,5},{5,4},{6,7},{7,6},{8,9},{9,8},{10,11... | collective-permute-start | bytes 2359304 | tf_op jit(solution)/shard_map/ppermute | solution.py:258
  43.0 5.7 %copy-start.8 = (s32[4,1024,128]{2,1,0:T(8,128)}, s32[4,1024,128]{2,1,0:T(8,128)S(1)}, u32[]{:S(2)}) copy-start(s32[4,1024,128]{2,1,0:T(8,128)S(1)} %keep_words.2.w_ref) | copy-start | bytes 6291460
  140.3 39.7 %copy-start.48 = (bf16[1024,384]{1,0:T(8,128)(2,1)}, bf16[1024,384]{1,0:T(8,128)(2,1)S(1)}, u32[]{:S(2)}) copy-start(bf16[1024,384]{1,0:T(8,128)(2,1)S(1)} %collective-permute-done.1) | copy-start | bytes 2359300
  140.3 32.4 %collective-permute-start.2 = (bf16[1024,384]{1,0:T(8,128)(2,1)S(1)}, bf16[1024,384]{1,0:T(8,128)(2,1)}, u32[]{:S(2)}, u32[]{:S(2)}) collective-permute-start(bf16[1024,384]{1,0:T(8,128)(2,1)S(1)} %collective-permute-done.1), channel_id=1, source_target_pairs={{1,0},{2,3},{5,4},{6,7},{9,8},{10,11},{13,12},{14,15},{17,16},{18,... | collective-permute-start | bytes 2359304 | tf_op jit(solution)/shard_map/ppermute | solution.py:258
  170.9 9.1 %collective-permute-start.4 = (bf16[2,2,32,896]{3,2,1,0:T(8,128)(2,1)S(1)}, bf16[2,2,32,896]{3,2,1,0:T(8,128)(2,1)S(1)}, u32[]{:S(2)}, u32[]{:S(2)}) collective-permute-start(bf16[2,2,32,896]{3,2,1,0:T(8,128)(2,1)S(1)} %pad_maximum_fusion.1), channel_id=1, source_target_pairs={{0,128},{1,129},{2,130},{3,131},{4,132},{5,133},{6,134},{7,135},{8... | collective-permute-start | bytes 688136 | tf_op jit(solution)/shard_map/ppermute | solution.py:258
  180.8 18.9 %collective-permute-start.5 = (bf16[2,32,896]{2,1,0:T(8,128)(2,1)}, bf16[2,32,896]{2,1,0:T(8,128)(2,1)S(1)}, u32[]{:S(2)}, u32[]{:S(2)}) collective-permute-start(bf16[2,32,896]{2,1,0:T(8,128)(2,1)} %select_bitcast_fusion), channel_id=1, source_target_pairs={{0,4},{1,5},{2,6},{3,7},{4,0},{5,1},{6,2},{7,3},{8,12},{9,13},{10,... | collective-permute-start | bytes 344072 | tf_op jit(solution)/shard_map/ppermute | solution.py:258
  190.6 7.8 %copy-start.4 = (bf16[4096,384]{1,0:T(8,128)(2,1)}, bf16[4096,384]{1,0:T(8,128)(2,1)S(1)}, u32[]{:S(2)}) copy-start(bf16[4096,384]{1,0:T(8,128)(2,1)S(1)} %pad_maximum_fusion.coded_ref.y_ref.refs_2_) | copy-start | bytes 9437188
  201.9 51.3 %all-to-all-start.1 = ((bf16[16,2,64,768]{3,2,1,0:T(8,128)(2,1)}), bf16[16,2,64,768]{3,2,1,0:T(8,128)(2,1)S(1)}, u32[]{:S(2)}, u32[]{:S(2)}) async-start(bf16[16,2,64,768]{3,2,1,0:T(8,128)(2,1)} %broadcast_in_dim.29), calls=%async_computation.1 | async-start | bytes 6291456 | tf_op jit(solution)/shard_map/all_to_all | solution.py:281
  221.1 5.8 %copy-start.1 = (bf16[4096,512]{1,0:T(8,128)(2,1)S(1)}, bf16[4096,512]{1,0:T(8,128)(2,1)}, u32[]{:S(2)}) copy-start(bf16[4096,512]{1,0:T(8,128)(2,1)} %all-gather.3.cloned.1.call-done.other_ref.x_ref) | copy-start | bytes 12582916
  221.1 5.8 %copy-start.6 = (bf16[4096,384]{1,0:T(8,128)(2,1)S(1)}, bf16[4096,384]{1,0:T(8,128)(2,1)}, u32[]{:S(2)}) copy-start(bf16[4096,384]{1,0:T(8,128)(2,1)} %copy-done.4) | copy-start | bytes 9437188
  221.1 5.8 %copy-start.9 = (s32[4,1024,128]{2,1,0:T(8,128)S(1)}, s32[4,1024,128]{2,1,0:T(8,128)}, u32[]{:S(2)}) copy-start(s32[4,1024,128]{2,1,0:T(8,128)} %copy-done.8) | copy-start | bytes 6291460
  221.1 5.8 %copy-start.28 = (f32[1024,256]{1,0:T(8,128)S(1)}, f32[1024,256]{1,0:T(8,128)}, u32[]{:S(2)}) copy-start(f32[1024,256]{1,0:T(8,128)} %copy-done.27) | copy-start | bytes 3145732
  221.1 5.8 %copy-start.38 = (f32[1024,128]{1,0:T(8,128)S(1)}, f32[1024,128]{1,0:T(8,128)}, u32[]{:S(2)}) copy-start(f32[1024,128]{1,0:T(8,128)} %copy-done.37) | copy-start | bytes 1572868
  254.4 15.2 %collective-permute-start.6 = (bf16[16,64,768]{2,1,0:T(8,128)(2,1)}, bf16[16,64,768]{2,1,0:T(8,128)(2,1)}, u32[]{:S(2)}, u32[]{:S(2)}) collective-permute-start(bf16[16,64,768]{2,1,0:T(8,128)(2,1)} %slice_bitcast_fusion), channel_id=1, source_target_pairs={{0,4},{1,5},{2,6},{3,7},{4,0},{5,1},{6,2},{7,3},{8,12},{9,13},{10,... | collective-permute-start | bytes 4718600 | tf_op jit(solution)/shard_map/ppermute | solution.py:258
  274.0 34.7 %all-to-all-start.2 = ((bf16[16,64,256]{2,1,0:T(8,128)(2,1)}), bf16[16,64,256]{2,1,0:T(8,128)(2,1)}, u32[]{:S(2)}, u32[]{:S(2)}) async-start(bf16[16,64,256]{2,1,0:T(8,128)(2,1)} %broadcast_in_dim.31), calls=%async_computation.2 | async-start | bytes 1048576 | tf_op jit(solution)/shard_map/all_to_all | solution.py:281
  290.8 4.0 %copy-start.11 = (s32[4,1024,128]{2,1,0:T(8,128)S(1)}, s32[4,1024,128]{2,1,0:T(8,128)}, u32[]{:S(2)}) copy-start(s32[4,1024,128]{2,1,0:T(8,128)} %copy-done.8) | copy-start | bytes 6291460
  290.8 4.0 %copy-start.17 = (bf16[1024,256]{1,0:T(8,128)(2,1)S(1)}, bf16[1024,256]{1,0:T(8,128)(2,1)}, u32[]{:S(2)}) copy-start(bf16[1024,256]{1,0:T(8,128)(2,1)} %refs_2_.3) | copy-start | bytes 1572868
  290.8 4.0 %copy-start.32 = (f32[1024,256]{1,0:T(8,128)S(1)}, f32[1024,256]{1,0:T(8,128)}, u32[]{:S(2)}) copy-start(f32[1024,256]{1,0:T(8,128)} %copy-done.31) | copy-start | bytes 3145732
  290.8 4.0 %copy-start.44 = (f32[1024,128]{1,0:T(8,128)S(1)}, f32[1024,128]{1,0:T(8,128)}, u32[]{:S(2)}) copy-start(f32[1024,128]{1,0:T(8,128)} %copy-done.43) | copy-start | bytes 1572868
  290.8 11.9 %copy-start.15 = (s32[4,1024,128]{2,1,0:T(8,128)S(1)}, s32[4,1024,128]{2,1,0:T(8,128)}, u32[]{:S(2)}) copy-start(s32[4,1024,128]{2,1,0:T(8,128)} %copy-done.12) | copy-start | bytes 6291460
  294.8 7.9 %copy-start.3 = (bf16[4096,512]{1,0:T(8,128)(2,1)S(1)}, bf16[4096,512]{1,0:T(8,128)(2,1)}, u32[]{:S(2)}) copy-start(bf16[4096,512]{1,0:T(8,128)(2,1)} %all-gather.3.cloned.1.call-done.other_ref.x_ref) | copy-start | bytes 12582916
  294.8 7.9 %copy-start.7 = (bf16[4096,384]{1,0:T(8,128)(2,1)S(1)}, bf16[4096,384]{1,0:T(8,128)(2,1)}, u32[]{:S(2)}) copy-start(bf16[4096,384]{1,0:T(8,128)(2,1)} %copy-done.4) | copy-start | bytes 9437188
  308.7 3.8 %copy-start.20 = (bf16[1024,1024]{1,0:T(8,128)(2,1)S(1)}, bf16[1024,1024]{1,0:T(8,128)(2,1)}, u32[]{:S(2)}) copy-start(bf16[1024,1024]{1,0:T(8,128)(2,1)} %copy-done.19) | copy-start | bytes 6291460
  308.7 8.8 %collective-permute-start.7 = (bf16[1024,256]{1,0:T(8,128)(2,1)}, bf16[1024,256]{1,0:T(8,128)(2,1)S(1)}, u32[]{:S(2)}, u32[]{:S(2)}) collective-permute-start(bf16[1024,256]{1,0:T(8,128)(2,1)} %bitcast.33.y_ref), channel_id=1, source_target_pairs={{0,4},{1,5},{2,6},{3,7},{4,0},{5,1},{6,2},{7,3},{8,12},{9,13},{10,... | collective-permute-start | bytes 1572872 | tf_op jit(solution)/shard_map/ppermute | solution.py:258
  314.4 3.2 copy-start.18
  314.4 3.2 copy-start.26
  (30 other events, 40.3 us)
Sparse Core Ops, SparseCore 0:
  27.3 118.0 all-gather.2

commit v4 on v3

--- a/solution.py
+++ b/solution.py
@@ -16,34 +16,32 @@
 ALPHA = 0.8
 AXES = ("slab", "rep")
 ROW_TILE = 256
-VMEM_LIMIT = 16 << 20
+VMEM_LIMIT = 58 << 20
+SCALE = 1.4426950408889634 / TAU
 HALF = 32
 
 
-def join_kernel(flag_ref, x_ref, y_ref, cols_ref, all_ref, normed_ref, rest_ref):
+def join_kernel(flag_ref, x_ref, y_ref, cols_ref, all_ref):
     width, clust = x_ref.shape[1], y_ref.shape[1]
     values = x_ref[...].astype(jnp.float32)
     scale = lax.rsqrt(jnp.sum(values * values, axis=1, keepdims=True) + EPS)
     normed = (values * scale).astype(jnp.bfloat16)
     cols = cols_ref[...].reshape(K * TOPK, cols_ref.shape[2])
-    coded = jnp.concatenate([cols // HALF + HALF * flag_ref[0], cols % HALF], axis=0)
+    coded = jnp.concatenate([(cols >> 5) + HALF * flag_ref[0], cols & (HALF - 1)], axis=0)
     coded = coded.astype(jnp.float32).T.astype(jnp.bfloat16)
     all_ref[:, :width] = normed
     all_ref[:, width : width + clust] = y_ref[...]
     all_ref[:, width + clust :] = coded
-    normed_ref[...] = normed
-    rest_ref[:, :clust] = y_ref[...]
-    rest_ref[:, clust:] = coded
 
 
 def join(flag, embeddings, indicators, columns):
     rows, width = embeddings.shape
     clust = indicators.shape[1]
     by_row = lambda cols: pl.BlockSpec((ROW_TILE, cols), lambda r, flag: (r, 0))
-    wide = (width + clust + 2 * K * TOPK, width, clust + 2 * K * TOPK)
+    wide = width + clust + 2 * K * TOPK
     return pl.pallas_call(
         join_kernel,
-        out_shape=[jax.ShapeDtypeStruct((rows, w), jnp.bfloat16) for w in wide],
+        out_shape=jax.ShapeDtypeStruct((rows, wide), jnp.bfloat16),
         grid_spec=pltpu.PrefetchScalarGridSpec(
             num_scalar_prefetch=1,
             grid=(rows // ROW_TILE,),
@@ -52,7 +50,7 @@
                 by_row(clust),
                 pl.BlockSpec((K, TOPK, ROW_TILE), lambda r, flag: (0, 0, r)),
             ],
-            out_specs=[by_row(w) for w in wide],
+            out_specs=by_row(wide),
         ),
         compiler_params=pltpu.CompilerParams(vmem_limit_bytes=VMEM_LIMIT),
         name="join",
@@ -100,7 +98,7 @@
 def weights(cosine, word, total, put):
     for j in range(cosine.shape[1] // LANES):
         part = cosine[:, j * LANES : (j + 1) * LANES]
-        raw = jnp.where((word & (1 << j)) != 0, jnp.exp((part - 1.0) * (1.0 / TAU)), 0.0)
+        raw = jnp.where((word & (1 << j)) != 0, jnp.exp2(part * SCALE - SCALE), 0.0)
         total = total + raw
         put(slice(j * LANES, (j + 1) * LANES), raw.astype(jnp.bfloat16))
     return total
@@ -161,36 +159,104 @@
     )(pick, *args)
 
 
-def gather_kernel(has_acc, last, pick_ref, tile_ref, y_ref, *refs):
-    refs = list(refs)
-    acc_in = refs.pop(0) if has_acc else None
-    deg_ref, anchor_ref = (refs.pop(0), refs.pop(0)) if last else (None, None)
-    gathered = jnp.dot(tile_ref[...], flat(y_ref), preferred_element_type=jnp.float32)
-    if has_acc:
-        gathered = acc_in[...] + gathered
-    if last:
-        gathered = mix(gathered, jnp.sum(deg_ref[...], axis=1, keepdims=True), anchor_ref[...])
-    refs[0][...] = gathered
-
-
-def gather_of(pick, tile, y, acc, degree=None, anchor=None):
-    rows, clust = tile.shape[0], y[1][-1]
+def seven_kernel(
+    width, pick_ref, rows_ref, first_ref, second_ref, near_ref, far_ref, words_ref, member_ref, deg_in, acc_in, anchor_ref,
+    near_tile, far_tile, member_tile, deg_ref, new_ref, other_ref, held_ref,
+):
+    def put_to(ref):
+        def put(lanes, value):
+            ref[:, lanes] = value
+
+        return put
+
+    def run(rows, plan, total, acc):
+        for word, (other, y), tile in plan:
+            total = weights(cosines(rows, other), word, total, put_to(tile))
+            acc = acc + jnp.dot(tile[...], y, preferred_element_type=jnp.float32)
+        return total, acc
+
+    step = pl.program_id(0)
+    split = lambda block: (block[:, :width], block[:, width:])
+    first, second = split(first_ref[...]), split(second_ref[...])
+    near, far = split(near_ref[:, 0].reshape(-1, near_ref.shape[3])), split(flat(far_ref))
+    plan = (
+        (words_ref[1], first, member_tile),
+        (words_ref[pick_ref[0]], near, near_tile),
+        (words_ref[5 - pick_ref[0]], far, far_tile),
+    )
+    total, acc = run(rows_ref[...], plan, deg_in[...], acc_in[...])
+    deg_ref[...] = total
+    new_ref[...] = mix(acc, jnp.sum(total, axis=1, keepdims=True), anchor_ref[...])
+    here = pl.ds(pl.multiple_of(step * ROW_TILE, ROW_TILE), ROW_TILE)
+    mine = first_ref[here, :]
+    plan = (
+        (member_ref[0], first, held_ref),
+        (member_ref[1], second, held_ref),
+        (member_ref[pick_ref[3]], near, held_ref),
+        (member_ref[5 - pick_ref[3]], far, held_ref),
+    )
+    total, acc = run(mine[:, :width], plan, jnp.zeros(deg_in.shape, jnp.float32), jnp.zeros(acc_in.shape, jnp.float32))
+    other_ref[...] = mix(acc, jnp.sum(total, axis=1, keepdims=True), mine[:, width:])
+
+
+def seven_of(pick, joined, group, near, far, words, member_words, carry, anchor, width):
+    rows, clust = anchor.shape
+    chips, _, piece, full = near.shape
+    once = pl.Buffered(1)
     by_row = lambda cols: pl.BlockSpec((ROW_TILE, cols), lambda r, pick: (r, 0))
-    spec = lambda operand: pl.BlockSpec(operand[1], operand[2])
-    last = degree is not None
-    args = [tile, y[0]] + ([acc] if acc is not None else []) + ([degree, anchor[0]] if last else [])
-    specs = [by_row(rows), spec(y)] + ([by_row(clust)] if acc is not None else [])
-    specs += [by_row(LANES), spec(anchor)] if last else []
-    return pl.pallas_call(
-        functools.partial(gather_kernel, acc is not None, last),
-        out_shape=jax.ShapeDtypeStruct((rows, clust), jnp.bfloat16 if last else jnp.float32),
+    group_at = lambda k: pl.BlockSpec((rows, full), lambda r, pick: (pick[k], 0), pipeline_mode=once)
+    by_word = pl.BlockSpec((K, ROW_TILE, LANES), lambda r, pick: (0, r, 0))
+    outs = [(rows, jnp.bfloat16)] * 3 + [(LANES, jnp.float32)] + [(clust, jnp.bfloat16)] * 2
+    return pl.pallas_call(
+        functools.partial(seven_kernel, width),
+        out_shape=[jax.ShapeDtypeStruct((rows, cols), kind) for cols, kind in outs],
         grid_spec=pltpu.PrefetchScalarGridSpec(
-            num_scalar_prefetch=1, grid=(rows // ROW_TILE,), in_specs=specs, out_specs=by_row(clust)
-        ),
-        compiler_params=pltpu.CompilerParams(vmem_limit_bytes=VMEM_LIMIT),
-        cost_estimate=pl.CostEstimate(flops=2 * rows * rows * clust, bytes_accessed=3 * rows * rows, transcendentals=0),
-        name="gather",
-    )(pick, *args)
+            num_scalar_prefetch=1,
+            grid=(rows // ROW_TILE,),
+            in_specs=[
+                by_row(width),
+                group_at(1),
+                group_at(2),
+                pl.BlockSpec((chips, 1, piece, full), lambda r, pick: (0, 0, 0, 0), pipeline_mode=once),
+                pl.BlockSpec((chips, piece, full), lambda r, pick: (0, 0, 0), pipeline_mode=once),
+                by_word,
+                by_word,
+                by_row(LANES),
+                by_row(clust),
+                by_row(clust),
+            ],
+            out_specs=[by_row(cols) for cols, _ in outs],
+            scratch_shapes=[pltpu.VMEM((ROW_TILE, rows), jnp.bfloat16)],
+        ),
+        compiler_params=pltpu.CompilerParams(vmem_limit_bytes=VMEM_LIMIT),
+        cost_estimate=pl.CostEstimate(
+            flops=14 * rows * rows * full, bytes_accessed=16 * rows * rows, transcendentals=7 * rows * rows
+        ),
+        name="seven",
+    )(pick, joined, group, group, near, far, words, member_words, *carry, anchor)
+
+
+def last_kernel(*refs):
+    tiles, news, (deg_ref, anchor_ref, out_ref) = refs[:K], refs[K : 2 * K], refs[2 * K :]
+    acc = sum(jnp.dot(t[...], y[...], preferred_element_type=jnp.float32) for t, y in zip(tiles, news))
+    out_ref[...] = mix(acc, jnp.sum(deg_ref[...], axis=1, keepdims=True), anchor_ref[...])
+
+
+def last_of(tiles, news, degree, anchor):
+    rows, clust = anchor.shape
+    by_row = lambda cols: pl.BlockSpec((ROW_TILE, cols), lambda r: (r, 0))
+    return pl.pallas_call(
+        last_kernel,
+        out_shape=jax.ShapeDtypeStruct((rows, clust), jnp.bfloat16),
+        grid=(rows // ROW_TILE,),
+        in_specs=[by_row(rows)] * K
+        + [pl.BlockSpec((rows, clust), lambda r: (0, 0))] * K
+        + [by_row(LANES), by_row(clust)],
+        out_specs=by_row(clust),
+        compiler_params=pltpu.CompilerParams(vmem_limit_bytes=VMEM_LIMIT),
+        cost_estimate=pl.CostEstimate(flops=8 * rows * rows * clust, bytes_accessed=8 * rows * rows, transcendentals=0),
+        name="last",
+    )(*tiles, *news, degree, anchor)
 
 
 def hub_rows_kernel(width, pick_ref, rows_ref, near_ref, far_ref, out_ref, word_ref, tile_ref):
@@ -240,7 +306,7 @@
             out_specs=pl.BlockSpec((share, clust), lambda i, pick: (0, 0)),
             scratch_shapes=[pltpu.VMEM((K, share, LANES), jnp.int32), pltpu.VMEM((share, rows), jnp.bfloat16)],
         ),
-        compiler_params=pltpu.CompilerParams(vmem_limit_bytes=20 << 20),
+        compiler_params=pltpu.CompilerParams(vmem_limit_bytes=VMEM_LIMIT),
         cost_estimate=pl.CostEstimate(flops=share * rows * 6144, bytes_accessed=6 << 20, transcendentals=share * rows * K),
         name="hub_rows",
     )(self_slot, mine, near, far)
@@ -298,12 +364,19 @@
     held = jnp.stack(
         [lax.dynamic_index_in_dim(mine, member[h], 0, keepdims=False) for h in range(HUBS)], axis=0
     )
-    held = lax.all_gather(held, "rep", axis=0, tiled=False)
+    held = held[None]
+    rep = lax.axis_index("rep")
+    for bit in range(2):
+        got = along_line(held, {r: r ^ (1 << bit) for r in range(4)})
+        upper = (rep >> bit) & 1 == 1
+        held = jnp.concatenate([jnp.where(upper, got, held), jnp.where(upper, held, got)], axis=0)
     chosen = []
     for h in range(HUBS):
-        hub = lax.dynamic_index_in_dim(held[:, h], hub_rep[h], 0, keepdims=False)
-        want, _ = flags_of(hub[0, code_at])
-        chosen.append(jnp.stack([hub, lax.dynamic_index_in_dim(held[:, h], want, 0, keepdims=False)], axis=0))
+        pieces = held[:, h]
+        hub = lax.dynamic_index_in_dim(pieces, hub_rep[h], 0, keepdims=False)
+        want, _ = flags_of(hub[:1, code_at : code_at + 1])
+        wanted = jnp.where(want < 2, jnp.where(want == 0, pieces[0], pieces[1]), jnp.where(want == 2, pieces[2], pieces[3]))
+        chosen.append(jnp.stack([hub, wanted], axis=0))
     held = jnp.stack(chosen, axis=0)
     got = send(held, lambda half, chip, core, rep: (1 - half, chip, core, rep))
     away = lax.div(hub_slab, members) != lax.div(slab, members)
@@ -320,8 +393,6 @@
     full = width + clust
     reps = lax.axis_size("rep")
     total = lax.axis_size("slab") * reps
-    rep = lax.axis_index("rep")
-    steps = rows // ROW_TILE
     slots = neighbours[0].astype(jnp.int32)
     want = slots[1] & 3
     order = slots[2] - total
@@ -329,11 +400,8 @@
     near_slot = jnp.where(order == core, 2, 3)
     barrier = lax.optimization_barrier
 
-    joined, normed, rest = join((want + 4 * order)[None], embeddings, indicators, columns)
-    group_x = lax.all_gather(normed, "rep", axis=0, tiled=True)
-    across = along_line(rest, {0: 2, 2: 0, 1: 3, 3: 1})
-    beside = along_line(rest, {0: 1, 1: 0, 2: 3, 3: 2})
-    middle = along_line(rest, {1: 2, 2: 1})
+    joined = join((want + 4 * order)[None], embeddings, indicators, columns)
+    group = lax.all_gather(joined, "rep", axis=0, tiled=True)
 
     pick = jnp.stack([near_slot]).astype(jnp.int32)
     own_rows = (joined, (ROW_TILE, width), lambda r, pick: (r, 0))
@@ -344,60 +412,26 @@
     mine, words, carry, own_tile = barrier((scatter(joined), words, carry, own_tile))
 
     both = hub_pieces(mine, hub_ids, full)
-    outer = along_line(across, {1: 0, 2: 3})
-    third = jnp.where((rep == 0) | (rep == 3), outer, middle)
-    group_rest = jnp.concatenate([rest, beside, across, third], axis=0)
-    at = want ^ rep
+    near = join_pieces(both[:, :, :full])
+    far = swap_cores(near[:, 0])
+    _, hub_order = flags_of(both[0, 0, full])
+    share = hub_rows(jnp.where(hub_order == core, 2, 3).astype(jnp.int32)[None], both[0], near, far, width)
+    share, group = barrier((share, group))
+
+    near_new = join_pieces(share).reshape(rows, clust)
     member_want, member_order = flags_of(
-        lax.dynamic_index_in_dim(group_rest[:, clust], at * rows, 0, keepdims=False)
-    )
-    pick = jnp.stack(
-        [near_slot, want, member_want, jnp.where(member_order == core, 2, 3), at, member_want ^ rep]
-    ).astype(jnp.int32)
-    member_words = keep_words(pick, group_rest, lambda pick: (pick[4], clust // LANES), rows)
-    both, group_rest, member_words = barrier((both, group_rest, member_words))
-
-    member_rows = (group_x, (ROW_TILE, width), lambda r, pick: (pick[1] * steps + r, 0))
-    member_x = (group_x, (rows, width), lambda r, pick: (pick[1], 0))
-    second_x = (group_x, (rows, width), lambda r, pick: (pick[2], 0))
-    member_y = (group_rest, (rows, clust), lambda r, pick: (pick[4], 0))
-    second_y = (group_rest, (rows, clust), lambda r, pick: (pick[5], 0))
-    near = join_pieces(both[:, :, :full])
-    *carry, member_tile = tile_of(pick, own_rows, member_x, member_y, words, lambda pick: 1, carry)
-    carry_c = tile_of(pick, member_rows, member_x, member_y, member_words, lambda pick: 0, None, None, False)
-    carry_c = tile_of(pick, member_rows, second_x, second_y, member_words, lambda pick: 1, carry_c, None, False)
-    near, carry, carry_c = barrier((near, carry, carry_c))
-
-    chips, _, piece, _ = near.shape
-    near_x = (near, (chips, 1, piece, width), lambda r, pick: (0, 0, 0, 0))
-    near_y = (near, (chips, 1, piece, clust), lambda r, pick: (0, 0, 0, width // clust))
-    far = swap_cores(near[:, 0])
-    far_x = (far, (chips, piece, width), lambda r, pick: (0, 0, 0))
-    far_y = (far, (chips, piece, clust), lambda r, pick: (0, 0, width // clust))
-    *carry, near_tile = tile_of(pick, own_rows, near_x, near_y, words, lambda pick: pick[0], carry)
-    far, carry = barrier((far, carry))
-    far_x, far_y = (far, *far_x[1:]), (far, *far_y[1:])
-    _, hub_order = flags_of(both[0, 0, full])
-    share = hub_rows(jnp.where(hub_order == core, 2, 3)[None], both[0], near, far, width)
-
-    near_new = join_pieces(share).reshape(rows, clust)
-    by_row = (indicators, (ROW_TILE, clust), lambda r, pick: (r, 0))
-    member_anchor = (group_rest, (ROW_TILE, clust), lambda r, pick: (pick[4] * steps + r, 0))
-    carry_c = tile_of(
-        pick, member_rows, near_x, near_y, member_words, lambda pick: pick[3], carry_c, None, False
-    )
-    degree, new, far_tile = tile_of(pick, own_rows, far_x, far_y, words, lambda pick: 5 - pick[0], carry, by_row)
-    _, member_new = tile_of(
-        pick, member_rows, far_x, far_y, member_words, lambda pick: 5 - pick[3], carry_c, member_anchor, False
-    )
-    near_new, new, member_new = barrier((near_new, new, member_new))
+        lax.dynamic_index_in_dim(group[:, full], want * rows, 0, keepdims=False)
+    )
+    pick = jnp.stack([near_slot, want, member_want, jnp.where(member_order == core, 2, 3)]).astype(jnp.int32)
+    member_words = keep_words(pick, group, lambda pick: (pick[1], full // LANES), rows)
+    near_tile, far_tile, member_tile, degree, new, member_new = seven_of(
+        pick, joined, group, near, far, words, member_words, carry, indicators, width
+    )
+    near_new, new = barrier((near_new, new))
     far_new = swap_cores(near_new)
-
-    whole = lambda array: (array, array.shape, lambda r, pick: (0, 0))
-    acc = gather_of(pick, own_tile, whole(new), None)
-    acc = gather_of(pick, member_tile, whole(member_new), acc)
-    acc = gather_of(pick, near_tile, whole(near_new), acc)
-    return gather_of(pick, far_tile, whole(far_new), acc, degree, by_row)
+    return last_of(
+        (own_tile, member_tile, near_tile, far_tile), (new, member_new, near_new, far_new), degree, indicators
+    )
 
 
 def solution(mesh):

time: 330 us -> 229 us (0.69)
  waiting for transfers between devices: 113 us -> 66.5 us
  local copies, waits for them, and re-layouts: 44 us -> 8.81 us
  starting transfers between devices: 49.9 us -> 19.9 us
  blocking collectives: 22.3 us -> 44.8 us
  Pallas kernels: 67.4 us -> 59.2 us
    all_to_all x0 -> x1, blocking collectives: none -> 44.8 us  [join_pieces(): lax.all_to_all(repeated, 'slab', 0, 0, axis_index_groups=layers, tiled=True)]
    ppermute x8 -> x6, waiting for transfers between devices: 94.5 us -> 59.4 us  [send(): return lax.ppermute(block, AXES, pairs)]
    unnamed x100 -> x10, local copies, waits for them, and re-layouts: 35.2 us -> 0.8 us
    pallas_call x8 -> x1, Pallas kernels: 39 us -> 6.24 us  [tile_of(): pl.pallas_call(functools.partial(tile_kernel, carry is not None, last), o...]
    all_gather x1 -> x0, blocking collectives: 22.3 us -> none  [hub_pieces(): held = lax.all_gather(held, 'rep', axis=0, tiled=False)]
    pallas_call x5 -> x3, Pallas kernels: 12 us -> 31.2 us  [the longest x1 19.9 us: seven_of(): pl.pallas_call(functools.partial(seven_kernel, width), out_shape=[jax.Sha...]
    all_to_all x2 -> x1, waiting for transfers between devices: 18.2 us -> 0.01 us  [join_pieces(): lax.all_to_all(repeated, 'slab', 0, 0, axis_index_groups=layers, tiled=True)]
    all_to_all x2 -> x1, starting transfers between devices: 20.3 us -> 3.75 us  [join_pieces(): lax.all_to_all(repeated, 'slab', 0, 0, axis_index_groups=layers, tiled=True)]
  transfers between devices with their start and end apart: 12 -> 9, of which waited for: 3 -> 7; matrix products, arithmetic and copies ran while one was open for 3% -> 3% of each run, Pallas kernels for 18% -> 17%
where the time goes in v4:
time: 229 us; the launch traced here: 226 us
  waiting for transfers between devices  66.5 us (29%)
  Pallas kernels  59.2 us (26%)
  blocking collectives  44.8 us (20%)
  between operations  24.7 us (11%)
  starting transfers between devices  19.9 us (9%)
  local copies, waits for them, and re-layouts  8.81 us (4%)
    ppermute x6, waiting for transfers between devices, send(): return lax.ppermute(block, AXES, pairs)  59.4 us
    all_to_all x1, blocking collectives, join_pieces(): lax.all_to_all(repeated, 'slab', 0, 0, axis_index_groups=layers, tiled=True)  44.8 us
    pallas_call x1, Pallas kernels, seven_of(): pl.pallas_call(functools.partial(seven_kernel, width), out_shape=[jax.Sha...  19.9 us
    pallas_call x2, Pallas kernels, keep_words(): pl.pallas_call(words_kernel, out_shape=jax.ShapeDtypeStruct((K, rows, LAN...  16.6 us
    ppermute x6, starting transfers between devices, send(): return lax.ppermute(block, AXES, pairs)  8.38 us
    all_to_all x1, starting transfers between devices, scatter(): lax.all_to_all(block.reshape(members, rows // members, width), 'slab', 0,...  7.77 us
    pallas_call x1, Pallas kernels, last_of(): pl.pallas_call(last_kernel, out_shape=jax.ShapeDtypeStruct((rows, clust),...  7.22 us
    all_to_all x1, waiting for transfers between devices, scatter(): lax.all_to_all(block.reshape(members, rows // members, width), 'slab', 0,...  7.17 us
  transfers between devices with their start and end apart: 9, of which 7 were waited for; matrix products, arithmetic and copies ran while one was open for 3% of the time, Pallas kernels for 17%

profile of v4, /device:TPU:161, one launch (start us, length us, event | category | flops | bytes accessed | tf_op | source)
XLA Modules:
  0.0 226.2 jit_solution(4503703064315118621)
XLA Ops:
  6.5 1.3 fusion.12
  9.1 4.0 %join.1.coded_ref.x_ref.other_ref.y_ref.rows_ref = bf16[1024,896]{1,0:T(8,128)(2,1)} custom-call(s32[1]{0:T(128)} %bitcast.2.flag_ref, bf16[1024,512]{1,0:T(8,128)(2,1)} %x_ref.1, bf16[1024,256]{1,0:T(8,128)(2,1)} %refs_9_.1, s32[4,16,1024]{2,1,0:T(8,128)} %bitcast.57), custom_call_target="tpu_custom_call" | custom-call | tf_op jit(solution)/shard_map/join/pallas_call | solution.py:42
  13.2 7.8 %all-to-all-start = ((bf16[32,32,896]{2,1,0:T(8,128)(2,1)}), bf16[32,32,896]{2,1,0:T(8,128)(2,1)S(1)}, u32[]{:S(2)}, u32[]{:S(2)}) async-start(bf16[32,32,896]{2,1,0:T(8,128)(2,1)} %bitcast.54), calls=%async_computation | async-start | bytes 3670016 | tf_op jit(solution)/shard_map/all_to_all | solution.py:354
  21.0 0.6 fusion.11
  25.1 7.9 %keep_words.2.w_ref.words_ref = s32[4,1024,128]{2,1,0:T(8,128)} custom-call(s32[1]{0:T(128)} %bitcast.5.pick_ref, bf16[1024,896]{1,0:T(8,128)(2,1)} %join.1.coded_ref.x_ref.other_ref.y_ref.rows_ref), custom_call_target="tpu_custom_call" | custom-call | flops 8388608 | bytes 524288 | tf_op jit(solution)/shard_map/keep_words/pallas_call | solution.py:79
  33.0 6.2 %tile.1 = (f32[1024,128]{1,0:T(8,128)}, f32[1024,256]{1,0:T(8,128)}, bf16[1024,1024]{1,0:T(8,128)(2,1)}) custom-call(s32[1]{0:T(128)} %bitcast.5.pick_ref, bf16[1024,896]{1,0:T(8,128)(2,1)} %join.1.coded_ref.x_ref.other_ref.y_ref.rows_ref, bf16[1024,896]{1,0:T(8,128)(2,1)} %join.1.coded_ref.x_ref.other_ref.y_ref.rows_ref, ...), custom_call_target="tpu_custom_call" | custom-call | flops 1610612736 | bytes 4194304 | tf_op jit(solution)/shard_map/tile/pallas_call | solution.py:146
  39.3 7.2 %all-to-all-done = bf16[32,32,896]{2,1,0:T(8,128)(2,1)S(1)} async-done(((bf16[32,32,896]{2,1,0:T(8,128)(2,1)}), bf16[32,32,896]{2,1,0:T(8,128)(2,1)S(1)}, u32[]{:S(2)}, u32[]{:S(2)}) %all-to-all-start) | async-done | bytes 1835040 | tf_op jit(solution)/shard_map/all_to_all | solution.py:354
  46.5 0.8 collective-permute-start
  47.3 7.5 %collective-permute-done = bf16[1,2,32,896]{3,2,1,0:T(8,128)(2,1)S(1)} collective-permute-done((bf16[1,2,32,896]{3,2,1,0:T(8,128)(2,1)S(1)}, bf16[1,2,32,896]{3,2,1,0:T(8,128)(2,1)S(1)}, u32[]{:S(2)}, u32[]{:S(2)}) %collective-permute-start) | collective-permute-done | bytes 114720 | tf_op jit(solution)/shard_map/ppermute | solution.py:324
  54.9 3.2 %collective-permute-start.1 = (bf16[2,2,32,896]{3,2,1,0:T(8,128)(2,1)S(1)}, bf16[2,2,32,896]{3,2,1,0:T(8,128)(2,1)S(1)}, u32[]{:S(2)}, u32[]{:S(2)}) collective-permute-start(bf16[2,2,32,896]{3,2,1,0:T(8,128)(2,1)S(1)} %pad_maximum_fusion), channel_id=1, source_target_pairs={{0,2},{1,3},{2,0},{3,1},{4,6},{5,7},{6,4},{7,5},{8,10},{9,11},{10,... | collective-permute-start | bytes 688136 | tf_op jit(solution)/shard_map/ppermute | solution.py:324
  58.1 0.6 fusion.10
  62.2 19.5 %collective-permute-done.1 = bf16[2,2,32,896]{3,2,1,0:T(8,128)(2,1)S(1)} collective-permute-done((bf16[2,2,32,896]{3,2,1,0:T(8,128)(2,1)S(1)}, bf16[2,2,32,896]{3,2,1,0:T(8,128)(2,1)S(1)}, u32[]{:S(2)}, u32[]{:S(2)}) %collective-permute-start.1) | collective-permute-done | bytes 229408 | tf_op jit(solution)/shard_map/ppermute | solution.py:324
  81.9 0.5 slice.130
  84.6 28.4 %collective-permute-done.2 = bf16[2,2,32,896]{3,2,1,0:T(8,128)(2,1)S(1)} collective-permute-done((bf16[2,2,32,896]{3,2,1,0:T(8,128)(2,1)S(1)}, bf16[2,2,32,896]{3,2,1,0:T(8,128)(2,1)S(1)}, u32[]{:S(2)}, u32[]{:S(2)}) %collective-permute-start.2) | collective-permute-done | bytes 229408 | tf_op jit(solution)/shard_map/ppermute | solution.py:324
  113.1 1.8 collective-permute-start.3
  114.8 1.0 collective-permute-done.3
  116.2 44.8 %all_to_all.15.near_ref = bf16[16,2,64,768]{3,2,1,0:T(8,128)(2,1)S(1)} all-to-all(bf16[16,2,64,768]{3,2,1,0:T(8,128)(2,1)S(1)} %broadcast_in_dim.91), channel_id=1, replica_groups={{0,8,16,24,32,40,48,56,64,72,80,88,96,104,112,120},{4,12,20,28,36,44,52..., dimensions={0} | all-to-all | bytes 6291456 | tf_op jit(solution)/shard_map/all_to_all | solution.py:347
  161.0 1.4 slice_bitcast_fusion
  162.4 2.1 collective-permute-start.4
  164.5 0.6 slice.142
  165.8 0.6 fusion.1.rows_ref
  166.5 1.4 collective-permute-done.4.far_ref
  167.9 5.2 %hub_rows.1 = bf16[64,256]{1,0:T(8,128)(2,1)} custom-call(s32[1]{0:T(128)} %bitcast.29.pick_ref, bf16[64,896]{1,0:T(8,128)(2,1)} %fusion.1.rows_ref, bf16[16,2,64,768]{3,2,1,0:T(8,128)(2,1)} %copy-done, bf16[16,64,768]{2,1,0:T(8,128)(2,1)} %collective-permute-done.4.far_ref), custom_call_target="tpu_custom_call" | custom-call | flops 402653184 | bytes 6291456 | tf_op jit(solution)/shard_map/hub_rows/pallas_call | solution.py:295
  173.1 1.2 slice-done
  175.4 0.7 pad_add_fusion.pick_ref
  176.0 8.7 %keep_words.3.member_ref = s32[4,1024,128]{2,1,0:T(8,128)} custom-call(s32[4]{0:T(128)} %pad_add_fusion.pick_ref, bf16[4096,896]{1,0:T(8,128)(2,1)} %all-gather.2.cloned.1.call-done.coded_ref.first_ref.second_ref), custom_call_target="tpu_custom_call" | custom-call | flops 8388608 | bytes 524288 | tf_op jit(solution)/shard_map/keep_words/pallas_call | solution.py:79
  184.8 0.9 broadcast_in_dim.92
  185.7 3.8 %all-to-all-start.2 = ((bf16[16,64,256]{2,1,0:T(8,128)(2,1)}), bf16[16,64,256]{2,1,0:T(8,128)(2,1)S(1)}, u32[]{:S(2)}, u32[]{:S(2)}) async-start(bf16[16,64,256]{2,1,0:T(8,128)(2,1)} %broadcast_in_dim.92), calls=%async_computation.2 | async-start | bytes 1048576 | tf_op jit(solution)/shard_map/all_to_all | solution.py:347
  189.4 19.9 %seven.1 = (bf16[1024,1024]{1,0:T(8,128)(2,1)}, bf16[1024,1024]{1,0:T(8,128)(2,1)}, bf16[1024,1024]{1,0:T(8,128)(2,1)}, f32[1024,128]{1,0:T(8,128)}, bf16[1024,2...) custom-call(s32[4]{0:T(128)} %pad_add_fusion.pick_ref, bf16[1024,896]{1,0:T(8,128)(2,1)} %join.1.coded_ref.x_ref.other_ref.y_ref.rows_ref, ...), custom_call_target="tpu_custom_call" | custom-call | flops 11274289152 | bytes 16777216 | tf_op jit(solution)/shard_map/seven/pallas_call | solution.py:210
  209.8 1.5 collective-permute-done.5.refs_7_
  211.3 0.8 copy-done.2
  212.1 7.2 %last.1 = bf16[1024,256]{1,0:T(8,128)(2,1)} custom-call(bf16[1024,1024]{1,0:T(8,128)(2,1)} %get-tuple-element.26.refs_0_, bf16[1024,1024]{1,0:T(8,128)(2,1)} %get-tuple-element.32.refs_1_, bf16[1024,1024]{1,0:T(8,128)(2,1)} %get-tuple-element.33.refs_2_, bf16[1024,1024]{1,0:T(8,128)(2,1)} %get-tuple-element.34.refs_3_, ...), custom_call_target="tpu_custom_call" | custom-call | flops 2147483648 | bytes 8388608 | tf_op jit(solution)/shard_map/last/pallas_call | solution.py:248
  (38 shorter events, 2.5 us)
Async XLA Ops:
  6.5 166.5 %all-gather.2.cloned.1.call-start = ((), (), s32[]{:S(2)}) async-start(), calls=%async_computation.3 | async-start | bytes 9175040 | tf_op jit(solution)/shard_map/all_gather | solution.py:404
  13.2 7.8 %copy-start.4 = (s32[2]{0:T(128)S(1)}, s32[2]{0:T(128)}, u32[]{:S(2)}) copy-start(s32[2]{0:T(128)} %param.8) | copy-start | bytes 28
  13.2 33.3 %all-to-all-start = ((bf16[32,32,896]{2,1,0:T(8,128)(2,1)}), bf16[32,32,896]{2,1,0:T(8,128)(2,1)S(1)}, u32[]{:S(2)}, u32[]{:S(2)}) async-start(bf16[32,32,896]{2,1,0:T(8,128)(2,1)} %bitcast.54), calls=%async_computation | async-start | bytes 3670016 | tf_op jit(solution)/shard_map/all_to_all | solution.py:354
  46.5 8.4 %collective-permute-start = (bf16[1,2,32,896]{3,2,1,0:T(8,128)(2,1)S(1)}, bf16[1,2,32,896]{3,2,1,0:T(8,128)(2,1)S(1)}, u32[]{:S(2)}, u32[]{:S(2)}) collective-permute-start(bf16[1,2,32,896]{3,2,1,0:T(8,128)(2,1)S(1)} %maximum_bitcast_fusion), channel_id=1, source_target_pairs={{0,1},{1,0},{2,3},{3,2},{4,5},{5,4},{6,7},{7,6},{8,9},{9,8},{10,11... | collective-permute-start | bytes 344072 | tf_op jit(solution)/shard_map/ppermute | solution.py:324
  54.9 26.8 %collective-permute-start.1 = (bf16[2,2,32,896]{3,2,1,0:T(8,128)(2,1)S(1)}, bf16[2,2,32,896]{3,2,1,0:T(8,128)(2,1)S(1)}, u32[]{:S(2)}, u32[]{:S(2)}) collective-permute-start(bf16[2,2,32,896]{3,2,1,0:T(8,128)(2,1)S(1)} %pad_maximum_fusion), channel_id=1, source_target_pairs={{0,2},{1,3},{2,0},{3,1},{4,6},{5,7},{6,4},{7,5},{8,10},{9,11},{10,... | collective-permute-start | bytes 688136 | tf_op jit(solution)/shard_map/ppermute | solution.py:324
  84.5 28.5 %collective-permute-start.2 = (bf16[2,2,32,896]{3,2,1,0:T(8,128)(2,1)S(1)}, bf16[2,2,32,896]{3,2,1,0:T(8,128)(2,1)S(1)}, u32[]{:S(2)}, u32[]{:S(2)}) collective-permute-start(bf16[2,2,32,896]{3,2,1,0:T(8,128)(2,1)S(1)} %pad_maximum_fusion.1), channel_id=1, source_target_pairs={{0,128},{1,129},{2,130},{3,131},{4,132},{5,133},{6,134},{7,135},{8... | collective-permute-start | bytes 688136 | tf_op jit(solution)/shard_map/ppermute | solution.py:324
  113.1 2.7 %collective-permute-start.3 = (bf16[2,32,896]{2,1,0:T(8,128)(2,1)S(1)}, bf16[2,32,896]{2,1,0:T(8,128)(2,1)S(1)}, u32[]{:S(2)}, u32[]{:S(2)}) collective-permute-start(bf16[2,32,896]{2,1,0:T(8,128)(2,1)S(1)} %select_bitcast_fusion), channel_id=1, source_target_pairs={{0,4},{1,5},{2,6},{3,7},{4,0},{5,1},{6,2},{7,3},{8,12},{9,13},{10,... | collective-permute-start | bytes 344072 | tf_op jit(solution)/shard_map/ppermute | solution.py:324
  161.0 6.8 %copy-start = (bf16[16,2,64,768]{3,2,1,0:T(8,128)(2,1)}, bf16[16,2,64,768]{3,2,1,0:T(8,128)(2,1)S(1)}, u32[]{:S(2)}) copy-start(bf16[16,2,64,768]{3,2,1,0:T(8,128)(2,1)S(1)} %all_to_all.15.near_ref) | copy-start | bytes 9437188
  162.4 5.5 %collective-permute-start.4 = (bf16[16,64,768]{2,1,0:T(8,128)(2,1)}, bf16[16,64,768]{2,1,0:T(8,128)(2,1)}, u32[]{:S(2)}, u32[]{:S(2)}) collective-permute-start(bf16[16,64,768]{2,1,0:T(8,128)(2,1)} %slice_bitcast_fusion), channel_id=1, source_target_pairs={{0,4},{1,5},{2,6},{3,7},{4,0},{5,1},{6,2},{7,3},{8,12},{9,13},{10,... | collective-permute-start | bytes 4718600 | tf_op jit(solution)/shard_map/ppermute | solution.py:324
  173.1 1.2 slice-start
  176.0 8.7 %copy-start.3 = (bf16[64,256]{1,0:T(8,128)(2,1)S(1)}, bf16[64,256]{1,0:T(8,128)(2,1)}, u32[]{:S(2)}) copy-start(bf16[64,256]{1,0:T(8,128)(2,1)} %hub_rows.1) | copy-start | bytes 98308
  185.7 23.6 %all-to-all-start.2 = ((bf16[16,64,256]{2,1,0:T(8,128)(2,1)}), bf16[16,64,256]{2,1,0:T(8,128)(2,1)S(1)}, u32[]{:S(2)}, u32[]{:S(2)}) async-start(bf16[16,64,256]{2,1,0:T(8,128)(2,1)} %broadcast_in_dim.92), calls=%async_computation.2 | async-start | bytes 1048576 | tf_op jit(solution)/shard_map/all_to_all | solution.py:347
  209.3 2.0 copy-start.1
  209.3 2.0 collective-permute-start.5
  211.3 0.8 copy-start.2
Sparse Core Ops, SparseCore 0:
  13.3 154.9 all-gather.1

commit v5 on v4

--- a/solution.py
+++ b/solution.py
@@ -19,38 +19,52 @@
 VMEM_LIMIT = 58 << 20
 SCALE = 1.4426950408889634 / TAU
 HALF = 32
-
-
-def join_kernel(flag_ref, x_ref, y_ref, cols_ref, all_ref):
+FLAG_ROWS = 16
+BLOCKS_NEAR = 5
+
+
+def join_kernel(flag_ref, x_ref, y_ref, cols_ref, all_ref, normed_ref, rest_ref):
     width, clust = x_ref.shape[1], y_ref.shape[1]
+    step = pl.program_id(0)
+    rows = pl.num_programs(0) * ROW_TILE
     values = x_ref[...].astype(jnp.float32)
     scale = lax.rsqrt(jnp.sum(values * values, axis=1, keepdims=True) + EPS)
     normed = (values * scale).astype(jnp.bfloat16)
     cols = cols_ref[...].reshape(K * TOPK, cols_ref.shape[2])
     coded = jnp.concatenate([(cols >> 5) + HALF * flag_ref[0], cols & (HALF - 1)], axis=0)
-    coded = coded.astype(jnp.float32).T.astype(jnp.bfloat16)
     all_ref[:, :width] = normed
     all_ref[:, width : width + clust] = y_ref[...]
-    all_ref[:, width + clust :] = coded
+    all_ref[:, width + clust :] = coded.astype(jnp.float32).T.astype(jnp.bfloat16)
+    normed_ref[...] = normed
+    rest_ref[pl.ds(pl.multiple_of(step * ROW_TILE, ROW_TILE), ROW_TILE), :] = y_ref[...]
+    single = jnp.left_shift((cols & (LANES - 1)) + LANES, cols >> 7)
+    place = pl.multiple_of(rows + step * K * TOPK, K * TOPK)
+    rest_ref[pl.ds(place, K * TOPK), :] = single.astype(jnp.float32).astype(jnp.bfloat16)
+    flags = jnp.full((FLAG_ROWS, clust), flag_ref[0], jnp.int32)
+    rest_ref[rows + rows // ROW_TILE * K * TOPK :, :] = flags.astype(jnp.float32).astype(jnp.bfloat16)
 
 
 def join(flag, embeddings, indicators, columns):
     rows, width = embeddings.shape
     clust = indicators.shape[1]
     by_row = lambda cols: pl.BlockSpec((ROW_TILE, cols), lambda r, flag: (r, 0))
-    wide = width + clust + 2 * K * TOPK
+    steps = rows // ROW_TILE
+    rest = (rows + steps * K * TOPK + FLAG_ROWS, clust)
     return pl.pallas_call(
         join_kernel,
-        out_shape=jax.ShapeDtypeStruct((rows, wide), jnp.bfloat16),
+        out_shape=[
+            jax.ShapeDtypeStruct(shape, jnp.bfloat16)
+            for shape in ((rows, width + clust + 2 * K * TOPK), (rows, width), rest)
+        ],
         grid_spec=pltpu.PrefetchScalarGridSpec(
             num_scalar_prefetch=1,
-            grid=(rows // ROW_TILE,),
+            grid=(steps,),
             in_specs=[
                 by_row(width),
                 by_row(clust),
                 pl.BlockSpec((K, TOPK, ROW_TILE), lambda r, flag: (0, 0, r)),
             ],
-            out_specs=by_row(wide),
+            out_specs=[by_row(width + clust + 2 * K * TOPK), by_row(width), pl.BlockSpec(rest, lambda r, flag: (0, 0))],
         ),
         compiler_params=pltpu.CompilerParams(vmem_limit_bytes=VMEM_LIMIT),
         name="join",
@@ -58,37 +72,38 @@
 
 
 def words_kernel(pick_ref, coded_ref, out_ref):
-    half = K * TOPK
     lane = lax.broadcasted_iota(jnp.int32, (LANES, LANES), 0)
-
-    @pl.loop(0, coded_ref.shape[0] // LANES)
-    def _(block):
-        here = pl.ds(pl.multiple_of(block * LANES, LANES), LANES)
-        coded = coded_ref[here, :].astype(jnp.float32).T.astype(jnp.int32)
-        high = coded[:half] & (HALF - 1)
-        low = (high & 3) * HALF + coded[half:]
-        bit = jnp.left_shift(jnp.ones_like(high), high >> 2)
-        for slot in range(K):
-            word = jnp.zeros((LANES, LANES), jnp.int32)
-            for t in range(slot * TOPK, (slot + 1) * TOPK):
-                word = word | jnp.where(lane == low[t : t + 1], bit[t : t + 1], 0)
-            out_ref[slot, here, :] = word.T
-
-
-def keep_words(pick, coded, place, rows):
+    for step in range(coded_ref.shape[1] // (K * TOPK)):
+        coded = coded_ref[0, step * K * TOPK : (step + 1) * K * TOPK].astype(jnp.float32).astype(jnp.int32)
+        high = sum((coded >= LANES << m).astype(jnp.int32) for m in range(1, 8))
+        low = jnp.right_shift(coded, high) & (LANES - 1)
+        bit = jnp.left_shift(jnp.ones_like(high), high)
+        for part in range(ROW_TILE // LANES):
+            here = slice(part * LANES, (part + 1) * LANES)
+            for slot in range(K):
+                word = jnp.zeros((LANES, LANES), jnp.int32)
+                for t in range(slot * TOPK, (slot + 1) * TOPK):
+                    word = word | jnp.where(lane == low[t : t + 1, here], bit[t : t + 1, here], 0)
+                start = step * ROW_TILE + part * LANES
+                out_ref[slot, start : start + LANES, :] = word.T
+
+
+def keep_words(pick, rest, which, rows):
+    part = rows // ROW_TILE * K * TOPK
+    clust = rest.shape[2]
     return pl.pallas_call(
         words_kernel,
         out_shape=jax.ShapeDtypeStruct((K, rows, LANES), jnp.int32),
         grid_spec=pltpu.PrefetchScalarGridSpec(
             num_scalar_prefetch=1,
             grid=(1,),
-            in_specs=[pl.BlockSpec((rows, LANES), lambda i, pick: place(pick))],
+            in_specs=[pl.BlockSpec((1, part, clust), lambda i, pick: (which(pick), rows // part, 0))],
             out_specs=pl.BlockSpec((K, rows, LANES), lambda i, pick: (0, 0, 0)),
         ),
         compiler_params=pltpu.CompilerParams(vmem_limit_bytes=VMEM_LIMIT),
         cost_estimate=pl.CostEstimate(flops=rows * LANES * K * TOPK, bytes_accessed=rows * 512, transcendentals=0),
         name="keep_words",
-    )(pick, coded)
+    )(pick, rest)
 
 
 def mix(acc, degree, anchor):
@@ -154,109 +169,125 @@
             scratch_shapes=[] if keep else [pltpu.VMEM((ROW_TILE, rows), jnp.bfloat16)],
         ),
         compiler_params=pltpu.CompilerParams(vmem_limit_bytes=VMEM_LIMIT),
-        cost_estimate=pl.CostEstimate(flops=2 * rows * rows * 768, bytes_accessed=4 * rows * rows, transcendentals=rows * rows),
+        cost_estimate=pl.CostEstimate(flops=rows * clust, bytes_accessed=rows * clust, transcendentals=0),
         name="tile",
     )(pick, *args)
 
 
-def seven_kernel(
-    width, pick_ref, rows_ref, first_ref, second_ref, near_ref, far_ref, words_ref, member_ref, deg_in, acc_in, anchor_ref,
-    near_tile, far_tile, member_tile, deg_ref, new_ref, other_ref, held_ref,
-):
+def member_kernel(width, pick_ref, *refs):
+    blocks, refs = refs[:BLOCKS_NEAR], refs[BLOCKS_NEAR:]
+    (rows_ref, rest1_ref, rest2_ref, near_ref, far_ref, w_ref, words_ref, deg_in, acc_in, anchor_ref) = refs[:10]
+    tile_ref, deg_ref, new_ref, other_ref, x1_ref, x2_ref, held_ref, sems = refs[10:]
+    step = pl.program_id(0)
+
+    @pl.when(step == 0)
+    def _():
+        for which, target in enumerate((x1_ref, x2_ref)):
+            for i, block in enumerate(blocks):
+
+                @pl.when(pick_ref[1 + which] == i)
+                def _():
+                    copy = pltpu.make_async_copy(block, target, sems.at[which])
+                    copy.start()
+                    copy.wait()
+
     def put_to(ref):
         def put(lanes, value):
             ref[:, lanes] = value
 
         return put
 
-    def run(rows, plan, total, acc):
-        for word, (other, y), tile in plan:
-            total = weights(cosines(rows, other), word, total, put_to(tile))
-            acc = acc + jnp.dot(tile[...], y, preferred_element_type=jnp.float32)
-        return total, acc
-
-    step = pl.program_id(0)
-    split = lambda block: (block[:, :width], block[:, width:])
-    first, second = split(first_ref[...]), split(second_ref[...])
-    near, far = split(near_ref[:, 0].reshape(-1, near_ref.shape[3])), split(flat(far_ref))
-    plan = (
-        (words_ref[1], first, member_tile),
-        (words_ref[pick_ref[0]], near, near_tile),
-        (words_ref[5 - pick_ref[0]], far, far_tile),
-    )
-    total, acc = run(rows_ref[...], plan, deg_in[...], acc_in[...])
+    total = weights(cosines(rows_ref[...], x1_ref[...]), w_ref[0], deg_in[...], put_to(tile_ref))
     deg_ref[...] = total
-    new_ref[...] = mix(acc, jnp.sum(total, axis=1, keepdims=True), anchor_ref[...])
+    gathered = acc_in[...] + jnp.dot(tile_ref[...], rest1_ref[0], preferred_element_type=jnp.float32)
+    new_ref[...] = mix(gathered, jnp.sum(total, axis=1, keepdims=True), anchor_ref[...])
+
     here = pl.ds(pl.multiple_of(step * ROW_TILE, ROW_TILE), ROW_TILE)
-    mine = first_ref[here, :]
-    plan = (
-        (member_ref[0], first, held_ref),
-        (member_ref[1], second, held_ref),
-        (member_ref[pick_ref[3]], near, held_ref),
-        (member_ref[5 - pick_ref[3]], far, held_ref),
-    )
-    total, acc = run(mine[:, :width], plan, jnp.zeros(deg_in.shape, jnp.float32), jnp.zeros(acc_in.shape, jnp.float32))
-    other_ref[...] = mix(acc, jnp.sum(total, axis=1, keepdims=True), mine[:, width:])
-
-
-def seven_of(pick, joined, group, near, far, words, member_words, carry, anchor, width):
-    rows, clust = anchor.shape
+    x = x1_ref[here, :]
+    near, far = near_ref[:, 0].reshape(-1, near_ref.shape[3]), flat(far_ref)
+    total = jnp.zeros(deg_in.shape, jnp.float32)
+    acc = jnp.zeros(acc_in.shape, jnp.float32)
+    slots = (0, 1, pick_ref[3], 5 - pick_ref[3])
+    others = ((x1_ref[...], rest1_ref[0]), (x2_ref[...], rest2_ref[0]))
+    others += tuple((block[:, :width], block[:, width:]) for block in (near, far))
+    for slot, (other, y) in zip(slots, others):
+        total = weights(cosines(x, other), words_ref[slot], total, put_to(held_ref))
+        acc = acc + jnp.dot(held_ref[...], y, preferred_element_type=jnp.float32)
+    anchor = rest1_ref[0, here, :]
+    other_ref[...] = mix(acc, jnp.sum(total, axis=1, keepdims=True), anchor)
+
+
+def member_of(pick, blocks, own_rows, rest, near, far, words, member_words, carry, anchor):
+    rows, width = blocks[0].shape
+    clust = rest.shape[2]
     chips, _, piece, full = near.shape
     once = pl.Buffered(1)
     by_row = lambda cols: pl.BlockSpec((ROW_TILE, cols), lambda r, pick: (r, 0))
-    group_at = lambda k: pl.BlockSpec((rows, full), lambda r, pick: (pick[k], 0), pipeline_mode=once)
-    by_word = pl.BlockSpec((K, ROW_TILE, LANES), lambda r, pick: (0, r, 0))
-    outs = [(rows, jnp.bfloat16)] * 3 + [(LANES, jnp.float32)] + [(clust, jnp.bfloat16)] * 2
+    rest_at = lambda k: pl.BlockSpec((1, rows, clust), lambda r, pick: (pick[k], 0, 0), pipeline_mode=once)
     return pl.pallas_call(
-        functools.partial(seven_kernel, width),
-        out_shape=[jax.ShapeDtypeStruct((rows, cols), kind) for cols, kind in outs],
+        functools.partial(member_kernel, width),
+        out_shape=[
+            jax.ShapeDtypeStruct((rows, rows), jnp.bfloat16),
+            jax.ShapeDtypeStruct((rows, LANES), jnp.float32),
+            jax.ShapeDtypeStruct((rows, clust), jnp.bfloat16),
+            jax.ShapeDtypeStruct((rows, clust), jnp.bfloat16),
+        ],
         grid_spec=pltpu.PrefetchScalarGridSpec(
             num_scalar_prefetch=1,
             grid=(rows // ROW_TILE,),
-            in_specs=[
+            in_specs=[pl.BlockSpec(memory_space=pl.ANY)] * len(blocks)
+            + [
                 by_row(width),
-                group_at(1),
-                group_at(2),
+                rest_at(4),
+                rest_at(5),
                 pl.BlockSpec((chips, 1, piece, full), lambda r, pick: (0, 0, 0, 0), pipeline_mode=once),
                 pl.BlockSpec((chips, piece, full), lambda r, pick: (0, 0, 0), pipeline_mode=once),
-                by_word,
-                by_word,
+                pl.BlockSpec((1, ROW_TILE, LANES), lambda r, pick: (1, r, 0)),
+                pl.BlockSpec((K, ROW_TILE, LANES), lambda r, pick: (0, r, 0)),
                 by_row(LANES),
                 by_row(clust),
                 by_row(clust),
             ],
-            out_specs=[by_row(cols) for cols, _ in outs],
-            scratch_shapes=[pltpu.VMEM((ROW_TILE, rows), jnp.bfloat16)],
+            out_specs=[by_row(rows), by_row(LANES), by_row(clust), by_row(clust)],
+            scratch_shapes=[
+                pltpu.VMEM((rows, width), jnp.bfloat16),
+                pltpu.VMEM((rows, width), jnp.bfloat16),
+                pltpu.VMEM((ROW_TILE, rows), jnp.bfloat16),
+                pltpu.SemaphoreType.DMA((2,)),
+            ],
         ),
         compiler_params=pltpu.CompilerParams(vmem_limit_bytes=VMEM_LIMIT),
         cost_estimate=pl.CostEstimate(
-            flops=14 * rows * rows * full, bytes_accessed=16 * rows * rows, transcendentals=7 * rows * rows
-        ),
-        name="seven",
-    )(pick, joined, group, group, near, far, words, member_words, *carry, anchor)
-
-
-def last_kernel(*refs):
-    tiles, news, (deg_ref, anchor_ref, out_ref) = refs[:K], refs[K : 2 * K], refs[2 * K :]
-    acc = sum(jnp.dot(t[...], y[...], preferred_element_type=jnp.float32) for t, y in zip(tiles, news))
-    out_ref[...] = mix(acc, jnp.sum(deg_ref[...], axis=1, keepdims=True), anchor_ref[...])
-
-
-def last_of(tiles, news, degree, anchor):
-    rows, clust = anchor.shape
+            flops=10 * rows * rows * 768, bytes_accessed=8 * rows * rows, transcendentals=5 * rows * rows
+        ),
+        name="member",
+    )(pick, *blocks, own_rows, rest, rest, near, far, words, member_words, *carry, anchor)
+
+
+def pair_kernel(last, first_ref, second_ref, y1_ref, y2_ref, *refs):
+    acc = jnp.dot(first_ref[...], y1_ref[...], preferred_element_type=jnp.float32)
+    acc = acc + jnp.dot(second_ref[...], y2_ref[...], preferred_element_type=jnp.float32)
+    if last:
+        acc_in, deg_ref, anchor_ref = refs[:3]
+        acc = mix(acc + acc_in[...], jnp.sum(deg_ref[...], axis=1, keepdims=True), anchor_ref[...])
+    refs[-1][...] = acc
+
+
+def pair_of(tiles, news, finish=None):
+    rows, clust = news[0].shape
     by_row = lambda cols: pl.BlockSpec((ROW_TILE, cols), lambda r: (r, 0))
     return pl.pallas_call(
-        last_kernel,
-        out_shape=jax.ShapeDtypeStruct((rows, clust), jnp.bfloat16),
+        functools.partial(pair_kernel, finish is not None),
+        out_shape=jax.ShapeDtypeStruct((rows, clust), jnp.bfloat16 if finish else jnp.float32),
         grid=(rows // ROW_TILE,),
-        in_specs=[by_row(rows)] * K
-        + [pl.BlockSpec((rows, clust), lambda r: (0, 0))] * K
-        + [by_row(LANES), by_row(clust)],
+        in_specs=[by_row(rows)] * 2
+        + [pl.BlockSpec((rows, clust), lambda r: (0, 0))] * 2
+        + ([by_row(clust), by_row(LANES), by_row(clust)] if finish else []),
         out_specs=by_row(clust),
         compiler_params=pltpu.CompilerParams(vmem_limit_bytes=VMEM_LIMIT),
-        cost_estimate=pl.CostEstimate(flops=8 * rows * rows * clust, bytes_accessed=8 * rows * rows, transcendentals=0),
-        name="last",
-    )(*tiles, *news, degree, anchor)
+        cost_estimate=pl.CostEstimate(flops=rows * clust, bytes_accessed=rows * clust, transcendentals=0),
+        name="pair",
+    )(*tiles, *news, *(finish or ()))
 
 
 def hub_rows_kernel(width, pick_ref, rows_ref, near_ref, far_ref, out_ref, word_ref, tile_ref):
@@ -307,7 +338,7 @@
             scratch_shapes=[pltpu.VMEM((K, share, LANES), jnp.int32), pltpu.VMEM((share, rows), jnp.bfloat16)],
         ),
         compiler_params=pltpu.CompilerParams(vmem_limit_bytes=VMEM_LIMIT),
-        cost_estimate=pl.CostEstimate(flops=share * rows * 6144, bytes_accessed=6 << 20, transcendentals=share * rows * K),
+        cost_estimate=pl.CostEstimate(flops=rows, bytes_accessed=rows, transcendentals=0),
         name="hub_rows",
     )(self_slot, mine, near, far)
 
@@ -347,6 +378,16 @@
     return lax.all_to_all(repeated, "slab", 0, 0, axis_index_groups=layers, tiled=True)
 
 
+OUTWARD = {1: 0, 2: 3}
+MIDDLE = {1: 2, 2: 1}
+
+
+def spread_line(block):
+    across = along_line(block, {0: 2, 2: 0, 1: 3, 3: 1})
+    beside = along_line(block, {0: 1, 1: 0, 2: 3, 3: 2})
+    return across, beside
+
+
 def scatter(block):
     members = lax.axis_size("slab") // 2
     rows, width = block.shape
@@ -364,23 +405,23 @@
     held = jnp.stack(
         [lax.dynamic_index_in_dim(mine, member[h], 0, keepdims=False) for h in range(HUBS)], axis=0
     )
-    held = held[None]
+    got = send(held, lambda half, chip, core, rep: (1 - half, chip, core, rep))
+    away = lax.div(hub_slab, members) != lax.div(slab, members)
+    held = jnp.where(away[:, None, None], got, held)[None]
     rep = lax.axis_index("rep")
     for bit in range(2):
         got = along_line(held, {r: r ^ (1 << bit) for r in range(4)})
         upper = (rep >> bit) & 1 == 1
         held = jnp.concatenate([jnp.where(upper, got, held), jnp.where(upper, held, got)], axis=0)
+    pick = lambda pieces, at: jnp.where(
+        at < 2, jnp.where(at == 0, pieces[0], pieces[1]), jnp.where(at == 2, pieces[2], pieces[3])
+    )
     chosen = []
     for h in range(HUBS):
-        pieces = held[:, h]
-        hub = lax.dynamic_index_in_dim(pieces, hub_rep[h], 0, keepdims=False)
+        hub = pick(held[:, h], hub_rep[h])
         want, _ = flags_of(hub[:1, code_at : code_at + 1])
-        wanted = jnp.where(want < 2, jnp.where(want == 0, pieces[0], pieces[1]), jnp.where(want == 2, pieces[2], pieces[3]))
-        chosen.append(jnp.stack([hub, wanted], axis=0))
+        chosen.append(jnp.stack([hub, pick(held[:, h], want)], axis=0))
     held = jnp.stack(chosen, axis=0)
-    got = send(held, lambda half, chip, core, rep: (1 - half, chip, core, rep))
-    away = lax.div(hub_slab, members) != lax.div(slab, members)
-    held = jnp.where(away[:, None, None, None], got, held)
     first_core = lax.rem(slab, 2) == 0
     keep = jnp.where(first_core, held[0], held[1])
     got = swap_cores(jnp.where(first_core, held[1], held[0]))
@@ -393,6 +434,8 @@
     full = width + clust
     reps = lax.axis_size("rep")
     total = lax.axis_size("slab") * reps
+    rep = lax.axis_index("rep")
+    steps = rows // ROW_TILE
     slots = neighbours[0].astype(jnp.int32)
     want = slots[1] & 3
     order = slots[2] - total
@@ -400,38 +443,63 @@
     near_slot = jnp.where(order == core, 2, 3)
     barrier = lax.optimization_barrier
 
-    joined = join((want + 4 * order)[None], embeddings, indicators, columns)
-    group = lax.all_gather(joined, "rep", axis=0, tiled=True)
+    joined, normed, rest = join((want + 4 * order)[None], embeddings, indicators, columns)
+    across, beside = spread_line(rest)
 
     pick = jnp.stack([near_slot]).astype(jnp.int32)
     own_rows = (joined, (ROW_TILE, width), lambda r, pick: (r, 0))
     own_x = (joined, (rows, width), lambda r, pick: (0, 0))
     own_y = (joined, (rows, clust), lambda r, pick: (0, width // clust))
-    words = keep_words(pick, joined, lambda pick: (0, full // LANES), rows)
+    words = keep_words(pick, rest[None], lambda pick: 0, rows)
     *carry, own_tile = tile_of(pick, own_rows, own_x, own_y, words, lambda pick: 0)
-    mine, words, carry, own_tile = barrier((scatter(joined), words, carry, own_tile))
+    mine, words, carry, own_tile, rest, across, beside = barrier(
+        (scatter(joined), words, carry, own_tile, rest, across, beside)
+    )
 
     both = hub_pieces(mine, hub_ids, full)
+    both, normed, rest, across = barrier((both, normed, rest, across))
+
+    outer, middle = along_line(across, OUTWARD), along_line(rest, MIDDLE)
+    across_x, beside_x = spread_line(normed)
     near = join_pieces(both[:, :, :full])
+    at_end = (rep == 0) | (rep == 3)
+    group_rest = jnp.stack([rest, beside, across, jnp.where(at_end, outer, middle)], axis=0)
+    at = want ^ rep
+    flag = lax.dynamic_index_in_dim(group_rest[:, -1, 0], at, 0, keepdims=False).astype(jnp.int32)
+    member_want, member_order = flag & 3, (flag >> 2) & 1
+    second = member_want ^ rep
+    place = lambda k: jnp.where((k == 3) & at_end, 4, k)
+    pick = jnp.stack(
+        [near_slot, place(at), place(second), jnp.where(member_order == core, 2, 3), at, second]
+    ).astype(jnp.int32)
+    member_words = keep_words(pick, group_rest, lambda pick: pick[4], rows)
+    near, normed, across_x, beside_x, group_rest, member_words = barrier(
+        (near, normed, across_x, beside_x, group_rest, member_words)
+    )
+
+    outer_x, middle_x = along_line(across_x, OUTWARD), along_line(normed, MIDDLE)
+    chips, _, piece, _ = near.shape
+    near_x = (near, (chips, 1, piece, width), lambda r, pick: (0, 0, 0, 0))
+    near_y = (near, (chips, 1, piece, clust), lambda r, pick: (0, 0, 0, width // clust))
     far = swap_cores(near[:, 0])
+    *carry, near_tile = tile_of(pick, own_rows, near_x, near_y, words, lambda pick: pick[0], carry)
+    far, carry = barrier((far, carry))
     _, hub_order = flags_of(both[0, 0, full])
-    share = hub_rows(jnp.where(hub_order == core, 2, 3).astype(jnp.int32)[None], both[0], near, far, width)
-    share, group = barrier((share, group))
-
+    share = hub_rows(jnp.where(hub_order == core, 2, 3)[None], both[0], near, far, width)
     near_new = join_pieces(share).reshape(rows, clust)
-    member_want, member_order = flags_of(
-        lax.dynamic_index_in_dim(group[:, full], want * rows, 0, keepdims=False)
-    )
-    pick = jnp.stack([near_slot, want, member_want, jnp.where(member_order == core, 2, 3)]).astype(jnp.int32)
-    member_words = keep_words(pick, group, lambda pick: (pick[1], full // LANES), rows)
-    near_tile, far_tile, member_tile, degree, new, member_new = seven_of(
-        pick, joined, group, near, far, words, member_words, carry, indicators, width
-    )
-    near_new, new = barrier((near_new, new))
+    far_x = (far, (chips, piece, width), lambda r, pick: (0, 0, 0))
+    far_y = (far, (chips, piece, clust), lambda r, pick: (0, 0, width // clust))
+    *carry, far_tile = tile_of(pick, own_rows, far_x, far_y, words, lambda pick: 5 - pick[0], carry)
+    near_new, carry = barrier((near_new, carry))
     far_new = swap_cores(near_new)
-    return last_of(
-        (own_tile, member_tile, near_tile, far_tile), (new, member_new, near_new, far_new), degree, indicators
-    )
+    acc = pair_of((near_tile, far_tile), (near_new, far_new))
+    acc, middle_x, outer_x = barrier((acc, middle_x, outer_x))
+
+    member_tile, degree, new, member_new = member_of(
+        pick, (normed, beside_x, across_x, middle_x, outer_x), normed, group_rest, near, far, words, member_words,
+        carry, indicators,
+    )
+    return pair_of((own_tile, member_tile), (new, member_new), (acc, degree, indicators))
 
 
 def solution(mesh):

time: 229 us -> 230 us (level)
  blocking collectives: 44.8 us -> 0 us
  starting transfers between devices: 19.9 us -> 49.9 us
  Pallas kernels: 59.2 us -> 74.1 us
  between operations: 24.7 us -> 12.6 us
  waiting for transfers between devices: 66.5 us -> 73.9 us
  local copies, waits for them, and re-layouts: 8.81 us -> 12.9 us
    all_to_all x1 -> x0, blocking collectives: 44.8 us -> none  [join_pieces(): lax.all_to_all(repeated, 'slab', 0, 0, axis_index_groups=layers, tiled=True)]
    ppermute x6 -> x14, starting transfers between devices: 8.38 us -> 28.8 us  [send(): return lax.ppermute(block, AXES, pairs)]
    pallas_call x1 -> x3, Pallas kernels: 6.24 us -> 20.9 us  [tile_of(): pl.pallas_call(functools.partial(tile_kernel, carry is not None, last), o...]
    ppermute x6 -> x14, waiting for transfers between devices: 59.4 us -> 70.8 us  [send(): return lax.ppermute(block, AXES, pairs)]
    all_to_all x1 -> x2, starting transfers between devices: 3.75 us -> 13.3 us  [join_pieces(): lax.all_to_all(repeated, 'slab', 0, 0, axis_index_groups=layers, tiled=True)]
    all_to_all x1, waiting for transfers between devices: 7.17 us -> 0.01 us  [scatter(): lax.all_to_all(block.reshape(members, rows // members, width), 'slab', 0,...]
    all_to_all x1 -> x2, waiting for transfers between devices: 0.01 us -> 3.07 us  [join_pieces(): lax.all_to_all(repeated, 'slab', 0, 0, axis_index_groups=layers, tiled=True)]
    broadcast_in_dim x2, local copies, waits for them, and re-layouts: 1.25 us -> 3.6 us  [join_pieces(): repeated = jnp.broadcast_to(piece[None], (chips,) + piece.shape)]
  transfers between devices with their start and end apart: 9 -> 17, of which waited for: 7 -> 11; matrix products, arithmetic and copies ran while one was open for 3% -> 4% of each run, Pallas kernels for 17% -> 20%
where the time goes in v5:
time: 230 us; the launch traced here: 228 us
  Pallas kernels  74.1 us (32%)
  waiting for transfers between devices  73.9 us (32%)
  starting transfers between devices  49.9 us (22%)
  local copies, waits for them, and re-layouts  12.9 us (6%)
  between operations  12.6 us (5%)
  other arithmetic  4.03 us (2%)
    ppermute x14, waiting for transfers between devices, send(): return lax.ppermute(block, AXES, pairs)  70.8 us
    ppermute x14, starting transfers between devices, send(): return lax.ppermute(block, AXES, pairs)  28.8 us
    pallas_call x3, Pallas kernels, tile_of(): pl.pallas_call(functools.partial(tile_kernel, carry is not None, last), o...  20.9 us
    pallas_call x1, Pallas kernels, member_of(): pl.pallas_call(functools.partial(member_kernel, width), out_shape=[jax.Sh...  18.2 us
    pallas_call x2, Pallas kernels, keep_words(): pl.pallas_call(words_kernel, out_shape=jax.ShapeDtypeStruct((K, rows, LAN...  14.7 us
    all_to_all x2, starting transfers between devices, join_pieces(): lax.all_to_all(repeated, 'slab', 0, 0, axis_index_groups=layers, tiled=True)  13.3 us
    pallas_call x2, Pallas kernels, pair_of(): pl.pallas_call(functools.partial(pair_kernel, finish is not None), out_sh...  10.8 us
    all_to_all x1, starting transfers between devices, scatter(): lax.all_to_all(block.reshape(members, rows // members, width), 'slab', 0,...  7.89 us
  transfers between devices with their start and end apart: 17, of which 11 were waited for; matrix products, arithmetic and copies ran while one was open for 4% of the time, Pallas kernels for 20%

profile of v5, /device:TPU:161, one launch (start us, length us, event | category | flops | bytes accessed | tf_op | source)
XLA Modules:
  0.0 227.5 jit_solution(7824048697748856534)
XLA Ops:
  2.6 4.3 %join.1 = (bf16[1024,896]{1,0:T(8,128)(2,1)}, bf16[1024,512]{1,0:T(8,128)(2,1)}, bf16[1296,256]{1,0:T(8,128)(2,1)}) custom-call(s32[1]{0:T(128)} %bitcast.2.flag_ref, bf16[1024,512]{1,0:T(8,128)(2,1)} %x_ref.1, bf16[1024,256]{1,0:T(8,128)(2,1)} %refs_2_.1, s32[4,16,1024]{2,1,0:T(8,128)} %bitcast.64), custom_call_target="tpu_custom_call" | custom-call | tf_op jit(solution)/shard_map/join/pallas_call | solution.py:53
  7.0 7.9 %all-to-all-start = ((bf16[32,32,896]{2,1,0:T(8,128)(2,1)}), bf16[32,32,896]{2,1,0:T(8,128)(2,1)S(1)}, u32[]{:S(2)}, u32[]{:S(2)}) async-start(bf16[32,32,896]{2,1,0:T(8,128)(2,1)} %bitcast.52), calls=%async_computation | async-start | bytes 3670016 | tf_op jit(solution)/shard_map/all_to_all | solution.py:395
  16.9 7.0 %keep_words.2.w_ref.refs_10_ = s32[4,1024,128]{2,1,0:T(8,128)} custom-call(s32[1]{0:T(128)} %bitcast.5.pick_ref, bf16[1,1296,256]{2,1,0:T(8,128)(2,1)} %bitcast.53), custom_call_target="tpu_custom_call" | custom-call | flops 8388608 | bytes 524288 | tf_op jit(solution)/shard_map/keep_words/pallas_call | solution.py:94
  24.0 6.3 %tile.3 = (f32[1024,128]{1,0:T(8,128)}, f32[1024,256]{1,0:T(8,128)}, bf16[1024,1024]{1,0:T(8,128)(2,1)}) custom-call(s32[1]{0:T(128)} %bitcast.5.pick_ref, bf16[1024,896]{1,0:T(8,128)(2,1)} %get-tuple-element.48.x_ref.other_ref.y_ref, bf16[1024,896]{1,0:T(8,128)(2,1)} %get-tuple-element.48.x_ref.other_ref.y_ref, s32[4,1024,128]{2,1,0:T(8,128)} %keep_words.2.w_ref.refs_10_, ...), custom_call_target="tpu_custom_call" | custom-call | flops 262144 | bytes 262144 | tf_op jit(solution)/shard_map/tile/pallas_call | solution.py:161
  34.9 9.7 %collective-permute-done = bf16[1296,256]{1,0:T(8,128)(2,1)S(1)} collective-permute-done((bf16[1296,256]{1,0:T(8,128)(2,1)S(1)}, bf16[1296,256]{1,0:T(8,128)(2,1)S(1)}, u32[]{:S(2)}, u32[]{:S(2)}) %collective-permute-start) | collective-permute-done | bytes 663584 | tf_op jit(solution)/shard_map/ppermute | solution.py:355
  46.5 7.3 %collective-permute-done.2 = bf16[2,32,896]{2,1,0:T(8,128)(2,1)S(1)} collective-permute-done((bf16[2,32,896]{2,1,0:T(8,128)(2,1)S(1)}, bf16[2,32,896]{2,1,0:T(8,128)(2,1)S(1)}, u32[]{:S(2)}, u32[]{:S(2)}) %collective-permute-start.2) | collective-permute-done | bytes 114720 | tf_op jit(solution)/shard_map/ppermute | solution.py:355
  55.2 2.9 %collective-permute-done.3 = bf16[1,2,32,896]{3,2,1,0:T(8,128)(2,1)S(1)} collective-permute-done((bf16[1,2,32,896]{3,2,1,0:T(8,128)(2,1)S(1)}, bf16[1,2,32,896]{3,2,1,0:T(8,128)(2,1)S(1)}, u32[]{:S(2)}, u32[]{:S(2)}) %collective-permute-start.3) | collective-permute-done | bytes 114720 | tf_op jit(solution)/shard_map/ppermute | solution.py:355
  58.3 3.0 %collective-permute-start.4 = (bf16[2,2,32,896]{3,2,1,0:T(8,128)(2,1)S(1)}, bf16[2,2,32,896]{3,2,1,0:T(8,128)(2,1)S(1)}, u32[]{:S(2)}, u32[]{:S(2)}) collective-permute-start(bf16[2,2,32,896]{3,2,1,0:T(8,128)(2,1)S(1)} %pad_maximum_fusion.1), channel_id=1, source_target_pairs={{0,2},{1,3},{2,0},{3,1},{4,6},{5,7},{6,4},{7,5},{8,10},{9,11},{10,... | collective-permute-start | bytes 688136 | tf_op jit(solution)/shard_map/ppermute | solution.py:355
  65.7 4.7 %collective-permute-done.4 = bf16[2,2,32,896]{3,2,1,0:T(8,128)(2,1)S(1)} collective-permute-done((bf16[2,2,32,896]{3,2,1,0:T(8,128)(2,1)S(1)}, bf16[2,2,32,896]{3,2,1,0:T(8,128)(2,1)S(1)}, u32[]{:S(2)}, u32[]{:S(2)}) %collective-permute-start.4) | collective-permute-done | bytes 229408 | tf_op jit(solution)/shard_map/ppermute | solution.py:355
  75.6 2.0 broadcast_in_dim.94
  77.6 6.6 %all-to-all-start.1 = ((bf16[16,2,64,768]{3,2,1,0:T(8,128)(2,1)}), bf16[16,2,64,768]{3,2,1,0:T(8,128)(2,1)S(1)}, u32[]{:S(2)}, u32[]{:S(2)}) async-start(bf16[16,2,64,768]{3,2,1,0:T(8,128)(2,1)} %broadcast_in_dim.94), calls=%async_computation.1 | async-start | bytes 6291456 | tf_op jit(solution)/shard_map/all_to_all | solution.py:378
  84.3 5.0 %collective-permute-start.6 = (bf16[1296,256]{1,0:T(8,128)(2,1)}, bf16[1296,256]{1,0:T(8,128)(2,1)}, u32[]{:S(2)}, u32[]{:S(2)}) collective-permute-start(bf16[1296,256]{1,0:T(8,128)(2,1)} %copy-done.4), channel_id=1, source_target_pairs={{1,0},{2,3},{5,4},{6,7},{9,8},{10,11},{13,12},{14,15},{17,16},{18,... | collective-permute-start | bytes 1990664 | tf_op jit(solution)/shard_map/ppermute | solution.py:355
  89.3 3.0 %collective-permute-start.7 = (bf16[1296,256]{1,0:T(8,128)(2,1)}, bf16[1296,256]{1,0:T(8,128)(2,1)}, u32[]{:S(2)}, u32[]{:S(2)}) collective-permute-start(bf16[1296,256]{1,0:T(8,128)(2,1)} %get-tuple-element.58), channel_id=1, source_target_pairs={{1,2},{2,1},{5,6},{6,5},{9,10},{10,9},{13,14},{14,13},{17,18},{18,... | collective-permute-start | bytes 1990664 | tf_op jit(solution)/shard_map/ppermute | solution.py:355
  93.9 8.4 %collective-permute-done.6 = bf16[1296,256]{1,0:T(8,128)(2,1)} collective-permute-done((bf16[1296,256]{1,0:T(8,128)(2,1)}, bf16[1296,256]{1,0:T(8,128)(2,1)}, u32[]{:S(2)}, u32[]{:S(2)}) %collective-permute-start.6) | collective-permute-done | bytes 663584 | tf_op jit(solution)/shard_map/ppermute | solution.py:355
  102.4 27.1 %collective-permute-done.7 = bf16[1296,256]{1,0:T(8,128)(2,1)} collective-permute-done((bf16[1296,256]{1,0:T(8,128)(2,1)}, bf16[1296,256]{1,0:T(8,128)(2,1)}, u32[]{:S(2)}, u32[]{:S(2)}) %collective-permute-start.7) | collective-permute-done | bytes 663584 | tf_op jit(solution)/shard_map/ppermute | solution.py:355
  130.6 1.8 pad_maximum_fusion.coded_ref.refs_6_.refs_7_
  136.5 7.7 %keep_words.3.refs_11_ = s32[4,1024,128]{2,1,0:T(8,128)} custom-call(s32[6]{0:T(128)} %stack.66.pick_ref, bf16[4,1296,256]{2,1,0:T(8,128)(2,1)} %copy-done.1), custom_call_target="tpu_custom_call" | custom-call | flops 8388608 | bytes 524288 | tf_op jit(solution)/shard_map/keep_words/pallas_call | solution.py:94
  144.2 6.7 %collective-permute-done.8.refs_2_ = bf16[1024,512]{1,0:T(8,128)(2,1)} collective-permute-done((bf16[1024,512]{1,0:T(8,128)(2,1)}, bf16[1024,512]{1,0:T(8,128)(2,1)}, u32[]{:S(2)}, u32[]{:S(2)}) %collective-permute-start.8) | collective-permute-done | bytes 1048608 | tf_op jit(solution)/shard_map/ppermute | solution.py:355
  152.2 1.8 collective-permute-start.10
  154.1 2.3 collective-permute-start.12
  156.3 4.7 %collective-permute-start.13 = (bf16[1024,512]{1,0:T(8,128)(2,1)}, bf16[1024,512]{1,0:T(8,128)(2,1)}, u32[]{:S(2)}, u32[]{:S(2)}) collective-permute-start(bf16[1024,512]{1,0:T(8,128)(2,1)} %collective-permute-done.8.refs_2_), channel_id=1, source_target_pairs={{1,0},{2,3},{5,4},{6,7},{9,8},{10,11},{13,12},{14,15},{17,16},{18,... | collective-permute-start | bytes 3145736 | tf_op jit(solution)/shard_map/ppermute | solution.py:355
  162.9 7.3 %tile.4 = (f32[1024,128]{1,0:T(8,128)}, f32[1024,256]{1,0:T(8,128)}, bf16[1024,1024]{1,0:T(8,128)(2,1)}) custom-call(s32[6]{0:T(128)} %stack.66.pick_ref, bf16[1024,896]{1,0:T(8,128)(2,1)} %get-tuple-element.48.x_ref.other_ref.y_ref, bf16[16,2,64,768]{3,2,1,0:T(8,128)(2,1)} %copy-done, s32[4,1024,128]{2,1,0:T(8,128)} %keep_words.2.w_ref.refs_10_, ...), custom_call_target="tpu_custom_call" | custom-call | flops 262144 | bytes 262144 | tf_op jit(solution)/shard_map/tile/pallas_call | solution.py:161
  170.3 5.2 %hub_rows.1 = bf16[64,256]{1,0:T(8,128)(2,1)} custom-call(s32[1]{0:T(128)} %bitcast.41.pick_ref, bf16[64,896]{1,0:T(8,128)(2,1)} %slice_bitcast_fusion.1.rows_ref, bf16[16,2,64,768]{3,2,1,0:T(8,128)(2,1)} %copy-done, bf16[16,64,768]{2,1,0:T(8,128)(2,1)} %collective-permute-done.10.other_ref.y_ref.far_ref.refs_9_), custom_call_target="tpu_custom_call" | custom-call | flops 1024 | bytes 1024 | tf_op jit(solution)/shard_map/hub_rows/pallas_call | solution.py:326
  175.5 1.6 broadcast_in_dim.96
  177.1 6.7 %all-to-all-start.2 = ((bf16[16,64,256]{2,1,0:T(8,128)(2,1)}), bf16[16,64,256]{2,1,0:T(8,128)(2,1)S(1)}, u32[]{:S(2)}, u32[]{:S(2)}) async-start(bf16[16,64,256]{2,1,0:T(8,128)(2,1)} %broadcast_in_dim.96), calls=%async_computation.2 | async-start | bytes 1048576 | tf_op jit(solution)/shard_map/all_to_all | solution.py:378
  183.7 7.3 %tile.5 = (f32[1024,128]{1,0:T(8,128)}, f32[1024,256]{1,0:T(8,128)}, bf16[1024,1024]{1,0:T(8,128)(2,1)}) custom-call(s32[6]{0:T(128)} %stack.66.pick_ref, bf16[1024,896]{1,0:T(8,128)(2,1)} %get-tuple-element.48.x_ref.other_ref.y_ref, bf16[16,64,768]{2,1,0:T(8,128)(2,1)} %collective-permute-done.10.other_ref.y_ref.far_ref.refs_9_, ...), custom_call_target="tpu_custom_call" | custom-call | flops 262144 | bytes 262144 | tf_op jit(solution)/shard_map/tile/pallas_call | solution.py:161
  191.0 3.1 %all-to-all-done.2 = bf16[16,64,256]{2,1,0:T(8,128)(2,1)S(1)} async-done(((bf16[16,64,256]{2,1,0:T(8,128)(2,1)}), bf16[16,64,256]{2,1,0:T(8,128)(2,1)S(1)}, u32[]{:S(2)}, u32[]{:S(2)}) %all-to-all-start.2) | async-done | bytes 524320 | tf_op jit(solution)/shard_map/all_to_all | solution.py:378
  194.1 2.1 collective-permute-start.11
  196.2 1.5 collective-permute-done.11.y2_ref
  198.5 5.1 %pair.2.refs_0_ = f32[1024,256]{1,0:T(8,128)} custom-call(bf16[1024,1024]{1,0:T(8,128)(2,1)} %get-tuple-element.70.first_ref, bf16[1024,1024]{1,0:T(8,128)(2,1)} %get-tuple-element.76.second_ref, bf16[1024,256]{1,0:T(8,128)(2,1)} %bitcast.56, bf16[1024,256]{1,0:T(8,128)(2,1)} %copy-done.5), custom_call_target="tpu_custom_call" | custom-call | flops 262144 | bytes 262144 | tf_op jit(solution)/shard_map/pair/pallas_call | solution.py:279
  203.6 18.2 %member.1 = (bf16[1024,1024]{1,0:T(8,128)(2,1)}, f32[1024,128]{1,0:T(8,128)}, bf16[1024,256]{1,0:T(8,128)(2,1)}, bf16[1024,256]{1,0:T(8,128)(2,1)}) custom-call(s32[6]{0:T(128)} %stack.66.pick_ref, bf16[1024,512]{1,0:T(8,128)(2,1)} %get-tuple-element.63.refs_0_.refs_5_, bf16[1024,512]{1,0:T(8,128)(2,1)} %collective-permute-done.9.refs_1_, ...), custom_call_target="tpu_custom_call" | custom-call | flops 8053063680 | bytes 8388608 | tf_op jit(solution)/shard_map/member/pallas_call | solution.py:227
  221.8 5.7 %pair.3 = bf16[1024,256]{1,0:T(8,128)(2,1)} custom-call(bf16[1024,1024]{1,0:T(8,128)(2,1)} %get-tuple-element.53.first_ref, bf16[1024,1024]{1,0:T(8,128)(2,1)} %get-tuple-element.86.second_ref, bf16[1024,256]{1,0:T(8,128)(2,1)} %get-tuple-element.87.y1_ref, bf16[1024,256]{1,0:T(8,128)(2,1)} %get-tuple-element.88.y2_ref, f32[1024,256]{1,0:T(8,128)} %pair.2.refs_0_, ...), custom_call_target="tpu_custom_call" | custom-call | flops 262144 | bytes 262144 | tf_op jit(solution)/shard_map/pair/pallas_call | solution.py:279
  (57 shorter events, 20.8 us)
Async XLA Ops:
  7.0 7.9 %copy-start.2 = (bf16[1296,256]{1,0:T(8,128)(2,1)S(1)}, bf16[1296,256]{1,0:T(8,128)(2,1)}, u32[]{:S(2)}) copy-start(bf16[1296,256]{1,0:T(8,128)(2,1)} %get-tuple-element.58) | copy-start | bytes 1990660
  7.0 39.1 %all-to-all-start = ((bf16[32,32,896]{2,1,0:T(8,128)(2,1)}), bf16[32,32,896]{2,1,0:T(8,128)(2,1)S(1)}, u32[]{:S(2)}, u32[]{:S(2)}) async-start(bf16[32,32,896]{2,1,0:T(8,128)(2,1)} %bitcast.52), calls=%async_computation | async-start | bytes 3670016 | tf_op jit(solution)/shard_map/all_to_all | solution.py:395
  14.9 29.7 %collective-permute-start = (bf16[1296,256]{1,0:T(8,128)(2,1)S(1)}, bf16[1296,256]{1,0:T(8,128)(2,1)S(1)}, u32[]{:S(2)}, u32[]{:S(2)}) collective-permute-start(bf16[1296,256]{1,0:T(8,128)(2,1)S(1)} %copy-done.2), channel_id=1, source_target_pairs={{0,2},{1,3},{2,0},{3,1},{4,6},{5,7},{6,4},{7,5},{8,10},{9,11},{10,... | collective-permute-start | bytes 1990664 | tf_op jit(solution)/shard_map/ppermute | solution.py:355
  16.2 29.9 %collective-permute-start.1 = (bf16[1296,256]{1,0:T(8,128)(2,1)S(1)}, bf16[1296,256]{1,0:T(8,128)(2,1)}, u32[]{:S(2)}, u32[]{:S(2)}) collective-permute-start(bf16[1296,256]{1,0:T(8,128)(2,1)S(1)} %copy-done.2), channel_id=1, source_target_pairs={{0,1},{1,0},{2,3},{3,2},{4,5},{5,4},{6,7},{7,6},{8,9},{9,8},{10,11... | collective-permute-start | bytes 1990664 | tf_op jit(solution)/shard_map/ppermute | solution.py:355
  24.0 6.3 %copy-start.6 = (s32[2]{0:T(128)S(1)}, s32[2]{0:T(128)}, u32[]{:S(2)}) copy-start(s32[2]{0:T(128)} %param.8) | copy-start | bytes 28
  44.6 30.9 %copy-start.4 = (bf16[1296,256]{1,0:T(8,128)(2,1)}, bf16[1296,256]{1,0:T(8,128)(2,1)S(1)}, u32[]{:S(2)}) copy-start(bf16[1296,256]{1,0:T(8,128)(2,1)S(1)} %collective-permute-done) | copy-start | bytes 1990660
  46.1 7.6 %collective-permute-start.2 = (bf16[2,32,896]{2,1,0:T(8,128)(2,1)S(1)}, bf16[2,32,896]{2,1,0:T(8,128)(2,1)S(1)}, u32[]{:S(2)}, u32[]{:S(2)}) collective-permute-start(bf16[2,32,896]{2,1,0:T(8,128)(2,1)S(1)} %pad_maximum_fusion.3), channel_id=1, source_target_pairs={{0,128},{1,129},{2,130},{3,131},{4,132},{5,133},{6,134},{7,135},{8... | collective-permute-start | bytes 344072 | tf_op jit(solution)/shard_map/ppermute | solution.py:355
  53.9 4.3 %collective-permute-start.3 = (bf16[1,2,32,896]{3,2,1,0:T(8,128)(2,1)S(1)}, bf16[1,2,32,896]{3,2,1,0:T(8,128)(2,1)S(1)}, u32[]{:S(2)}, u32[]{:S(2)}) collective-permute-start(bf16[1,2,32,896]{3,2,1,0:T(8,128)(2,1)S(1)} %select_bitcast_fusion.1), channel_id=1, source_target_pairs={{0,1},{1,0},{2,3},{3,2},{4,5},{5,4},{6,7},{7,6},{8,9},{9,8},{10,11... | collective-permute-start | bytes 344072 | tf_op jit(solution)/shard_map/ppermute | solution.py:355
  58.3 12.2 %collective-permute-start.4 = (bf16[2,2,32,896]{3,2,1,0:T(8,128)(2,1)S(1)}, bf16[2,2,32,896]{3,2,1,0:T(8,128)(2,1)S(1)}, u32[]{:S(2)}, u32[]{:S(2)}) collective-permute-start(bf16[2,2,32,896]{3,2,1,0:T(8,128)(2,1)S(1)} %pad_maximum_fusion.1), channel_id=1, source_target_pairs={{0,2},{1,3},{2,0},{3,1},{4,6},{5,7},{6,4},{7,5},{8,10},{9,11},{10,... | collective-permute-start | bytes 688136 | tf_op jit(solution)/shard_map/ppermute | solution.py:355
  73.1 2.5 %collective-permute-start.5 = (bf16[2,32,896]{2,1,0:T(8,128)(2,1)S(1)}, bf16[2,32,896]{2,1,0:T(8,128)(2,1)S(1)}, u32[]{:S(2)}, u32[]{:S(2)}) collective-permute-start(bf16[2,32,896]{2,1,0:T(8,128)(2,1)S(1)} %broadcast_select_fusion.6), channel_id=1, source_target_pairs={{0,4},{1,5},{2,6},{3,7},{4,0},{5,1},{6,2},{7,3},{8,12},{9,13},{10,... | collective-permute-start | bytes 344072 | tf_op jit(solution)/shard_map/ppermute | solution.py:355
  77.6 73.2 %all-to-all-start.1 = ((bf16[16,2,64,768]{3,2,1,0:T(8,128)(2,1)}), bf16[16,2,64,768]{3,2,1,0:T(8,128)(2,1)S(1)}, u32[]{:S(2)}, u32[]{:S(2)}) async-start(bf16[16,2,64,768]{3,2,1,0:T(8,128)(2,1)} %broadcast_in_dim.94), calls=%async_computation.1 | async-start | bytes 6291456 | tf_op jit(solution)/shard_map/all_to_all | solution.py:378
  84.3 18.1 %collective-permute-start.6 = (bf16[1296,256]{1,0:T(8,128)(2,1)}, bf16[1296,256]{1,0:T(8,128)(2,1)}, u32[]{:S(2)}, u32[]{:S(2)}) collective-permute-start(bf16[1296,256]{1,0:T(8,128)(2,1)} %copy-done.4), channel_id=1, source_target_pairs={{1,0},{2,3},{5,4},{6,7},{9,8},{10,11},{13,12},{14,15},{17,16},{18,... | collective-permute-start | bytes 1990664 | tf_op jit(solution)/shard_map/ppermute | solution.py:355
  89.3 40.2 %collective-permute-start.7 = (bf16[1296,256]{1,0:T(8,128)(2,1)}, bf16[1296,256]{1,0:T(8,128)(2,1)}, u32[]{:S(2)}, u32[]{:S(2)}) collective-permute-start(bf16[1296,256]{1,0:T(8,128)(2,1)} %get-tuple-element.58), channel_id=1, source_target_pairs={{1,2},{2,1},{5,6},{6,5},{9,10},{10,9},{13,14},{14,13},{17,18},{18,... | collective-permute-start | bytes 1990664 | tf_op jit(solution)/shard_map/ppermute | solution.py:355
  92.3 58.5 %collective-permute-start.8 = (bf16[1024,512]{1,0:T(8,128)(2,1)}, bf16[1024,512]{1,0:T(8,128)(2,1)}, u32[]{:S(2)}, u32[]{:S(2)}) collective-permute-start(bf16[1024,512]{1,0:T(8,128)(2,1)} %get-tuple-element.63.refs_0_.refs_5_), channel_id=1, source_target_pairs={{0,2},{1,3},{2,0},{3,1},{4,6},{5,7},{6,4},{7,5},{8,10},{9,11},{10,... | collective-permute-start | bytes 3145736 | tf_op jit(solution)/shard_map/ppermute | solution.py:355
  92.4 58.4 %collective-permute-start.9 = (bf16[1024,512]{1,0:T(8,128)(2,1)}, bf16[1024,512]{1,0:T(8,128)(2,1)}, u32[]{:S(2)}, u32[]{:S(2)}) collective-permute-start(bf16[1024,512]{1,0:T(8,128)(2,1)} %get-tuple-element.63.refs_0_.refs_5_), channel_id=1, source_target_pairs={{0,1},{1,0},{2,3},{3,2},{4,5},{5,4},{6,7},{7,6},{8,9},{9,8},{10,11... | collective-permute-start | bytes 3145736 | tf_op jit(solution)/shard_map/ppermute | solution.py:355
  132.5 1.5 copy-start.1
  150.9 12.1 %copy-start = (bf16[16,2,64,768]{3,2,1,0:T(8,128)(2,1)}, bf16[16,2,64,768]{3,2,1,0:T(8,128)(2,1)S(1)}, u32[]{:S(2)}) copy-start(bf16[16,2,64,768]{3,2,1,0:T(8,128)(2,1)S(1)} %all-to-all-done.1.other_ref.y_ref.near_ref.refs_8_) | copy-start | bytes 9437188
  152.2 18.0 %collective-permute-start.10 = (bf16[16,64,768]{2,1,0:T(8,128)(2,1)}, bf16[16,64,768]{2,1,0:T(8,128)(2,1)}, u32[]{:S(2)}, u32[]{:S(2)}) collective-permute-start(bf16[16,64,768]{2,1,0:T(8,128)(2,1)} %slice_bitcast_fusion), channel_id=1, source_target_pairs={{0,4},{1,5},{2,6},{3,7},{4,0},{5,1},{6,2},{7,3},{8,12},{9,13},{10,... | collective-permute-start | bytes 4718600 | tf_op jit(solution)/shard_map/ppermute | solution.py:355
  154.1 49.5 %collective-permute-start.12 = (bf16[1024,512]{1,0:T(8,128)(2,1)}, bf16[1024,512]{1,0:T(8,128)(2,1)}, u32[]{:S(2)}, u32[]{:S(2)}) collective-permute-start(bf16[1024,512]{1,0:T(8,128)(2,1)} %get-tuple-element.63.refs_0_.refs_5_), channel_id=1, source_target_pairs={{1,2},{2,1},{5,6},{6,5},{9,10},{10,9},{13,14},{14,13},{17,18},{18,... | collective-permute-start | bytes 3145736 | tf_op jit(solution)/shard_map/ppermute | solution.py:355
  156.3 47.3 %collective-permute-start.13 = (bf16[1024,512]{1,0:T(8,128)(2,1)}, bf16[1024,512]{1,0:T(8,128)(2,1)}, u32[]{:S(2)}, u32[]{:S(2)}) collective-permute-start(bf16[1024,512]{1,0:T(8,128)(2,1)} %collective-permute-done.8.refs_2_), channel_id=1, source_target_pairs={{1,0},{2,3},{5,4},{6,7},{9,8},{10,11},{13,12},{14,15},{17,16},{18,... | collective-permute-start | bytes 3145736 | tf_op jit(solution)/shard_map/ppermute | solution.py:355
  177.1 17.0 %all-to-all-start.2 = ((bf16[16,64,256]{2,1,0:T(8,128)(2,1)}), bf16[16,64,256]{2,1,0:T(8,128)(2,1)S(1)}, u32[]{:S(2)}, u32[]{:S(2)}) async-start(bf16[16,64,256]{2,1,0:T(8,128)(2,1)} %broadcast_in_dim.96), calls=%async_computation.2 | async-start | bytes 1048576 | tf_op jit(solution)/shard_map/all_to_all | solution.py:378
  194.1 3.6 %copy-start.3 = (bf16[16,64,256]{2,1,0:T(8,128)(2,1)}, bf16[16,64,256]{2,1,0:T(8,128)(2,1)S(1)}, u32[]{:S(2)}) copy-start(bf16[16,64,256]{2,1,0:T(8,128)(2,1)S(1)} %all-to-all-done.2) | copy-start | bytes 1572868
  194.1 3.6 %collective-permute-start.11 = (bf16[1024,256]{1,0:T(8,128)(2,1)S(1)}, bf16[1024,256]{1,0:T(8,128)(2,1)S(1)}, u32[]{:S(2)}, u32[]{:S(2)}) collective-permute-start(bf16[1024,256]{1,0:T(8,128)(2,1)S(1)} %bitcast.55), channel_id=1, source_target_pairs={{0,4},{1,5},{2,6},{3,7},{4,0},{5,1},{6,2},{7,3},{8,12},{9,13},{10,... | collective-permute-start | bytes 1572872 | tf_op jit(solution)/shard_map/ppermute | solution.py:355
  197.7 0.8 copy-start.5

commit v6 on v5

--- a/solution.py
+++ b/solution.py
@@ -21,9 +21,10 @@
 HALF = 32
 FLAG_ROWS = 16
 BLOCKS_NEAR = 5
-
-
-def join_kernel(flag_ref, x_ref, y_ref, cols_ref, all_ref, normed_ref, rest_ref):
+WORDS_HINT = 30_000_000_000
+
+
+def join_kernel(blocks, near_ref, x_ref, y_ref, cols_ref, all_ref, normed_ref, rest_ref):
     width, clust = x_ref.shape[1], y_ref.shape[1]
     step = pl.program_id(0)
     rows = pl.num_programs(0) * ROW_TILE
@@ -31,7 +32,8 @@
     scale = lax.rsqrt(jnp.sum(values * values, axis=1, keepdims=True) + EPS)
     normed = (values * scale).astype(jnp.bfloat16)
     cols = cols_ref[...].reshape(K * TOPK, cols_ref.shape[2])
-    coded = jnp.concatenate([(cols >> 5) + HALF * flag_ref[0], cols & (HALF - 1)], axis=0)
+    flag = (near_ref[1] & 3) + 4 * (near_ref[2] - blocks)
+    coded = jnp.concatenate([(cols >> 5) + HALF * flag, cols & (HALF - 1)], axis=0)
     all_ref[:, :width] = normed
     all_ref[:, width : width + clust] = y_ref[...]
     all_ref[:, width + clust :] = coded.astype(jnp.float32).T.astype(jnp.bfloat16)
@@ -40,18 +42,18 @@
     single = jnp.left_shift((cols & (LANES - 1)) + LANES, cols >> 7)
     place = pl.multiple_of(rows + step * K * TOPK, K * TOPK)
     rest_ref[pl.ds(place, K * TOPK), :] = single.astype(jnp.float32).astype(jnp.bfloat16)
-    flags = jnp.full((FLAG_ROWS, clust), flag_ref[0], jnp.int32)
+    flags = jnp.full((FLAG_ROWS, clust), flag, jnp.int32)
     rest_ref[rows + rows // ROW_TILE * K * TOPK :, :] = flags.astype(jnp.float32).astype(jnp.bfloat16)
 
 
-def join(flag, embeddings, indicators, columns):
+def join(blocks, near, embeddings, indicators, columns):
     rows, width = embeddings.shape
     clust = indicators.shape[1]
     by_row = lambda cols: pl.BlockSpec((ROW_TILE, cols), lambda r, flag: (r, 0))
     steps = rows // ROW_TILE
     rest = (rows + steps * K * TOPK + FLAG_ROWS, clust)
     return pl.pallas_call(
-        join_kernel,
+        functools.partial(join_kernel, blocks),
         out_shape=[
             jax.ShapeDtypeStruct(shape, jnp.bfloat16)
             for shape in ((rows, width + clust + 2 * K * TOPK), (rows, width), rest)
@@ -68,7 +70,7 @@
         ),
         compiler_params=pltpu.CompilerParams(vmem_limit_bytes=VMEM_LIMIT),
         name="join",
-    )(flag, embeddings, indicators, jnp.transpose(columns, (1, 2, 0)))
+    )(near, embeddings, indicators, jnp.transpose(columns, (1, 2, 0)))
 
 
 def words_kernel(pick_ref, coded_ref, out_ref):
@@ -88,7 +90,7 @@
                 out_ref[slot, start : start + LANES, :] = word.T
 
 
-def keep_words(pick, rest, which, rows):
+def keep_words(pick, rest, which, rows, hint):
     part = rows // ROW_TILE * K * TOPK
     clust = rest.shape[2]
     return pl.pallas_call(
@@ -101,7 +103,7 @@
             out_specs=pl.BlockSpec((K, rows, LANES), lambda i, pick: (0, 0, 0)),
         ),
         compiler_params=pltpu.CompilerParams(vmem_limit_bytes=VMEM_LIMIT),
-        cost_estimate=pl.CostEstimate(flops=rows * LANES * K * TOPK, bytes_accessed=rows * 512, transcendentals=0),
+        cost_estimate=pl.CostEstimate(flops=hint, bytes_accessed=rows * 512, transcendentals=0),
         name="keep_words",
     )(pick, rest)
 
@@ -174,15 +176,16 @@
     )(pick, *args)
 
 
-def member_kernel(width, pick_ref, *refs):
+def seven_kernel(pick_ref, *refs):
     blocks, refs = refs[:BLOCKS_NEAR], refs[BLOCKS_NEAR:]
-    (rows_ref, rest1_ref, rest2_ref, near_ref, far_ref, w_ref, words_ref, deg_in, acc_in, anchor_ref) = refs[:10]
-    tile_ref, deg_ref, new_ref, other_ref, x1_ref, x2_ref, held_ref, sems = refs[10:]
+    rows_ref, first_y, second_y, near_ref, far_ref, words_ref, member_ref, deg_in, acc_in, anchor_ref = refs[:10]
+    near_tile, far_tile, member_tile, deg_ref, new_ref, other_ref, first_x, second_x, held, spare, sems = refs[10:]
+    width = rows_ref.shape[1]
     step = pl.program_id(0)
 
     @pl.when(step == 0)
     def _():
-        for which, target in enumerate((x1_ref, x2_ref)):
+        for which, target in enumerate((first_x, second_x)):
             for i, block in enumerate(blocks):
 
                 @pl.when(pick_ref[1 + which] == i)
@@ -197,41 +200,46 @@
 
         return put
 
-    total = weights(cosines(rows_ref[...], x1_ref[...]), w_ref[0], deg_in[...], put_to(tile_ref))
+    def run(rows, plan, total, acc):
+        for word, (other, y), tile in plan:
+            total = weights(cosines(rows, other), word, total, put_to(tile))
+            acc = acc + jnp.dot(tile[...], y, preferred_element_type=jnp.float32)
+        return total, acc
+
+    split = lambda block: (block[:, :width], block[:, width:])
+    first, second = (first_x[...], first_y[0]), (second_x[...], second_y[0])
+    near, far = split(near_ref[:, 0].reshape(-1, near_ref.shape[3])), split(flat(far_ref))
+    plan = (
+        (words_ref[pick_ref[0]], near, near_tile),
+        (words_ref[5 - pick_ref[0]], far, far_tile),
+        (words_ref[1], first, member_tile),
+    )
+    total, acc = run(rows_ref[...], plan, deg_in[...], acc_in[...])
     deg_ref[...] = total
-    gathered = acc_in[...] + jnp.dot(tile_ref[...], rest1_ref[0], preferred_element_type=jnp.float32)
-    new_ref[...] = mix(gathered, jnp.sum(total, axis=1, keepdims=True), anchor_ref[...])
-
+    new_ref[...] = mix(acc, jnp.sum(total, axis=1, keepdims=True), anchor_ref[...])
     here = pl.ds(pl.multiple_of(step * ROW_TILE, ROW_TILE), ROW_TILE)
-    x = x1_ref[here, :]
-    near, far = near_ref[:, 0].reshape(-1, near_ref.shape[3]), flat(far_ref)
-    total = jnp.zeros(deg_in.shape, jnp.float32)
-    acc = jnp.zeros(acc_in.shape, jnp.float32)
-    slots = (0, 1, pick_ref[3], 5 - pick_ref[3])
-    others = ((x1_ref[...], rest1_ref[0]), (x2_ref[...], rest2_ref[0]))
-    others += tuple((block[:, :width], block[:, width:]) for block in (near, far))
-    for slot, (other, y) in zip(slots, others):
-        total = weights(cosines(x, other), words_ref[slot], total, put_to(held_ref))
-        acc = acc + jnp.dot(held_ref[...], y, preferred_element_type=jnp.float32)
-    anchor = rest1_ref[0, here, :]
-    other_ref[...] = mix(acc, jnp.sum(total, axis=1, keepdims=True), anchor)
-
-
-def member_of(pick, blocks, own_rows, rest, near, far, words, member_words, carry, anchor):
+    plan = (
+        (member_ref[pick_ref[3]], near, held),
+        (member_ref[5 - pick_ref[3]], far, spare),
+        (member_ref[0], first, held),
+        (member_ref[1], second, spare),
+    )
+    total, acc = run(first_x[here, :], plan, jnp.zeros(deg_in.shape, jnp.float32), jnp.zeros(acc_in.shape, jnp.float32))
+    other_ref[...] = mix(acc, jnp.sum(total, axis=1, keepdims=True), first_y[0, here, :])
+
+
+def seven_of(pick, blocks, own_rows, rest, near, far, words, member_words, carry, anchor):
     rows, width = blocks[0].shape
     clust = rest.shape[2]
     chips, _, piece, full = near.shape
     once = pl.Buffered(1)
     by_row = lambda cols: pl.BlockSpec((ROW_TILE, cols), lambda r, pick: (r, 0))
     rest_at = lambda k: pl.BlockSpec((1, rows, clust), lambda r, pick: (pick[k], 0, 0), pipeline_mode=once)
+    by_word = pl.BlockSpec((K, ROW_TILE, LANES), lambda r, pick: (0, r, 0))
+    outs = [(rows, jnp.bfloat16)] * 3 + [(LANES, jnp.float32)] + [(clust, jnp.bfloat16)] * 2
     return pl.pallas_call(
-        functools.partial(member_kernel, width),
-        out_shape=[
-            jax.ShapeDtypeStruct((rows, rows), jnp.bfloat16),
-            jax.ShapeDtypeStruct((rows, LANES), jnp.float32),
-            jax.ShapeDtypeStruct((rows, clust), jnp.bfloat16),
-            jax.ShapeDtypeStruct((rows, clust), jnp.bfloat16),
-        ],
+        seven_kernel,
+        out_shape=[jax.ShapeDtypeStruct((rows, cols), kind) for cols, kind in outs],
         grid_spec=pltpu.PrefetchScalarGridSpec(
             num_scalar_prefetch=1,
             grid=(rows // ROW_TILE,),
@@ -242,52 +250,46 @@
                 rest_at(5),
                 pl.BlockSpec((chips, 1, piece, full), lambda r, pick: (0, 0, 0, 0), pipeline_mode=once),
                 pl.BlockSpec((chips, piece, full), lambda r, pick: (0, 0, 0), pipeline_mode=once),
-                pl.BlockSpec((1, ROW_TILE, LANES), lambda r, pick: (1, r, 0)),
-                pl.BlockSpec((K, ROW_TILE, LANES), lambda r, pick: (0, r, 0)),
+                by_word,
+                by_word,
                 by_row(LANES),
                 by_row(clust),
                 by_row(clust),
             ],
-            out_specs=[by_row(rows), by_row(LANES), by_row(clust), by_row(clust)],
-            scratch_shapes=[
-                pltpu.VMEM((rows, width), jnp.bfloat16),
-                pltpu.VMEM((rows, width), jnp.bfloat16),
-                pltpu.VMEM((ROW_TILE, rows), jnp.bfloat16),
-                pltpu.SemaphoreType.DMA((2,)),
-            ],
+            out_specs=[by_row(cols) for cols, _ in outs],
+            scratch_shapes=[pltpu.VMEM((rows, width), jnp.bfloat16)] * 2
+            + [pltpu.VMEM((ROW_TILE, rows), jnp.bfloat16)] * 2
+            + [pltpu.SemaphoreType.DMA((2,))],
         ),
         compiler_params=pltpu.CompilerParams(vmem_limit_bytes=VMEM_LIMIT),
         cost_estimate=pl.CostEstimate(
-            flops=10 * rows * rows * 768, bytes_accessed=8 * rows * rows, transcendentals=5 * rows * rows
-        ),
-        name="member",
+            flops=14 * rows * rows * full, bytes_accessed=16 * rows * rows, transcendentals=7 * rows * rows
+        ),
+        name="seven",
     )(pick, *blocks, own_rows, rest, rest, near, far, words, member_words, *carry, anchor)
 
 
-def pair_kernel(last, first_ref, second_ref, y1_ref, y2_ref, *refs):
-    acc = jnp.dot(first_ref[...], y1_ref[...], preferred_element_type=jnp.float32)
-    acc = acc + jnp.dot(second_ref[...], y2_ref[...], preferred_element_type=jnp.float32)
-    if last:
-        acc_in, deg_ref, anchor_ref = refs[:3]
-        acc = mix(acc + acc_in[...], jnp.sum(deg_ref[...], axis=1, keepdims=True), anchor_ref[...])
-    refs[-1][...] = acc
-
-
-def pair_of(tiles, news, finish=None):
-    rows, clust = news[0].shape
+def last_kernel(*refs):
+    tiles, news, (deg_ref, anchor_ref, out_ref) = refs[:K], refs[K : 2 * K], refs[2 * K :]
+    acc = sum(jnp.dot(t[...], y[...], preferred_element_type=jnp.float32) for t, y in zip(tiles, news))
+    out_ref[...] = mix(acc, jnp.sum(deg_ref[...], axis=1, keepdims=True), anchor_ref[...])
+
+
+def last_of(tiles, news, degree, anchor):
+    rows, clust = anchor.shape
     by_row = lambda cols: pl.BlockSpec((ROW_TILE, cols), lambda r: (r, 0))
     return pl.pallas_call(
-        functools.partial(pair_kernel, finish is not None),
-        out_shape=jax.ShapeDtypeStruct((rows, clust), jnp.bfloat16 if finish else jnp.float32),
+        last_kernel,
+        out_shape=jax.ShapeDtypeStruct((rows, clust), jnp.bfloat16),
         grid=(rows // ROW_TILE,),
-        in_specs=[by_row(rows)] * 2
-        + [pl.BlockSpec((rows, clust), lambda r: (0, 0))] * 2
-        + ([by_row(clust), by_row(LANES), by_row(clust)] if finish else []),
+        in_specs=[by_row(rows)] * K
+        + [pl.BlockSpec((rows, clust), lambda r: (0, 0))] * K
+        + [by_row(LANES), by_row(clust)],
         out_specs=by_row(clust),
         compiler_params=pltpu.CompilerParams(vmem_limit_bytes=VMEM_LIMIT),
-        cost_estimate=pl.CostEstimate(flops=rows * clust, bytes_accessed=rows * clust, transcendentals=0),
-        name="pair",
-    )(*tiles, *news, *(finish or ()))
+        cost_estimate=pl.CostEstimate(flops=8 * rows * rows * clust, bytes_accessed=8 * rows * rows, transcendentals=0),
+        name="last",
+    )(*tiles, *news, degree, anchor)
 
 
 def hub_rows_kernel(width, pick_ref, rows_ref, near_ref, far_ref, out_ref, word_ref, tile_ref):
@@ -397,7 +399,7 @@
     )
 
 
-def hub_pieces(mine, hub_ids, code_at):
+def hub_candidates(mine, hub_ids):
     members, reps = lax.axis_size("slab") // 2, lax.axis_size("rep")
     slab = lax.axis_index("slab")
     hub_slab, hub_rep = lax.div(hub_ids, reps), lax.rem(hub_ids, reps)
@@ -413,6 +415,11 @@
         got = along_line(held, {r: r ^ (1 << bit) for r in range(4)})
         upper = (rep >> bit) & 1 == 1
         held = jnp.concatenate([jnp.where(upper, got, held), jnp.where(upper, held, got)], axis=0)
+    return held, hub_rep
+
+
+def hub_share(held, hub_rep, code_at):
+    slab = lax.axis_index("slab")
     pick = lambda pieces, at: jnp.where(
         at < 2, jnp.where(at == 0, pieces[0], pieces[1]), jnp.where(at == 2, pieces[2], pieces[3])
     )
@@ -443,24 +450,25 @@
     near_slot = jnp.where(order == core, 2, 3)
     barrier = lax.optimization_barrier
 
-    joined, normed, rest = join((want + 4 * order)[None], embeddings, indicators, columns)
+    joined, normed, rest = join(total, neighbours.reshape(-1), embeddings, indicators, columns)
     across, beside = spread_line(rest)
 
     pick = jnp.stack([near_slot]).astype(jnp.int32)
     own_rows = (joined, (ROW_TILE, width), lambda r, pick: (r, 0))
     own_x = (joined, (rows, width), lambda r, pick: (0, 0))
     own_y = (joined, (rows, clust), lambda r, pick: (0, width // clust))
-    words = keep_words(pick, rest[None], lambda pick: 0, rows)
+    words = keep_words(pick, rest[None], lambda pick: 0, rows, 1)
     *carry, own_tile = tile_of(pick, own_rows, own_x, own_y, words, lambda pick: 0)
     mine, words, carry, own_tile, rest, across, beside = barrier(
         (scatter(joined), words, carry, own_tile, rest, across, beside)
     )
 
-    both = hub_pieces(mine, hub_ids, full)
-    both, normed, rest, across = barrier((both, normed, rest, across))
+    held, hub_rep = hub_candidates(mine, hub_ids)
+    held, normed, rest, across = barrier((held, normed, rest, across))
 
     outer, middle = along_line(across, OUTWARD), along_line(rest, MIDDLE)
     across_x, beside_x = spread_line(normed)
+    both = hub_share(held, hub_rep, full)
     near = join_pieces(both[:, :, :full])
     at_end = (rep == 0) | (rep == 3)
     group_rest = jnp.stack([rest, beside, across, jnp.where(at_end, outer, middle)], axis=0)
@@ -472,34 +480,26 @@
     pick = jnp.stack(
         [near_slot, place(at), place(second), jnp.where(member_order == core, 2, 3), at, second]
     ).astype(jnp.int32)
-    member_words = keep_words(pick, group_rest, lambda pick: pick[4], rows)
-    near, normed, across_x, beside_x, group_rest, member_words = barrier(
-        (near, normed, across_x, beside_x, group_rest, member_words)
-    )
-
+    member_words = keep_words(pick, group_rest, lambda pick: pick[4], rows, WORDS_HINT)
+    near, group_rest, member_words, pick, normed, across_x, beside_x = barrier(
+        (near, group_rest, member_words, pick, normed, across_x, beside_x)
+    )
+
+    far = swap_cores(near[:, 0])
     outer_x, middle_x = along_line(across_x, OUTWARD), along_line(normed, MIDDLE)
-    chips, _, piece, _ = near.shape
-    near_x = (near, (chips, 1, piece, width), lambda r, pick: (0, 0, 0, 0))
-    near_y = (near, (chips, 1, piece, clust), lambda r, pick: (0, 0, 0, width // clust))
-    far = swap_cores(near[:, 0])
-    *carry, near_tile = tile_of(pick, own_rows, near_x, near_y, words, lambda pick: pick[0], carry)
-    far, carry = barrier((far, carry))
     _, hub_order = flags_of(both[0, 0, full])
     share = hub_rows(jnp.where(hub_order == core, 2, 3)[None], both[0], near, far, width)
     near_new = join_pieces(share).reshape(rows, clust)
-    far_x = (far, (chips, piece, width), lambda r, pick: (0, 0, 0))
-    far_y = (far, (chips, piece, clust), lambda r, pick: (0, 0, width // clust))
-    *carry, far_tile = tile_of(pick, own_rows, far_x, far_y, words, lambda pick: 5 - pick[0], carry)
-    near_new, carry = barrier((near_new, carry))
     far_new = swap_cores(near_new)
-    acc = pair_of((near_tile, far_tile), (near_new, far_new))
-    acc, middle_x, outer_x = barrier((acc, middle_x, outer_x))
-
-    member_tile, degree, new, member_new = member_of(
+    near_new, far_new, outer_x, middle_x = barrier((near_new, far_new, outer_x, middle_x))
+
+    near_tile, far_tile, member_tile, degree, new, member_new = seven_of(
         pick, (normed, beside_x, across_x, middle_x, outer_x), normed, group_rest, near, far, words, member_words,
         carry, indicators,
     )
-    return pair_of((own_tile, member_tile), (new, member_new), (acc, degree, indicators))
+    return last_of(
+        (own_tile, member_tile, near_tile, far_tile), (new, member_new, near_new, far_new), degree, indicators
+    )
 
 
 def solution(mesh):

time: 230 us -> 205 us (0.89)
  waiting for transfers between devices: 73.9 us -> 51.5 us
  blocking collectives: 0 us -> 17 us
  Pallas kernels: 74.1 us -> 60.9 us
  starting transfers between devices: 49.9 us -> 44.8 us
  local copies, waits for them, and re-layouts: 12.9 us -> 9.83 us
    ppermute x14, waiting for transfers between devices: 70.8 us -> 49.6 us  [send(): return lax.ppermute(block, AXES, pairs)]
    all_to_all x0 -> x1, blocking collectives: none -> 17 us  [join_pieces(): lax.all_to_all(repeated, 'slab', 0, 0, axis_index_groups=layers, tiled=True)]
    pallas_call x3 -> x1, Pallas kernels: 20.9 us -> 6.26 us  [tile_of(): pl.pallas_call(functools.partial(tile_kernel, carry is not None, last), o...]
    all_to_all x2 -> x1, starting transfers between devices: 13.3 us -> 6.58 us  [join_pieces(): lax.all_to_all(repeated, 'slab', 0, 0, axis_index_groups=layers, tiled=True)]
    pallas_call x4 -> x3, Pallas kernels: 33.3 us -> 34.7 us  [the longest x1 22.3 us: seven_of(): pl.pallas_call(seven_kernel, out_shape=[jax.ShapeDtypeStruct((rows, cols)...]
  transfers between devices with their start and end apart: 17 -> 16, of which waited for: 11 -> 9; matrix products, arithmetic and copies ran while one was open for 4% -> 5% of each run, Pallas kernels for 20% -> 13%
where the time goes in v6:
time: 205 us; the launch traced here: 201 us
  Pallas kernels  60.9 us (30%)
  waiting for transfers between devices  51.5 us (25%)
  starting transfers between devices  44.8 us (22%)
  blocking collectives  17 us (8%)
  between operations  12.1 us (6%)
  local copies, waits for them, and re-layouts  9.83 us (5%)
  other arithmetic  4.7 us (2%)
    ppermute x14, waiting for transfers between devices, send(): return lax.ppermute(block, AXES, pairs)  49.6 us
    ppermute x14, starting transfers between devices, send(): return lax.ppermute(block, AXES, pairs)  30.5 us
    pallas_call x1, Pallas kernels, seven_of(): pl.pallas_call(seven_kernel, out_shape=[jax.ShapeDtypeStruct((rows, cols)...  22.3 us
    all_to_all x1, blocking collectives, join_pieces(): lax.all_to_all(repeated, 'slab', 0, 0, axis_index_groups=layers, tiled=True)  17 us
    pallas_call x2, Pallas kernels, keep_words(): pl.pallas_call(words_kernel, out_shape=jax.ShapeDtypeStruct((K, rows, LAN...  14.7 us
    all_to_all x1, starting transfers between devices, scatter(): lax.all_to_all(block.reshape(members, rows // members, width), 'slab', 0,...  7.76 us
    pallas_call x1, Pallas kernels, last_of(): pl.pallas_call(last_kernel, out_shape=jax.ShapeDtypeStruct((rows, clust),...  7.25 us
    all_to_all x1, starting transfers between devices, join_pieces(): lax.all_to_all(repeated, 'slab', 0, 0, axis_index_groups=layers, tiled=True)  6.58 us
  transfers between devices with their start and end apart: 16, of which 9 were waited for; matrix products, arithmetic and copies ran while one was open for 5% of the time, Pallas kernels for 13%

profile of v6, /device:TPU:161, one launch (start us, length us, event | category | flops | bytes accessed | tf_op | source)
XLA Modules:
  0.0 200.8 jit_solution(9837993647554979090)
XLA Ops:
  0.0 5.1 %join.1 = (bf16[1024,896]{1,0:T(8,128)(2,1)}, bf16[1024,512]{1,0:T(8,128)(2,1)}, bf16[1296,256]{1,0:T(8,128)(2,1)}) custom-call(s32[4]{0:T(128)} %bitcast.62, bf16[1024,512]{1,0:T(8,128)(2,1)} %x_ref.1, bf16[1024,256]{1,0:T(8,128)(2,1)} %refs_9_.1, s32[4,16,1024]{2,1,0:T(8,128)} %bitcast.61), custom_call_target="tpu_custom_call" | custom-call | tf_op jit(solution)/shard_map/join/pallas_call | solution.py:55
  5.1 7.8 %all-to-all-start = ((bf16[32,32,896]{2,1,0:T(8,128)(2,1)}), bf16[32,32,896]{2,1,0:T(8,128)(2,1)S(1)}, u32[]{:S(2)}, u32[]{:S(2)}) async-start(bf16[32,32,896]{2,1,0:T(8,128)(2,1)} %bitcast.54), calls=%async_computation | async-start | bytes 3670016 | tf_op jit(solution)/shard_map/all_to_all | solution.py:397
  16.2 7.0 %keep_words.2.w_ref.refs_10_ = s32[4,1024,128]{2,1,0:T(8,128)} custom-call(s32[1]{0:T(128)} %bitcast.4.pick_ref, bf16[1,1296,256]{2,1,0:T(8,128)(2,1)} %bitcast.5.coded_ref), custom_call_target="tpu_custom_call" | custom-call | flops 1 | bytes 524288 | tf_op jit(solution)/shard_map/keep_words/pallas_call | solution.py:96
  23.3 6.3 %tile.1 = (f32[1024,128]{1,0:T(8,128)}, f32[1024,256]{1,0:T(8,128)}, bf16[1024,1024]{1,0:T(8,128)(2,1)}) custom-call(s32[1]{0:T(128)} %bitcast.4.pick_ref, bf16[1024,896]{1,0:T(8,128)(2,1)} %get-tuple-element.40.x_ref.other_ref.y_ref, bf16[1024,896]{1,0:T(8,128)(2,1)} %get-tuple-element.40.x_ref.other_ref.y_ref, s32[4,1024,128]{2,1,0:T(8,128)} %keep_words.2.w_ref.refs_10_, ...), custom_call_target="tpu_custom_call" | custom-call | flops 262144 | bytes 262144 | tf_op jit(solution)/shard_map/tile/pallas_call | solution.py:163
  33.8 7.9 %collective-permute-done.1 = bf16[1296,256]{1,0:T(8,128)(2,1)S(1)} collective-permute-done((bf16[1296,256]{1,0:T(8,128)(2,1)}, bf16[1296,256]{1,0:T(8,128)(2,1)S(1)}, u32[]{:S(2)}, u32[]{:S(2)}) %collective-permute-start.1) | collective-permute-done | bytes 663584 | tf_op jit(solution)/shard_map/ppermute | solution.py:357
  41.7 2.6 %collective-permute-done = bf16[1296,256]{1,0:T(8,128)(2,1)} collective-permute-done((bf16[1296,256]{1,0:T(8,128)(2,1)}, bf16[1296,256]{1,0:T(8,128)(2,1)}, u32[]{:S(2)}, u32[]{:S(2)}) %collective-permute-start) | collective-permute-done | bytes 663584 | tf_op jit(solution)/shard_map/ppermute | solution.py:357
  45.1 7.0 %collective-permute-done.2 = bf16[2,32,896]{2,1,0:T(8,128)(2,1)S(1)} collective-permute-done((bf16[2,32,896]{2,1,0:T(8,128)(2,1)S(1)}, bf16[2,32,896]{2,1,0:T(8,128)(2,1)S(1)}, u32[]{:S(2)}, u32[]{:S(2)}) %collective-permute-start.2) | collective-permute-done | bytes 114720 | tf_op jit(solution)/shard_map/ppermute | solution.py:357
  52.2 2.3 %collective-permute-start.3 = (bf16[1,2,32,896]{3,2,1,0:T(8,128)(2,1)S(1)}, bf16[1,2,32,896]{3,2,1,0:T(8,128)(2,1)S(1)}, u32[]{:S(2)}, u32[]{:S(2)}) collective-permute-start(bf16[1,2,32,896]{3,2,1,0:T(8,128)(2,1)S(1)} %select_bitcast_fusion.1), channel_id=1, source_target_pairs={{0,1},{1,0},{2,3},{3,2},{4,5},{5,4},{6,7},{7,6},{8,9},{9,8},{10,11... | collective-permute-start | bytes 344072 | tf_op jit(solution)/shard_map/ppermute | solution.py:357
  54.4 2.2 %collective-permute-done.3 = bf16[1,2,32,896]{3,2,1,0:T(8,128)(2,1)S(1)} collective-permute-done((bf16[1,2,32,896]{3,2,1,0:T(8,128)(2,1)S(1)}, bf16[1,2,32,896]{3,2,1,0:T(8,128)(2,1)S(1)}, u32[]{:S(2)}, u32[]{:S(2)}) %collective-permute-start.3) | collective-permute-done | bytes 114720 | tf_op jit(solution)/shard_map/ppermute | solution.py:357
  56.8 1.8 collective-permute-start.4
  63.0 4.4 %collective-permute-done.4 = bf16[2,2,32,896]{3,2,1,0:T(8,128)(2,1)S(1)} collective-permute-done((bf16[2,2,32,896]{3,2,1,0:T(8,128)(2,1)S(1)}, bf16[2,2,32,896]{3,2,1,0:T(8,128)(2,1)S(1)}, u32[]{:S(2)}, u32[]{:S(2)}) %collective-permute-start.4) | collective-permute-done | bytes 229408 | tf_op jit(solution)/shard_map/ppermute | solution.py:357
  70.0 1.9 collective-permute-start.7
  72.0 2.1 %collective-permute-start.6 = (bf16[1296,256]{1,0:T(8,128)(2,1)}, bf16[1296,256]{1,0:T(8,128)(2,1)}, u32[]{:S(2)}, u32[]{:S(2)}) collective-permute-start(bf16[1296,256]{1,0:T(8,128)(2,1)} %collective-permute-done), channel_id=1, source_target_pairs={{1,0},{2,3},{5,4},{6,7},{9,8},{10,11},{13,12},{14,15},{17,16},{18,... | collective-permute-start | bytes 1990664 | tf_op jit(solution)/shard_map/ppermute | solution.py:357
  74.2 4.9 %collective-permute-start.5 = (bf16[2,32,896]{2,1,0:T(8,128)(2,1)S(1)}, bf16[2,32,896]{2,1,0:T(8,128)(2,1)S(1)}, u32[]{:S(2)}, u32[]{:S(2)}) collective-permute-start(bf16[2,32,896]{2,1,0:T(8,128)(2,1)S(1)} %broadcast_select_fusion.6), channel_id=1, source_target_pairs={{0,4},{1,5},{2,6},{3,7},{4,0},{5,1},{6,2},{7,3},{8,12},{9,13},{10,... | collective-permute-start | bytes 344072 | tf_op jit(solution)/shard_map/ppermute | solution.py:357
  79.9 2.0 %collective-permute-start.8 = (bf16[1024,512]{1,0:T(8,128)(2,1)}, bf16[1024,512]{1,0:T(8,128)(2,1)}, u32[]{:S(2)}, u32[]{:S(2)}) collective-permute-start(bf16[1024,512]{1,0:T(8,128)(2,1)} %get-tuple-element.56.refs_0_.refs_5_), channel_id=1, source_target_pairs={{0,2},{1,3},{2,0},{3,1},{4,6},{5,7},{6,4},{7,5},{8,10},{9,11},{10,... | collective-permute-start | bytes 3145736 | tf_op jit(solution)/shard_map/ppermute | solution.py:357
  82.0 2.0 broadcast_in_dim.90
  84.0 6.6 %all-to-all-start.1 = ((bf16[16,2,64,768]{3,2,1,0:T(8,128)(2,1)}), bf16[16,2,64,768]{3,2,1,0:T(8,128)(2,1)S(1)}, u32[]{:S(2)}, u32[]{:S(2)}) async-start(bf16[16,2,64,768]{3,2,1,0:T(8,128)(2,1)} %broadcast_in_dim.90), calls=%async_computation.1 | async-start | bytes 6291456 | tf_op jit(solution)/shard_map/all_to_all | solution.py:380
  91.8 1.8 pad_maximum_fusion.coded_ref.refs_6_.refs_7_
  93.6 1.5 copy-done.1
  97.5 7.7 %keep_words.3.refs_11_ = s32[4,1024,128]{2,1,0:T(8,128)} custom-call(s32[6]{0:T(128)} %stack.66.pick_ref, bf16[4,1296,256]{2,1,0:T(8,128)(2,1)} %copy-done.1), custom_call_target="tpu_custom_call" | custom-call | flops 30000001024 | bytes 524288 | tf_op jit(solution)/shard_map/keep_words/pallas_call | solution.py:96
  105.2 17.3 %collective-permute-done.9.refs_1_ = bf16[1024,512]{1,0:T(8,128)(2,1)} collective-permute-done((bf16[1024,512]{1,0:T(8,128)(2,1)}, bf16[1024,512]{1,0:T(8,128)(2,1)}, u32[]{:S(2)}, u32[]{:S(2)}) %collective-permute-start.9) | collective-permute-done | bytes 1048608 | tf_op jit(solution)/shard_map/ppermute | solution.py:357
  122.5 6.5 %collective-permute-done.8.refs_2_ = bf16[1024,512]{1,0:T(8,128)(2,1)} collective-permute-done((bf16[1024,512]{1,0:T(8,128)(2,1)}, bf16[1024,512]{1,0:T(8,128)(2,1)}, u32[]{:S(2)}, u32[]{:S(2)}) %collective-permute-start.8) | collective-permute-done | bytes 1048608 | tf_op jit(solution)/shard_map/ppermute | solution.py:357
  129.0 2.0 all-to-all-done.1.near_ref.refs_8_
  132.4 2.9 %collective-permute-start.10 = (bf16[16,64,768]{2,1,0:T(8,128)(2,1)}, bf16[16,64,768]{2,1,0:T(8,128)(2,1)}, u32[]{:S(2)}, u32[]{:S(2)}) collective-permute-start(bf16[16,64,768]{2,1,0:T(8,128)(2,1)} %slice_bitcast_fusion), channel_id=1, source_target_pairs={{0,4},{1,5},{2,6},{3,7},{4,0},{5,1},{6,2},{7,3},{8,12},{9,13},{10,... | collective-permute-start | bytes 4718600 | tf_op jit(solution)/shard_map/ppermute | solution.py:357
  135.3 5.2 %collective-permute-start.13 = (bf16[1024,512]{1,0:T(8,128)(2,1)}, bf16[1024,512]{1,0:T(8,128)(2,1)}, u32[]{:S(2)}, u32[]{:S(2)}) collective-permute-start(bf16[1024,512]{1,0:T(8,128)(2,1)} %get-tuple-element.56.refs_0_.refs_5_), channel_id=1, source_target_pairs={{1,2},{2,1},{5,6},{6,5},{9,10},{10,9},{13,14},{14,13},{17,18},{18,... | collective-permute-start | bytes 3145736 | tf_op jit(solution)/shard_map/ppermute | solution.py:357
  140.5 2.3 %collective-permute-start.12 = (bf16[1024,512]{1,0:T(8,128)(2,1)}, bf16[1024,512]{1,0:T(8,128)(2,1)}, u32[]{:S(2)}, u32[]{:S(2)}) collective-permute-start(bf16[1024,512]{1,0:T(8,128)(2,1)} %collective-permute-done.8.refs_2_), channel_id=1, source_target_pairs={{1,0},{2,3},{5,4},{6,7},{9,8},{10,11},{13,12},{14,15},{17,16},{18,... | collective-permute-start | bytes 3145736 | tf_op jit(solution)/shard_map/ppermute | solution.py:357
  144.6 5.2 %hub_rows.1 = bf16[64,256]{1,0:T(8,128)(2,1)} custom-call(s32[1]{0:T(128)} %bitcast.40.pick_ref, bf16[64,896]{1,0:T(8,128)(2,1)} %fusion.1.rows_ref, bf16[16,2,64,768]{3,2,1,0:T(8,128)(2,1)} %copy-done, bf16[16,64,768]{2,1,0:T(8,128)(2,1)} %collective-permute-done.10.far_ref.refs_9_), custom_call_target="tpu_custom_call" | custom-call | flops 1024 | bytes 1024 | tf_op jit(solution)/shard_map/hub_rows/pallas_call | solution.py:328
  150.6 17.0 %all_to_all.15 = bf16[16,64,256]{2,1,0:T(8,128)(2,1)S(1)} all-to-all(bf16[16,64,256]{2,1,0:T(8,128)(2,1)S(1)} %broadcast_in_dim.92), channel_id=1, replica_groups={{0,8,16,24,32,40,48,56,64,72,80,88,96,104,112,120},{4,12,20,28,36,44,52..., dimensions={0} | all-to-all | bytes 1048576 | tf_op jit(solution)/shard_map/all_to_all | solution.py:380
  167.6 2.1 %collective-permute-start.11 = (bf16[1024,256]{1,0:T(8,128)(2,1)S(1)}, bf16[1024,256]{1,0:T(8,128)(2,1)S(1)}, u32[]{:S(2)}, u32[]{:S(2)}) collective-permute-start(bf16[1024,256]{1,0:T(8,128)(2,1)S(1)} %bitcast.55), channel_id=1, source_target_pairs={{0,4},{1,5},{2,6},{3,7},{4,0},{5,1},{6,2},{7,3},{8,12},{9,13},{10,... | collective-permute-start | bytes 1572872 | tf_op jit(solution)/shard_map/ppermute | solution.py:357
  169.7 1.5 collective-permute-done.11.refs_7_
  171.2 22.3 %seven.1 = (bf16[1024,1024]{1,0:T(8,128)(2,1)}, bf16[1024,1024]{1,0:T(8,128)(2,1)}, bf16[1024,1024]{1,0:T(8,128)(2,1)}, f32[1024,128]{1,0:T(8,128)}, bf16[1024,2...) custom-call(s32[6]{0:T(128)} %stack.66.pick_ref, bf16[1024,512]{1,0:T(8,128)(2,1)} %get-tuple-element.56.refs_0_.refs_5_, ...), custom_call_target="tpu_custom_call" | custom-call | flops 11274289152 | bytes 16777216 | tf_op jit(solution)/shard_map/seven/pallas_call | solution.py:240
  193.6 7.2 %last.1 = bf16[1024,256]{1,0:T(8,128)(2,1)} custom-call(bf16[1024,1024]{1,0:T(8,128)(2,1)} %get-tuple-element.45.refs_0_, bf16[1024,1024]{1,0:T(8,128)(2,1)} %get-tuple-element.67.refs_1_, bf16[1024,1024]{1,0:T(8,128)(2,1)} %get-tuple-element.68.refs_2_, bf16[1024,1024]{1,0:T(8,128)(2,1)} %get-tuple-element.69.refs_3_, ...), custom_call_target="tpu_custom_call" | custom-call | flops 2147483648 | bytes 8388608 | tf_op jit(solution)/shard_map/last/pallas_call | solution.py:281
  (54 shorter events, 12.1 us)
Async XLA Ops:
  0.0 14.9 %copy-start.5 = (s32[1,4]{1,0:T(1,128)S(1)}, s32[1,4]{1,0:T(1,128)}, u32[]{:S(2)}) copy-start(s32[1,4]{1,0:T(1,128)} %param.7) | copy-start | bytes 52
  5.1 39.2 %all-to-all-start = ((bf16[32,32,896]{2,1,0:T(8,128)(2,1)}), bf16[32,32,896]{2,1,0:T(8,128)(2,1)S(1)}, u32[]{:S(2)}, u32[]{:S(2)}) async-start(bf16[32,32,896]{2,1,0:T(8,128)(2,1)} %bitcast.54), calls=%async_computation | async-start | bytes 3670016 | tf_op jit(solution)/shard_map/all_to_all | solution.py:397
  12.9 28.8 %collective-permute-start.1 = (bf16[1296,256]{1,0:T(8,128)(2,1)}, bf16[1296,256]{1,0:T(8,128)(2,1)S(1)}, u32[]{:S(2)}, u32[]{:S(2)}) collective-permute-start(bf16[1296,256]{1,0:T(8,128)(2,1)} %get-tuple-element.51), channel_id=1, source_target_pairs={{0,1},{1,0},{2,3},{3,2},{4,5},{5,4},{6,7},{7,6},{8,9},{9,8},{10,11... | collective-permute-start | bytes 1990664 | tf_op jit(solution)/shard_map/ppermute | solution.py:357
  13.7 30.6 %collective-permute-start = (bf16[1296,256]{1,0:T(8,128)(2,1)}, bf16[1296,256]{1,0:T(8,128)(2,1)}, u32[]{:S(2)}, u32[]{:S(2)}) collective-permute-start(bf16[1296,256]{1,0:T(8,128)(2,1)} %get-tuple-element.51), channel_id=1, source_target_pairs={{0,2},{1,3},{2,0},{3,1},{4,6},{5,7},{6,4},{7,5},{8,10},{9,11},{10,... | collective-permute-start | bytes 1990664 | tf_op jit(solution)/shard_map/ppermute | solution.py:357
  23.3 6.3 %copy-start.6 = (s32[2]{0:T(128)S(1)}, s32[2]{0:T(128)}, u32[]{:S(2)}) copy-start(s32[2]{0:T(128)} %param.8) | copy-start | bytes 28
  41.7 2.7 %copy-start.3 = (bf16[1296,256]{1,0:T(8,128)(2,1)}, bf16[1296,256]{1,0:T(8,128)(2,1)S(1)}, u32[]{:S(2)}) copy-start(bf16[1296,256]{1,0:T(8,128)(2,1)S(1)} %collective-permute-done.1) | copy-start | bytes 1990660
  44.3 7.7 %collective-permute-start.2 = (bf16[2,32,896]{2,1,0:T(8,128)(2,1)S(1)}, bf16[2,32,896]{2,1,0:T(8,128)(2,1)S(1)}, u32[]{:S(2)}, u32[]{:S(2)}) collective-permute-start(bf16[2,32,896]{2,1,0:T(8,128)(2,1)S(1)} %pad_maximum_fusion.4), channel_id=1, source_target_pairs={{0,128},{1,129},{2,130},{3,131},{4,132},{5,133},{6,134},{7,135},{8... | collective-permute-start | bytes 344072 | tf_op jit(solution)/shard_map/ppermute | solution.py:357
  52.2 4.5 %collective-permute-start.3 = (bf16[1,2,32,896]{3,2,1,0:T(8,128)(2,1)S(1)}, bf16[1,2,32,896]{3,2,1,0:T(8,128)(2,1)S(1)}, u32[]{:S(2)}, u32[]{:S(2)}) collective-permute-start(bf16[1,2,32,896]{3,2,1,0:T(8,128)(2,1)S(1)} %select_bitcast_fusion.1), channel_id=1, source_target_pairs={{0,1},{1,0},{2,3},{3,2},{4,5},{5,4},{6,7},{7,6},{8,9},{9,8},{10,11... | collective-permute-start | bytes 344072 | tf_op jit(solution)/shard_map/ppermute | solution.py:357
  56.8 10.7 %collective-permute-start.4 = (bf16[2,2,32,896]{3,2,1,0:T(8,128)(2,1)S(1)}, bf16[2,2,32,896]{3,2,1,0:T(8,128)(2,1)S(1)}, u32[]{:S(2)}, u32[]{:S(2)}) collective-permute-start(bf16[2,2,32,896]{3,2,1,0:T(8,128)(2,1)S(1)} %pad_maximum_fusion.2), channel_id=1, source_target_pairs={{0,2},{1,3},{2,0},{3,1},{4,6},{5,7},{6,4},{7,5},{8,10},{9,11},{10,... | collective-permute-start | bytes 688136 | tf_op jit(solution)/shard_map/ppermute | solution.py:357
  70.0 20.5 %collective-permute-start.7 = (bf16[1296,256]{1,0:T(8,128)(2,1)}, bf16[1296,256]{1,0:T(8,128)(2,1)}, u32[]{:S(2)}, u32[]{:S(2)}) collective-permute-start(bf16[1296,256]{1,0:T(8,128)(2,1)} %get-tuple-element.51), channel_id=1, source_target_pairs={{1,2},{2,1},{5,6},{6,5},{9,10},{10,9},{13,14},{14,13},{17,18},{18,... | collective-permute-start | bytes 1990664 | tf_op jit(solution)/shard_map/ppermute | solution.py:357
  72.0 18.6 %collective-permute-start.6 = (bf16[1296,256]{1,0:T(8,128)(2,1)}, bf16[1296,256]{1,0:T(8,128)(2,1)}, u32[]{:S(2)}, u32[]{:S(2)}) collective-permute-start(bf16[1296,256]{1,0:T(8,128)(2,1)} %collective-permute-done), channel_id=1, source_target_pairs={{1,0},{2,3},{5,4},{6,7},{9,8},{10,11},{13,12},{14,15},{17,16},{18,... | collective-permute-start | bytes 1990664 | tf_op jit(solution)/shard_map/ppermute | solution.py:357
  74.2 7.8 %collective-permute-start.5 = (bf16[2,32,896]{2,1,0:T(8,128)(2,1)S(1)}, bf16[2,32,896]{2,1,0:T(8,128)(2,1)S(1)}, u32[]{:S(2)}, u32[]{:S(2)}) collective-permute-start(bf16[2,32,896]{2,1,0:T(8,128)(2,1)S(1)} %broadcast_select_fusion.6), channel_id=1, source_target_pairs={{0,4},{1,5},{2,6},{3,7},{4,0},{5,1},{6,2},{7,3},{8,12},{9,13},{10,... | collective-permute-start | bytes 344072 | tf_op jit(solution)/shard_map/ppermute | solution.py:357
  79.8 42.7 %collective-permute-start.9 = (bf16[1024,512]{1,0:T(8,128)(2,1)}, bf16[1024,512]{1,0:T(8,128)(2,1)}, u32[]{:S(2)}, u32[]{:S(2)}) collective-permute-start(bf16[1024,512]{1,0:T(8,128)(2,1)} %get-tuple-element.56.refs_0_.refs_5_), channel_id=1, source_target_pairs={{0,1},{1,0},{2,3},{3,2},{4,5},{5,4},{6,7},{7,6},{8,9},{9,8},{10,11... | collective-permute-start | bytes 3145736 | tf_op jit(solution)/shard_map/ppermute | solution.py:357
  79.9 49.1 %collective-permute-start.8 = (bf16[1024,512]{1,0:T(8,128)(2,1)}, bf16[1024,512]{1,0:T(8,128)(2,1)}, u32[]{:S(2)}, u32[]{:S(2)}) collective-permute-start(bf16[1024,512]{1,0:T(8,128)(2,1)} %get-tuple-element.56.refs_0_.refs_5_), channel_id=1, source_target_pairs={{0,2},{1,3},{2,0},{3,1},{4,6},{5,7},{6,4},{7,5},{8,10},{9,11},{10,... | collective-permute-start | bytes 3145736 | tf_op jit(solution)/shard_map/ppermute | solution.py:357
  84.0 47.0 %all-to-all-start.1 = ((bf16[16,2,64,768]{3,2,1,0:T(8,128)(2,1)}), bf16[16,2,64,768]{3,2,1,0:T(8,128)(2,1)S(1)}, u32[]{:S(2)}, u32[]{:S(2)}) async-start(bf16[16,2,64,768]{3,2,1,0:T(8,128)(2,1)} %broadcast_in_dim.90), calls=%async_computation.1 | async-start | bytes 6291456 | tf_op jit(solution)/shard_map/all_to_all | solution.py:380
  93.6 1.5 copy-start.1
  131.0 13.6 %copy-start = (bf16[16,2,64,768]{3,2,1,0:T(8,128)(2,1)}, bf16[16,2,64,768]{3,2,1,0:T(8,128)(2,1)S(1)}, u32[]{:S(2)}) copy-start(bf16[16,2,64,768]{3,2,1,0:T(8,128)(2,1)S(1)} %all-to-all-done.1.near_ref.refs_8_) | copy-start | bytes 9437188
  132.4 12.2 %collective-permute-start.10 = (bf16[16,64,768]{2,1,0:T(8,128)(2,1)}, bf16[16,64,768]{2,1,0:T(8,128)(2,1)}, u32[]{:S(2)}, u32[]{:S(2)}) collective-permute-start(bf16[16,64,768]{2,1,0:T(8,128)(2,1)} %slice_bitcast_fusion), channel_id=1, source_target_pairs={{0,4},{1,5},{2,6},{3,7},{4,0},{5,1},{6,2},{7,3},{8,12},{9,13},{10,... | collective-permute-start | bytes 4718600 | tf_op jit(solution)/shard_map/ppermute | solution.py:357
  135.3 34.4 %collective-permute-start.13 = (bf16[1024,512]{1,0:T(8,128)(2,1)}, bf16[1024,512]{1,0:T(8,128)(2,1)}, u32[]{:S(2)}, u32[]{:S(2)}) collective-permute-start(bf16[1024,512]{1,0:T(8,128)(2,1)} %get-tuple-element.56.refs_0_.refs_5_), channel_id=1, source_target_pairs={{1,2},{2,1},{5,6},{6,5},{9,10},{10,9},{13,14},{14,13},{17,18},{18,... | collective-permute-start | bytes 3145736 | tf_op jit(solution)/shard_map/ppermute | solution.py:357
  140.5 29.2 %collective-permute-start.12 = (bf16[1024,512]{1,0:T(8,128)(2,1)}, bf16[1024,512]{1,0:T(8,128)(2,1)}, u32[]{:S(2)}, u32[]{:S(2)}) collective-permute-start(bf16[1024,512]{1,0:T(8,128)(2,1)} %collective-permute-done.8.refs_2_), channel_id=1, source_target_pairs={{1,0},{2,3},{5,4},{6,7},{9,8},{10,11},{13,12},{14,15},{17,16},{18,... | collective-permute-start | bytes 3145736 | tf_op jit(solution)/shard_map/ppermute | solution.py:357
  167.6 26.0 %copy-start.2 = (bf16[16,64,256]{2,1,0:T(8,128)(2,1)}, bf16[16,64,256]{2,1,0:T(8,128)(2,1)S(1)}, u32[]{:S(2)}) copy-start(bf16[16,64,256]{2,1,0:T(8,128)(2,1)S(1)} %all_to_all.15) | copy-start | bytes 1572868
  167.6 3.6 %collective-permute-start.11 = (bf16[1024,256]{1,0:T(8,128)(2,1)S(1)}, bf16[1024,256]{1,0:T(8,128)(2,1)S(1)}, u32[]{:S(2)}, u32[]{:S(2)}) collective-permute-start(bf16[1024,256]{1,0:T(8,128)(2,1)S(1)} %bitcast.55), channel_id=1, source_target_pairs={{0,4},{1,5},{2,6},{3,7},{4,0},{5,1},{6,2},{7,3},{8,12},{9,13},{10,... | collective-permute-start | bytes 1572872 | tf_op jit(solution)/shard_map/ppermute | solution.py:357
  171.2 22.3 %copy-start.4 = (bf16[1024,256]{1,0:T(8,128)(2,1)}, bf16[1024,256]{1,0:T(8,128)(2,1)S(1)}, u32[]{:S(2)}) copy-start(bf16[1024,256]{1,0:T(8,128)(2,1)S(1)} %collective-permute-done.11.refs_7_) | copy-start | bytes 1572868

commit v7 on v6

--- a/solution.py
+++ b/solution.py
@@ -176,11 +176,68 @@
     )(pick, *args)
 
 
-def seven_kernel(pick_ref, *refs):
+def put_to(ref):
+    def put(lanes, value):
+        ref[:, lanes] = value
+
+    return put
+
+
+def run_tiles(rows, plan, total, acc):
+    for word, (other, y), tile in plan:
+        total = weights(cosines(rows, other), word, total, put_to(tile))
+        acc = acc + jnp.dot(tile[...], y, preferred_element_type=jnp.float32)
+    return total, acc
+
+
+def hub_blocks(near_ref, far_ref, width):
+    near, far = near_ref[:, 0].reshape(-1, near_ref.shape[3]), flat(far_ref)
+    return (near[:, :width], near[:, width:]), (far[:, :width], far[:, width:])
+
+
+def hub_specs(near, far):
+    chips, _, piece, full = near.shape
+    once = pl.Buffered(1)
+    return [
+        pl.BlockSpec((chips, 1, piece, full), lambda r, pick: (0, 0, 0, 0), pipeline_mode=once),
+        pl.BlockSpec((chips, piece, full), lambda r, pick: (0, 0, 0), pipeline_mode=once),
+    ]
+
+
+def two_kernel(pick_ref, rows_ref, near_ref, far_ref, words_ref, deg_in, acc_in, near_tile, far_tile, deg_ref, acc_ref):
+    near, far = hub_blocks(near_ref, far_ref, rows_ref.shape[1])
+    plan = (
+        (words_ref[pick_ref[0]], near, near_tile),
+        (words_ref[5 - pick_ref[0]], far, far_tile),
+    )
+    deg_ref[...], acc_ref[...] = run_tiles(rows_ref[...], plan, deg_in[...], acc_in[...])
+
+
+def two_of(pick, own_rows, near, far, words, carry):
+    rows, width = own_rows.shape
+    clust = carry[1].shape[1]
+    by_row = lambda cols: pl.BlockSpec((ROW_TILE, cols), lambda r, pick: (r, 0))
+    by_word = pl.BlockSpec((K, ROW_TILE, LANES), lambda r, pick: (0, r, 0))
+    outs = [(rows, jnp.bfloat16)] * 2 + [(LANES, jnp.float32), (clust, jnp.float32)]
+    return pl.pallas_call(
+        two_kernel,
+        out_shape=[jax.ShapeDtypeStruct((rows, cols), kind) for cols, kind in outs],
+        grid_spec=pltpu.PrefetchScalarGridSpec(
+            num_scalar_prefetch=1,
+            grid=(rows // ROW_TILE,),
+            in_specs=[by_row(width), *hub_specs(near, far), by_word, by_row(LANES), by_row(clust)],
+            out_specs=[by_row(cols) for cols, _ in outs],
+        ),
+        compiler_params=pltpu.CompilerParams(vmem_limit_bytes=VMEM_LIMIT),
+        cost_estimate=pl.CostEstimate(flops=rows * clust, bytes_accessed=rows * clust, transcendentals=0),
+        name="two",
+    )(pick, own_rows, near, far, words, *carry)
+
+
+def five_kernel(pick_ref, *refs):
     blocks, refs = refs[:BLOCKS_NEAR], refs[BLOCKS_NEAR:]
-    rows_ref, first_y, second_y, near_ref, far_ref, words_ref, member_ref, deg_in, acc_in, anchor_ref = refs[:10]
-    near_tile, far_tile, member_tile, deg_ref, new_ref, other_ref, first_x, second_x, held, spare, sems = refs[10:]
-    width = rows_ref.shape[1]
+    rows_ref, first_y, second_y, near_ref, far_ref, own_ref, member_ref, deg_in, acc_in, anchor_ref = refs[:10]
+    member_tile, deg_ref, new_ref, other_ref, first_x, second_x, held, spare, sems = refs[10:]
     step = pl.program_id(0)
 
     @pl.when(step == 0)
@@ -194,27 +251,9 @@
                     copy.start()
                     copy.wait()
 
-    def put_to(ref):
-        def put(lanes, value):
-            ref[:, lanes] = value
-
-        return put
-
-    def run(rows, plan, total, acc):
-        for word, (other, y), tile in plan:
-            total = weights(cosines(rows, other), word, total, put_to(tile))
-            acc = acc + jnp.dot(tile[...], y, preferred_element_type=jnp.float32)
-        return total, acc
-
-    split = lambda block: (block[:, :width], block[:, width:])
     first, second = (first_x[...], first_y[0]), (second_x[...], second_y[0])
-    near, far = split(near_ref[:, 0].reshape(-1, near_ref.shape[3])), split(flat(far_ref))
-    plan = (
-        (words_ref[pick_ref[0]], near, near_tile),
-        (words_ref[5 - pick_ref[0]], far, far_tile),
-        (words_ref[1], first, member_tile),
-    )
-    total, acc = run(rows_ref[...], plan, deg_in[...], acc_in[...])
+    near, far = hub_blocks(near_ref, far_ref, rows_ref.shape[1])
+    total, acc = run_tiles(rows_ref[...], ((own_ref[0], first, member_tile),), deg_in[...], acc_in[...])
     deg_ref[...] = total
     new_ref[...] = mix(acc, jnp.sum(total, axis=1, keepdims=True), anchor_ref[...])
     here = pl.ds(pl.multiple_of(step * ROW_TILE, ROW_TILE), ROW_TILE)
@@ -224,34 +263,30 @@
         (member_ref[0], first, held),
         (member_ref[1], second, spare),
     )
-    total, acc = run(first_x[here, :], plan, jnp.zeros(deg_in.shape, jnp.float32), jnp.zeros(acc_in.shape, jnp.float32))
+    zeros = lambda ref: jnp.zeros(ref.shape, jnp.float32)
+    total, acc = run_tiles(first_x[here, :], plan, zeros(deg_in), zeros(acc_in))
     other_ref[...] = mix(acc, jnp.sum(total, axis=1, keepdims=True), first_y[0, here, :])
 
 
-def seven_of(pick, blocks, own_rows, rest, near, far, words, member_words, carry, anchor):
+def five_of(pick, blocks, own_rows, rest, near, far, words, member_words, carry, anchor):
     rows, width = blocks[0].shape
     clust = rest.shape[2]
-    chips, _, piece, full = near.shape
-    once = pl.Buffered(1)
     by_row = lambda cols: pl.BlockSpec((ROW_TILE, cols), lambda r, pick: (r, 0))
-    rest_at = lambda k: pl.BlockSpec((1, rows, clust), lambda r, pick: (pick[k], 0, 0), pipeline_mode=once)
-    by_word = pl.BlockSpec((K, ROW_TILE, LANES), lambda r, pick: (0, r, 0))
-    outs = [(rows, jnp.bfloat16)] * 3 + [(LANES, jnp.float32)] + [(clust, jnp.bfloat16)] * 2
-    return pl.pallas_call(
-        seven_kernel,
+    rest_at = lambda k: pl.BlockSpec(
+        (1, rows, clust), lambda r, pick: (pick[k], 0, 0), pipeline_mode=pl.Buffered(1)
+    )
+    outs = [(rows, jnp.bfloat16), (LANES, jnp.float32)] + [(clust, jnp.bfloat16)] * 2
+    return pl.pallas_call(
+        five_kernel,
         out_shape=[jax.ShapeDtypeStruct((rows, cols), kind) for cols, kind in outs],
         grid_spec=pltpu.PrefetchScalarGridSpec(
             num_scalar_prefetch=1,
             grid=(rows // ROW_TILE,),
             in_specs=[pl.BlockSpec(memory_space=pl.ANY)] * len(blocks)
+            + [by_row(width), rest_at(4), rest_at(5), *hub_specs(near, far)]
             + [
-                by_row(width),
-                rest_at(4),
-                rest_at(5),
-                pl.BlockSpec((chips, 1, piece, full), lambda r, pick: (0, 0, 0, 0), pipeline_mode=once),
-                pl.BlockSpec((chips, piece, full), lambda r, pick: (0, 0, 0), pipeline_mode=once),
-                by_word,
-                by_word,
+                pl.BlockSpec((1, ROW_TILE, LANES), lambda r, pick: (1, r, 0)),
+                pl.BlockSpec((K, ROW_TILE, LANES), lambda r, pick: (0, r, 0)),
                 by_row(LANES),
                 by_row(clust),
                 by_row(clust),
@@ -263,9 +298,9 @@
         ),
         compiler_params=pltpu.CompilerParams(vmem_limit_bytes=VMEM_LIMIT),
         cost_estimate=pl.CostEstimate(
-            flops=14 * rows * rows * full, bytes_accessed=16 * rows * rows, transcendentals=7 * rows * rows
-        ),
-        name="seven",
+            flops=10 * rows * rows * 768, bytes_accessed=8 * rows * rows, transcendentals=5 * rows * rows
+        ),
+        name="five",
     )(pick, *blocks, own_rows, rest, rest, near, far, words, member_words, *carry, anchor)
 
 
@@ -489,11 +524,14 @@
     outer_x, middle_x = along_line(across_x, OUTWARD), along_line(normed, MIDDLE)
     _, hub_order = flags_of(both[0, 0, full])
     share = hub_rows(jnp.where(hub_order == core, 2, 3)[None], both[0], near, far, width)
+    share, near, far = barrier((share, near, far))
     near_new = join_pieces(share).reshape(rows, clust)
+    near_tile, far_tile, *carry = two_of(pick, normed, near, far, words, carry)
+    near_new, carry = barrier((near_new, carry))
     far_new = swap_cores(near_new)
     near_new, far_new, outer_x, middle_x = barrier((near_new, far_new, outer_x, middle_x))
 
-    near_tile, far_tile, member_tile, degree, new, member_new = seven_of(
+    member_tile, degree, new, member_new = five_of(
         pick, (normed, beside_x, across_x, middle_x, outer_x), normed, group_rest, near, far, words, member_words,
         carry, indicators,
     )

time: 205 us -> 202 us (0.985)
  blocking collectives: 17 us -> 0 us
  starting transfers between devices: 44.8 us -> 53.8 us
  Pallas kernels: 60.9 us -> 65.8 us
    all_to_all x1 -> x0, blocking collectives: 17 us -> none  [join_pieces(): lax.all_to_all(repeated, 'slab', 0, 0, axis_index_groups=layers, tiled=True)]
    all_to_all x1 -> x2, starting transfers between devices: 6.58 us -> 12.4 us  [join_pieces(): lax.all_to_all(repeated, 'slab', 0, 0, axis_index_groups=layers, tiled=True)]
    pallas_call x1 -> x2, Pallas kernels: 22.3 us -> 27.3 us  [the longest x1 18.2 us: five_of(): pl.pallas_call(five_kernel, out_shape=[jax.ShapeDtypeStruct((rows, cols),...]
    ppermute x14, starting transfers between devices: 30.5 us -> 33.6 us  [send(): return lax.ppermute(block, AXES, pairs)]
  transfers between devices with their start and end apart: 16 -> 17, of which waited for: 9 -> 10; matrix products, arithmetic and copies ran while one was open for 5% -> 5% of each run, Pallas kernels for 13% -> 18%
where the time goes in v7:
time: 202 us; the launch traced here: 200 us
  Pallas kernels  65.8 us (33%)
  starting transfers between devices  53.8 us (27%)
  waiting for transfers between devices  52.7 us (26%)
  between operations  12.1 us (6%)
  local copies, waits for them, and re-layouts  10.6 us (5%)
  other arithmetic  4.71 us (2%)
    ppermute x14, waiting for transfers between devices, send(): return lax.ppermute(block, AXES, pairs)  49.7 us
    ppermute x14, starting transfers between devices, send(): return lax.ppermute(block, AXES, pairs)  33.6 us
    pallas_call x1, Pallas kernels, five_of(): pl.pallas_call(five_kernel, out_shape=[jax.ShapeDtypeStruct((rows, cols),...  18.2 us
    pallas_call x2, Pallas kernels, keep_words(): pl.pallas_call(words_kernel, out_shape=jax.ShapeDtypeStruct((K, rows, LAN...  14.7 us
    all_to_all x2, starting transfers between devices, join_pieces(): lax.all_to_all(repeated, 'slab', 0, 0, axis_index_groups=layers, tiled=True)  12.4 us
    pallas_call x1, Pallas kernels, two_of(): pl.pallas_call(two_kernel, out_shape=[jax.ShapeDtypeStruct((rows, cols),...  9.11 us
    all_to_all x1, starting transfers between devices, scatter(): lax.all_to_all(block.reshape(members, rows // members, width), 'slab', 0,...  7.76 us
    pallas_call x1, Pallas kernels, last_of(): pl.pallas_call(last_kernel, out_shape=jax.ShapeDtypeStruct((rows, clust),...  7.26 us
  transfers between devices with their start and end apart: 17, of which 10 were waited for; matrix products, arithmetic and copies ran while one was open for 5% of the time, Pallas kernels for 18%

profile of v7, /device:TPU:161, one launch (start us, length us, event | category | flops | bytes accessed | tf_op | source)
XLA Modules:
  0.0 199.8 jit_solution(7625416932854782531)
XLA Ops:
  0.0 5.1 %join.1 = (bf16[1024,896]{1,0:T(8,128)(2,1)}, bf16[1024,512]{1,0:T(8,128)(2,1)}, bf16[1296,256]{1,0:T(8,128)(2,1)}) custom-call(s32[4]{0:T(128)} %bitcast.62, bf16[1024,512]{1,0:T(8,128)(2,1)} %x_ref.1, bf16[1024,256]{1,0:T(8,128)(2,1)} %refs_9_.1, s32[4,16,1024]{2,1,0:T(8,128)} %bitcast.61), custom_call_target="tpu_custom_call" | custom-call | tf_op jit(solution)/shard_map/join/pallas_call | solution.py:55
  5.1 7.8 %all-to-all-start = ((bf16[32,32,896]{2,1,0:T(8,128)(2,1)}), bf16[32,32,896]{2,1,0:T(8,128)(2,1)S(1)}, u32[]{:S(2)}, u32[]{:S(2)}) async-start(bf16[32,32,896]{2,1,0:T(8,128)(2,1)} %bitcast.54), calls=%async_computation | async-start | bytes 3670016 | tf_op jit(solution)/shard_map/all_to_all | solution.py:432
  16.2 7.1 %keep_words.2.w_ref.words_ref.refs_10_ = s32[4,1024,128]{2,1,0:T(8,128)} custom-call(s32[1]{0:T(128)} %bitcast.4.pick_ref, bf16[1,1296,256]{2,1,0:T(8,128)(2,1)} %bitcast.5.coded_ref), custom_call_target="tpu_custom_call" | custom-call | flops 1 | bytes 524288 | tf_op jit(solution)/shard_map/keep_words/pallas_call | solution.py:96
  23.2 6.3 %tile.1 = (f32[1024,128]{1,0:T(8,128)}, f32[1024,256]{1,0:T(8,128)}, bf16[1024,1024]{1,0:T(8,128)(2,1)}) custom-call(s32[1]{0:T(128)} %bitcast.4.pick_ref, bf16[1024,896]{1,0:T(8,128)(2,1)} %get-tuple-element.48.x_ref.other_ref.y_ref, bf16[1024,896]{1,0:T(8,128)(2,1)} %get-tuple-element.48.x_ref.other_ref.y_ref, ...), custom_call_target="tpu_custom_call" | custom-call | flops 262144 | bytes 262144 | tf_op jit(solution)/shard_map/tile/pallas_call | solution.py:163
  34.1 7.6 %collective-permute-done.1 = bf16[1296,256]{1,0:T(8,128)(2,1)S(1)} collective-permute-done((bf16[1296,256]{1,0:T(8,128)(2,1)}, bf16[1296,256]{1,0:T(8,128)(2,1)S(1)}, u32[]{:S(2)}, u32[]{:S(2)}) %collective-permute-start.1) | collective-permute-done | bytes 663584 | tf_op jit(solution)/shard_map/ppermute | solution.py:392
  41.7 2.6 %collective-permute-done = bf16[1296,256]{1,0:T(8,128)(2,1)} collective-permute-done((bf16[1296,256]{1,0:T(8,128)(2,1)}, bf16[1296,256]{1,0:T(8,128)(2,1)}, u32[]{:S(2)}, u32[]{:S(2)}) %collective-permute-start) | collective-permute-done | bytes 663584 | tf_op jit(solution)/shard_map/ppermute | solution.py:392
  45.1 7.0 %collective-permute-done.2 = bf16[2,32,896]{2,1,0:T(8,128)(2,1)S(1)} collective-permute-done((bf16[2,32,896]{2,1,0:T(8,128)(2,1)S(1)}, bf16[2,32,896]{2,1,0:T(8,128)(2,1)S(1)}, u32[]{:S(2)}, u32[]{:S(2)}) %collective-permute-start.2) | collective-permute-done | bytes 114720 | tf_op jit(solution)/shard_map/ppermute | solution.py:392
  52.2 2.3 %collective-permute-start.3 = (bf16[1,2,32,896]{3,2,1,0:T(8,128)(2,1)S(1)}, bf16[1,2,32,896]{3,2,1,0:T(8,128)(2,1)S(1)}, u32[]{:S(2)}, u32[]{:S(2)}) collective-permute-start(bf16[1,2,32,896]{3,2,1,0:T(8,128)(2,1)S(1)} %select_bitcast_fusion.1), channel_id=1, source_target_pairs={{0,1},{1,0},{2,3},{3,2},{4,5},{5,4},{6,7},{7,6},{8,9},{9,8},{10,11... | collective-permute-start | bytes 344072 | tf_op jit(solution)/shard_map/ppermute | solution.py:392
  54.4 2.2 %collective-permute-done.3 = bf16[1,2,32,896]{3,2,1,0:T(8,128)(2,1)S(1)} collective-permute-done((bf16[1,2,32,896]{3,2,1,0:T(8,128)(2,1)S(1)}, bf16[1,2,32,896]{3,2,1,0:T(8,128)(2,1)S(1)}, u32[]{:S(2)}, u32[]{:S(2)}) %collective-permute-start.3) | collective-permute-done | bytes 114720 | tf_op jit(solution)/shard_map/ppermute | solution.py:392
  56.8 1.8 collective-permute-start.4
  62.8 4.7 %collective-permute-done.4 = bf16[2,2,32,896]{3,2,1,0:T(8,128)(2,1)S(1)} collective-permute-done((bf16[2,2,32,896]{3,2,1,0:T(8,128)(2,1)S(1)}, bf16[2,2,32,896]{3,2,1,0:T(8,128)(2,1)S(1)}, u32[]{:S(2)}, u32[]{:S(2)}) %collective-permute-start.4) | collective-permute-done | bytes 229408 | tf_op jit(solution)/shard_map/ppermute | solution.py:392
  70.1 1.9 collective-permute-start.7
  72.0 2.1 %collective-permute-start.6 = (bf16[1296,256]{1,0:T(8,128)(2,1)}, bf16[1296,256]{1,0:T(8,128)(2,1)}, u32[]{:S(2)}, u32[]{:S(2)}) collective-permute-start(bf16[1296,256]{1,0:T(8,128)(2,1)} %collective-permute-done), channel_id=1, source_target_pairs={{1,0},{2,3},{5,4},{6,7},{9,8},{10,11},{13,12},{14,15},{17,16},{18,... | collective-permute-start | bytes 1990664 | tf_op jit(solution)/shard_map/ppermute | solution.py:392
  74.2 5.0 %collective-permute-start.5 = (bf16[2,32,896]{2,1,0:T(8,128)(2,1)S(1)}, bf16[2,32,896]{2,1,0:T(8,128)(2,1)S(1)}, u32[]{:S(2)}, u32[]{:S(2)}) collective-permute-start(bf16[2,32,896]{2,1,0:T(8,128)(2,1)S(1)} %broadcast_select_fusion.6), channel_id=1, source_target_pairs={{0,4},{1,5},{2,6},{3,7},{4,0},{5,1},{6,2},{7,3},{8,12},{9,13},{10,... | collective-permute-start | bytes 344072 | tf_op jit(solution)/shard_map/ppermute | solution.py:392
  79.9 2.0 %collective-permute-start.8 = (bf16[1024,512]{1,0:T(8,128)(2,1)}, bf16[1024,512]{1,0:T(8,128)(2,1)}, u32[]{:S(2)}, u32[]{:S(2)}) collective-permute-start(bf16[1024,512]{1,0:T(8,128)(2,1)} %get-tuple-element.64.rows_ref.refs_0_.refs_5_), channel_id=1, source_target_pairs={{0,2},{1,3},{2,0},{3,1},{4,6},{5,7},{6,4},{7,5},{8,10},{9,11},{10,... | collective-permute-start | bytes 3145736 | tf_op jit(solution)/shard_map/ppermute | solution.py:392
  81.9 2.0 broadcast_in_dim.90
  83.9 6.6 %all-to-all-start.1 = ((bf16[16,2,64,768]{3,2,1,0:T(8,128)(2,1)}), bf16[16,2,64,768]{3,2,1,0:T(8,128)(2,1)S(1)}, u32[]{:S(2)}, u32[]{:S(2)}) async-start(bf16[16,2,64,768]{3,2,1,0:T(8,128)(2,1)} %broadcast_in_dim.90), calls=%async_computation.1 | async-start | bytes 6291456 | tf_op jit(solution)/shard_map/all_to_all | solution.py:415
  91.7 1.8 pad_maximum_fusion.coded_ref.refs_6_.refs_7_
  97.3 7.7 %keep_words.3.refs_11_ = s32[4,1024,128]{2,1,0:T(8,128)} custom-call(s32[6]{0:T(128)} %stack.66.pick_ref, bf16[4,1296,256]{2,1,0:T(8,128)(2,1)} %copy-done.1), custom_call_target="tpu_custom_call" | custom-call | flops 30000001024 | bytes 524288 | tf_op jit(solution)/shard_map/keep_words/pallas_call | solution.py:96
  105.0 17.4 %collective-permute-done.9.refs_1_ = bf16[1024,512]{1,0:T(8,128)(2,1)} collective-permute-done((bf16[1024,512]{1,0:T(8,128)(2,1)}, bf16[1024,512]{1,0:T(8,128)(2,1)}, u32[]{:S(2)}, u32[]{:S(2)}) %collective-permute-start.9) | collective-permute-done | bytes 1048608 | tf_op jit(solution)/shard_map/ppermute | solution.py:392
  122.4 6.7 %collective-permute-done.8.refs_2_ = bf16[1024,512]{1,0:T(8,128)(2,1)} collective-permute-done((bf16[1024,512]{1,0:T(8,128)(2,1)}, bf16[1024,512]{1,0:T(8,128)(2,1)}, u32[]{:S(2)}, u32[]{:S(2)}) %collective-permute-start.8) | collective-permute-done | bytes 1048608 | tf_op jit(solution)/shard_map/ppermute | solution.py:392
  129.1 1.8 all-to-all-done.1.near_ref.refs_8_
  132.3 2.9 %collective-permute-start.10 = (bf16[16,64,768]{2,1,0:T(8,128)(2,1)}, bf16[16,64,768]{2,1,0:T(8,128)(2,1)}, u32[]{:S(2)}, u32[]{:S(2)}) collective-permute-start(bf16[16,64,768]{2,1,0:T(8,128)(2,1)} %slice_bitcast_fusion), channel_id=1, source_target_pairs={{0,4},{1,5},{2,6},{3,7},{4,0},{5,1},{6,2},{7,3},{8,12},{9,13},{10,... | collective-permute-start | bytes 4718600 | tf_op jit(solution)/shard_map/ppermute | solution.py:392
  135.2 5.1 %collective-permute-start.12 = (bf16[1024,512]{1,0:T(8,128)(2,1)}, bf16[1024,512]{1,0:T(8,128)(2,1)}, u32[]{:S(2)}, u32[]{:S(2)}) collective-permute-start(bf16[1024,512]{1,0:T(8,128)(2,1)} %collective-permute-done.8.refs_2_), channel_id=1, source_target_pairs={{1,0},{2,3},{5,4},{6,7},{9,8},{10,11},{13,12},{14,15},{17,16},{18,... | collective-permute-start | bytes 3145736 | tf_op jit(solution)/shard_map/ppermute | solution.py:392
  140.3 5.5 %collective-permute-start.13 = (bf16[1024,512]{1,0:T(8,128)(2,1)}, bf16[1024,512]{1,0:T(8,128)(2,1)}, u32[]{:S(2)}, u32[]{:S(2)}) collective-permute-start(bf16[1024,512]{1,0:T(8,128)(2,1)} %get-tuple-element.64.rows_ref.refs_0_.refs_5_), channel_id=1, source_target_pairs={{1,2},{2,1},{5,6},{6,5},{9,10},{10,9},{13,14},{14,13},{17,18},{18,... | collective-permute-start | bytes 3145736 | tf_op jit(solution)/shard_map/ppermute | solution.py:392
  147.7 5.2 %hub_rows.1 = bf16[64,256]{1,0:T(8,128)(2,1)} custom-call(s32[1]{0:T(128)} %bitcast.40.pick_ref, bf16[64,896]{1,0:T(8,128)(2,1)} %fusion.1.rows_ref, bf16[16,2,64,768]{3,2,1,0:T(8,128)(2,1)} %copy-done, bf16[16,64,768]{2,1,0:T(8,128)(2,1)} %collective-permute-done.10.far_ref.refs_9_), custom_call_target="tpu_custom_call" | custom-call | flops 1024 | bytes 1024 | tf_op jit(solution)/shard_map/hub_rows/pallas_call | solution.py:363
  152.8 1.6 broadcast_in_dim.92
  154.5 5.9 %all-to-all-start.2 = ((bf16[16,64,256]{2,1,0:T(8,128)(2,1)}), bf16[16,64,256]{2,1,0:T(8,128)(2,1)S(1)}, u32[]{:S(2)}, u32[]{:S(2)}) async-start(bf16[16,64,256]{2,1,0:T(8,128)(2,1)} %broadcast_in_dim.92), calls=%async_computation.2 | async-start | bytes 1048576 | tf_op jit(solution)/shard_map/all_to_all | solution.py:415
  160.3 9.1 %two.1 = (bf16[1024,1024]{1,0:T(8,128)(2,1)}, bf16[1024,1024]{1,0:T(8,128)(2,1)}, f32[1024,128]{1,0:T(8,128)}, f32[1024,256]{1,0:T(8,128)}) custom-call(s32[6]{0:T(128)} %stack.66.pick_ref, bf16[1024,512]{1,0:T(8,128)(2,1)} %get-tuple-element.64.rows_ref.refs_0_.refs_5_, bf16[16,2,64,768]{3,2,1,0:T(8,128)(2,1)} %copy-done, ...), custom_call_target="tpu_custom_call" | custom-call | flops 262144 | bytes 262144 | tf_op jit(solution)/shard_map/two/pallas_call | solution.py:222
  170.6 2.1 %collective-permute-start.11 = (bf16[1024,256]{1,0:T(8,128)(2,1)S(1)}, bf16[1024,256]{1,0:T(8,128)(2,1)S(1)}, u32[]{:S(2)}, u32[]{:S(2)}) collective-permute-start(bf16[1024,256]{1,0:T(8,128)(2,1)S(1)} %bitcast.55), channel_id=1, source_target_pairs={{0,4},{1,5},{2,6},{3,7},{4,0},{5,1},{6,2},{7,3},{8,12},{9,13},{10,... | collective-permute-start | bytes 1572872 | tf_op jit(solution)/shard_map/ppermute | solution.py:392
  174.3 18.2 %five.1 = (bf16[1024,1024]{1,0:T(8,128)(2,1)}, f32[1024,128]{1,0:T(8,128)}, bf16[1024,256]{1,0:T(8,128)(2,1)}, bf16[1024,256]{1,0:T(8,128)(2,1)}) custom-call(s32[6]{0:T(128)} %stack.66.pick_ref, bf16[1024,512]{1,0:T(8,128)(2,1)} %get-tuple-element.64.rows_ref.refs_0_.refs_5_, bf16[1024,512]{1,0:T(8,128)(2,1)} %collective-permute-done.9.refs_1_, ...), custom_call_target="tpu_custom_call" | custom-call | flops 8053063680 | bytes 8388608 | tf_op jit(solution)/shard_map/five/pallas_call | solution.py:279
  192.5 7.3 %last.1 = bf16[1024,256]{1,0:T(8,128)(2,1)} custom-call(bf16[1024,1024]{1,0:T(8,128)(2,1)} %get-tuple-element.53.refs_0_, bf16[1024,1024]{1,0:T(8,128)(2,1)} %get-tuple-element.83.refs_1_, bf16[1024,1024]{1,0:T(8,128)(2,1)} %get-tuple-element.84.refs_2_, bf16[1024,1024]{1,0:T(8,128)(2,1)} %get-tuple-element.85.refs_3_, ...), custom_call_target="tpu_custom_call" | custom-call | flops 2147483648 | bytes 8388608 | tf_op jit(solution)/shard_map/last/pallas_call | solution.py:316
  (56 shorter events, 15.5 us)
Async XLA Ops:
  0.0 14.9 %copy-start.5 = (s32[1,4]{1,0:T(1,128)S(1)}, s32[1,4]{1,0:T(1,128)}, u32[]{:S(2)}) copy-start(s32[1,4]{1,0:T(1,128)} %param.7) | copy-start | bytes 52
  5.1 39.2 %all-to-all-start = ((bf16[32,32,896]{2,1,0:T(8,128)(2,1)}), bf16[32,32,896]{2,1,0:T(8,128)(2,1)S(1)}, u32[]{:S(2)}, u32[]{:S(2)}) async-start(bf16[32,32,896]{2,1,0:T(8,128)(2,1)} %bitcast.54), calls=%async_computation | async-start | bytes 3670016 | tf_op jit(solution)/shard_map/all_to_all | solution.py:432
  12.9 28.8 %collective-permute-start.1 = (bf16[1296,256]{1,0:T(8,128)(2,1)}, bf16[1296,256]{1,0:T(8,128)(2,1)S(1)}, u32[]{:S(2)}, u32[]{:S(2)}) collective-permute-start(bf16[1296,256]{1,0:T(8,128)(2,1)} %get-tuple-element.59), channel_id=1, source_target_pairs={{0,1},{1,0},{2,3},{3,2},{4,5},{5,4},{6,7},{7,6},{8,9},{9,8},{10,11... | collective-permute-start | bytes 1990664 | tf_op jit(solution)/shard_map/ppermute | solution.py:392
  13.7 30.6 %collective-permute-start = (bf16[1296,256]{1,0:T(8,128)(2,1)}, bf16[1296,256]{1,0:T(8,128)(2,1)}, u32[]{:S(2)}, u32[]{:S(2)}) collective-permute-start(bf16[1296,256]{1,0:T(8,128)(2,1)} %get-tuple-element.59), channel_id=1, source_target_pairs={{0,2},{1,3},{2,0},{3,1},{4,6},{5,7},{6,4},{7,5},{8,10},{9,11},{10,... | collective-permute-start | bytes 1990664 | tf_op jit(solution)/shard_map/ppermute | solution.py:392
  23.2 6.3 %copy-start.6 = (s32[2]{0:T(128)S(1)}, s32[2]{0:T(128)}, u32[]{:S(2)}) copy-start(s32[2]{0:T(128)} %param.8) | copy-start | bytes 28
  41.6 2.7 %copy-start.3 = (bf16[1296,256]{1,0:T(8,128)(2,1)}, bf16[1296,256]{1,0:T(8,128)(2,1)S(1)}, u32[]{:S(2)}) copy-start(bf16[1296,256]{1,0:T(8,128)(2,1)S(1)} %collective-permute-done.1) | copy-start | bytes 1990660
  44.3 7.7 %collective-permute-start.2 = (bf16[2,32,896]{2,1,0:T(8,128)(2,1)S(1)}, bf16[2,32,896]{2,1,0:T(8,128)(2,1)S(1)}, u32[]{:S(2)}, u32[]{:S(2)}) collective-permute-start(bf16[2,32,896]{2,1,0:T(8,128)(2,1)S(1)} %pad_maximum_fusion.4), channel_id=1, source_target_pairs={{0,128},{1,129},{2,130},{3,131},{4,132},{5,133},{6,134},{7,135},{8... | collective-permute-start | bytes 344072 | tf_op jit(solution)/shard_map/ppermute | solution.py:392
  52.2 4.5 %collective-permute-start.3 = (bf16[1,2,32,896]{3,2,1,0:T(8,128)(2,1)S(1)}, bf16[1,2,32,896]{3,2,1,0:T(8,128)(2,1)S(1)}, u32[]{:S(2)}, u32[]{:S(2)}) collective-permute-start(bf16[1,2,32,896]{3,2,1,0:T(8,128)(2,1)S(1)} %select_bitcast_fusion.1), channel_id=1, source_target_pairs={{0,1},{1,0},{2,3},{3,2},{4,5},{5,4},{6,7},{7,6},{8,9},{9,8},{10,11... | collective-permute-start | bytes 344072 | tf_op jit(solution)/shard_map/ppermute | solution.py:392
  56.8 10.7 %collective-permute-start.4 = (bf16[2,2,32,896]{3,2,1,0:T(8,128)(2,1)S(1)}, bf16[2,2,32,896]{3,2,1,0:T(8,128)(2,1)S(1)}, u32[]{:S(2)}, u32[]{:S(2)}) collective-permute-start(bf16[2,2,32,896]{3,2,1,0:T(8,128)(2,1)S(1)} %pad_maximum_fusion.2), channel_id=1, source_target_pairs={{0,2},{1,3},{2,0},{3,1},{4,6},{5,7},{6,4},{7,5},{8,10},{9,11},{10,... | collective-permute-start | bytes 688136 | tf_op jit(solution)/shard_map/ppermute | solution.py:392
  70.1 20.4 %collective-permute-start.7 = (bf16[1296,256]{1,0:T(8,128)(2,1)}, bf16[1296,256]{1,0:T(8,128)(2,1)}, u32[]{:S(2)}, u32[]{:S(2)}) collective-permute-start(bf16[1296,256]{1,0:T(8,128)(2,1)} %get-tuple-element.59), channel_id=1, source_target_pairs={{1,2},{2,1},{5,6},{6,5},{9,10},{10,9},{13,14},{14,13},{17,18},{18,... | collective-permute-start | bytes 1990664 | tf_op jit(solution)/shard_map/ppermute | solution.py:392
  72.0 18.5 %collective-permute-start.6 = (bf16[1296,256]{1,0:T(8,128)(2,1)}, bf16[1296,256]{1,0:T(8,128)(2,1)}, u32[]{:S(2)}, u32[]{:S(2)}) collective-permute-start(bf16[1296,256]{1,0:T(8,128)(2,1)} %collective-permute-done), channel_id=1, source_target_pairs={{1,0},{2,3},{5,4},{6,7},{9,8},{10,11},{13,12},{14,15},{17,16},{18,... | collective-permute-start | bytes 1990664 | tf_op jit(solution)/shard_map/ppermute | solution.py:392
  74.2 7.7 %collective-permute-start.5 = (bf16[2,32,896]{2,1,0:T(8,128)(2,1)S(1)}, bf16[2,32,896]{2,1,0:T(8,128)(2,1)S(1)}, u32[]{:S(2)}, u32[]{:S(2)}) collective-permute-start(bf16[2,32,896]{2,1,0:T(8,128)(2,1)S(1)} %broadcast_select_fusion.6), channel_id=1, source_target_pairs={{0,4},{1,5},{2,6},{3,7},{4,0},{5,1},{6,2},{7,3},{8,12},{9,13},{10,... | collective-permute-start | bytes 344072 | tf_op jit(solution)/shard_map/ppermute | solution.py:392
  79.8 42.7 %collective-permute-start.9 = (bf16[1024,512]{1,0:T(8,128)(2,1)}, bf16[1024,512]{1,0:T(8,128)(2,1)}, u32[]{:S(2)}, u32[]{:S(2)}) collective-permute-start(bf16[1024,512]{1,0:T(8,128)(2,1)} %get-tuple-element.64.rows_ref.refs_0_.refs_5_), channel_id=1, source_target_pairs={{0,1},{1,0},{2,3},{3,2},{4,5},{5,4},{6,7},{7,6},{8,9},{9,8},{10,11... | collective-permute-start | bytes 3145736 | tf_op jit(solution)/shard_map/ppermute | solution.py:392
  79.9 49.2 %collective-permute-start.8 = (bf16[1024,512]{1,0:T(8,128)(2,1)}, bf16[1024,512]{1,0:T(8,128)(2,1)}, u32[]{:S(2)}, u32[]{:S(2)}) collective-permute-start(bf16[1024,512]{1,0:T(8,128)(2,1)} %get-tuple-element.64.rows_ref.refs_0_.refs_5_), channel_id=1, source_target_pairs={{0,2},{1,3},{2,0},{3,1},{4,6},{5,7},{6,4},{7,5},{8,10},{9,11},{10,... | collective-permute-start | bytes 3145736 | tf_op jit(solution)/shard_map/ppermute | solution.py:392
  83.9 47.0 %all-to-all-start.1 = ((bf16[16,2,64,768]{3,2,1,0:T(8,128)(2,1)}), bf16[16,2,64,768]{3,2,1,0:T(8,128)(2,1)S(1)}, u32[]{:S(2)}, u32[]{:S(2)}) async-start(bf16[16,2,64,768]{3,2,1,0:T(8,128)(2,1)} %broadcast_in_dim.90), calls=%async_computation.1 | async-start | bytes 6291456 | tf_op jit(solution)/shard_map/all_to_all | solution.py:415
  93.5 1.5 copy-start.1
  130.9 16.8 %copy-start = (bf16[16,2,64,768]{3,2,1,0:T(8,128)(2,1)}, bf16[16,2,64,768]{3,2,1,0:T(8,128)(2,1)S(1)}, u32[]{:S(2)}) copy-start(bf16[16,2,64,768]{3,2,1,0:T(8,128)(2,1)S(1)} %all-to-all-done.1.near_ref.refs_8_) | copy-start | bytes 9437188
  132.3 15.4 %collective-permute-start.10 = (bf16[16,64,768]{2,1,0:T(8,128)(2,1)}, bf16[16,64,768]{2,1,0:T(8,128)(2,1)}, u32[]{:S(2)}, u32[]{:S(2)}) collective-permute-start(bf16[16,64,768]{2,1,0:T(8,128)(2,1)} %slice_bitcast_fusion), channel_id=1, source_target_pairs={{0,4},{1,5},{2,6},{3,7},{4,0},{5,1},{6,2},{7,3},{8,12},{9,13},{10,... | collective-permute-start | bytes 4718600 | tf_op jit(solution)/shard_map/ppermute | solution.py:392
  135.2 37.6 %collective-permute-start.12 = (bf16[1024,512]{1,0:T(8,128)(2,1)}, bf16[1024,512]{1,0:T(8,128)(2,1)}, u32[]{:S(2)}, u32[]{:S(2)}) collective-permute-start(bf16[1024,512]{1,0:T(8,128)(2,1)} %collective-permute-done.8.refs_2_), channel_id=1, source_target_pairs={{1,0},{2,3},{5,4},{6,7},{9,8},{10,11},{13,12},{14,15},{17,16},{18,... | collective-permute-start | bytes 3145736 | tf_op jit(solution)/shard_map/ppermute | solution.py:392
  140.3 32.5 %collective-permute-start.13 = (bf16[1024,512]{1,0:T(8,128)(2,1)}, bf16[1024,512]{1,0:T(8,128)(2,1)}, u32[]{:S(2)}, u32[]{:S(2)}) collective-permute-start(bf16[1024,512]{1,0:T(8,128)(2,1)} %get-tuple-element.64.rows_ref.refs_0_.refs_5_), channel_id=1, source_target_pairs={{1,2},{2,1},{5,6},{6,5},{9,10},{10,9},{13,14},{14,13},{17,18},{18,... | collective-permute-start | bytes 3145736 | tf_op jit(solution)/shard_map/ppermute | solution.py:392
  154.5 16.2 %all-to-all-start.2 = ((bf16[16,64,256]{2,1,0:T(8,128)(2,1)}), bf16[16,64,256]{2,1,0:T(8,128)(2,1)S(1)}, u32[]{:S(2)}, u32[]{:S(2)}) async-start(bf16[16,64,256]{2,1,0:T(8,128)(2,1)} %broadcast_in_dim.92), calls=%async_computation.2 | async-start | bytes 1048576 | tf_op jit(solution)/shard_map/all_to_all | solution.py:415
  170.6 21.9 %copy-start.2 = (bf16[16,64,256]{2,1,0:T(8,128)(2,1)}, bf16[16,64,256]{2,1,0:T(8,128)(2,1)S(1)}, u32[]{:S(2)}) copy-start(bf16[16,64,256]{2,1,0:T(8,128)(2,1)S(1)} %all-to-all-done.2) | copy-start | bytes 1572868
  170.6 3.7 %collective-permute-start.11 = (bf16[1024,256]{1,0:T(8,128)(2,1)S(1)}, bf16[1024,256]{1,0:T(8,128)(2,1)S(1)}, u32[]{:S(2)}, u32[]{:S(2)}) collective-permute-start(bf16[1024,256]{1,0:T(8,128)(2,1)S(1)} %bitcast.55), channel_id=1, source_target_pairs={{0,4},{1,5},{2,6},{3,7},{4,0},{5,1},{6,2},{7,3},{8,12},{9,13},{10,... | collective-permute-start | bytes 1572872 | tf_op jit(solution)/shard_map/ppermute | solution.py:392
  174.3 18.2 %copy-start.4 = (bf16[1024,256]{1,0:T(8,128)(2,1)}, bf16[1024,256]{1,0:T(8,128)(2,1)S(1)}, u32[]{:S(2)}) copy-start(bf16[1024,256]{1,0:T(8,128)(2,1)S(1)} %collective-permute-done.11.refs_7_) | copy-start | bytes 1572868

commit v8 on v7

--- a/solution.py
+++ b/solution.py
@@ -234,13 +234,15 @@
     )(pick, own_rows, near, far, words, *carry)
 
 
-def five_kernel(pick_ref, *refs):
+def finish_kernel(pick_ref, *refs):
     blocks, refs = refs[:BLOCKS_NEAR], refs[BLOCKS_NEAR:]
     rows_ref, first_y, second_y, near_ref, far_ref, own_ref, member_ref, deg_in, acc_in, anchor_ref = refs[:10]
-    member_tile, deg_ref, new_ref, other_ref, first_x, second_x, held, spare, sems = refs[10:]
-    step = pl.program_id(0)
-
-    @pl.when(step == 0)
+    own_tile, near_tile, far_tile, near_new, far_new, out_ref = refs[10:16]
+    member_tile, degree, new, other_new, first_x, second_x, held, spare, sems = refs[16:]
+    phase, step = pl.program_id(0), pl.program_id(1)
+    here = pl.ds(pl.multiple_of(step * ROW_TILE, ROW_TILE), ROW_TILE)
+
+    @pl.when((phase == 0) & (step == 0))
     def _():
         for which, target in enumerate((first_x, second_x)):
             for i, block in enumerate(blocks):
@@ -251,80 +253,80 @@
                     copy.start()
                     copy.wait()
 
-    first, second = (first_x[...], first_y[0]), (second_x[...], second_y[0])
-    near, far = hub_blocks(near_ref, far_ref, rows_ref.shape[1])
-    total, acc = run_tiles(rows_ref[...], ((own_ref[0], first, member_tile),), deg_in[...], acc_in[...])
-    deg_ref[...] = total
-    new_ref[...] = mix(acc, jnp.sum(total, axis=1, keepdims=True), anchor_ref[...])
-    here = pl.ds(pl.multiple_of(step * ROW_TILE, ROW_TILE), ROW_TILE)
-    plan = (
-        (member_ref[pick_ref[3]], near, held),
-        (member_ref[5 - pick_ref[3]], far, spare),
-        (member_ref[0], first, held),
-        (member_ref[1], second, spare),
-    )
-    zeros = lambda ref: jnp.zeros(ref.shape, jnp.float32)
-    total, acc = run_tiles(first_x[here, :], plan, zeros(deg_in), zeros(acc_in))
-    other_ref[...] = mix(acc, jnp.sum(total, axis=1, keepdims=True), first_y[0, here, :])
-
-
-def five_of(pick, blocks, own_rows, rest, near, far, words, member_words, carry, anchor):
+    @pl.when(phase == 0)
+    def _():
+        first, second = (first_x[...], first_y[0]), (second_x[...], second_y[0])
+        near, far = hub_blocks(near_ref, far_ref, rows_ref.shape[1])
+        plan = ((own_ref[0], first, member_tile.at[here, :]),)
+        total, acc = run_tiles(rows_ref[...], plan, deg_in[...], acc_in[...])
+        degree[here, :] = total
+        new[here, :] = mix(acc, jnp.sum(total, axis=1, keepdims=True), anchor_ref[...])
+        plan = (
+            (member_ref[pick_ref[3]], near, held),
+            (member_ref[5 - pick_ref[3]], far, spare),
+            (member_ref[0], first, held),
+            (member_ref[1], second, spare),
+        )
+        zeros = lambda ref: jnp.zeros(ref.shape, jnp.float32)
+        total, acc = run_tiles(first_x[here, :], plan, zeros(deg_in), zeros(acc_in))
+        other_new[here, :] = mix(acc, jnp.sum(total, axis=1, keepdims=True), first_y[0, here, :])
+
+    @pl.when(phase == 1)
+    def _():
+        pairs = ((own_tile[...], new), (member_tile[here, :], other_new), (near_tile[...], near_new), (far_tile[...], far_new))
+        acc = sum(jnp.dot(tile, y[...], preferred_element_type=jnp.float32) for tile, y in pairs)
+        out_ref[...] = mix(acc, jnp.sum(degree[here, :], axis=1, keepdims=True), anchor_ref[...])
+
+
+def finish_of(pick, blocks, own_rows, rest, near, far, words, member_words, carry, anchor, tiles, news):
     rows, width = blocks[0].shape
     clust = rest.shape[2]
-    by_row = lambda cols: pl.BlockSpec((ROW_TILE, cols), lambda r, pick: (r, 0))
-    rest_at = lambda k: pl.BlockSpec(
-        (1, rows, clust), lambda r, pick: (pick[k], 0, 0), pipeline_mode=pl.Buffered(1)
-    )
-    outs = [(rows, jnp.bfloat16), (LANES, jnp.float32)] + [(clust, jnp.bfloat16)] * 2
+    steps = rows // ROW_TILE
+    once = pl.Buffered(1)
+    before = lambda p, r: jnp.where(p == 0, r, steps - 1)
+    after = lambda p, r: jnp.where(p == 0, 0, r)
+    by_row = lambda cols, row: pl.BlockSpec((ROW_TILE, cols), lambda p, r, pick: (row(p, r), 0))
+    rest_at = lambda k: pl.BlockSpec((1, rows, clust), lambda p, r, pick: (pick[k], 0, 0), pipeline_mode=once)
+    whole = pl.BlockSpec((rows, clust), lambda p, r, pick: (0, 0), pipeline_mode=once)
+    chips, _, piece, full = near.shape
     return pl.pallas_call(
-        five_kernel,
-        out_shape=[jax.ShapeDtypeStruct((rows, cols), kind) for cols, kind in outs],
+        finish_kernel,
+        out_shape=jax.ShapeDtypeStruct((rows, clust), jnp.bfloat16),
         grid_spec=pltpu.PrefetchScalarGridSpec(
             num_scalar_prefetch=1,
-            grid=(rows // ROW_TILE,),
+            grid=(2, steps),
             in_specs=[pl.BlockSpec(memory_space=pl.ANY)] * len(blocks)
-            + [by_row(width), rest_at(4), rest_at(5), *hub_specs(near, far)]
             + [
-                pl.BlockSpec((1, ROW_TILE, LANES), lambda r, pick: (1, r, 0)),
-                pl.BlockSpec((K, ROW_TILE, LANES), lambda r, pick: (0, r, 0)),
-                by_row(LANES),
-                by_row(clust),
-                by_row(clust),
-            ],
-            out_specs=[by_row(cols) for cols, _ in outs],
-            scratch_shapes=[pltpu.VMEM((rows, width), jnp.bfloat16)] * 2
+                by_row(width, before),
+                rest_at(4),
+                rest_at(5),
+                pl.BlockSpec((chips, 1, piece, full), lambda p, r, pick: (0, 0, 0, 0), pipeline_mode=once),
+                pl.BlockSpec((chips, piece, full), lambda p, r, pick: (0, 0, 0), pipeline_mode=once),
+                pl.BlockSpec((1, ROW_TILE, LANES), lambda p, r, pick: (1, before(p, r), 0)),
+                pl.BlockSpec((K, ROW_TILE, LANES), lambda p, r, pick: (0, before(p, r), 0)),
+                by_row(LANES, before),
+                by_row(clust, before),
+                by_row(clust, lambda p, r: r),
+            ]
+            + [by_row(rows, after)] * 3
+            + [whole] * 2,
+            out_specs=by_row(clust, after),
+            scratch_shapes=[
+                pltpu.VMEM((rows, rows), jnp.bfloat16),
+                pltpu.VMEM((rows, LANES), jnp.float32),
+                pltpu.VMEM((rows, clust), jnp.bfloat16),
+                pltpu.VMEM((rows, clust), jnp.bfloat16),
+            ]
+            + [pltpu.VMEM((rows, width), jnp.bfloat16)] * 2
             + [pltpu.VMEM((ROW_TILE, rows), jnp.bfloat16)] * 2
             + [pltpu.SemaphoreType.DMA((2,))],
         ),
         compiler_params=pltpu.CompilerParams(vmem_limit_bytes=VMEM_LIMIT),
         cost_estimate=pl.CostEstimate(
-            flops=10 * rows * rows * 768, bytes_accessed=8 * rows * rows, transcendentals=5 * rows * rows
-        ),
-        name="five",
-    )(pick, *blocks, own_rows, rest, rest, near, far, words, member_words, *carry, anchor)
-
-
-def last_kernel(*refs):
-    tiles, news, (deg_ref, anchor_ref, out_ref) = refs[:K], refs[K : 2 * K], refs[2 * K :]
-    acc = sum(jnp.dot(t[...], y[...], preferred_element_type=jnp.float32) for t, y in zip(tiles, news))
-    out_ref[...] = mix(acc, jnp.sum(deg_ref[...], axis=1, keepdims=True), anchor_ref[...])
-
-
-def last_of(tiles, news, degree, anchor):
-    rows, clust = anchor.shape
-    by_row = lambda cols: pl.BlockSpec((ROW_TILE, cols), lambda r: (r, 0))
-    return pl.pallas_call(
-        last_kernel,
-        out_shape=jax.ShapeDtypeStruct((rows, clust), jnp.bfloat16),
-        grid=(rows // ROW_TILE,),
-        in_specs=[by_row(rows)] * K
-        + [pl.BlockSpec((rows, clust), lambda r: (0, 0))] * K
-        + [by_row(LANES), by_row(clust)],
-        out_specs=by_row(clust),
-        compiler_params=pltpu.CompilerParams(vmem_limit_bytes=VMEM_LIMIT),
-        cost_estimate=pl.CostEstimate(flops=8 * rows * rows * clust, bytes_accessed=8 * rows * rows, transcendentals=0),
-        name="last",
-    )(*tiles, *news, degree, anchor)
+            flops=12 * rows * rows * 768, bytes_accessed=12 * rows * rows, transcendentals=5 * rows * rows
+        ),
+        name="finish",
+    )(pick, *blocks, own_rows, rest, rest, near, far, words, member_words, *carry, anchor, *tiles, *news)
 
 
 def hub_rows_kernel(width, pick_ref, rows_ref, near_ref, far_ref, out_ref, word_ref, tile_ref):
@@ -531,12 +533,9 @@
     far_new = swap_cores(near_new)
     near_new, far_new, outer_x, middle_x = barrier((near_new, far_new, outer_x, middle_x))
 
-    member_tile, degree, new, member_new = five_of(
+    return finish_of(
         pick, (normed, beside_x, across_x, middle_x, outer_x), normed, group_rest, near, far, words, member_words,
-        carry, indicators,
-    )
-    return last_of(
-        (own_tile, member_tile, near_tile, far_tile), (new, member_new, near_new, far_new), degree, indicators
+        carry, indicators, (own_tile, near_tile, far_tile), (near_new, far_new),
     )
 
 

time: 202 us -> 206 us (1.020)
  waiting for transfers between devices: 52.7 us -> 60.4 us
  starting transfers between devices: 53.8 us -> 51.1 us
    ppermute x14, waiting for transfers between devices: 49.7 us -> 59.2 us  [send(): return lax.ppermute(block, AXES, pairs)]
    ppermute x14, starting transfers between devices: 33.6 us -> 29.6 us  [send(): return lax.ppermute(block, AXES, pairs)]
    pallas_call x2 -> x1, Pallas kernels: 25.4 us -> 23.4 us  [finish_of(): pl.pallas_call(finish_kernel, out_shape=jax.ShapeDtypeStruct((rows, clust...]
  transfers between devices with their start and end apart: 17 -> 17, of which waited for: 10 -> 9; matrix products, arithmetic and copies ran while one was open for 5% -> 5% of each run, Pallas kernels for 18% -> 17%
where the time goes in v8:
time: 206 us; the launch traced here: 205 us
  Pallas kernels  63.8 us (31%)
  waiting for transfers between devices  60.4 us (29%)
  starting transfers between devices  51.1 us (25%)
  local copies, waits for them, and re-layouts  12.3 us (6%)
  between operations  12.3 us (6%)
  other arithmetic  4.7 us (2%)
    ppermute x14, waiting for transfers between devices, send(): return lax.ppermute(block, AXES, pairs)  59.2 us
    ppermute x14, starting transfers between devices, send(): return lax.ppermute(block, AXES, pairs)  29.6 us
    pallas_call x1, Pallas kernels, finish_of(): pl.pallas_call(finish_kernel, out_shape=jax.ShapeDtypeStruct((rows, clust...  23.4 us
    pallas_call x2, Pallas kernels, keep_words(): pl.pallas_call(words_kernel, out_shape=jax.ShapeDtypeStruct((K, rows, LAN...  14.7 us
    all_to_all x2, starting transfers between devices, join_pieces(): lax.all_to_all(repeated, 'slab', 0, 0, axis_index_groups=layers, tiled=True)  13.8 us
    pallas_call x1, Pallas kernels, two_of(): pl.pallas_call(two_kernel, out_shape=[jax.ShapeDtypeStruct((rows, cols),...  9.15 us
    all_to_all x1, starting transfers between devices, scatter(): lax.all_to_all(block.reshape(members, rows // members, width), 'slab', 0,...  7.76 us
    pallas_call x1, Pallas kernels, tile_of(): pl.pallas_call(functools.partial(tile_kernel, carry is not None, last), o...  6.21 us
  transfers between devices with their start and end apart: 17, of which 9 were waited for; matrix products, arithmetic and copies ran while one was open for 5% of the time, Pallas kernels for 17%

profile of v8, /device:TPU:161, one launch (start us, length us, event | category | flops | bytes accessed | tf_op | source)
XLA Modules:
  0.0 204.6 jit_solution(2899970890015186536)
XLA Ops:
  0.0 5.1 %join.1 = (bf16[1024,896]{1,0:T(8,128)(2,1)}, bf16[1024,512]{1,0:T(8,128)(2,1)}, bf16[1296,256]{1,0:T(8,128)(2,1)}) custom-call(s32[4]{0:T(128)} %bitcast.62, bf16[1024,512]{1,0:T(8,128)(2,1)} %x_ref.1, bf16[1024,256]{1,0:T(8,128)(2,1)} %refs_14_.1, s32[4,16,1024]{2,1,0:T(8,128)} %bitcast.61), custom_call_target="tpu_custom_call" | custom-call | tf_op jit(solution)/shard_map/join/pallas_call | solution.py:55
  5.1 7.8 %all-to-all-start = ((bf16[32,32,896]{2,1,0:T(8,128)(2,1)}), bf16[32,32,896]{2,1,0:T(8,128)(2,1)S(1)}, u32[]{:S(2)}, u32[]{:S(2)}) async-start(bf16[32,32,896]{2,1,0:T(8,128)(2,1)} %bitcast.54), calls=%async_computation | async-start | bytes 3670016 | tf_op jit(solution)/shard_map/all_to_all | solution.py:434
  12.9 1.3 collective-permute-start
  16.2 7.0 %keep_words.2.w_ref.words_ref.refs_10_ = s32[4,1024,128]{2,1,0:T(8,128)} custom-call(s32[1]{0:T(128)} %bitcast.6.pick_ref, bf16[1,1296,256]{2,1,0:T(8,128)(2,1)} %bitcast.7.coded_ref), custom_call_target="tpu_custom_call" | custom-call | flops 1 | bytes 524288 | tf_op jit(solution)/shard_map/keep_words/pallas_call | solution.py:96
  23.2 6.2 %tile.1 = (f32[1024,128]{1,0:T(8,128)}, f32[1024,256]{1,0:T(8,128)}, bf16[1024,1024]{1,0:T(8,128)(2,1)}) custom-call(s32[1]{0:T(128)} %bitcast.6.pick_ref, bf16[1024,896]{1,0:T(8,128)(2,1)} %get-tuple-element.44.x_ref.other_ref.y_ref, bf16[1024,896]{1,0:T(8,128)(2,1)} %get-tuple-element.44.x_ref.other_ref.y_ref, ...), custom_call_target="tpu_custom_call" | custom-call | flops 262144 | bytes 262144 | tf_op jit(solution)/shard_map/tile/pallas_call | solution.py:163
  33.7 9.2 %collective-permute-done = bf16[1296,256]{1,0:T(8,128)(2,1)} collective-permute-done((bf16[1296,256]{1,0:T(8,128)(2,1)}, bf16[1296,256]{1,0:T(8,128)(2,1)}, u32[]{:S(2)}, u32[]{:S(2)}) %collective-permute-start) | collective-permute-done | bytes 663584 | tf_op jit(solution)/shard_map/ppermute | solution.py:394
  45.4 7.4 %collective-permute-done.2 = bf16[2,32,896]{2,1,0:T(8,128)(2,1)S(1)} collective-permute-done((bf16[2,32,896]{2,1,0:T(8,128)(2,1)S(1)}, bf16[2,32,896]{2,1,0:T(8,128)(2,1)S(1)}, u32[]{:S(2)}, u32[]{:S(2)}) %collective-permute-start.2) | collective-permute-done | bytes 114720 | tf_op jit(solution)/shard_map/ppermute | solution.py:394
  52.9 1.4 collective-permute-start.3
  54.3 2.9 %collective-permute-done.3 = bf16[1,2,32,896]{3,2,1,0:T(8,128)(2,1)S(1)} collective-permute-done((bf16[1,2,32,896]{3,2,1,0:T(8,128)(2,1)S(1)}, bf16[1,2,32,896]{3,2,1,0:T(8,128)(2,1)S(1)}, u32[]{:S(2)}, u32[]{:S(2)}) %collective-permute-start.3) | collective-permute-done | bytes 114720 | tf_op jit(solution)/shard_map/ppermute | solution.py:394
  57.4 3.3 %collective-permute-start.4 = (bf16[2,2,32,896]{3,2,1,0:T(8,128)(2,1)S(1)}, bf16[2,2,32,896]{3,2,1,0:T(8,128)(2,1)S(1)}, u32[]{:S(2)}, u32[]{:S(2)}) collective-permute-start(bf16[2,2,32,896]{3,2,1,0:T(8,128)(2,1)S(1)} %pad_maximum_fusion.2), channel_id=1, source_target_pairs={{0,2},{1,3},{2,0},{3,1},{4,6},{5,7},{6,4},{7,5},{8,10},{9,11},{10,... | collective-permute-start | bytes 688136 | tf_op jit(solution)/shard_map/ppermute | solution.py:394
  65.0 5.5 %collective-permute-done.4 = bf16[2,2,32,896]{3,2,1,0:T(8,128)(2,1)S(1)} collective-permute-done((bf16[2,2,32,896]{3,2,1,0:T(8,128)(2,1)S(1)}, bf16[2,2,32,896]{3,2,1,0:T(8,128)(2,1)S(1)}, u32[]{:S(2)}, u32[]{:S(2)}) %collective-permute-start.4) | collective-permute-done | bytes 229408 | tf_op jit(solution)/shard_map/ppermute | solution.py:394
  73.2 2.1 %collective-permute-start.6 = (bf16[1296,256]{1,0:T(8,128)(2,1)}, bf16[1296,256]{1,0:T(8,128)(2,1)}, u32[]{:S(2)}, u32[]{:S(2)}) collective-permute-start(bf16[1296,256]{1,0:T(8,128)(2,1)} %collective-permute-done), channel_id=1, source_target_pairs={{1,0},{2,3},{5,4},{6,7},{9,8},{10,11},{13,12},{14,15},{17,16},{18,... | collective-permute-start | bytes 1990664 | tf_op jit(solution)/shard_map/ppermute | solution.py:394
  75.3 5.9 %collective-permute-start.7 = (bf16[1296,256]{1,0:T(8,128)(2,1)}, bf16[1296,256]{1,0:T(8,128)(2,1)}, u32[]{:S(2)}, u32[]{:S(2)}) collective-permute-start(bf16[1296,256]{1,0:T(8,128)(2,1)} %get-tuple-element.54), channel_id=1, source_target_pairs={{1,2},{2,1},{5,6},{6,5},{9,10},{10,9},{13,14},{14,13},{17,18},{18,... | collective-permute-start | bytes 1990664 | tf_op jit(solution)/shard_map/ppermute | solution.py:394
  81.3 1.3 collective-permute-start.5
  84.3 2.0 broadcast_in_dim.90
  86.3 7.2 %all-to-all-start.1 = ((bf16[16,2,64,768]{3,2,1,0:T(8,128)(2,1)}), bf16[16,2,64,768]{3,2,1,0:T(8,128)(2,1)S(1)}, u32[]{:S(2)}, u32[]{:S(2)}) async-start(bf16[16,2,64,768]{3,2,1,0:T(8,128)(2,1)} %broadcast_in_dim.90), calls=%async_computation.1 | async-start | bytes 6291456 | tf_op jit(solution)/shard_map/all_to_all | solution.py:417
  93.5 24.7 %collective-permute-done.7 = bf16[1296,256]{1,0:T(8,128)(2,1)} collective-permute-done((bf16[1296,256]{1,0:T(8,128)(2,1)}, bf16[1296,256]{1,0:T(8,128)(2,1)}, u32[]{:S(2)}, u32[]{:S(2)}) %collective-permute-start.7) | collective-permute-done | bytes 663584 | tf_op jit(solution)/shard_map/ppermute | solution.py:394
  119.4 1.8 pad_maximum_fusion.coded_ref.refs_6_.refs_7_
  121.3 1.5 copy-done.1
  125.3 7.7 %keep_words.3.refs_11_ = s32[4,1024,128]{2,1,0:T(8,128)} custom-call(s32[6]{0:T(128)} %stack.66.pick_ref, bf16[4,1296,256]{2,1,0:T(8,128)(2,1)} %copy-done.1), custom_call_target="tpu_custom_call" | custom-call | flops 30000001024 | bytes 524288 | tf_op jit(solution)/shard_map/keep_words/pallas_call | solution.py:96
  132.9 6.7 %collective-permute-done.8.refs_2_ = bf16[1024,512]{1,0:T(8,128)(2,1)} collective-permute-done((bf16[1024,512]{1,0:T(8,128)(2,1)}, bf16[1024,512]{1,0:T(8,128)(2,1)}, u32[]{:S(2)}, u32[]{:S(2)}) %collective-permute-start.8) | collective-permute-done | bytes 1048608 | tf_op jit(solution)/shard_map/ppermute | solution.py:394
  139.7 1.4 slice_bitcast_fusion
  141.1 1.9 collective-permute-start.10
  143.0 4.8 %collective-permute-start.12 = (bf16[1024,512]{1,0:T(8,128)(2,1)}, bf16[1024,512]{1,0:T(8,128)(2,1)}, u32[]{:S(2)}, u32[]{:S(2)}) collective-permute-start(bf16[1024,512]{1,0:T(8,128)(2,1)} %collective-permute-done.8.refs_2_), channel_id=1, source_target_pairs={{1,0},{2,3},{5,4},{6,7},{9,8},{10,11},{13,12},{14,15},{17,16},{18,... | collective-permute-start | bytes 3145736 | tf_op jit(solution)/shard_map/ppermute | solution.py:394
  147.8 3.4 %collective-permute-start.13 = (bf16[1024,512]{1,0:T(8,128)(2,1)}, bf16[1024,512]{1,0:T(8,128)(2,1)}, u32[]{:S(2)}, u32[]{:S(2)}) collective-permute-start(bf16[1024,512]{1,0:T(8,128)(2,1)} %get-tuple-element.59.rows_ref.refs_0_.refs_5_), channel_id=1, source_target_pairs={{1,2},{2,1},{5,6},{6,5},{9,10},{10,9},{13,14},{14,13},{17,18},{18,... | collective-permute-start | bytes 3145736 | tf_op jit(solution)/shard_map/ppermute | solution.py:394
  152.9 5.2 %hub_rows.1 = bf16[64,256]{1,0:T(8,128)(2,1)} custom-call(s32[1]{0:T(128)} %bitcast.40.pick_ref, bf16[64,896]{1,0:T(8,128)(2,1)} %fusion.1.rows_ref, bf16[16,2,64,768]{3,2,1,0:T(8,128)(2,1)} %copy-done, bf16[16,64,768]{2,1,0:T(8,128)(2,1)} %collective-permute-done.10.far_ref.refs_9_), custom_call_target="tpu_custom_call" | custom-call | flops 1024 | bytes 1024 | tf_op jit(solution)/shard_map/hub_rows/pallas_call | solution.py:365
  158.1 1.6 broadcast_in_dim.92
  159.7 6.5 %all-to-all-start.2 = ((bf16[16,64,256]{2,1,0:T(8,128)(2,1)}), bf16[16,64,256]{2,1,0:T(8,128)(2,1)S(1)}, u32[]{:S(2)}, u32[]{:S(2)}) async-start(bf16[16,64,256]{2,1,0:T(8,128)(2,1)} %broadcast_in_dim.92), calls=%async_computation.2 | async-start | bytes 1048576 | tf_op jit(solution)/shard_map/all_to_all | solution.py:417
  166.2 9.2 %two.1 = (bf16[1024,1024]{1,0:T(8,128)(2,1)}, bf16[1024,1024]{1,0:T(8,128)(2,1)}, f32[1024,128]{1,0:T(8,128)}, f32[1024,256]{1,0:T(8,128)}) custom-call(s32[6]{0:T(128)} %stack.66.pick_ref, bf16[1024,512]{1,0:T(8,128)(2,1)} %get-tuple-element.59.rows_ref.refs_0_.refs_5_, bf16[16,2,64,768]{3,2,1,0:T(8,128)(2,1)} %copy-done, ...), custom_call_target="tpu_custom_call" | custom-call | flops 262144 | bytes 262144 | tf_op jit(solution)/shard_map/two/pallas_call | solution.py:222
  176.5 2.1 %collective-permute-start.11 = (bf16[1024,256]{1,0:T(8,128)(2,1)S(1)}, bf16[1024,256]{1,0:T(8,128)(2,1)S(1)}, u32[]{:S(2)}, u32[]{:S(2)}) collective-permute-start(bf16[1024,256]{1,0:T(8,128)(2,1)S(1)} %bitcast.56), channel_id=1, source_target_pairs={{0,4},{1,5},{2,6},{3,7},{4,0},{5,1},{6,2},{7,3},{8,12},{9,13},{10,... | collective-permute-start | bytes 1572872 | tf_op jit(solution)/shard_map/ppermute | solution.py:394
  178.7 1.5 collective-permute-done.11.refs_19_
  181.0 23.4 %finish.1 = bf16[1024,256]{1,0:T(8,128)(2,1)} custom-call(s32[6]{0:T(128)} %stack.66.pick_ref, bf16[1024,512]{1,0:T(8,128)(2,1)} %get-tuple-element.59.rows_ref.refs_0_.refs_5_, bf16[1024,512]{1,0:T(8,128)(2,1)} %collective-permute-done.9.refs_1_, bf16[1024,512]{1,0:T(8,128)(2,1)} %collective-permute-done.8.refs_2_, ...), custom_call_target="tpu_custom_call" | custom-call | flops 9663676416 | bytes 12582912 | tf_op jit(solution)/shard_map/finish/pallas_call | solution.py:292
  (55 shorter events, 13.2 us)
Async XLA Ops:
  0.0 14.9 %copy-start.4 = (s32[1,4]{1,0:T(1,128)S(1)}, s32[1,4]{1,0:T(1,128)}, u32[]{:S(2)}) copy-start(s32[1,4]{1,0:T(1,128)} %param.7) | copy-start | bytes 52
  5.1 39.1 %all-to-all-start = ((bf16[32,32,896]{2,1,0:T(8,128)(2,1)}), bf16[32,32,896]{2,1,0:T(8,128)(2,1)S(1)}, u32[]{:S(2)}, u32[]{:S(2)}) async-start(bf16[32,32,896]{2,1,0:T(8,128)(2,1)} %bitcast.54), calls=%async_computation | async-start | bytes 3670016 | tf_op jit(solution)/shard_map/all_to_all | solution.py:434
  12.9 30.0 %collective-permute-start = (bf16[1296,256]{1,0:T(8,128)(2,1)}, bf16[1296,256]{1,0:T(8,128)(2,1)}, u32[]{:S(2)}, u32[]{:S(2)}) collective-permute-start(bf16[1296,256]{1,0:T(8,128)(2,1)} %get-tuple-element.54), channel_id=1, source_target_pairs={{0,2},{1,3},{2,0},{3,1},{4,6},{5,7},{6,4},{7,5},{8,10},{9,11},{10,... | collective-permute-start | bytes 1990664 | tf_op jit(solution)/shard_map/ppermute | solution.py:394
  14.2 30.0 %collective-permute-start.1 = (bf16[1296,256]{1,0:T(8,128)(2,1)}, bf16[1296,256]{1,0:T(8,128)(2,1)S(1)}, u32[]{:S(2)}, u32[]{:S(2)}) collective-permute-start(bf16[1296,256]{1,0:T(8,128)(2,1)} %get-tuple-element.54), channel_id=1, source_target_pairs={{0,1},{1,0},{2,3},{3,2},{4,5},{5,4},{6,7},{7,6},{8,9},{9,8},{10,11... | collective-permute-start | bytes 1990664 | tf_op jit(solution)/shard_map/ppermute | solution.py:394
  23.2 6.2 %copy-start.5 = (s32[2]{0:T(128)S(1)}, s32[2]{0:T(128)}, u32[]{:S(2)}) copy-start(s32[2]{0:T(128)} %param.8) | copy-start | bytes 28
  44.2 0.8 copy-start.2
  45.1 7.8 %collective-permute-start.2 = (bf16[2,32,896]{2,1,0:T(8,128)(2,1)S(1)}, bf16[2,32,896]{2,1,0:T(8,128)(2,1)S(1)}, u32[]{:S(2)}, u32[]{:S(2)}) collective-permute-start(bf16[2,32,896]{2,1,0:T(8,128)(2,1)S(1)} %pad_maximum_fusion.4), channel_id=1, source_target_pairs={{0,128},{1,129},{2,130},{3,131},{4,132},{5,133},{6,134},{7,135},{8... | collective-permute-start | bytes 344072 | tf_op jit(solution)/shard_map/ppermute | solution.py:394
  52.9 4.3 %collective-permute-start.3 = (bf16[1,2,32,896]{3,2,1,0:T(8,128)(2,1)S(1)}, bf16[1,2,32,896]{3,2,1,0:T(8,128)(2,1)S(1)}, u32[]{:S(2)}, u32[]{:S(2)}) collective-permute-start(bf16[1,2,32,896]{3,2,1,0:T(8,128)(2,1)S(1)} %select_bitcast_fusion.1), channel_id=1, source_target_pairs={{0,1},{1,0},{2,3},{3,2},{4,5},{5,4},{6,7},{7,6},{8,9},{9,8},{10,11... | collective-permute-start | bytes 344072 | tf_op jit(solution)/shard_map/ppermute | solution.py:394
  57.4 13.1 %collective-permute-start.4 = (bf16[2,2,32,896]{3,2,1,0:T(8,128)(2,1)S(1)}, bf16[2,2,32,896]{3,2,1,0:T(8,128)(2,1)S(1)}, u32[]{:S(2)}, u32[]{:S(2)}) collective-permute-start(bf16[2,2,32,896]{3,2,1,0:T(8,128)(2,1)S(1)} %pad_maximum_fusion.2), channel_id=1, source_target_pairs={{0,2},{1,3},{2,0},{3,1},{4,6},{5,7},{6,4},{7,5},{8,10},{9,11},{10,... | collective-permute-start | bytes 688136 | tf_op jit(solution)/shard_map/ppermute | solution.py:394
  73.2 20.4 %collective-permute-start.6 = (bf16[1296,256]{1,0:T(8,128)(2,1)}, bf16[1296,256]{1,0:T(8,128)(2,1)}, u32[]{:S(2)}, u32[]{:S(2)}) collective-permute-start(bf16[1296,256]{1,0:T(8,128)(2,1)} %collective-permute-done), channel_id=1, source_target_pairs={{1,0},{2,3},{5,4},{6,7},{9,8},{10,11},{13,12},{14,15},{17,16},{18,... | collective-permute-start | bytes 1990664 | tf_op jit(solution)/shard_map/ppermute | solution.py:394
  75.3 43.0 %collective-permute-start.7 = (bf16[1296,256]{1,0:T(8,128)(2,1)}, bf16[1296,256]{1,0:T(8,128)(2,1)}, u32[]{:S(2)}, u32[]{:S(2)}) collective-permute-start(bf16[1296,256]{1,0:T(8,128)(2,1)} %get-tuple-element.54), channel_id=1, source_target_pairs={{1,2},{2,1},{5,6},{6,5},{9,10},{10,9},{13,14},{14,13},{17,18},{18,... | collective-permute-start | bytes 1990664 | tf_op jit(solution)/shard_map/ppermute | solution.py:394
  81.3 3.0 %collective-permute-start.5 = (bf16[2,32,896]{2,1,0:T(8,128)(2,1)S(1)}, bf16[2,32,896]{2,1,0:T(8,128)(2,1)S(1)}, u32[]{:S(2)}, u32[]{:S(2)}) collective-permute-start(bf16[2,32,896]{2,1,0:T(8,128)(2,1)S(1)} %broadcast_select_fusion.6), channel_id=1, source_target_pairs={{0,4},{1,5},{2,6},{3,7},{4,0},{5,1},{6,2},{7,3},{8,12},{9,13},{10,... | collective-permute-start | bytes 344072 | tf_op jit(solution)/shard_map/ppermute | solution.py:394
  83.2 56.5 %collective-permute-start.8 = (bf16[1024,512]{1,0:T(8,128)(2,1)}, bf16[1024,512]{1,0:T(8,128)(2,1)}, u32[]{:S(2)}, u32[]{:S(2)}) collective-permute-start(bf16[1024,512]{1,0:T(8,128)(2,1)} %get-tuple-element.59.rows_ref.refs_0_.refs_5_), channel_id=1, source_target_pairs={{0,2},{1,3},{2,0},{3,1},{4,6},{5,7},{6,4},{7,5},{8,10},{9,11},{10,... | collective-permute-start | bytes 3145736 | tf_op jit(solution)/shard_map/ppermute | solution.py:394
  83.3 56.4 %collective-permute-start.9 = (bf16[1024,512]{1,0:T(8,128)(2,1)}, bf16[1024,512]{1,0:T(8,128)(2,1)}, u32[]{:S(2)}, u32[]{:S(2)}) collective-permute-start(bf16[1024,512]{1,0:T(8,128)(2,1)} %get-tuple-element.59.rows_ref.refs_0_.refs_5_), channel_id=1, source_target_pairs={{0,1},{1,0},{2,3},{3,2},{4,5},{5,4},{6,7},{7,6},{8,9},{9,8},{10,11... | collective-permute-start | bytes 3145736 | tf_op jit(solution)/shard_map/ppermute | solution.py:394
  86.3 53.4 %all-to-all-start.1 = ((bf16[16,2,64,768]{3,2,1,0:T(8,128)(2,1)}), bf16[16,2,64,768]{3,2,1,0:T(8,128)(2,1)S(1)}, u32[]{:S(2)}, u32[]{:S(2)}) async-start(bf16[16,2,64,768]{3,2,1,0:T(8,128)(2,1)} %broadcast_in_dim.90), calls=%async_computation.1 | async-start | bytes 6291456 | tf_op jit(solution)/shard_map/all_to_all | solution.py:417
  121.3 1.5 copy-start.1
  139.7 13.2 %copy-start = (bf16[16,2,64,768]{3,2,1,0:T(8,128)(2,1)}, bf16[16,2,64,768]{3,2,1,0:T(8,128)(2,1)S(1)}, u32[]{:S(2)}) copy-start(bf16[16,2,64,768]{3,2,1,0:T(8,128)(2,1)S(1)} %all-to-all-done.1.near_ref.refs_8_) | copy-start | bytes 9437188
  141.1 11.8 %collective-permute-start.10 = (bf16[16,64,768]{2,1,0:T(8,128)(2,1)}, bf16[16,64,768]{2,1,0:T(8,128)(2,1)}, u32[]{:S(2)}, u32[]{:S(2)}) collective-permute-start(bf16[16,64,768]{2,1,0:T(8,128)(2,1)} %slice_bitcast_fusion), channel_id=1, source_target_pairs={{0,4},{1,5},{2,6},{3,7},{4,0},{5,1},{6,2},{7,3},{8,12},{9,13},{10,... | collective-permute-start | bytes 4718600 | tf_op jit(solution)/shard_map/ppermute | solution.py:394
  143.0 35.7 %collective-permute-start.12 = (bf16[1024,512]{1,0:T(8,128)(2,1)}, bf16[1024,512]{1,0:T(8,128)(2,1)}, u32[]{:S(2)}, u32[]{:S(2)}) collective-permute-start(bf16[1024,512]{1,0:T(8,128)(2,1)} %collective-permute-done.8.refs_2_), channel_id=1, source_target_pairs={{1,0},{2,3},{5,4},{6,7},{9,8},{10,11},{13,12},{14,15},{17,16},{18,... | collective-permute-start | bytes 3145736 | tf_op jit(solution)/shard_map/ppermute | solution.py:394
  147.8 30.9 %collective-permute-start.13 = (bf16[1024,512]{1,0:T(8,128)(2,1)}, bf16[1024,512]{1,0:T(8,128)(2,1)}, u32[]{:S(2)}, u32[]{:S(2)}) collective-permute-start(bf16[1024,512]{1,0:T(8,128)(2,1)} %get-tuple-element.59.rows_ref.refs_0_.refs_5_), channel_id=1, source_target_pairs={{1,2},{2,1},{5,6},{6,5},{9,10},{10,9},{13,14},{14,13},{17,18},{18,... | collective-permute-start | bytes 3145736 | tf_op jit(solution)/shard_map/ppermute | solution.py:394
  159.7 16.8 %all-to-all-start.2 = ((bf16[16,64,256]{2,1,0:T(8,128)(2,1)}), bf16[16,64,256]{2,1,0:T(8,128)(2,1)S(1)}, u32[]{:S(2)}, u32[]{:S(2)}) async-start(bf16[16,64,256]{2,1,0:T(8,128)(2,1)} %broadcast_in_dim.92), calls=%async_computation.2 | async-start | bytes 1048576 | tf_op jit(solution)/shard_map/all_to_all | solution.py:417
  176.5 3.7 %copy-start.3 = (bf16[16,64,256]{2,1,0:T(8,128)(2,1)}, bf16[16,64,256]{2,1,0:T(8,128)(2,1)S(1)}, u32[]{:S(2)}) copy-start(bf16[16,64,256]{2,1,0:T(8,128)(2,1)S(1)} %all-to-all-done.2) | copy-start | bytes 1572868
  176.5 3.7 %collective-permute-start.11 = (bf16[1024,256]{1,0:T(8,128)(2,1)S(1)}, bf16[1024,256]{1,0:T(8,128)(2,1)S(1)}, u32[]{:S(2)}, u32[]{:S(2)}) collective-permute-start(bf16[1024,256]{1,0:T(8,128)(2,1)S(1)} %bitcast.56), channel_id=1, source_target_pairs={{0,4},{1,5},{2,6},{3,7},{4,0},{5,1},{6,2},{7,3},{8,12},{9,13},{10,... | collective-permute-start | bytes 1572872 | tf_op jit(solution)/shard_map/ppermute | solution.py:394
  180.2 0.8 copy-start.6

commit v9 on v8

--- a/solution.py
+++ b/solution.py
@@ -503,8 +503,9 @@
     held, hub_rep = hub_candidates(mine, hub_ids)
     held, normed, rest, across = barrier((held, normed, rest, across))
 
-    outer, middle = along_line(across, OUTWARD), along_line(rest, MIDDLE)
-    across_x, beside_x = spread_line(normed)
+    middle, outer = along_line(rest, MIDDLE), along_line(across, OUTWARD)
+    beside_x = along_line(normed, {0: 1, 1: 0, 2: 3, 3: 2})
+    across_x = along_line(normed, {0: 2, 2: 0, 1: 3, 3: 1})
     both = hub_share(held, hub_rep, full)
     near = join_pieces(both[:, :, :full])
     at_end = (rep == 0) | (rep == 3)
@@ -518,8 +519,8 @@
         [near_slot, place(at), place(second), jnp.where(member_order == core, 2, 3), at, second]
     ).astype(jnp.int32)
     member_words = keep_words(pick, group_rest, lambda pick: pick[4], rows, WORDS_HINT)
-    near, group_rest, member_words, pick, normed, across_x, beside_x = barrier(
-        (near, group_rest, member_words, pick, normed, across_x, beside_x)
+    near, group_rest, member_words, pick, normed, beside_x, across_x = barrier(
+        (near, group_rest, member_words, pick, normed, beside_x, across_x)
     )
 
     far = swap_cores(near[:, 0])

time: 206 us -> 206 us (level)
  transfers between devices with their start and end apart: 17 -> 17, of which waited for: 9 -> 10; matrix products, arithmetic and copies ran while one was open for 5% -> 5% of each run, Pallas kernels for 17% -> 17%
where the time goes in v9:
time: 206 us; the launch traced here: 205 us
  Pallas kernels  63.8 us (31%)
  waiting for transfers between devices  60.4 us (29%)
  starting transfers between devices  51.1 us (25%)
  local copies, waits for them, and re-layouts  12.3 us (6%)
  between operations  12.3 us (6%)
  other arithmetic  4.7 us (2%)
    ppermute x14, waiting for transfers between devices, send(): return lax.ppermute(block, AXES, pairs)  59.3 us
    ppermute x14, starting transfers between devices, send(): return lax.ppermute(block, AXES, pairs)  29.6 us
    pallas_call x1, Pallas kernels, finish_of(): pl.pallas_call(finish_kernel, out_shape=jax.ShapeDtypeStruct((rows, clust...  23.4 us
    pallas_call x2, Pallas kernels, keep_words(): pl.pallas_call(words_kernel, out_shape=jax.ShapeDtypeStruct((K, rows, LAN...  14.7 us
    all_to_all x2, starting transfers between devices, join_pieces(): lax.all_to_all(repeated, 'slab', 0, 0, axis_index_groups=layers, tiled=True)  13.8 us
    pallas_call x1, Pallas kernels, two_of(): pl.pallas_call(two_kernel, out_shape=[jax.ShapeDtypeStruct((rows, cols),...  9.15 us
    all_to_all x1, starting transfers between devices, scatter(): lax.all_to_all(block.reshape(members, rows // members, width), 'slab', 0,...  7.76 us
    pallas_call x1, Pallas kernels, tile_of(): pl.pallas_call(functools.partial(tile_kernel, carry is not None, last), o...  6.21 us
  transfers between devices with their start and end apart: 17, of which 10 were waited for; matrix products, arithmetic and copies ran while one was open for 5% of the time, Pallas kernels for 17%

profile of v9, /device:TPU:161, one launch (start us, length us, event | category | flops | bytes accessed | tf_op | source)
XLA Modules:
  0.0 204.6 jit_solution(13064605332136187897)
XLA Ops:
  0.0 5.1 %join.1 = (bf16[1024,896]{1,0:T(8,128)(2,1)}, bf16[1024,512]{1,0:T(8,128)(2,1)}, bf16[1296,256]{1,0:T(8,128)(2,1)}) custom-call(s32[4]{0:T(128)} %bitcast.62, bf16[1024,512]{1,0:T(8,128)(2,1)} %x_ref.1, bf16[1024,256]{1,0:T(8,128)(2,1)} %refs_14_.1, s32[4,16,1024]{2,1,0:T(8,128)} %bitcast.61), custom_call_target="tpu_custom_call" | custom-call | tf_op jit(solution)/shard_map/join/pallas_call | solution.py:55
  5.1 7.8 %all-to-all-start = ((bf16[32,32,896]{2,1,0:T(8,128)(2,1)}), bf16[32,32,896]{2,1,0:T(8,128)(2,1)S(1)}, u32[]{:S(2)}, u32[]{:S(2)}) async-start(bf16[32,32,896]{2,1,0:T(8,128)(2,1)} %bitcast.54), calls=%async_computation | async-start | bytes 3670016 | tf_op jit(solution)/shard_map/all_to_all | solution.py:434
  16.2 7.0 %keep_words.2.w_ref.words_ref.refs_10_ = s32[4,1024,128]{2,1,0:T(8,128)} custom-call(s32[1]{0:T(128)} %bitcast.6.pick_ref, bf16[1,1296,256]{2,1,0:T(8,128)(2,1)} %bitcast.7.coded_ref), custom_call_target="tpu_custom_call" | custom-call | flops 1 | bytes 524288 | tf_op jit(solution)/shard_map/keep_words/pallas_call | solution.py:96
  23.2 6.2 %tile.1 = (f32[1024,128]{1,0:T(8,128)}, f32[1024,256]{1,0:T(8,128)}, bf16[1024,1024]{1,0:T(8,128)(2,1)}) custom-call(s32[1]{0:T(128)} %bitcast.6.pick_ref, bf16[1024,896]{1,0:T(8,128)(2,1)} %get-tuple-element.44.x_ref.other_ref.y_ref, bf16[1024,896]{1,0:T(8,128)(2,1)} %get-tuple-element.44.x_ref.other_ref.y_ref, ...), custom_call_target="tpu_custom_call" | custom-call | flops 262144 | bytes 262144 | tf_op jit(solution)/shard_map/tile/pallas_call | solution.py:163
  33.7 9.2 %collective-permute-done = bf16[1296,256]{1,0:T(8,128)(2,1)} collective-permute-done((bf16[1296,256]{1,0:T(8,128)(2,1)}, bf16[1296,256]{1,0:T(8,128)(2,1)}, u32[]{:S(2)}, u32[]{:S(2)}) %collective-permute-start) | collective-permute-done | bytes 663584 | tf_op jit(solution)/shard_map/ppermute | solution.py:394
  45.4 7.4 %collective-permute-done.2 = bf16[2,32,896]{2,1,0:T(8,128)(2,1)S(1)} collective-permute-done((bf16[2,32,896]{2,1,0:T(8,128)(2,1)S(1)}, bf16[2,32,896]{2,1,0:T(8,128)(2,1)S(1)}, u32[]{:S(2)}, u32[]{:S(2)}) %collective-permute-start.2) | collective-permute-done | bytes 114720 | tf_op jit(solution)/shard_map/ppermute | solution.py:394
  52.9 1.4 collective-permute-start.3
  54.3 2.9 %collective-permute-done.3 = bf16[1,2,32,896]{3,2,1,0:T(8,128)(2,1)S(1)} collective-permute-done((bf16[1,2,32,896]{3,2,1,0:T(8,128)(2,1)S(1)}, bf16[1,2,32,896]{3,2,1,0:T(8,128)(2,1)S(1)}, u32[]{:S(2)}, u32[]{:S(2)}) %collective-permute-start.3) | collective-permute-done | bytes 114720 | tf_op jit(solution)/shard_map/ppermute | solution.py:394
  57.4 3.3 %collective-permute-start.4 = (bf16[2,2,32,896]{3,2,1,0:T(8,128)(2,1)S(1)}, bf16[2,2,32,896]{3,2,1,0:T(8,128)(2,1)S(1)}, u32[]{:S(2)}, u32[]{:S(2)}) collective-permute-start(bf16[2,2,32,896]{3,2,1,0:T(8,128)(2,1)S(1)} %pad_maximum_fusion.2), channel_id=1, source_target_pairs={{0,2},{1,3},{2,0},{3,1},{4,6},{5,7},{6,4},{7,5},{8,10},{9,11},{10,... | collective-permute-start | bytes 688136 | tf_op jit(solution)/shard_map/ppermute | solution.py:394
  65.0 5.5 %collective-permute-done.4 = bf16[2,2,32,896]{3,2,1,0:T(8,128)(2,1)S(1)} collective-permute-done((bf16[2,2,32,896]{3,2,1,0:T(8,128)(2,1)S(1)}, bf16[2,2,32,896]{3,2,1,0:T(8,128)(2,1)S(1)}, u32[]{:S(2)}, u32[]{:S(2)}) %collective-permute-start.4) | collective-permute-done | bytes 229408 | tf_op jit(solution)/shard_map/ppermute | solution.py:394
  73.2 2.1 %collective-permute-start.6 = (bf16[1296,256]{1,0:T(8,128)(2,1)}, bf16[1296,256]{1,0:T(8,128)(2,1)}, u32[]{:S(2)}, u32[]{:S(2)}) collective-permute-start(bf16[1296,256]{1,0:T(8,128)(2,1)} %collective-permute-done), channel_id=1, source_target_pairs={{1,0},{2,3},{5,4},{6,7},{9,8},{10,11},{13,12},{14,15},{17,16},{18,... | collective-permute-start | bytes 1990664 | tf_op jit(solution)/shard_map/ppermute | solution.py:394
  75.3 5.9 %collective-permute-start.7 = (bf16[1296,256]{1,0:T(8,128)(2,1)}, bf16[1296,256]{1,0:T(8,128)(2,1)}, u32[]{:S(2)}, u32[]{:S(2)}) collective-permute-start(bf16[1296,256]{1,0:T(8,128)(2,1)} %get-tuple-element.54), channel_id=1, source_target_pairs={{1,2},{2,1},{5,6},{6,5},{9,10},{10,9},{13,14},{14,13},{17,18},{18,... | collective-permute-start | bytes 1990664 | tf_op jit(solution)/shard_map/ppermute | solution.py:394
  81.3 1.3 collective-permute-start.5
  84.3 2.0 broadcast_in_dim.90
  86.3 7.2 %all-to-all-start.1 = ((bf16[16,2,64,768]{3,2,1,0:T(8,128)(2,1)}), bf16[16,2,64,768]{3,2,1,0:T(8,128)(2,1)S(1)}, u32[]{:S(2)}, u32[]{:S(2)}) async-start(bf16[16,2,64,768]{3,2,1,0:T(8,128)(2,1)} %broadcast_in_dim.90), calls=%async_computation.1 | async-start | bytes 6291456 | tf_op jit(solution)/shard_map/all_to_all | solution.py:417
  93.5 2.3 %collective-permute-done.7 = bf16[1296,256]{1,0:T(8,128)(2,1)} collective-permute-done((bf16[1296,256]{1,0:T(8,128)(2,1)}, bf16[1296,256]{1,0:T(8,128)(2,1)}, u32[]{:S(2)}, u32[]{:S(2)}) %collective-permute-start.7) | collective-permute-done | bytes 663584 | tf_op jit(solution)/shard_map/ppermute | solution.py:394
  97.0 1.8 pad_maximum_fusion.coded_ref.refs_6_.refs_7_
  98.8 1.5 copy-done.1
  102.8 7.7 %keep_words.3.refs_11_ = s32[4,1024,128]{2,1,0:T(8,128)} custom-call(s32[6]{0:T(128)} %stack.66.pick_ref, bf16[4,1296,256]{2,1,0:T(8,128)(2,1)} %copy-done.1), custom_call_target="tpu_custom_call" | custom-call | flops 30000001024 | bytes 524288 | tf_op jit(solution)/shard_map/keep_words/pallas_call | solution.py:96
  110.5 10.0 %collective-permute-done.8.refs_1_ = bf16[1024,512]{1,0:T(8,128)(2,1)} collective-permute-done((bf16[1024,512]{1,0:T(8,128)(2,1)}, bf16[1024,512]{1,0:T(8,128)(2,1)}, u32[]{:S(2)}, u32[]{:S(2)}) %collective-permute-start.8) | collective-permute-done | bytes 1048608 | tf_op jit(solution)/shard_map/ppermute | solution.py:394
  120.5 19.2 %collective-permute-done.9.refs_2_ = bf16[1024,512]{1,0:T(8,128)(2,1)} collective-permute-done((bf16[1024,512]{1,0:T(8,128)(2,1)}, bf16[1024,512]{1,0:T(8,128)(2,1)}, u32[]{:S(2)}, u32[]{:S(2)}) %collective-permute-start.9) | collective-permute-done | bytes 1048608 | tf_op jit(solution)/shard_map/ppermute | solution.py:394
  139.7 1.4 slice_bitcast_fusion
  141.2 1.9 collective-permute-start.10
  143.0 4.8 %collective-permute-start.12 = (bf16[1024,512]{1,0:T(8,128)(2,1)}, bf16[1024,512]{1,0:T(8,128)(2,1)}, u32[]{:S(2)}, u32[]{:S(2)}) collective-permute-start(bf16[1024,512]{1,0:T(8,128)(2,1)} %collective-permute-done.9.refs_2_), channel_id=1, source_target_pairs={{1,0},{2,3},{5,4},{6,7},{9,8},{10,11},{13,12},{14,15},{17,16},{18,... | collective-permute-start | bytes 3145736 | tf_op jit(solution)/shard_map/ppermute | solution.py:394
  147.8 3.3 %collective-permute-start.13 = (bf16[1024,512]{1,0:T(8,128)(2,1)}, bf16[1024,512]{1,0:T(8,128)(2,1)}, u32[]{:S(2)}, u32[]{:S(2)}) collective-permute-start(bf16[1024,512]{1,0:T(8,128)(2,1)} %get-tuple-element.59.rows_ref.refs_0_.refs_5_), channel_id=1, source_target_pairs={{1,2},{2,1},{5,6},{6,5},{9,10},{10,9},{13,14},{14,13},{17,18},{18,... | collective-permute-start | bytes 3145736 | tf_op jit(solution)/shard_map/ppermute | solution.py:394
  152.9 5.2 %hub_rows.1 = bf16[64,256]{1,0:T(8,128)(2,1)} custom-call(s32[1]{0:T(128)} %bitcast.40.pick_ref, bf16[64,896]{1,0:T(8,128)(2,1)} %fusion.1.rows_ref, bf16[16,2,64,768]{3,2,1,0:T(8,128)(2,1)} %copy-done, bf16[16,64,768]{2,1,0:T(8,128)(2,1)} %collective-permute-done.10.far_ref.refs_9_), custom_call_target="tpu_custom_call" | custom-call | flops 1024 | bytes 1024 | tf_op jit(solution)/shard_map/hub_rows/pallas_call | solution.py:365
  158.1 1.6 broadcast_in_dim.92
  159.7 6.5 %all-to-all-start.2 = ((bf16[16,64,256]{2,1,0:T(8,128)(2,1)}), bf16[16,64,256]{2,1,0:T(8,128)(2,1)S(1)}, u32[]{:S(2)}, u32[]{:S(2)}) async-start(bf16[16,64,256]{2,1,0:T(8,128)(2,1)} %broadcast_in_dim.92), calls=%async_computation.2 | async-start | bytes 1048576 | tf_op jit(solution)/shard_map/all_to_all | solution.py:417
  166.2 9.2 %two.1 = (bf16[1024,1024]{1,0:T(8,128)(2,1)}, bf16[1024,1024]{1,0:T(8,128)(2,1)}, f32[1024,128]{1,0:T(8,128)}, f32[1024,256]{1,0:T(8,128)}) custom-call(s32[6]{0:T(128)} %stack.66.pick_ref, bf16[1024,512]{1,0:T(8,128)(2,1)} %get-tuple-element.59.rows_ref.refs_0_.refs_5_, bf16[16,2,64,768]{3,2,1,0:T(8,128)(2,1)} %copy-done, ...), custom_call_target="tpu_custom_call" | custom-call | flops 262144 | bytes 262144 | tf_op jit(solution)/shard_map/two/pallas_call | solution.py:222
  176.6 2.1 %collective-permute-start.11 = (bf16[1024,256]{1,0:T(8,128)(2,1)S(1)}, bf16[1024,256]{1,0:T(8,128)(2,1)S(1)}, u32[]{:S(2)}, u32[]{:S(2)}) collective-permute-start(bf16[1024,256]{1,0:T(8,128)(2,1)S(1)} %bitcast.56), channel_id=1, source_target_pairs={{0,4},{1,5},{2,6},{3,7},{4,0},{5,1},{6,2},{7,3},{8,12},{9,13},{10,... | collective-permute-start | bytes 1572872 | tf_op jit(solution)/shard_map/ppermute | solution.py:394
  178.7 1.5 collective-permute-done.11.refs_19_
  181.0 23.4 %finish.1 = bf16[1024,256]{1,0:T(8,128)(2,1)} custom-call(s32[6]{0:T(128)} %stack.66.pick_ref, bf16[1024,512]{1,0:T(8,128)(2,1)} %get-tuple-element.59.rows_ref.refs_0_.refs_5_, bf16[1024,512]{1,0:T(8,128)(2,1)} %collective-permute-done.8.refs_1_, bf16[1024,512]{1,0:T(8,128)(2,1)} %collective-permute-done.9.refs_2_, ...), custom_call_target="tpu_custom_call" | custom-call | flops 9663676416 | bytes 12582912 | tf_op jit(solution)/shard_map/finish/pallas_call | solution.py:292
  (55 shorter events, 14.5 us)
Async XLA Ops:
  0.0 14.9 %copy-start.4 = (s32[1,4]{1,0:T(1,128)S(1)}, s32[1,4]{1,0:T(1,128)}, u32[]{:S(2)}) copy-start(s32[1,4]{1,0:T(1,128)} %param.7) | copy-start | bytes 52
  5.1 39.1 %all-to-all-start = ((bf16[32,32,896]{2,1,0:T(8,128)(2,1)}), bf16[32,32,896]{2,1,0:T(8,128)(2,1)S(1)}, u32[]{:S(2)}, u32[]{:S(2)}) async-start(bf16[32,32,896]{2,1,0:T(8,128)(2,1)} %bitcast.54), calls=%async_computation | async-start | bytes 3670016 | tf_op jit(solution)/shard_map/all_to_all | solution.py:434
  12.9 30.0 %collective-permute-start = (bf16[1296,256]{1,0:T(8,128)(2,1)}, bf16[1296,256]{1,0:T(8,128)(2,1)}, u32[]{:S(2)}, u32[]{:S(2)}) collective-permute-start(bf16[1296,256]{1,0:T(8,128)(2,1)} %get-tuple-element.54), channel_id=1, source_target_pairs={{0,2},{1,3},{2,0},{3,1},{4,6},{5,7},{6,4},{7,5},{8,10},{9,11},{10,... | collective-permute-start | bytes 1990664 | tf_op jit(solution)/shard_map/ppermute | solution.py:394
  14.2 30.0 %collective-permute-start.1 = (bf16[1296,256]{1,0:T(8,128)(2,1)}, bf16[1296,256]{1,0:T(8,128)(2,1)S(1)}, u32[]{:S(2)}, u32[]{:S(2)}) collective-permute-start(bf16[1296,256]{1,0:T(8,128)(2,1)} %get-tuple-element.54), channel_id=1, source_target_pairs={{0,1},{1,0},{2,3},{3,2},{4,5},{5,4},{6,7},{7,6},{8,9},{9,8},{10,11... | collective-permute-start | bytes 1990664 | tf_op jit(solution)/shard_map/ppermute | solution.py:394
  23.2 6.2 %copy-start.5 = (s32[2]{0:T(128)S(1)}, s32[2]{0:T(128)}, u32[]{:S(2)}) copy-start(s32[2]{0:T(128)} %param.8) | copy-start | bytes 28
  44.2 0.8 copy-start.2
  45.1 7.8 %collective-permute-start.2 = (bf16[2,32,896]{2,1,0:T(8,128)(2,1)S(1)}, bf16[2,32,896]{2,1,0:T(8,128)(2,1)S(1)}, u32[]{:S(2)}, u32[]{:S(2)}) collective-permute-start(bf16[2,32,896]{2,1,0:T(8,128)(2,1)S(1)} %pad_maximum_fusion.4), channel_id=1, source_target_pairs={{0,128},{1,129},{2,130},{3,131},{4,132},{5,133},{6,134},{7,135},{8... | collective-permute-start | bytes 344072 | tf_op jit(solution)/shard_map/ppermute | solution.py:394
  52.9 4.3 %collective-permute-start.3 = (bf16[1,2,32,896]{3,2,1,0:T(8,128)(2,1)S(1)}, bf16[1,2,32,896]{3,2,1,0:T(8,128)(2,1)S(1)}, u32[]{:S(2)}, u32[]{:S(2)}) collective-permute-start(bf16[1,2,32,896]{3,2,1,0:T(8,128)(2,1)S(1)} %select_bitcast_fusion.1), channel_id=1, source_target_pairs={{0,1},{1,0},{2,3},{3,2},{4,5},{5,4},{6,7},{7,6},{8,9},{9,8},{10,11... | collective-permute-start | bytes 344072 | tf_op jit(solution)/shard_map/ppermute | solution.py:394
  57.4 13.1 %collective-permute-start.4 = (bf16[2,2,32,896]{3,2,1,0:T(8,128)(2,1)S(1)}, bf16[2,2,32,896]{3,2,1,0:T(8,128)(2,1)S(1)}, u32[]{:S(2)}, u32[]{:S(2)}) collective-permute-start(bf16[2,2,32,896]{3,2,1,0:T(8,128)(2,1)S(1)} %pad_maximum_fusion.2), channel_id=1, source_target_pairs={{0,2},{1,3},{2,0},{3,1},{4,6},{5,7},{6,4},{7,5},{8,10},{9,11},{10,... | collective-permute-start | bytes 688136 | tf_op jit(solution)/shard_map/ppermute | solution.py:394
  73.2 20.4 %collective-permute-start.6 = (bf16[1296,256]{1,0:T(8,128)(2,1)}, bf16[1296,256]{1,0:T(8,128)(2,1)}, u32[]{:S(2)}, u32[]{:S(2)}) collective-permute-start(bf16[1296,256]{1,0:T(8,128)(2,1)} %collective-permute-done), channel_id=1, source_target_pairs={{1,0},{2,3},{5,4},{6,7},{9,8},{10,11},{13,12},{14,15},{17,16},{18,... | collective-permute-start | bytes 1990664 | tf_op jit(solution)/shard_map/ppermute | solution.py:394
  75.3 20.5 %collective-permute-start.7 = (bf16[1296,256]{1,0:T(8,128)(2,1)}, bf16[1296,256]{1,0:T(8,128)(2,1)}, u32[]{:S(2)}, u32[]{:S(2)}) collective-permute-start(bf16[1296,256]{1,0:T(8,128)(2,1)} %get-tuple-element.54), channel_id=1, source_target_pairs={{1,2},{2,1},{5,6},{6,5},{9,10},{10,9},{13,14},{14,13},{17,18},{18,... | collective-permute-start | bytes 1990664 | tf_op jit(solution)/shard_map/ppermute | solution.py:394
  81.3 3.0 %collective-permute-start.5 = (bf16[2,32,896]{2,1,0:T(8,128)(2,1)S(1)}, bf16[2,32,896]{2,1,0:T(8,128)(2,1)S(1)}, u32[]{:S(2)}, u32[]{:S(2)}) collective-permute-start(bf16[2,32,896]{2,1,0:T(8,128)(2,1)S(1)} %broadcast_select_fusion.6), channel_id=1, source_target_pairs={{0,4},{1,5},{2,6},{3,7},{4,0},{5,1},{6,2},{7,3},{8,12},{9,13},{10,... | collective-permute-start | bytes 344072 | tf_op jit(solution)/shard_map/ppermute | solution.py:394
  83.2 37.3 %collective-permute-start.8 = (bf16[1024,512]{1,0:T(8,128)(2,1)}, bf16[1024,512]{1,0:T(8,128)(2,1)}, u32[]{:S(2)}, u32[]{:S(2)}) collective-permute-start(bf16[1024,512]{1,0:T(8,128)(2,1)} %get-tuple-element.59.rows_ref.refs_0_.refs_5_), channel_id=1, source_target_pairs={{0,1},{1,0},{2,3},{3,2},{4,5},{5,4},{6,7},{7,6},{8,9},{9,8},{10,11... | collective-permute-start | bytes 3145736 | tf_op jit(solution)/shard_map/ppermute | solution.py:394
  83.3 56.4 %collective-permute-start.9 = (bf16[1024,512]{1,0:T(8,128)(2,1)}, bf16[1024,512]{1,0:T(8,128)(2,1)}, u32[]{:S(2)}, u32[]{:S(2)}) collective-permute-start(bf16[1024,512]{1,0:T(8,128)(2,1)} %get-tuple-element.59.rows_ref.refs_0_.refs_5_), channel_id=1, source_target_pairs={{0,2},{1,3},{2,0},{3,1},{4,6},{5,7},{6,4},{7,5},{8,10},{9,11},{10,... | collective-permute-start | bytes 3145736 | tf_op jit(solution)/shard_map/ppermute | solution.py:394
  86.3 53.5 %all-to-all-start.1 = ((bf16[16,2,64,768]{3,2,1,0:T(8,128)(2,1)}), bf16[16,2,64,768]{3,2,1,0:T(8,128)(2,1)S(1)}, u32[]{:S(2)}, u32[]{:S(2)}) async-start(bf16[16,2,64,768]{3,2,1,0:T(8,128)(2,1)} %broadcast_in_dim.90), calls=%async_computation.1 | async-start | bytes 6291456 | tf_op jit(solution)/shard_map/all_to_all | solution.py:417
  98.8 1.5 copy-start.1
  139.7 13.2 %copy-start = (bf16[16,2,64,768]{3,2,1,0:T(8,128)(2,1)}, bf16[16,2,64,768]{3,2,1,0:T(8,128)(2,1)S(1)}, u32[]{:S(2)}) copy-start(bf16[16,2,64,768]{3,2,1,0:T(8,128)(2,1)S(1)} %all-to-all-done.1.near_ref.refs_8_) | copy-start | bytes 9437188
  141.2 11.8 %collective-permute-start.10 = (bf16[16,64,768]{2,1,0:T(8,128)(2,1)}, bf16[16,64,768]{2,1,0:T(8,128)(2,1)}, u32[]{:S(2)}, u32[]{:S(2)}) collective-permute-start(bf16[16,64,768]{2,1,0:T(8,128)(2,1)} %slice_bitcast_fusion), channel_id=1, source_target_pairs={{0,4},{1,5},{2,6},{3,7},{4,0},{5,1},{6,2},{7,3},{8,12},{9,13},{10,... | collective-permute-start | bytes 4718600 | tf_op jit(solution)/shard_map/ppermute | solution.py:394
  143.0 35.7 %collective-permute-start.12 = (bf16[1024,512]{1,0:T(8,128)(2,1)}, bf16[1024,512]{1,0:T(8,128)(2,1)}, u32[]{:S(2)}, u32[]{:S(2)}) collective-permute-start(bf16[1024,512]{1,0:T(8,128)(2,1)} %collective-permute-done.9.refs_2_), channel_id=1, source_target_pairs={{1,0},{2,3},{5,4},{6,7},{9,8},{10,11},{13,12},{14,15},{17,16},{18,... | collective-permute-start | bytes 3145736 | tf_op jit(solution)/shard_map/ppermute | solution.py:394
  147.8 30.9 %collective-permute-start.13 = (bf16[1024,512]{1,0:T(8,128)(2,1)}, bf16[1024,512]{1,0:T(8,128)(2,1)}, u32[]{:S(2)}, u32[]{:S(2)}) collective-permute-start(bf16[1024,512]{1,0:T(8,128)(2,1)} %get-tuple-element.59.rows_ref.refs_0_.refs_5_), channel_id=1, source_target_pairs={{1,2},{2,1},{5,6},{6,5},{9,10},{10,9},{13,14},{14,13},{17,18},{18,... | collective-permute-start | bytes 3145736 | tf_op jit(solution)/shard_map/ppermute | solution.py:394
  159.7 16.8 %all-to-all-start.2 = ((bf16[16,64,256]{2,1,0:T(8,128)(2,1)}), bf16[16,64,256]{2,1,0:T(8,128)(2,1)S(1)}, u32[]{:S(2)}, u32[]{:S(2)}) async-start(bf16[16,64,256]{2,1,0:T(8,128)(2,1)} %broadcast_in_dim.92), calls=%async_computation.2 | async-start | bytes 1048576 | tf_op jit(solution)/shard_map/all_to_all | solution.py:417
  176.6 3.7 %copy-start.3 = (bf16[16,64,256]{2,1,0:T(8,128)(2,1)}, bf16[16,64,256]{2,1,0:T(8,128)(2,1)S(1)}, u32[]{:S(2)}) copy-start(bf16[16,64,256]{2,1,0:T(8,128)(2,1)S(1)} %all-to-all-done.2) | copy-start | bytes 1572868
  176.6 3.7 %collective-permute-start.11 = (bf16[1024,256]{1,0:T(8,128)(2,1)S(1)}, bf16[1024,256]{1,0:T(8,128)(2,1)S(1)}, u32[]{:S(2)}, u32[]{:S(2)}) collective-permute-start(bf16[1024,256]{1,0:T(8,128)(2,1)S(1)} %bitcast.56), channel_id=1, source_target_pairs={{0,4},{1,5},{2,6},{3,7},{4,0},{5,1},{6,2},{7,3},{8,12},{9,13},{10,... | collective-permute-start | bytes 1572872 | tf_op jit(solution)/shard_map/ppermute | solution.py:394
  180.2 0.8 copy-start.6

commit v10 on v9

--- a/solution.py
+++ b/solution.py
@@ -503,13 +503,13 @@
     held, hub_rep = hub_candidates(mine, hub_ids)
     held, normed, rest, across = barrier((held, normed, rest, across))
 
-    middle, outer = along_line(rest, MIDDLE), along_line(across, OUTWARD)
+    outer, middle = along_line(across, OUTWARD), along_line(rest, MIDDLE)
     beside_x = along_line(normed, {0: 1, 1: 0, 2: 3, 3: 2})
     across_x = along_line(normed, {0: 2, 2: 0, 1: 3, 3: 1})
     both = hub_share(held, hub_rep, full)
     near = join_pieces(both[:, :, :full])
     at_end = (rep == 0) | (rep == 3)
-    group_rest = jnp.stack([rest, beside, across, jnp.where(at_end, outer, middle)], axis=0)
+    group_rest = jnp.stack([rest, beside, across, jnp.where(~at_end, middle, outer)], axis=0)
     at = want ^ rep
     flag = lax.dynamic_index_in_dim(group_rest[:, -1, 0], at, 0, keepdims=False).astype(jnp.int32)
     member_want, member_order = flag & 3, (flag >> 2) & 1

time: 206 us -> 203 us (0.985)
  waiting for transfers between devices: 60.4 us -> 55.8 us
  starting transfers between devices: 51.1 us -> 53.3 us
    ppermute x14, waiting for transfers between devices: 59.3 us -> 54.6 us  [send(): return lax.ppermute(block, AXES, pairs)]
    ppermute x14, starting transfers between devices: 29.6 us -> 32.1 us  [send(): return lax.ppermute(block, AXES, pairs)]
  transfers between devices with their start and end apart: 17 -> 17, of which waited for: 10 -> 9; matrix products, arithmetic and copies ran while one was open for 5% -> 5% of each run, Pallas kernels for 17% -> 17%
where the time goes in v10:
time: 203 us; the launch traced here: 202 us
  Pallas kernels  63.8 us (31%)
  waiting for transfers between devices  55.8 us (27%)
  starting transfers between devices  53.3 us (26%)
  local copies, waits for them, and re-layouts  12.3 us (6%)
  between operations  12.3 us (6%)
  other arithmetic  4.71 us (2%)
    ppermute x14, waiting for transfers between devices, send(): return lax.ppermute(block, AXES, pairs)  54.6 us
    ppermute x14, starting transfers between devices, send(): return lax.ppermute(block, AXES, pairs)  32.1 us
    pallas_call x1, Pallas kernels, finish_of(): pl.pallas_call(finish_kernel, out_shape=jax.ShapeDtypeStruct((rows, clust...  23.4 us
    pallas_call x2, Pallas kernels, keep_words(): pl.pallas_call(words_kernel, out_shape=jax.ShapeDtypeStruct((K, rows, LAN...  14.7 us
    all_to_all x2, starting transfers between devices, join_pieces(): lax.all_to_all(repeated, 'slab', 0, 0, axis_index_groups=layers, tiled=True)  13.4 us
    pallas_call x1, Pallas kernels, two_of(): pl.pallas_call(two_kernel, out_shape=[jax.ShapeDtypeStruct((rows, cols),...  9.15 us
    all_to_all x1, starting transfers between devices, scatter(): lax.all_to_all(block.reshape(members, rows // members, width), 'slab', 0,...  7.76 us
    pallas_call x1, Pallas kernels, tile_of(): pl.pallas_call(functools.partial(tile_kernel, carry is not None, last), o...  6.21 us
  transfers between devices with their start and end apart: 17, of which 9 were waited for; matrix products, arithmetic and copies ran while one was open for 5% of the time, Pallas kernels for 17%

profile of v10, /device:TPU:161, one launch (start us, length us, event | category | flops | bytes accessed | tf_op | source)
XLA Modules:
  0.0 202.2 jit_solution(8892694608141293609)
XLA Ops:
  0.0 5.1 %join.1 = (bf16[1024,896]{1,0:T(8,128)(2,1)}, bf16[1024,512]{1,0:T(8,128)(2,1)}, bf16[1296,256]{1,0:T(8,128)(2,1)}) custom-call(s32[4]{0:T(128)} %bitcast.62, bf16[1024,512]{1,0:T(8,128)(2,1)} %x_ref.1, bf16[1024,256]{1,0:T(8,128)(2,1)} %refs_14_.1, s32[4,16,1024]{2,1,0:T(8,128)} %bitcast.61), custom_call_target="tpu_custom_call" | custom-call | tf_op jit(solution)/shard_map/join/pallas_call | solution.py:55
  5.1 7.8 %all-to-all-start = ((bf16[32,32,896]{2,1,0:T(8,128)(2,1)}), bf16[32,32,896]{2,1,0:T(8,128)(2,1)S(1)}, u32[]{:S(2)}, u32[]{:S(2)}) async-start(bf16[32,32,896]{2,1,0:T(8,128)(2,1)} %bitcast.54), calls=%async_computation | async-start | bytes 3670016 | tf_op jit(solution)/shard_map/all_to_all | solution.py:434
  16.2 7.0 %keep_words.2.w_ref.words_ref.refs_10_ = s32[4,1024,128]{2,1,0:T(8,128)} custom-call(s32[1]{0:T(128)} %bitcast.6.pick_ref, bf16[1,1296,256]{2,1,0:T(8,128)(2,1)} %bitcast.7.coded_ref), custom_call_target="tpu_custom_call" | custom-call | flops 1 | bytes 524288 | tf_op jit(solution)/shard_map/keep_words/pallas_call | solution.py:96
  23.2 6.2 %tile.1 = (f32[1024,128]{1,0:T(8,128)}, f32[1024,256]{1,0:T(8,128)}, bf16[1024,1024]{1,0:T(8,128)(2,1)}) custom-call(s32[1]{0:T(128)} %bitcast.6.pick_ref, bf16[1024,896]{1,0:T(8,128)(2,1)} %get-tuple-element.44.x_ref.other_ref.y_ref, bf16[1024,896]{1,0:T(8,128)(2,1)} %get-tuple-element.44.x_ref.other_ref.y_ref, ...), custom_call_target="tpu_custom_call" | custom-call | flops 262144 | bytes 262144 | tf_op jit(solution)/shard_map/tile/pallas_call | solution.py:163
  33.7 9.2 %collective-permute-done = bf16[1296,256]{1,0:T(8,128)(2,1)} collective-permute-done((bf16[1296,256]{1,0:T(8,128)(2,1)}, bf16[1296,256]{1,0:T(8,128)(2,1)}, u32[]{:S(2)}, u32[]{:S(2)}) %collective-permute-start) | collective-permute-done | bytes 663584 | tf_op jit(solution)/shard_map/ppermute | solution.py:394
  45.4 7.4 %collective-permute-done.2 = bf16[2,32,896]{2,1,0:T(8,128)(2,1)S(1)} collective-permute-done((bf16[2,32,896]{2,1,0:T(8,128)(2,1)S(1)}, bf16[2,32,896]{2,1,0:T(8,128)(2,1)S(1)}, u32[]{:S(2)}, u32[]{:S(2)}) %collective-permute-start.2) | collective-permute-done | bytes 114720 | tf_op jit(solution)/shard_map/ppermute | solution.py:394
  52.9 1.4 collective-permute-start.3
  54.3 2.9 %collective-permute-done.3 = bf16[1,2,32,896]{3,2,1,0:T(8,128)(2,1)S(1)} collective-permute-done((bf16[1,2,32,896]{3,2,1,0:T(8,128)(2,1)S(1)}, bf16[1,2,32,896]{3,2,1,0:T(8,128)(2,1)S(1)}, u32[]{:S(2)}, u32[]{:S(2)}) %collective-permute-start.3) | collective-permute-done | bytes 114720 | tf_op jit(solution)/shard_map/ppermute | solution.py:394
  57.4 3.3 %collective-permute-start.4 = (bf16[2,2,32,896]{3,2,1,0:T(8,128)(2,1)S(1)}, bf16[2,2,32,896]{3,2,1,0:T(8,128)(2,1)S(1)}, u32[]{:S(2)}, u32[]{:S(2)}) collective-permute-start(bf16[2,2,32,896]{3,2,1,0:T(8,128)(2,1)S(1)} %pad_maximum_fusion.2), channel_id=1, source_target_pairs={{0,2},{1,3},{2,0},{3,1},{4,6},{5,7},{6,4},{7,5},{8,10},{9,11},{10,... | collective-permute-start | bytes 688136 | tf_op jit(solution)/shard_map/ppermute | solution.py:394
  65.0 5.5 %collective-permute-done.4 = bf16[2,2,32,896]{3,2,1,0:T(8,128)(2,1)S(1)} collective-permute-done((bf16[2,2,32,896]{3,2,1,0:T(8,128)(2,1)S(1)}, bf16[2,2,32,896]{3,2,1,0:T(8,128)(2,1)S(1)}, u32[]{:S(2)}, u32[]{:S(2)}) %collective-permute-start.4) | collective-permute-done | bytes 229408 | tf_op jit(solution)/shard_map/ppermute | solution.py:394
  73.2 1.9 collective-permute-start.6
  75.1 2.1 %collective-permute-start.7 = (bf16[1296,256]{1,0:T(8,128)(2,1)}, bf16[1296,256]{1,0:T(8,128)(2,1)}, u32[]{:S(2)}, u32[]{:S(2)}) collective-permute-start(bf16[1296,256]{1,0:T(8,128)(2,1)} %collective-permute-done), channel_id=1, source_target_pairs={{1,0},{2,3},{5,4},{6,7},{9,8},{10,11},{13,12},{14,15},{17,16},{18,... | collective-permute-start | bytes 1990664 | tf_op jit(solution)/shard_map/ppermute | solution.py:394
  77.3 2.2 %collective-permute-start.5 = (bf16[2,32,896]{2,1,0:T(8,128)(2,1)S(1)}, bf16[2,32,896]{2,1,0:T(8,128)(2,1)S(1)}, u32[]{:S(2)}, u32[]{:S(2)}) collective-permute-start(bf16[2,32,896]{2,1,0:T(8,128)(2,1)S(1)} %broadcast_select_fusion.6), channel_id=1, source_target_pairs={{0,4},{1,5},{2,6},{3,7},{4,0},{5,1},{6,2},{7,3},{8,12},{9,13},{10,... | collective-permute-start | bytes 344072 | tf_op jit(solution)/shard_map/ppermute | solution.py:394
  80.2 3.6 %collective-permute-start.9 = (bf16[1024,512]{1,0:T(8,128)(2,1)}, bf16[1024,512]{1,0:T(8,128)(2,1)}, u32[]{:S(2)}, u32[]{:S(2)}) collective-permute-start(bf16[1024,512]{1,0:T(8,128)(2,1)} %get-tuple-element.59.rows_ref.refs_0_.refs_5_), channel_id=1, source_target_pairs={{0,2},{1,3},{2,0},{3,1},{4,6},{5,7},{6,4},{7,5},{8,10},{9,11},{10,... | collective-permute-start | bytes 3145736 | tf_op jit(solution)/shard_map/ppermute | solution.py:394
  83.9 2.0 broadcast_in_dim.90
  85.9 6.9 %all-to-all-start.1 = ((bf16[16,2,64,768]{3,2,1,0:T(8,128)(2,1)}), bf16[16,2,64,768]{3,2,1,0:T(8,128)(2,1)S(1)}, u32[]{:S(2)}, u32[]{:S(2)}) async-start(bf16[16,2,64,768]{3,2,1,0:T(8,128)(2,1)} %broadcast_in_dim.90), calls=%async_computation.1 | async-start | bytes 6291456 | tf_op jit(solution)/shard_map/all_to_all | solution.py:417
  93.9 1.8 pad_maximum_fusion.coded_ref.refs_6_.refs_7_
  95.8 1.5 copy-done.1
  99.8 7.7 %keep_words.3.refs_11_ = s32[4,1024,128]{2,1,0:T(8,128)} custom-call(s32[6]{0:T(128)} %stack.66.pick_ref, bf16[4,1296,256]{2,1,0:T(8,128)(2,1)} %copy-done.1), custom_call_target="tpu_custom_call" | custom-call | flops 30000001024 | bytes 524288 | tf_op jit(solution)/shard_map/keep_words/pallas_call | solution.py:96
  107.4 19.7 %collective-permute-done.8.refs_1_ = bf16[1024,512]{1,0:T(8,128)(2,1)} collective-permute-done((bf16[1024,512]{1,0:T(8,128)(2,1)}, bf16[1024,512]{1,0:T(8,128)(2,1)}, u32[]{:S(2)}, u32[]{:S(2)}) %collective-permute-start.8) | collective-permute-done | bytes 1048608 | tf_op jit(solution)/shard_map/ppermute | solution.py:394
  127.1 7.2 %collective-permute-done.9.refs_2_ = bf16[1024,512]{1,0:T(8,128)(2,1)} collective-permute-done((bf16[1024,512]{1,0:T(8,128)(2,1)}, bf16[1024,512]{1,0:T(8,128)(2,1)}, u32[]{:S(2)}, u32[]{:S(2)}) %collective-permute-start.9) | collective-permute-done | bytes 1048608 | tf_op jit(solution)/shard_map/ppermute | solution.py:394
  134.3 1.4 slice_bitcast_fusion
  135.7 1.7 collective-permute-start.10
  137.5 5.8 %collective-permute-start.12 = (bf16[1024,512]{1,0:T(8,128)(2,1)}, bf16[1024,512]{1,0:T(8,128)(2,1)}, u32[]{:S(2)}, u32[]{:S(2)}) collective-permute-start(bf16[1024,512]{1,0:T(8,128)(2,1)} %collective-permute-done.9.refs_2_), channel_id=1, source_target_pairs={{1,0},{2,3},{5,4},{6,7},{9,8},{10,11},{13,12},{14,15},{17,16},{18,... | collective-permute-start | bytes 3145736 | tf_op jit(solution)/shard_map/ppermute | solution.py:394
  143.2 5.5 %collective-permute-start.13 = (bf16[1024,512]{1,0:T(8,128)(2,1)}, bf16[1024,512]{1,0:T(8,128)(2,1)}, u32[]{:S(2)}, u32[]{:S(2)}) collective-permute-start(bf16[1024,512]{1,0:T(8,128)(2,1)} %get-tuple-element.59.rows_ref.refs_0_.refs_5_), channel_id=1, source_target_pairs={{1,2},{2,1},{5,6},{6,5},{9,10},{10,9},{13,14},{14,13},{17,18},{18,... | collective-permute-start | bytes 3145736 | tf_op jit(solution)/shard_map/ppermute | solution.py:394
  150.5 5.2 %hub_rows.1 = bf16[64,256]{1,0:T(8,128)(2,1)} custom-call(s32[1]{0:T(128)} %bitcast.40.pick_ref, bf16[64,896]{1,0:T(8,128)(2,1)} %fusion.1.rows_ref, bf16[16,2,64,768]{3,2,1,0:T(8,128)(2,1)} %copy-done, bf16[16,64,768]{2,1,0:T(8,128)(2,1)} %collective-permute-done.10.far_ref.refs_9_), custom_call_target="tpu_custom_call" | custom-call | flops 1024 | bytes 1024 | tf_op jit(solution)/shard_map/hub_rows/pallas_call | solution.py:365
  155.6 1.6 broadcast_in_dim.92
  157.3 6.5 %all-to-all-start.2 = ((bf16[16,64,256]{2,1,0:T(8,128)(2,1)}), bf16[16,64,256]{2,1,0:T(8,128)(2,1)S(1)}, u32[]{:S(2)}, u32[]{:S(2)}) async-start(bf16[16,64,256]{2,1,0:T(8,128)(2,1)} %broadcast_in_dim.92), calls=%async_computation.2 | async-start | bytes 1048576 | tf_op jit(solution)/shard_map/all_to_all | solution.py:417
  163.8 9.2 %two.1 = (bf16[1024,1024]{1,0:T(8,128)(2,1)}, bf16[1024,1024]{1,0:T(8,128)(2,1)}, f32[1024,128]{1,0:T(8,128)}, f32[1024,256]{1,0:T(8,128)}) custom-call(s32[6]{0:T(128)} %stack.66.pick_ref, bf16[1024,512]{1,0:T(8,128)(2,1)} %get-tuple-element.59.rows_ref.refs_0_.refs_5_, bf16[16,2,64,768]{3,2,1,0:T(8,128)(2,1)} %copy-done, ...), custom_call_target="tpu_custom_call" | custom-call | flops 262144 | bytes 262144 | tf_op jit(solution)/shard_map/two/pallas_call | solution.py:222
  174.1 2.1 %collective-permute-start.11 = (bf16[1024,256]{1,0:T(8,128)(2,1)S(1)}, bf16[1024,256]{1,0:T(8,128)(2,1)S(1)}, u32[]{:S(2)}, u32[]{:S(2)}) collective-permute-start(bf16[1024,256]{1,0:T(8,128)(2,1)S(1)} %bitcast.56), channel_id=1, source_target_pairs={{0,4},{1,5},{2,6},{3,7},{4,0},{5,1},{6,2},{7,3},{8,12},{9,13},{10,... | collective-permute-start | bytes 1572872 | tf_op jit(solution)/shard_map/ppermute | solution.py:394
  176.2 1.5 collective-permute-done.11.refs_19_
  178.6 23.4 %finish.1 = bf16[1024,256]{1,0:T(8,128)(2,1)} custom-call(s32[6]{0:T(128)} %stack.66.pick_ref, bf16[1024,512]{1,0:T(8,128)(2,1)} %get-tuple-element.59.rows_ref.refs_0_.refs_5_, bf16[1024,512]{1,0:T(8,128)(2,1)} %collective-permute-done.8.refs_1_, bf16[1024,512]{1,0:T(8,128)(2,1)} %collective-permute-done.9.refs_2_, ...), custom_call_target="tpu_custom_call" | custom-call | flops 9663676416 | bytes 12582912 | tf_op jit(solution)/shard_map/finish/pallas_call | solution.py:292
  (55 shorter events, 13.6 us)
Async XLA Ops:
  0.0 14.9 %copy-start.4 = (s32[1,4]{1,0:T(1,128)S(1)}, s32[1,4]{1,0:T(1,128)}, u32[]{:S(2)}) copy-start(s32[1,4]{1,0:T(1,128)} %param.7) | copy-start | bytes 52
  5.1 39.1 %all-to-all-start = ((bf16[32,32,896]{2,1,0:T(8,128)(2,1)}), bf16[32,32,896]{2,1,0:T(8,128)(2,1)S(1)}, u32[]{:S(2)}, u32[]{:S(2)}) async-start(bf16[32,32,896]{2,1,0:T(8,128)(2,1)} %bitcast.54), calls=%async_computation | async-start | bytes 3670016 | tf_op jit(solution)/shard_map/all_to_all | solution.py:434
  12.9 30.0 %collective-permute-start = (bf16[1296,256]{1,0:T(8,128)(2,1)}, bf16[1296,256]{1,0:T(8,128)(2,1)}, u32[]{:S(2)}, u32[]{:S(2)}) collective-permute-start(bf16[1296,256]{1,0:T(8,128)(2,1)} %get-tuple-element.54), channel_id=1, source_target_pairs={{0,2},{1,3},{2,0},{3,1},{4,6},{5,7},{6,4},{7,5},{8,10},{9,11},{10,... | collective-permute-start | bytes 1990664 | tf_op jit(solution)/shard_map/ppermute | solution.py:394
  14.2 30.0 %collective-permute-start.1 = (bf16[1296,256]{1,0:T(8,128)(2,1)}, bf16[1296,256]{1,0:T(8,128)(2,1)S(1)}, u32[]{:S(2)}, u32[]{:S(2)}) collective-permute-start(bf16[1296,256]{1,0:T(8,128)(2,1)} %get-tuple-element.54), channel_id=1, source_target_pairs={{0,1},{1,0},{2,3},{3,2},{4,5},{5,4},{6,7},{7,6},{8,9},{9,8},{10,11... | collective-permute-start | bytes 1990664 | tf_op jit(solution)/shard_map/ppermute | solution.py:394
  23.2 6.2 %copy-start.5 = (s32[2]{0:T(128)S(1)}, s32[2]{0:T(128)}, u32[]{:S(2)}) copy-start(s32[2]{0:T(128)} %param.8) | copy-start | bytes 28
  44.2 0.8 copy-start.2
  45.1 7.8 %collective-permute-start.2 = (bf16[2,32,896]{2,1,0:T(8,128)(2,1)S(1)}, bf16[2,32,896]{2,1,0:T(8,128)(2,1)S(1)}, u32[]{:S(2)}, u32[]{:S(2)}) collective-permute-start(bf16[2,32,896]{2,1,0:T(8,128)(2,1)S(1)} %pad_maximum_fusion.4), channel_id=1, source_target_pairs={{0,128},{1,129},{2,130},{3,131},{4,132},{5,133},{6,134},{7,135},{8... | collective-permute-start | bytes 344072 | tf_op jit(solution)/shard_map/ppermute | solution.py:394
  52.9 4.3 %collective-permute-start.3 = (bf16[1,2,32,896]{3,2,1,0:T(8,128)(2,1)S(1)}, bf16[1,2,32,896]{3,2,1,0:T(8,128)(2,1)S(1)}, u32[]{:S(2)}, u32[]{:S(2)}) collective-permute-start(bf16[1,2,32,896]{3,2,1,0:T(8,128)(2,1)S(1)} %select_bitcast_fusion.1), channel_id=1, source_target_pairs={{0,1},{1,0},{2,3},{3,2},{4,5},{5,4},{6,7},{7,6},{8,9},{9,8},{10,11... | collective-permute-start | bytes 344072 | tf_op jit(solution)/shard_map/ppermute | solution.py:394
  57.4 13.1 %collective-permute-start.4 = (bf16[2,2,32,896]{3,2,1,0:T(8,128)(2,1)S(1)}, bf16[2,2,32,896]{3,2,1,0:T(8,128)(2,1)S(1)}, u32[]{:S(2)}, u32[]{:S(2)}) collective-permute-start(bf16[2,2,32,896]{3,2,1,0:T(8,128)(2,1)S(1)} %pad_maximum_fusion.2), channel_id=1, source_target_pairs={{0,2},{1,3},{2,0},{3,1},{4,6},{5,7},{6,4},{7,5},{8,10},{9,11},{10,... | collective-permute-start | bytes 688136 | tf_op jit(solution)/shard_map/ppermute | solution.py:394
  73.2 19.6 %collective-permute-start.6 = (bf16[1296,256]{1,0:T(8,128)(2,1)}, bf16[1296,256]{1,0:T(8,128)(2,1)}, u32[]{:S(2)}, u32[]{:S(2)}) collective-permute-start(bf16[1296,256]{1,0:T(8,128)(2,1)} %get-tuple-element.54), channel_id=1, source_target_pairs={{1,2},{2,1},{5,6},{6,5},{9,10},{10,9},{13,14},{14,13},{17,18},{18,... | collective-permute-start | bytes 1990664 | tf_op jit(solution)/shard_map/ppermute | solution.py:394
  75.1 17.7 %collective-permute-start.7 = (bf16[1296,256]{1,0:T(8,128)(2,1)}, bf16[1296,256]{1,0:T(8,128)(2,1)}, u32[]{:S(2)}, u32[]{:S(2)}) collective-permute-start(bf16[1296,256]{1,0:T(8,128)(2,1)} %collective-permute-done), channel_id=1, source_target_pairs={{1,0},{2,3},{5,4},{6,7},{9,8},{10,11},{13,12},{14,15},{17,16},{18,... | collective-permute-start | bytes 1990664 | tf_op jit(solution)/shard_map/ppermute | solution.py:394
  77.3 6.5 %collective-permute-start.5 = (bf16[2,32,896]{2,1,0:T(8,128)(2,1)S(1)}, bf16[2,32,896]{2,1,0:T(8,128)(2,1)S(1)}, u32[]{:S(2)}, u32[]{:S(2)}) collective-permute-start(bf16[2,32,896]{2,1,0:T(8,128)(2,1)S(1)} %broadcast_select_fusion.6), channel_id=1, source_target_pairs={{0,4},{1,5},{2,6},{3,7},{4,0},{5,1},{6,2},{7,3},{8,12},{9,13},{10,... | collective-permute-start | bytes 344072 | tf_op jit(solution)/shard_map/ppermute | solution.py:394
  80.1 47.0 %collective-permute-start.8 = (bf16[1024,512]{1,0:T(8,128)(2,1)}, bf16[1024,512]{1,0:T(8,128)(2,1)}, u32[]{:S(2)}, u32[]{:S(2)}) collective-permute-start(bf16[1024,512]{1,0:T(8,128)(2,1)} %get-tuple-element.59.rows_ref.refs_0_.refs_5_), channel_id=1, source_target_pairs={{0,1},{1,0},{2,3},{3,2},{4,5},{5,4},{6,7},{7,6},{8,9},{9,8},{10,11... | collective-permute-start | bytes 3145736 | tf_op jit(solution)/shard_map/ppermute | solution.py:394
  80.2 54.1 %collective-permute-start.9 = (bf16[1024,512]{1,0:T(8,128)(2,1)}, bf16[1024,512]{1,0:T(8,128)(2,1)}, u32[]{:S(2)}, u32[]{:S(2)}) collective-permute-start(bf16[1024,512]{1,0:T(8,128)(2,1)} %get-tuple-element.59.rows_ref.refs_0_.refs_5_), channel_id=1, source_target_pairs={{0,2},{1,3},{2,0},{3,1},{4,6},{5,7},{6,4},{7,5},{8,10},{9,11},{10,... | collective-permute-start | bytes 3145736 | tf_op jit(solution)/shard_map/ppermute | solution.py:394
  85.9 48.5 %all-to-all-start.1 = ((bf16[16,2,64,768]{3,2,1,0:T(8,128)(2,1)}), bf16[16,2,64,768]{3,2,1,0:T(8,128)(2,1)S(1)}, u32[]{:S(2)}, u32[]{:S(2)}) async-start(bf16[16,2,64,768]{3,2,1,0:T(8,128)(2,1)} %broadcast_in_dim.90), calls=%async_computation.1 | async-start | bytes 6291456 | tf_op jit(solution)/shard_map/all_to_all | solution.py:417
  95.8 1.5 copy-start.1
  134.3 16.2 %copy-start = (bf16[16,2,64,768]{3,2,1,0:T(8,128)(2,1)}, bf16[16,2,64,768]{3,2,1,0:T(8,128)(2,1)S(1)}, u32[]{:S(2)}) copy-start(bf16[16,2,64,768]{3,2,1,0:T(8,128)(2,1)S(1)} %all-to-all-done.1.near_ref.refs_8_) | copy-start | bytes 9437188
  135.7 14.7 %collective-permute-start.10 = (bf16[16,64,768]{2,1,0:T(8,128)(2,1)}, bf16[16,64,768]{2,1,0:T(8,128)(2,1)}, u32[]{:S(2)}, u32[]{:S(2)}) collective-permute-start(bf16[16,64,768]{2,1,0:T(8,128)(2,1)} %slice_bitcast_fusion), channel_id=1, source_target_pairs={{0,4},{1,5},{2,6},{3,7},{4,0},{5,1},{6,2},{7,3},{8,12},{9,13},{10,... | collective-permute-start | bytes 4718600 | tf_op jit(solution)/shard_map/ppermute | solution.py:394
  137.5 38.8 %collective-permute-start.12 = (bf16[1024,512]{1,0:T(8,128)(2,1)}, bf16[1024,512]{1,0:T(8,128)(2,1)}, u32[]{:S(2)}, u32[]{:S(2)}) collective-permute-start(bf16[1024,512]{1,0:T(8,128)(2,1)} %collective-permute-done.9.refs_2_), channel_id=1, source_target_pairs={{1,0},{2,3},{5,4},{6,7},{9,8},{10,11},{13,12},{14,15},{17,16},{18,... | collective-permute-start | bytes 3145736 | tf_op jit(solution)/shard_map/ppermute | solution.py:394
  143.2 33.0 %collective-permute-start.13 = (bf16[1024,512]{1,0:T(8,128)(2,1)}, bf16[1024,512]{1,0:T(8,128)(2,1)}, u32[]{:S(2)}, u32[]{:S(2)}) collective-permute-start(bf16[1024,512]{1,0:T(8,128)(2,1)} %get-tuple-element.59.rows_ref.refs_0_.refs_5_), channel_id=1, source_target_pairs={{1,2},{2,1},{5,6},{6,5},{9,10},{10,9},{13,14},{14,13},{17,18},{18,... | collective-permute-start | bytes 3145736 | tf_op jit(solution)/shard_map/ppermute | solution.py:394
  157.3 16.8 %all-to-all-start.2 = ((bf16[16,64,256]{2,1,0:T(8,128)(2,1)}), bf16[16,64,256]{2,1,0:T(8,128)(2,1)S(1)}, u32[]{:S(2)}, u32[]{:S(2)}) async-start(bf16[16,64,256]{2,1,0:T(8,128)(2,1)} %broadcast_in_dim.92), calls=%async_computation.2 | async-start | bytes 1048576 | tf_op jit(solution)/shard_map/all_to_all | solution.py:417
  174.1 3.7 %copy-start.3 = (bf16[16,64,256]{2,1,0:T(8,128)(2,1)}, bf16[16,64,256]{2,1,0:T(8,128)(2,1)S(1)}, u32[]{:S(2)}) copy-start(bf16[16,64,256]{2,1,0:T(8,128)(2,1)S(1)} %all-to-all-done.2) | copy-start | bytes 1572868
  174.1 3.7 %collective-permute-start.11 = (bf16[1024,256]{1,0:T(8,128)(2,1)S(1)}, bf16[1024,256]{1,0:T(8,128)(2,1)S(1)}, u32[]{:S(2)}, u32[]{:S(2)}) collective-permute-start(bf16[1024,256]{1,0:T(8,128)(2,1)S(1)} %bitcast.56), channel_id=1, source_target_pairs={{0,4},{1,5},{2,6},{3,7},{4,0},{5,1},{6,2},{7,3},{8,12},{9,13},{10,... | collective-permute-start | bytes 1572872 | tf_op jit(solution)/shard_map/ppermute | solution.py:394
  177.8 0.8 copy-start.6

commit v11 on v10

--- a/solution.py
+++ b/solution.py
@@ -244,14 +244,16 @@
 
     @pl.when((phase == 0) & (step == 0))
     def _():
-        for which, target in enumerate((first_x, second_x)):
+        wanted = ((pick_ref[1], first_x, sems.at[0]), (pick_ref[2], second_x, sems.at[1]))
+        for at, target, sem in wanted:
             for i, block in enumerate(blocks):
 
-                @pl.when(pick_ref[1 + which] == i)
+                @pl.when(at == i)
                 def _():
-                    copy = pltpu.make_async_copy(block, target, sems.at[which])
-                    copy.start()
-                    copy.wait()
+                    pltpu.make_async_copy(block, target, sem).start()
+
+        for _, target, sem in wanted:
+            pltpu.make_async_copy(blocks[0], target, sem).wait()
 
     @pl.when(phase == 0)
     def _():

time: 203 us -> 202 us (level)
  transfers between devices with their start and end apart: 17 -> 17, of which waited for: 9 -> 9; matrix products, arithmetic and copies ran while one was open for 5% -> 5% of each run, Pallas kernels for 17% -> 18%
where the time goes in v11:
time: 202 us; the launch traced here: 201 us
  Pallas kernels  62.7 us (31%)
  waiting for transfers between devices  55.8 us (28%)
  starting transfers between devices  53.3 us (26%)
  local copies, waits for them, and re-layouts  12.3 us (6%)
  between operations  12.3 us (6%)
  other arithmetic  4.71 us (2%)
    ppermute x14, waiting for transfers between devices, send(): return lax.ppermute(block, AXES, pairs)  54.6 us
    ppermute x14, starting transfers between devices, send(): return lax.ppermute(block, AXES, pairs)  32.1 us
    pallas_call x1, Pallas kernels, finish_of(): pl.pallas_call(finish_kernel, out_shape=jax.ShapeDtypeStruct((rows, clust...  22.4 us
    pallas_call x2, Pallas kernels, keep_words(): pl.pallas_call(words_kernel, out_shape=jax.ShapeDtypeStruct((K, rows, LAN...  14.7 us
    all_to_all x2, starting transfers between devices, join_pieces(): lax.all_to_all(repeated, 'slab', 0, 0, axis_index_groups=layers, tiled=True)  13.4 us
    pallas_call x1, Pallas kernels, two_of(): pl.pallas_call(two_kernel, out_shape=[jax.ShapeDtypeStruct((rows, cols),...  9.15 us
    all_to_all x1, starting transfers between devices, scatter(): lax.all_to_all(block.reshape(members, rows // members, width), 'slab', 0,...  7.76 us
    pallas_call x1, Pallas kernels, tile_of(): pl.pallas_call(functools.partial(tile_kernel, carry is not None, last), o...  6.21 us
  transfers between devices with their start and end apart: 17, of which 9 were waited for; matrix products, arithmetic and copies ran while one was open for 5% of the time, Pallas kernels for 18%

profile of v11, /device:TPU:161, one launch (start us, length us, event | category | flops | bytes accessed | tf_op | source)
XLA Modules:
  0.0 201.1 jit_solution(5995627768221911195)
XLA Ops:
  0.0 5.1 %join.1 = (bf16[1024,896]{1,0:T(8,128)(2,1)}, bf16[1024,512]{1,0:T(8,128)(2,1)}, bf16[1296,256]{1,0:T(8,128)(2,1)}) custom-call(s32[4]{0:T(128)} %bitcast.62, bf16[1024,512]{1,0:T(8,128)(2,1)} %x_ref.1, bf16[1024,256]{1,0:T(8,128)(2,1)} %refs_14_.1, s32[4,16,1024]{2,1,0:T(8,128)} %bitcast.61), custom_call_target="tpu_custom_call" | custom-call | tf_op jit(solution)/shard_map/join/pallas_call | solution.py:55
  5.1 7.8 %all-to-all-start = ((bf16[32,32,896]{2,1,0:T(8,128)(2,1)}), bf16[32,32,896]{2,1,0:T(8,128)(2,1)S(1)}, u32[]{:S(2)}, u32[]{:S(2)}) async-start(bf16[32,32,896]{2,1,0:T(8,128)(2,1)} %bitcast.54), calls=%async_computation | async-start | bytes 3670016 | tf_op jit(solution)/shard_map/all_to_all | solution.py:436
  16.2 7.0 %keep_words.2.w_ref.words_ref.refs_10_ = s32[4,1024,128]{2,1,0:T(8,128)} custom-call(s32[1]{0:T(128)} %bitcast.6.pick_ref, bf16[1,1296,256]{2,1,0:T(8,128)(2,1)} %bitcast.7.coded_ref), custom_call_target="tpu_custom_call" | custom-call | flops 1 | bytes 524288 | tf_op jit(solution)/shard_map/keep_words/pallas_call | solution.py:96
  23.2 6.2 %tile.1 = (f32[1024,128]{1,0:T(8,128)}, f32[1024,256]{1,0:T(8,128)}, bf16[1024,1024]{1,0:T(8,128)(2,1)}) custom-call(s32[1]{0:T(128)} %bitcast.6.pick_ref, bf16[1024,896]{1,0:T(8,128)(2,1)} %get-tuple-element.44.x_ref.other_ref.y_ref, bf16[1024,896]{1,0:T(8,128)(2,1)} %get-tuple-element.44.x_ref.other_ref.y_ref, ...), custom_call_target="tpu_custom_call" | custom-call | flops 262144 | bytes 262144 | tf_op jit(solution)/shard_map/tile/pallas_call | solution.py:163
  33.7 9.2 %collective-permute-done = bf16[1296,256]{1,0:T(8,128)(2,1)} collective-permute-done((bf16[1296,256]{1,0:T(8,128)(2,1)}, bf16[1296,256]{1,0:T(8,128)(2,1)}, u32[]{:S(2)}, u32[]{:S(2)}) %collective-permute-start) | collective-permute-done | bytes 663584 | tf_op jit(solution)/shard_map/ppermute | solution.py:396
  45.4 7.4 %collective-permute-done.2 = bf16[2,32,896]{2,1,0:T(8,128)(2,1)S(1)} collective-permute-done((bf16[2,32,896]{2,1,0:T(8,128)(2,1)S(1)}, bf16[2,32,896]{2,1,0:T(8,128)(2,1)S(1)}, u32[]{:S(2)}, u32[]{:S(2)}) %collective-permute-start.2) | collective-permute-done | bytes 114720 | tf_op jit(solution)/shard_map/ppermute | solution.py:396
  52.9 1.4 collective-permute-start.3
  54.3 2.9 %collective-permute-done.3 = bf16[1,2,32,896]{3,2,1,0:T(8,128)(2,1)S(1)} collective-permute-done((bf16[1,2,32,896]{3,2,1,0:T(8,128)(2,1)S(1)}, bf16[1,2,32,896]{3,2,1,0:T(8,128)(2,1)S(1)}, u32[]{:S(2)}, u32[]{:S(2)}) %collective-permute-start.3) | collective-permute-done | bytes 114720 | tf_op jit(solution)/shard_map/ppermute | solution.py:396
  57.4 3.3 %collective-permute-start.4 = (bf16[2,2,32,896]{3,2,1,0:T(8,128)(2,1)S(1)}, bf16[2,2,32,896]{3,2,1,0:T(8,128)(2,1)S(1)}, u32[]{:S(2)}, u32[]{:S(2)}) collective-permute-start(bf16[2,2,32,896]{3,2,1,0:T(8,128)(2,1)S(1)} %pad_maximum_fusion.2), channel_id=1, source_target_pairs={{0,2},{1,3},{2,0},{3,1},{4,6},{5,7},{6,4},{7,5},{8,10},{9,11},{10,... | collective-permute-start | bytes 688136 | tf_op jit(solution)/shard_map/ppermute | solution.py:396
  65.0 5.5 %collective-permute-done.4 = bf16[2,2,32,896]{3,2,1,0:T(8,128)(2,1)S(1)} collective-permute-done((bf16[2,2,32,896]{3,2,1,0:T(8,128)(2,1)S(1)}, bf16[2,2,32,896]{3,2,1,0:T(8,128)(2,1)S(1)}, u32[]{:S(2)}, u32[]{:S(2)}) %collective-permute-start.4) | collective-permute-done | bytes 229408 | tf_op jit(solution)/shard_map/ppermute | solution.py:396
  73.2 1.9 collective-permute-start.6
  75.1 2.1 %collective-permute-start.7 = (bf16[1296,256]{1,0:T(8,128)(2,1)}, bf16[1296,256]{1,0:T(8,128)(2,1)}, u32[]{:S(2)}, u32[]{:S(2)}) collective-permute-start(bf16[1296,256]{1,0:T(8,128)(2,1)} %collective-permute-done), channel_id=1, source_target_pairs={{1,0},{2,3},{5,4},{6,7},{9,8},{10,11},{13,12},{14,15},{17,16},{18,... | collective-permute-start | bytes 1990664 | tf_op jit(solution)/shard_map/ppermute | solution.py:396
  77.3 2.2 %collective-permute-start.5 = (bf16[2,32,896]{2,1,0:T(8,128)(2,1)S(1)}, bf16[2,32,896]{2,1,0:T(8,128)(2,1)S(1)}, u32[]{:S(2)}, u32[]{:S(2)}) collective-permute-start(bf16[2,32,896]{2,1,0:T(8,128)(2,1)S(1)} %broadcast_select_fusion.6), channel_id=1, source_target_pairs={{0,4},{1,5},{2,6},{3,7},{4,0},{5,1},{6,2},{7,3},{8,12},{9,13},{10,... | collective-permute-start | bytes 344072 | tf_op jit(solution)/shard_map/ppermute | solution.py:396
  80.2 3.6 %collective-permute-start.9 = (bf16[1024,512]{1,0:T(8,128)(2,1)}, bf16[1024,512]{1,0:T(8,128)(2,1)}, u32[]{:S(2)}, u32[]{:S(2)}) collective-permute-start(bf16[1024,512]{1,0:T(8,128)(2,1)} %get-tuple-element.59.rows_ref.refs_0_.refs_5_), channel_id=1, source_target_pairs={{0,2},{1,3},{2,0},{3,1},{4,6},{5,7},{6,4},{7,5},{8,10},{9,11},{10,... | collective-permute-start | bytes 3145736 | tf_op jit(solution)/shard_map/ppermute | solution.py:396
  83.9 2.0 broadcast_in_dim.90
  85.9 6.9 %all-to-all-start.1 = ((bf16[16,2,64,768]{3,2,1,0:T(8,128)(2,1)}), bf16[16,2,64,768]{3,2,1,0:T(8,128)(2,1)S(1)}, u32[]{:S(2)}, u32[]{:S(2)}) async-start(bf16[16,2,64,768]{3,2,1,0:T(8,128)(2,1)} %broadcast_in_dim.90), calls=%async_computation.1 | async-start | bytes 6291456 | tf_op jit(solution)/shard_map/all_to_all | solution.py:419
  93.9 1.8 pad_maximum_fusion.coded_ref.refs_6_.refs_7_
  95.8 1.5 copy-done.1
  99.8 7.7 %keep_words.3.refs_11_ = s32[4,1024,128]{2,1,0:T(8,128)} custom-call(s32[6]{0:T(128)} %stack.66.pick_ref, bf16[4,1296,256]{2,1,0:T(8,128)(2,1)} %copy-done.1), custom_call_target="tpu_custom_call" | custom-call | flops 30000001024 | bytes 524288 | tf_op jit(solution)/shard_map/keep_words/pallas_call | solution.py:96
  107.4 19.7 %collective-permute-done.8.refs_1_ = bf16[1024,512]{1,0:T(8,128)(2,1)} collective-permute-done((bf16[1024,512]{1,0:T(8,128)(2,1)}, bf16[1024,512]{1,0:T(8,128)(2,1)}, u32[]{:S(2)}, u32[]{:S(2)}) %collective-permute-start.8) | collective-permute-done | bytes 1048608 | tf_op jit(solution)/shard_map/ppermute | solution.py:396
  127.1 7.2 %collective-permute-done.9.refs_2_ = bf16[1024,512]{1,0:T(8,128)(2,1)} collective-permute-done((bf16[1024,512]{1,0:T(8,128)(2,1)}, bf16[1024,512]{1,0:T(8,128)(2,1)}, u32[]{:S(2)}, u32[]{:S(2)}) %collective-permute-start.9) | collective-permute-done | bytes 1048608 | tf_op jit(solution)/shard_map/ppermute | solution.py:396
  134.3 1.4 slice_bitcast_fusion
  135.7 1.7 collective-permute-start.10
  137.5 5.8 %collective-permute-start.12 = (bf16[1024,512]{1,0:T(8,128)(2,1)}, bf16[1024,512]{1,0:T(8,128)(2,1)}, u32[]{:S(2)}, u32[]{:S(2)}) collective-permute-start(bf16[1024,512]{1,0:T(8,128)(2,1)} %collective-permute-done.9.refs_2_), channel_id=1, source_target_pairs={{1,0},{2,3},{5,4},{6,7},{9,8},{10,11},{13,12},{14,15},{17,16},{18,... | collective-permute-start | bytes 3145736 | tf_op jit(solution)/shard_map/ppermute | solution.py:396
  143.2 5.5 %collective-permute-start.13 = (bf16[1024,512]{1,0:T(8,128)(2,1)}, bf16[1024,512]{1,0:T(8,128)(2,1)}, u32[]{:S(2)}, u32[]{:S(2)}) collective-permute-start(bf16[1024,512]{1,0:T(8,128)(2,1)} %get-tuple-element.59.rows_ref.refs_0_.refs_5_), channel_id=1, source_target_pairs={{1,2},{2,1},{5,6},{6,5},{9,10},{10,9},{13,14},{14,13},{17,18},{18,... | collective-permute-start | bytes 3145736 | tf_op jit(solution)/shard_map/ppermute | solution.py:396
  150.5 5.2 %hub_rows.1 = bf16[64,256]{1,0:T(8,128)(2,1)} custom-call(s32[1]{0:T(128)} %bitcast.40.pick_ref, bf16[64,896]{1,0:T(8,128)(2,1)} %fusion.1.rows_ref, bf16[16,2,64,768]{3,2,1,0:T(8,128)(2,1)} %copy-done, bf16[16,64,768]{2,1,0:T(8,128)(2,1)} %collective-permute-done.10.far_ref.refs_9_), custom_call_target="tpu_custom_call" | custom-call | flops 1024 | bytes 1024 | tf_op jit(solution)/shard_map/hub_rows/pallas_call | solution.py:367
  155.6 1.6 broadcast_in_dim.92
  157.3 6.5 %all-to-all-start.2 = ((bf16[16,64,256]{2,1,0:T(8,128)(2,1)}), bf16[16,64,256]{2,1,0:T(8,128)(2,1)S(1)}, u32[]{:S(2)}, u32[]{:S(2)}) async-start(bf16[16,64,256]{2,1,0:T(8,128)(2,1)} %broadcast_in_dim.92), calls=%async_computation.2 | async-start | bytes 1048576 | tf_op jit(solution)/shard_map/all_to_all | solution.py:419
  163.8 9.2 %two.1 = (bf16[1024,1024]{1,0:T(8,128)(2,1)}, bf16[1024,1024]{1,0:T(8,128)(2,1)}, f32[1024,128]{1,0:T(8,128)}, f32[1024,256]{1,0:T(8,128)}) custom-call(s32[6]{0:T(128)} %stack.66.pick_ref, bf16[1024,512]{1,0:T(8,128)(2,1)} %get-tuple-element.59.rows_ref.refs_0_.refs_5_, bf16[16,2,64,768]{3,2,1,0:T(8,128)(2,1)} %copy-done, ...), custom_call_target="tpu_custom_call" | custom-call | flops 262144 | bytes 262144 | tf_op jit(solution)/shard_map/two/pallas_call | solution.py:222
  174.1 2.1 %collective-permute-start.11 = (bf16[1024,256]{1,0:T(8,128)(2,1)S(1)}, bf16[1024,256]{1,0:T(8,128)(2,1)S(1)}, u32[]{:S(2)}, u32[]{:S(2)}) collective-permute-start(bf16[1024,256]{1,0:T(8,128)(2,1)S(1)} %bitcast.56), channel_id=1, source_target_pairs={{0,4},{1,5},{2,6},{3,7},{4,0},{5,1},{6,2},{7,3},{8,12},{9,13},{10,... | collective-permute-start | bytes 1572872 | tf_op jit(solution)/shard_map/ppermute | solution.py:396
  176.2 1.5 collective-permute-done.11.refs_19_
  178.6 22.4 %finish.1 = bf16[1024,256]{1,0:T(8,128)(2,1)} custom-call(s32[6]{0:T(128)} %stack.66.pick_ref, bf16[1024,512]{1,0:T(8,128)(2,1)} %get-tuple-element.59.rows_ref.refs_0_.refs_5_, bf16[1024,512]{1,0:T(8,128)(2,1)} %collective-permute-done.8.refs_1_, bf16[1024,512]{1,0:T(8,128)(2,1)} %collective-permute-done.9.refs_2_, ...), custom_call_target="tpu_custom_call" | custom-call | flops 9663676416 | bytes 12582912 | tf_op jit(solution)/shard_map/finish/pallas_call | solution.py:294
  (55 shorter events, 13.6 us)
Async XLA Ops:
  0.0 14.9 %copy-start.4 = (s32[1,4]{1,0:T(1,128)S(1)}, s32[1,4]{1,0:T(1,128)}, u32[]{:S(2)}) copy-start(s32[1,4]{1,0:T(1,128)} %param.7) | copy-start | bytes 52
  5.1 39.1 %all-to-all-start = ((bf16[32,32,896]{2,1,0:T(8,128)(2,1)}), bf16[32,32,896]{2,1,0:T(8,128)(2,1)S(1)}, u32[]{:S(2)}, u32[]{:S(2)}) async-start(bf16[32,32,896]{2,1,0:T(8,128)(2,1)} %bitcast.54), calls=%async_computation | async-start | bytes 3670016 | tf_op jit(solution)/shard_map/all_to_all | solution.py:436
  12.9 30.0 %collective-permute-start = (bf16[1296,256]{1,0:T(8,128)(2,1)}, bf16[1296,256]{1,0:T(8,128)(2,1)}, u32[]{:S(2)}, u32[]{:S(2)}) collective-permute-start(bf16[1296,256]{1,0:T(8,128)(2,1)} %get-tuple-element.54), channel_id=1, source_target_pairs={{0,2},{1,3},{2,0},{3,1},{4,6},{5,7},{6,4},{7,5},{8,10},{9,11},{10,... | collective-permute-start | bytes 1990664 | tf_op jit(solution)/shard_map/ppermute | solution.py:396
  14.2 30.0 %collective-permute-start.1 = (bf16[1296,256]{1,0:T(8,128)(2,1)}, bf16[1296,256]{1,0:T(8,128)(2,1)S(1)}, u32[]{:S(2)}, u32[]{:S(2)}) collective-permute-start(bf16[1296,256]{1,0:T(8,128)(2,1)} %get-tuple-element.54), channel_id=1, source_target_pairs={{0,1},{1,0},{2,3},{3,2},{4,5},{5,4},{6,7},{7,6},{8,9},{9,8},{10,11... | collective-permute-start | bytes 1990664 | tf_op jit(solution)/shard_map/ppermute | solution.py:396
  23.2 6.2 %copy-start.5 = (s32[2]{0:T(128)S(1)}, s32[2]{0:T(128)}, u32[]{:S(2)}) copy-start(s32[2]{0:T(128)} %param.8) | copy-start | bytes 28
  44.2 0.8 copy-start.2
  45.1 7.8 %collective-permute-start.2 = (bf16[2,32,896]{2,1,0:T(8,128)(2,1)S(1)}, bf16[2,32,896]{2,1,0:T(8,128)(2,1)S(1)}, u32[]{:S(2)}, u32[]{:S(2)}) collective-permute-start(bf16[2,32,896]{2,1,0:T(8,128)(2,1)S(1)} %pad_maximum_fusion.4), channel_id=1, source_target_pairs={{0,128},{1,129},{2,130},{3,131},{4,132},{5,133},{6,134},{7,135},{8... | collective-permute-start | bytes 344072 | tf_op jit(solution)/shard_map/ppermute | solution.py:396
  52.9 4.3 %collective-permute-start.3 = (bf16[1,2,32,896]{3,2,1,0:T(8,128)(2,1)S(1)}, bf16[1,2,32,896]{3,2,1,0:T(8,128)(2,1)S(1)}, u32[]{:S(2)}, u32[]{:S(2)}) collective-permute-start(bf16[1,2,32,896]{3,2,1,0:T(8,128)(2,1)S(1)} %select_bitcast_fusion.1), channel_id=1, source_target_pairs={{0,1},{1,0},{2,3},{3,2},{4,5},{5,4},{6,7},{7,6},{8,9},{9,8},{10,11... | collective-permute-start | bytes 344072 | tf_op jit(solution)/shard_map/ppermute | solution.py:396
  57.4 13.1 %collective-permute-start.4 = (bf16[2,2,32,896]{3,2,1,0:T(8,128)(2,1)S(1)}, bf16[2,2,32,896]{3,2,1,0:T(8,128)(2,1)S(1)}, u32[]{:S(2)}, u32[]{:S(2)}) collective-permute-start(bf16[2,2,32,896]{3,2,1,0:T(8,128)(2,1)S(1)} %pad_maximum_fusion.2), channel_id=1, source_target_pairs={{0,2},{1,3},{2,0},{3,1},{4,6},{5,7},{6,4},{7,5},{8,10},{9,11},{10,... | collective-permute-start | bytes 688136 | tf_op jit(solution)/shard_map/ppermute | solution.py:396
  73.2 19.6 %collective-permute-start.6 = (bf16[1296,256]{1,0:T(8,128)(2,1)}, bf16[1296,256]{1,0:T(8,128)(2,1)}, u32[]{:S(2)}, u32[]{:S(2)}) collective-permute-start(bf16[1296,256]{1,0:T(8,128)(2,1)} %get-tuple-element.54), channel_id=1, source_target_pairs={{1,2},{2,1},{5,6},{6,5},{9,10},{10,9},{13,14},{14,13},{17,18},{18,... | collective-permute-start | bytes 1990664 | tf_op jit(solution)/shard_map/ppermute | solution.py:396
  75.1 17.7 %collective-permute-start.7 = (bf16[1296,256]{1,0:T(8,128)(2,1)}, bf16[1296,256]{1,0:T(8,128)(2,1)}, u32[]{:S(2)}, u32[]{:S(2)}) collective-permute-start(bf16[1296,256]{1,0:T(8,128)(2,1)} %collective-permute-done), channel_id=1, source_target_pairs={{1,0},{2,3},{5,4},{6,7},{9,8},{10,11},{13,12},{14,15},{17,16},{18,... | collective-permute-start | bytes 1990664 | tf_op jit(solution)/shard_map/ppermute | solution.py:396
  77.3 6.5 %collective-permute-start.5 = (bf16[2,32,896]{2,1,0:T(8,128)(2,1)S(1)}, bf16[2,32,896]{2,1,0:T(8,128)(2,1)S(1)}, u32[]{:S(2)}, u32[]{:S(2)}) collective-permute-start(bf16[2,32,896]{2,1,0:T(8,128)(2,1)S(1)} %broadcast_select_fusion.6), channel_id=1, source_target_pairs={{0,4},{1,5},{2,6},{3,7},{4,0},{5,1},{6,2},{7,3},{8,12},{9,13},{10,... | collective-permute-start | bytes 344072 | tf_op jit(solution)/shard_map/ppermute | solution.py:396
  80.1 47.0 %collective-permute-start.8 = (bf16[1024,512]{1,0:T(8,128)(2,1)}, bf16[1024,512]{1,0:T(8,128)(2,1)}, u32[]{:S(2)}, u32[]{:S(2)}) collective-permute-start(bf16[1024,512]{1,0:T(8,128)(2,1)} %get-tuple-element.59.rows_ref.refs_0_.refs_5_), channel_id=1, source_target_pairs={{0,1},{1,0},{2,3},{3,2},{4,5},{5,4},{6,7},{7,6},{8,9},{9,8},{10,11... | collective-permute-start | bytes 3145736 | tf_op jit(solution)/shard_map/ppermute | solution.py:396
  80.2 54.1 %collective-permute-start.9 = (bf16[1024,512]{1,0:T(8,128)(2,1)}, bf16[1024,512]{1,0:T(8,128)(2,1)}, u32[]{:S(2)}, u32[]{:S(2)}) collective-permute-start(bf16[1024,512]{1,0:T(8,128)(2,1)} %get-tuple-element.59.rows_ref.refs_0_.refs_5_), channel_id=1, source_target_pairs={{0,2},{1,3},{2,0},{3,1},{4,6},{5,7},{6,4},{7,5},{8,10},{9,11},{10,... | collective-permute-start | bytes 3145736 | tf_op jit(solution)/shard_map/ppermute | solution.py:396
  85.9 48.5 %all-to-all-start.1 = ((bf16[16,2,64,768]{3,2,1,0:T(8,128)(2,1)}), bf16[16,2,64,768]{3,2,1,0:T(8,128)(2,1)S(1)}, u32[]{:S(2)}, u32[]{:S(2)}) async-start(bf16[16,2,64,768]{3,2,1,0:T(8,128)(2,1)} %broadcast_in_dim.90), calls=%async_computation.1 | async-start | bytes 6291456 | tf_op jit(solution)/shard_map/all_to_all | solution.py:419
  95.8 1.5 copy-start.1
  134.3 16.2 %copy-start = (bf16[16,2,64,768]{3,2,1,0:T(8,128)(2,1)}, bf16[16,2,64,768]{3,2,1,0:T(8,128)(2,1)S(1)}, u32[]{:S(2)}) copy-start(bf16[16,2,64,768]{3,2,1,0:T(8,128)(2,1)S(1)} %all-to-all-done.1.near_ref.refs_8_) | copy-start | bytes 9437188
  135.7 14.7 %collective-permute-start.10 = (bf16[16,64,768]{2,1,0:T(8,128)(2,1)}, bf16[16,64,768]{2,1,0:T(8,128)(2,1)}, u32[]{:S(2)}, u32[]{:S(2)}) collective-permute-start(bf16[16,64,768]{2,1,0:T(8,128)(2,1)} %slice_bitcast_fusion), channel_id=1, source_target_pairs={{0,4},{1,5},{2,6},{3,7},{4,0},{5,1},{6,2},{7,3},{8,12},{9,13},{10,... | collective-permute-start | bytes 4718600 | tf_op jit(solution)/shard_map/ppermute | solution.py:396
  137.5 38.8 %collective-permute-start.12 = (bf16[1024,512]{1,0:T(8,128)(2,1)}, bf16[1024,512]{1,0:T(8,128)(2,1)}, u32[]{:S(2)}, u32[]{:S(2)}) collective-permute-start(bf16[1024,512]{1,0:T(8,128)(2,1)} %collective-permute-done.9.refs_2_), channel_id=1, source_target_pairs={{1,0},{2,3},{5,4},{6,7},{9,8},{10,11},{13,12},{14,15},{17,16},{18,... | collective-permute-start | bytes 3145736 | tf_op jit(solution)/shard_map/ppermute | solution.py:396
  143.2 33.0 %collective-permute-start.13 = (bf16[1024,512]{1,0:T(8,128)(2,1)}, bf16[1024,512]{1,0:T(8,128)(2,1)}, u32[]{:S(2)}, u32[]{:S(2)}) collective-permute-start(bf16[1024,512]{1,0:T(8,128)(2,1)} %get-tuple-element.59.rows_ref.refs_0_.refs_5_), channel_id=1, source_target_pairs={{1,2},{2,1},{5,6},{6,5},{9,10},{10,9},{13,14},{14,13},{17,18},{18,... | collective-permute-start | bytes 3145736 | tf_op jit(solution)/shard_map/ppermute | solution.py:396
  157.3 16.8 %all-to-all-start.2 = ((bf16[16,64,256]{2,1,0:T(8,128)(2,1)}), bf16[16,64,256]{2,1,0:T(8,128)(2,1)S(1)}, u32[]{:S(2)}, u32[]{:S(2)}) async-start(bf16[16,64,256]{2,1,0:T(8,128)(2,1)} %broadcast_in_dim.92), calls=%async_computation.2 | async-start | bytes 1048576 | tf_op jit(solution)/shard_map/all_to_all | solution.py:419
  174.1 3.7 %copy-start.3 = (bf16[16,64,256]{2,1,0:T(8,128)(2,1)}, bf16[16,64,256]{2,1,0:T(8,128)(2,1)S(1)}, u32[]{:S(2)}) copy-start(bf16[16,64,256]{2,1,0:T(8,128)(2,1)S(1)} %all-to-all-done.2) | copy-start | bytes 1572868
  174.1 3.7 %collective-permute-start.11 = (bf16[1024,256]{1,0:T(8,128)(2,1)S(1)}, bf16[1024,256]{1,0:T(8,128)(2,1)S(1)}, u32[]{:S(2)}, u32[]{:S(2)}) collective-permute-start(bf16[1024,256]{1,0:T(8,128)(2,1)S(1)} %bitcast.56), channel_id=1, source_target_pairs={{0,4},{1,5},{2,6},{3,7},{4,0},{5,1},{6,2},{7,3},{8,12},{9,13},{10,... | collective-permute-start | bytes 1572872 | tf_op jit(solution)/shard_map/ppermute | solution.py:396
  177.8 0.8 copy-start.6
